TPU v7x, 512 devices: a whole 4x4x16 slice. The times are simulated.
512 devices in a mesh: atom: 64 (over y, z_lo, x), wave: 8 (over z_hi, core).
Axes of the slice: x: 4, y: 4, z: 16 (z_hi: 4, z_lo: 4; z = z_hi * 4 + z_lo), core: 2. Of those that a mesh axis runs over, the one named last changes fastest.
Arguments:
- features: bfloat16 [131072, 256], P('atom'), may hold values from -6 to 6
- coords: int32 [3, 131072], P(None, 'atom'), may hold values from 0 to 65535
- miller: int32 [3, 4096], P(None, 'wave'), may hold values from -8 to 8
- filter_weights: float32 [4096, 256], P('wave'), may hold values from -6 to 6
- norm_gain: float32 [256], replicated, may hold values from 0.1 to 1.9
- w_in: bfloat16 [256, 256], replicated, may hold values from -0.375 to 0.375
- w_out: bfloat16 [256, 256], replicated, may hold values from -0.375 to 0.375
Outputs:
- updated_features: bfloat16 [131072, 256], P(('atom', 'wave'))
All inputs are finite; a program needn't handle non-finite values.
Results may differ from a plain program's by a relative error of at most 0.013.
Values may be sent and summed in bfloat16 or wider, within the bound.
No kernel may reach another device: no remote copies, remote signals or barrier semaphores. Data moves between devices by JAX's collectives and lax.ppermute only.
A program may use at most 64 MiB of HBM per device.

v0:
```python
import math

import jax
import jax.numpy as jnp
from jax import lax
from jax.sharding import PartitionSpec as P

K = 4096


def cut_along(shard, dim, peers):
    lengths = shard.shape
    pieces = shard.reshape(*lengths[:dim], peers, lengths[dim] // peers, *lengths[dim + 1 :])
    return jnp.moveaxis(pieces, dim, 0)


def summed_on_arrival(shard, axis, dim):
    pieces = cut_along(shard, dim, lax.axis_size(axis))
    arrived = lax.all_to_all(pieces, axis, split_axis=0, concat_axis=0, tiled=True)
    return arrived.sum(axis=0)


def joined_along(pieces, dim):
    lengths = list(pieces.shape[1:])
    lengths[dim] *= pieces.shape[0]
    return jnp.moveaxis(pieces, 0, dim).reshape(lengths)


def sent_to_all(shard, axis):
    copies = jnp.broadcast_to(shard, (lax.axis_size(axis), *shard.shape))
    return lax.all_to_all(copies, axis, split_axis=0, concat_axis=0, tiled=True)


def gather_directly(shard, axis, dim):
    return joined_along(sent_to_all(shard, axis), dim)


def phase_tables(miller_block, coords):
    steps = miller_block[0][:, None] * coords[0][None, :]
    steps = steps + miller_block[1][:, None] * coords[1][None, :]
    steps = steps + miller_block[2][:, None] * coords[2][None, :]
    steps = jnp.mod(steps, 65536)
    angles = steps.astype(jnp.float32) * (2.0 * math.pi / 65536.0)
    tables = jnp.stack([jnp.cos(angles), jnp.sin(angles)], axis=1).astype(jnp.bfloat16)
    return tables.reshape(tables.shape[0] * 2, tables.shape[2])


def filter_factors(factors, weights):
    power = jnp.mean(factors * factors, axis=(1, 2), keepdims=True)
    scaled = factors / jnp.sqrt(power + 1e-05)
    return (scaled * weights[:, None, :]).astype(jnp.bfloat16)


def spread_back(tables, filtered):
    width = filtered.shape[2]
    return lax.dot_general(
        tables,
        filtered.reshape(filtered.shape[0] * 2, width),
        (((0,), (0,)), ((), ())),
        preferred_element_type=jnp.float32,
    )


def on_device(features, coords, miller, filter_weights, norm_gain, w_in, w_out):
    width = features.shape[1]
    wave_count = miller.shape[1]
    tables = phase_tables(miller, coords)
    partial_sums = jnp.dot(tables, features, preferred_element_type=jnp.float32).reshape(
        wave_count, 2, width
    )
    share_rows = wave_count // lax.axis_size("atom")
    shares = summed_on_arrival(partial_sums, "atom", 0)
    own_weights = lax.dynamic_slice_in_dim(
        filter_weights, lax.axis_index("atom") * share_rows, share_rows, 0
    )
    own_filtered = filter_factors(shares, own_weights)
    filtered = gather_directly(own_filtered, "atom", 0)
    message = spread_back(tables, filtered)
    summed = lax.psum_scatter(
        message.astype(jnp.bfloat16), "wave", scatter_dimension=0, tiled=True
    ).astype(jnp.float32)
    own_count = summed.shape[0]
    own_features = lax.dynamic_slice_in_dim(
        features, lax.axis_index("wave") * own_count, own_count, 0
    )
    updated = own_features.astype(jnp.float32) + summed / math.sqrt(K)
    normed = (
        updated / jnp.sqrt(jnp.mean(updated * updated, axis=1, keepdims=True) + 1e-06) * norm_gain
    ).astype(jnp.bfloat16)
    hidden = jax.nn.silu(jnp.dot(normed, w_in, preferred_element_type=jnp.float32)).astype(
        jnp.bfloat16
    )
    return (updated + jnp.dot(hidden, w_out, preferred_element_type=jnp.float32)).astype(
        jnp.bfloat16
    )


def solution(mesh):
    in_specs = (P("atom", None), P(None, "atom"), P(None, "wave"), P("wave", None), P(), P(), P())
    out_specs = P(("atom", "wave"), None)
    return jax.shard_map(
        on_device, mesh=mesh, in_specs=in_specs, out_specs=out_specs, check_vma=False
    )
```

profile of v0, /device:TPU:1, one launch (start us, length us, event | category | flops | bytes accessed | tf_op | source)
XLA Modules:
  0.0 182.6 jit_solution(9306827987991250151)
XLA Ops:
  6.5 0.0 copy-start
  6.5 0.0 copy-start.1
  6.5 0.9 slice_reduce_fusion.2
  7.4 0.9 fusion.22
  8.3 0.1 mul.202
  8.4 0.1 mul.206
  8.5 0.1 mul.210
  8.6 17.9 %cosine_convert_fusion = (bf16[64,8,1,2048]{3,1,2,0:T(8,128)(2,1)S(1)}, bf16[64,8,1,2048]{3,1,2,0:T(8,128)(2,1)S(1)}) fusion(s32[2048]{0:T(1024)S(1)} %bitcast.17, s32[64,8]{1,0:T(8,128)S(1)} %mul.210, s32[2048]{0:T(1024)S(1)} %bitcast.19, s32[64,8]{1,0:T(8,128)S(1)} %mul.206, s32[2048]{0:T(1024)S(1)} %bitcast.15, s32[64,8]{1,0:T(8,128)S(1)} %mul.202), kind=kLoop, calls=%fused_computation.18 | loop fusion | flops 20971520 | bytes 4225024 | tf_op jit(solution)/shard_map/convert
  26.5 0.0 copy-done.1
  26.5 2.3 %fusion.6 = f32[64,8,2,256]{3,1,2,0:T(8,128)} fusion(bf16[64,8,1,2048]{3,1,2,0:T(8,128)(2,1)S(1)} %get-tuple-element.9, bf16[64,8,1,2048]{3,1,2,0:T(8,128)(2,1)S(1)} %get-tuple-element.8, bf16[2048,256]{1,0:T(8,128)(2,1)S(1)} %copy-done.1), kind=kOutput, calls=%fused_computation.13 | convolution fusion | flops 1075838976 | bytes 6291456 | tf_op jit(solution)/shard_map/dot_general | solution.py:68
  28.7 12.5 %all-to-all-start = ((f32[64,8,2,256]{3,1,2,0:T(8,128)}), f32[64,8,2,256]{3,1,2,0:T(8,128)S(1)}, u32[]{:S(2)}, u32[]{:S(2)}) async-start(f32[64,8,2,256]{3,1,2,0:T(8,128)} %fusion.6), calls=%async_computation | async-start | bytes 2097152 | tf_op jit(solution)/shard_map/all_to_all | solution.py:19
  41.3 0.0 copy-done
  41.3 28.1 %all-to-all-done = f32[64,8,2,256]{3,1,2,0:T(8,128)S(1)} async-done(((f32[64,8,2,256]{3,1,2,0:T(8,128)}), f32[64,8,2,256]{3,1,2,0:T(8,128)S(1)}, u32[]{:S(2)}, u32[]{:S(2)}) %all-to-all-start) | async-done | bytes 1048608 | tf_op jit(solution)/shard_map/all_to_all | solution.py:19
  69.4 0.1 reduce_sum.27
  69.5 0.1 multiply_reduce_fusion.1
  69.6 0.1 multiply_convert_fusion.8
  69.7 1.1 broadcast_in_dim.2
  70.9 5.8 %all-to-all-start.1 = ((bf16[64,8,2,256]{3,2,1,0:T(2,128)(2,1)}), bf16[64,8,2,256]{3,2,1,0:T(2,128)(2,1)S(1)}, u32[]{:S(2)}, u32[]{:S(2)}) async-start(bf16[64,8,2,256]{3,2,1,0:T(2,128)(2,1)} %broadcast_in_dim.2), calls=%async_computation.1 | async-start | bytes 1048576 | tf_op jit(solution)/shard_map/all_to_all | solution.py:31
  76.7 0.2 reduce-scatter.2.cloned.1.call-start
  76.9 18.0 %cosine_convert_fusion.1 = (bf16[512,1,2048]{2,0,1:T(8,128)(2,1)S(1)}, bf16[512,1,2048]{2,0,1:T(8,128)(2,1)S(1)}) fusion(s32[2048]{0:T(1024)S(1)} %bitcast.18, s32[512]{0:T(512)S(1)} %bitcast.22, s32[2048]{0:T(1024)S(1)} %bitcast.20, s32[512]{0:T(512)S(1)} %bitcast.23, s32[2048]{0:T(1024)S(1)} %bitcast.16, s32[512]{0:T(512)S(1)} %bitcast.21), kind=kLoop, calls=%fused_computation.20 | loop fusion | flops 20971520 | bytes 4225024 | tf_op jit(solution)/shard_map/convert.2
  94.9 0.4 pad_maximum_fusion
  95.3 6.3 %copy.10 = bf16[512,2,2048]{2,1,0:T(2,128)(2,1)} copy(bf16[512,2,2048]{2,0,1:T(8,128)(2,1)S(1)} %pad_maximum_fusion) | data formatting | bytes 8388608 | tf_op jit(solution)/shard_map/stack | solution.py:44
  101.6 7.2 %convert_element_type.59 = bf16[1024,2048]{1,0:T(8,128)(2,1)} reshape(bf16[512,2,2048]{2,1,0:T(2,128)(2,1)} %copy.10) | data formatting | bytes 8388608 | tf_op jit(solution)/shard_map/convert_element_type | solution.py:44
  108.8 0.0 all-to-all-done.1
  108.8 0.2 reshape_reshape.4
  109.0 0.0 copy-start.2
  109.0 0.0 copy-start.3
  109.0 0.0 copy-start.4
  109.0 4.5 %convolution_convert_fusion = bf16[2048,256]{1,0:T(8,128)(2,1)} fusion(bf16[1024,2048]{1,0:T(8,128)(2,1)} %convert_element_type.59, bf16[1024,256]{1,0:T(8,128)(2,1)S(1)} %reshape_reshape.4), kind=kOutput, calls=%fused_computation.21 | convolution fusion | flops 1074266112 | bytes 5767168 | tf_op jit(solution)/shard_map/dot_general | solution.py:56
  113.6 0.0 reduce-scatter.2.cloned.1.call-update
  113.6 59.1 %reduce-scatter.2.cloned.1.call-done = bf16[256,256]{1,0:T(8,128)(2,1)} async-done(((bf16[2048,256]{1,0:T(8,128)(2,1)}), bf16[256,256]{1,0:T(8,128)(2,1)}) %reduce-scatter.2.cloned.1.call-update) | async-done | bytes 131088 | tf_op jit(solution)/shard_map/reduce_scatter | solution.py:79
  172.7 1.0 multiply_reduce_fusion
  173.7 0.0 copy-done.2
  173.7 0.0 copy-done.3
  173.8 0.0 copy-done.4
  173.8 2.0 %fusion.10 = bf16[256,256]{1,0:T(8,128)(2,1)} fusion(bf16[256,256]{1,0:T(8,128)(2,1)S(1)} %copy-done.2, bf16[256,256]{1,0:T(8,128)(2,1)} %reduce-scatter.2.cloned.1.call-done, bf16[256,256]{1,0:T(8,128)(2,1)S(1)} %copy-done.3, f32[256]{0:T(256)S(1)} %copy-done.4, f32[256]{0:T(256)S(1)} %add_sqrt_fusion, bf16[2048,256]{1,0:T(8,128)(2,1)S(1)} %copy-done.1, ...), kind=kOutput, calls=%fused_computation.23 | convolution fusion | flops 68288512 | bytes 920576 | tf_op jit(solution)/shard_map/dot_general | solution.py:93
  (4 shorter events, 0.0 us)
Async XLA Ops:
  6.5 34.7 %copy-start = (f32[512,256]{1,0:T(8,128)S(1)}, f32[512,256]{1,0:T(8,128)}, u32[]{:S(2)}) copy-start(f32[512,256]{1,0:T(8,128)} %param.10) | copy-start | bytes 1572868
  6.5 19.9 %copy-start.1 = (bf16[2048,256]{1,0:T(8,128)(2,1)S(1)}, bf16[2048,256]{1,0:T(8,128)(2,1)}, u32[]{:S(2)}) copy-start(bf16[2048,256]{1,0:T(8,128)(2,1)} %param.7) | copy-start | bytes 3145732
  28.7 40.7 %all-to-all-start = ((f32[64,8,2,256]{3,1,2,0:T(8,128)}), f32[64,8,2,256]{3,1,2,0:T(8,128)S(1)}, u32[]{:S(2)}, u32[]{:S(2)}) async-start(f32[64,8,2,256]{3,1,2,0:T(8,128)} %fusion.6), calls=%async_computation | async-start | bytes 2097152 | tf_op jit(solution)/shard_map/all_to_all | solution.py:19
  70.9 37.9 %all-to-all-start.1 = ((bf16[64,8,2,256]{3,2,1,0:T(2,128)(2,1)}), bf16[64,8,2,256]{3,2,1,0:T(2,128)(2,1)S(1)}, u32[]{:S(2)}, u32[]{:S(2)}) async-start(bf16[64,8,2,256]{3,2,1,0:T(2,128)(2,1)} %broadcast_in_dim.2), calls=%async_computation.1 | async-start | bytes 1048576 | tf_op jit(solution)/shard_map/all_to_all | solution.py:31
  76.7 96.0 %reduce-scatter.2.cloned.1.call-start = ((), (), s32[]{:S(2)}) async-start(), calls=%async_computation.3 | async-start | bytes 1179648 | tf_op jit(solution)/shard_map/reduce_scatter | solution.py:79
  109.0 64.7 %copy-start.2 = (bf16[256,256]{1,0:T(8,128)(2,1)S(1)}, bf16[256,256]{1,0:T(8,128)(2,1)}, u32[]{:S(2)}) copy-start(bf16[256,256]{1,0:T(8,128)(2,1)} %param.13) | copy-start | bytes 393220
  109.0 64.7 %copy-start.3 = (bf16[256,256]{1,0:T(8,128)(2,1)S(1)}, bf16[256,256]{1,0:T(8,128)(2,1)}, u32[]{:S(2)}) copy-start(bf16[256,256]{1,0:T(8,128)(2,1)} %param.12) | copy-start | bytes 393220
  109.0 64.7 %copy-start.4 = (f32[256]{0:T(256)S(1)}, f32[256]{0:T(256)}, u32[]{:S(2)}) copy-start(f32[256]{0:T(256)} %param.11) | copy-start | bytes 3076
Sparse Core Ops, SparseCore 0:
  113.7 58.9 reduce-scatter.1
where the time goes:
time: 184 us; the launch traced here: 183 us
  waiting for transfers between devices  87.2 us (47%)
  other arithmetic  37.6 us (20%)
  starting transfers between devices  18.5 us (10%)
  local copies, waits for them, and re-layouts  16.9 us (9%)
  between operations  13.6 us (7%)
  matrix products  8.84 us (5%)
    reduce_scatter x1, waiting for transfers between devices, on_device(): lax.psum_scatter(message.astype(jnp.bfloat16), 'wave', scatter_dimension=...  59.1 us
    another operation x2, other arithmetic  35.9 us
    all_to_all x1, waiting for transfers between devices, summed_on_arrival(): lax.all_to_all(pieces, axis, split_axis=0, concat_axis=0, tiled=True)  28.1 us
    all_to_all x1, starting transfers between devices, summed_on_arrival(): lax.all_to_all(pieces, axis, split_axis=0, concat_axis=0, tiled=True)  12.5 us
    convert_element_type x1, local copies, waits for them, and re-layouts, phase_tables(): jnp.stack([jnp.cos(angles), jnp.sin(angles)], axis=1).astype(jnp.bfloat16)  7.21 us
    another operation x1, local copies, waits for them, and re-layouts, phase_tables(): jnp.stack([jnp.cos(angles), jnp.sin(angles)], axis=1).astype(jnp.bfloat16)  6.28 us
    all_to_all x1, starting transfers between devices, sent_to_all(): return lax.all_to_all(copies, axis, split_axis=0, concat_axis=0, tiled=True)  5.79 us
    dot_general x1, matrix products, spread_back(): lax.dot_general(tables, filtered.reshape(filtered.shape[0] * 2, width), (...  4.54 us
  transfers between devices with their start and end apart: 3, of which 2 were waited for; matrix products, arithmetic and copies ran while one was open for 17% of the time, Pallas kernels for 0%

commit v1 on v0

v1 whole, which is shorter than its diff:
```python
import itertools
import math

import jax
import jax.numpy as jnp
import numpy as np
from jax import lax
from jax.experimental import pallas as pl
from jax.experimental.pallas import tpu as pltpu
from jax.sharding import PartitionSpec as P

K = 4096
KMAX = 8
SIDE = 2 * KMAX + 1
PLANE = SIDE * SIDE
HALF = PLANE // 2
STRIP = 24
SHARDS = 8
POINTS = 320
PLANES = 16
LAYERS = 4
OWN = POINTS // (PLANES * LAYERS)
ROWS = 2 * POINTS
F = 256
TILE = 512
AXES = ("atom", "wave")
BOTH = (((1,), (0,)), ((), ()))
OUTER = (((0,), (0,)), ((), ()))


def device(y, z_lo, x, z_hi, core):
    return (((y * 4 + z_lo) * 4 + x) * 4 + z_hi) * 2 + core


FOUR = range(4)
TWO = range(2)
GROUPS_XY = [
    [device(y, l, x, h, c) for y in FOUR for x in FOUR] for l in FOUR for h in FOUR for c in TWO
]
GROUPS_LO = [
    [device(y, l, x, h, c) for l in FOUR] for y in FOUR for x in FOUR for h in FOUR for c in TWO
]
GROUPS_Z = [
    [device(y, l, x, h, c) for h in FOUR for l in FOUR] for y in FOUR for x in FOUR for c in TWO
]
SWAP = [
    (device(y, l, x, h, c), device(y, l, x, h, 1 - c))
    for y, l, x, h, c in itertools.product(FOUR, FOUR, FOUR, FOUR, TWO)
]


def wavevector(shard, point):
    if point < PLANE:
        return point // SIDE - KMAX, point % SIDE - KMAX, shard + 1
    strip = shard * STRIP + point - PLANE
    if point - PLANE >= STRIP or strip > HALF:
        return None
    return (strip + HALF) // SIDE - KMAX, (strip + HALF) % SIDE - KMAX, 0


def row_steps(shard):
    steps = np.zeros((8, ROWS), np.float32)
    for row in range(ROWS):
        chunk, part, own = row // (2 * OWN), row % (2 * OWN) // OWN, row % OWN
        vector = wavevector(shard, chunk * OWN + own)
        if vector is None:
            steps[6, row] = -0.25
            continue
        steps[0:3, row] = vector
        steps[3:6, row] = vector
        steps[6, row] = -0.25 * part
    return steps


def split_coords(coords):
    high = (coords >> 8).astype(jnp.float32) * (1.0 / 256.0)
    low = (coords & 255).astype(jnp.float32) * (1.0 / 65536.0)
    ones = jnp.ones((2, coords.shape[1]), jnp.float32)
    return jnp.concatenate([high, low, ones], axis=0).astype(jnp.bfloat16)


def cosine_coefficients():
    nodes = 0.125 + 0.125 * np.cos(np.pi * (np.arange(400) + 0.5) / 400)
    fit = np.polynomial.chebyshev.Chebyshev.fit(
        nodes, np.cos(2 * np.pi * np.sqrt(nodes)), 6, domain=[0, 0.25]
    )
    return [float(c) for c in fit.convert(kind=np.polynomial.Polynomial).coef]


COSINE = cosine_coefficients()


def cosine_of_turns(turns):
    left = turns - jnp.round(turns)
    square = left * left
    total = jnp.full_like(square, COSINE[-1])
    for c in COSINE[-2::-1]:
        total = total * square + c
    return total


def factors_kernel(place_ref, steps_ref, coords_ref, features_ref, out_ref, tables, total):
    tile = pl.program_id(0)
    parts = split_coords(coords_ref[...])
    steps = steps_ref[0].astype(jnp.bfloat16)
    block = 128
    for start in range(0, ROWS, block):
        turns = lax.dot_general(
            steps[:, start : start + block], parts, OUTER, preferred_element_type=jnp.float32
        )
        tables[start : start + block, :] = cosine_of_turns(turns).astype(jnp.bfloat16)
    added = jnp.dot(tables[...], features_ref[...], preferred_element_type=jnp.float32)

    @pl.when(tile == 0)
    def _():
        total[...] = added

    @pl.when(tile > 0)
    def _():
        total[...] += added

    @pl.when(tile == pl.num_programs(0) - 1)
    def _():
        out_ref[...] = total[...].astype(jnp.bfloat16)


def partial_factors(place, steps, coords, features):
    atoms = features.shape[0]
    return pl.pallas_call(
        factors_kernel,
        out_shape=jax.ShapeDtypeStruct((ROWS, F), jnp.bfloat16),
        grid_spec=pltpu.PrefetchScalarGridSpec(
            num_scalar_prefetch=1,
            grid=(atoms // TILE,),
            in_specs=[
                pl.BlockSpec((1, 8, ROWS), lambda t, place: (place[0], 0, 0)),
                pl.BlockSpec((3, TILE), lambda t, place: (0, t)),
                pl.BlockSpec((TILE, F), lambda t, place: (t, 0)),
            ],
            out_specs=pl.BlockSpec((ROWS, F), lambda t, place: (0, 0)),
            scratch_shapes=[
                pltpu.VMEM((ROWS, TILE), jnp.bfloat16),
                pltpu.VMEM((ROWS, F), jnp.float32),
            ],
        ),
        cost_estimate=pl.CostEstimate(
            flops=2 * ROWS * atoms * F, bytes_accessed=atoms * F * 2, transcendentals=0
        ),
        name="factors",
    )(place, steps, coords, features)


WROWS = 32


def weights_kernel(place_ref, miller_ref, weights_ref, own_ref, other_ref):
    core, plane, layer = place_ref[1], place_ref[2], place_ref[3]
    m0, m1, m2 = miller_ref[0:1, :], miller_ref[1:2, :], miller_ref[2:3, :]
    flat = (m0 + KMAX) * SIDE + (m1 + KMAX)
    flip = (m2 < 0) | ((m2 == 0) & (flat < HALF))
    flat = jnp.where(flip, 2 * HALF - flat, flat)
    strip = flat - HALF
    strip_shard = (
        (strip >= STRIP).astype(jnp.int32)
        + (strip >= 2 * STRIP).astype(jnp.int32)
        + (strip >= 3 * STRIP).astype(jnp.int32)
        + (strip >= 4 * STRIP).astype(jnp.int32)
        + (strip >= 5 * STRIP).astype(jnp.int32)
        + (strip >= 6 * STRIP).astype(jnp.int32)
    )
    shard = jnp.where(m2 == 0, strip_shard, jnp.abs(m2) - 1)
    point = jnp.where(m2 == 0, PLANE + strip - strip_shard * STRIP, flat)
    spot = shard * POINTS + point
    row = lax.broadcasted_iota(jnp.int32, (WROWS, miller_ref.shape[1]), 0)
    high = (
        (row >= OWN).astype(jnp.int32)
        + (row >= 2 * OWN).astype(jnp.int32)
        + (row >= 3 * OWN).astype(jnp.int32)
    )
    base = (plane * LAYERS + layer) * OWN + row - high * OWN
    weights = weights_ref[...]
    upper = weights.astype(jnp.bfloat16)
    lower = (weights - upper.astype(jnp.float32)).astype(jnp.bfloat16)
    for held, out_ref in ((core, own_ref), (1 - core, other_ref)):
        wanted = (high * 2 + held) * POINTS + base
        match = jnp.where((wanted == spot) & (row < 4 * OWN), 1.0, 0.0).astype(jnp.bfloat16)
        summed = jnp.dot(match, upper, preferred_element_type=jnp.float32)
        summed += jnp.dot(match, lower, preferred_element_type=jnp.float32)
        out_ref[...] = summed.astype(jnp.bfloat16)


def grid_weights(place, miller, weights):
    shape = jax.ShapeDtypeStruct((WROWS, F), jnp.bfloat16)
    return pl.pallas_call(
        weights_kernel,
        out_shape=(shape, shape),
        in_specs=[
            pl.BlockSpec(memory_space=pltpu.SMEM),
            pl.BlockSpec(memory_space=pltpu.VMEM),
            pl.BlockSpec(memory_space=pltpu.VMEM),
        ],
        out_specs=(pl.BlockSpec(memory_space=pltpu.VMEM),) * 2,
        cost_estimate=pl.CostEstimate(
            flops=8 * WROWS * 512 * F, bytes_accessed=512 * F * 4, transcendentals=0
        ),
        name="grid_weights",
    )(place, miller, weights)


def plane_sum_kernel(arrived_ref, out_ref, total):
    total[...] = jnp.sum(arrived_ref[...].astype(jnp.float32), axis=0)
    for layer in range(LAYERS):
        rows = total[layer * 2 * OWN : (layer + 1) * 2 * OWN, :]
        out_ref[layer] = rows.astype(jnp.bfloat16)


def plane_sum(arrived):
    rows = 2 * OWN * LAYERS
    return pl.pallas_call(
        plane_sum_kernel,
        out_shape=jax.ShapeDtypeStruct((LAYERS, 2 * OWN, F), jnp.bfloat16),
        in_specs=[pl.BlockSpec(memory_space=pltpu.VMEM)],
        out_specs=pl.BlockSpec(memory_space=pltpu.VMEM),
        scratch_shapes=[pltpu.VMEM((rows, F), jnp.float32)],
        name="plane_sum",
    )(arrived)


PACKED = 32


def scale_kernel(arrived_ref, own_ref, other_ref, out_ref, packed):
    total = jnp.sum(arrived_ref[...].astype(jnp.float32), axis=0)
    cosines, sines = total[:OWN], total[OWN:]
    power = jnp.sum(cosines * cosines + sines * sines, axis=1, keepdims=True) * (1.0 / (2 * F))
    scale = 1.0 / jnp.sqrt(power + 1e-05)
    packed[0:OWN, :] = cosines * scale
    packed[OWN : 2 * OWN, :] = sines * scale
    weights = own_ref[...].astype(jnp.float32) + other_ref[...].astype(jnp.float32)
    packed[2 * OWN : 6 * OWN, :] = weights[: 4 * OWN]
    packed[6 * OWN :, :] = jnp.zeros((PACKED - 6 * OWN, F), jnp.float32)
    sent = packed[...].astype(jnp.bfloat16)
    for peer in range(PLANES):
        out_ref[peer] = sent


def scale_factors(arrived, own, other):
    return pl.pallas_call(
        scale_kernel,
        out_shape=jax.ShapeDtypeStruct((PLANES, PACKED, F), jnp.bfloat16),
        in_specs=[pl.BlockSpec(memory_space=pltpu.VMEM)] * 3,
        out_specs=pl.BlockSpec(memory_space=pltpu.VMEM),
        scratch_shapes=[pltpu.VMEM((PACKED, F), jnp.float32)],
        name="scale_factors",
    )(arrived, own, other)


COLUMN = 2 * OWN * PLANES


def column_picks():
    factor = np.zeros((COLUMN, PLANES * PACKED), np.float32)
    weight = np.zeros((COLUMN, PLANES * PACKED), np.float32)
    for row in range(COLUMN):
        rank, spot = row // (2 * OWN), row % (2 * OWN)
        high, low = rank // LAYERS, rank % LAYERS
        factor[row, rank * PACKED + spot] = 1
        for source in range(4):
            at = (source * LAYERS + low) * PACKED + 2 * OWN + high * OWN + spot % OWN
            weight[row, at] = 1
    return factor, weight


def filter_kernel(arrived_ref, factor_ref, weight_ref, out_ref):
    arrived = arrived_ref[...]
    factors = jnp.dot(factor_ref[...], arrived, preferred_element_type=jnp.float32)
    weights = jnp.dot(weight_ref[...], arrived, preferred_element_type=jnp.float32)
    filtered = (factors * weights).astype(jnp.bfloat16)
    for peer in range(PLANES):
        out_ref[peer] = filtered


def filter_column(arrived, factor, weight):
    return pl.pallas_call(
        filter_kernel,
        out_shape=jax.ShapeDtypeStruct((PLANES, COLUMN, F), jnp.bfloat16),
        in_specs=[pl.BlockSpec(memory_space=pltpu.VMEM)] * 3,
        out_specs=pl.BlockSpec(memory_space=pltpu.VMEM),
        name="filter_column",
    )(arrived, factor, weight)


ALL_ROWS = COLUMN * PLANES


def tables_kernel(place_ref, steps_ref, coords_ref, out_ref):
    parts = split_coords(coords_ref[...])
    steps = steps_ref[0].astype(jnp.bfloat16)
    block = 128
    for start in range(0, TILE, block):
        turns = lax.dot_general(
            parts[:, start : start + block], steps, OUTER, preferred_element_type=jnp.float32
        )
        out_ref[start : start + block, :] = cosine_of_turns(turns).astype(jnp.bfloat16)


def message_tables(place, steps, coords):
    width = 512
    return pl.pallas_call(
        tables_kernel,
        out_shape=jax.ShapeDtypeStruct((TILE, ALL_ROWS), jnp.bfloat16),
        grid_spec=pltpu.PrefetchScalarGridSpec(
            num_scalar_prefetch=1,
            grid=(ALL_ROWS // width,),
            in_specs=[
                pl.BlockSpec((1, 8, width), lambda t, place: (place[1], 0, t)),
                pl.BlockSpec((3, TILE), lambda t, place: (0, place[4])),
            ],
            out_specs=pl.BlockSpec((TILE, width), lambda t, place: (0, t)),
        ),
        cost_estimate=pl.CostEstimate(
            flops=16 * TILE * ALL_ROWS, bytes_accessed=TILE * ALL_ROWS * 2, transcendentals=0
        ),
        name="message_tables",
    )(place, steps, coords)


def message_kernel(place_ref, tables_ref, filtered_ref, own_ref, other_ref, total):
    core = place_ref[1]
    total[...] = jnp.dot(tables_ref[...], filtered_ref[...], preferred_element_type=jnp.float32)
    half = TILE // 2
    own_ref[...] = total[pl.ds(pl.multiple_of(core * half, half), half), :]
    other = total[pl.ds(pl.multiple_of((1 - core) * half, half), half), :]
    other_ref[...] = other.astype(jnp.bfloat16)


def message_parts(place, tables, filtered):
    half = TILE // 2
    return pl.pallas_call(
        message_kernel,
        out_shape=(
            jax.ShapeDtypeStruct((half, F), jnp.float32),
            jax.ShapeDtypeStruct((half, F), jnp.bfloat16),
        ),
        in_specs=[
            pl.BlockSpec(memory_space=pltpu.SMEM),
            pl.BlockSpec(memory_space=pltpu.VMEM),
            pl.BlockSpec(memory_space=pltpu.VMEM),
        ],
        out_specs=(pl.BlockSpec(memory_space=pltpu.VMEM),) * 2,
        scratch_shapes=[pltpu.VMEM((TILE, F), jnp.float32)],
        name="message",
    )(place, tables, filtered)


def update_kernel(
    place_ref, features_ref, own_ref, other_ref, gain_ref, w_in_ref, w_out_ref, out_ref
):
    message = own_ref[...] + other_ref[...].astype(jnp.float32)
    updated = features_ref[...].astype(jnp.float32) + message * (1.0 / math.sqrt(K))
    power = jnp.mean(updated * updated, axis=1, keepdims=True)
    normed = (updated / jnp.sqrt(power + 1e-06) * gain_ref[...]).astype(jnp.bfloat16)
    hidden = jnp.dot(normed, w_in_ref[...], preferred_element_type=jnp.float32)
    hidden = (hidden / (1.0 + jnp.exp(-hidden))).astype(jnp.bfloat16)
    added = jnp.dot(hidden, w_out_ref[...], preferred_element_type=jnp.float32)
    out_ref[...] = (updated + added).astype(jnp.bfloat16)


def update(place, features, own, other, gain, w_in, w_out):
    half = TILE // 2
    return pl.pallas_call(
        update_kernel,
        out_shape=jax.ShapeDtypeStruct((half, F), jnp.bfloat16),
        grid_spec=pltpu.PrefetchScalarGridSpec(
            num_scalar_prefetch=1,
            grid=(1,),
            in_specs=[
                pl.BlockSpec((half, F), lambda t, place: (place[0], 0)),
                pl.BlockSpec((half, F), lambda t, place: (0, 0)),
                pl.BlockSpec((half, F), lambda t, place: (0, 0)),
                pl.BlockSpec((1, F), lambda t, place: (0, 0)),
                pl.BlockSpec((F, F), lambda t, place: (0, 0)),
                pl.BlockSpec((F, F), lambda t, place: (0, 0)),
            ],
            out_specs=pl.BlockSpec((half, F), lambda t, place: (0, 0)),
        ),
        name="update",
    )(place, features, own, other, gain, w_in, w_out)


def exchange(pieces, groups):
    return lax.all_to_all(
        pieces, AXES, split_axis=0, concat_axis=0, tiled=True, axis_index_groups=groups
    )


def shard_steps():
    return np.stack([row_steps(shard) for shard in range(SHARDS)])


def column_steps(steps):
    by_core = steps.reshape(4, 2, 8, PLANES, 2 * OWN * LAYERS)
    return by_core.transpose(1, 2, 3, 0, 4).reshape(2, 8, ALL_ROWS)


STEPS = shard_steps()
COLUMN_STEPS = column_steps(STEPS)
PICK_FACTOR, PICK_WEIGHT = column_picks()


def on_device(features, coords, miller, filter_weights, norm_gain, w_in, w_out):
    atom, wave = lax.axis_index("atom"), lax.axis_index("wave")
    core, high = wave % 2, wave // 2
    plane = atom // 16 * 4 + atom % 4
    layer = atom // 4 % 4
    place = jnp.stack([wave, core, plane, layer, high]).astype(jnp.int32)

    factors = partial_factors(place, jnp.asarray(STEPS), coords, features)
    factors, coords, miller = lax.optimization_barrier((factors, coords, miller))
    arrived = exchange(factors.reshape(PLANES, 2 * OWN * LAYERS, F), GROUPS_XY)
    own_weights, other_weights = grid_weights(place, miller, filter_weights)
    other_weights = lax.ppermute(other_weights, AXES, SWAP)
    tables = message_tables(place, jnp.asarray(COLUMN_STEPS), coords)
    shares = exchange(plane_sum(arrived), GROUPS_LO)
    packed = exchange(scale_factors(shares, own_weights, other_weights), GROUPS_Z)
    filtered = filter_column(
        packed.reshape(PLANES * PACKED, F),
        jnp.asarray(PICK_FACTOR, jnp.bfloat16),
        jnp.asarray(PICK_WEIGHT, jnp.bfloat16),
    )
    filtered = exchange(filtered, GROUPS_XY).reshape(ALL_ROWS, F)
    own, other = message_parts(place, tables, filtered)
    other = lax.ppermute(other, AXES, SWAP)
    return update(place, features, own, other, norm_gain.reshape(1, F), w_in, w_out)


def solution(mesh):
    in_specs = (P("atom", None), P(None, "atom"), P(None, "wave"), P("wave", None), P(), P(), P())
    out_specs = P(("atom", "wave"), None)
    return jax.shard_map(
        on_device, mesh=mesh, in_specs=in_specs, out_specs=out_specs, check_vma=False
    )
```

time: 184 us -> 110 us (0.60)
  the two profiles are of different devices: /device:TPU:1 before, /device:TPU:33 now
where the time goes in v1:
time: 110 us; the launch traced here: 109 us
  blocking collectives  45.9 us (42%)
  Pallas kernels  27.1 us (25%)
  starting transfers between devices  18.5 us (17%)
  waiting for transfers between devices  14.5 us (13%)
  local copies, waits for them, and re-layouts  2.91 us (3%)
    all_to_all x2, blocking collectives, exchange(): lax.all_to_all(pieces, AXES, split_axis=0, concat_axis=0, tiled=True, axi...  45.9 us
    all_to_all x2, waiting for transfers between devices, exchange(): lax.all_to_all(pieces, AXES, split_axis=0, concat_axis=0, tiled=True, axi...  12.3 us
    all_to_all x2, starting transfers between devices, exchange(): lax.all_to_all(pieces, AXES, split_axis=0, concat_axis=0, tiled=True, axi...  9.14 us
    pallas_call x1, Pallas kernels, partial_factors(): pl.pallas_call(factors_kernel, out_shape=jax.ShapeDtypeStruct((ROWS, F),...  6.65 us
    pallas_call x1, Pallas kernels, message_tables(): pl.pallas_call(tables_kernel, out_shape=jax.ShapeDtypeStruct((TILE, ALL_R...  6.16 us
    ppermute x1, starting transfers between devices, on_device(): other = lax.ppermute(other, AXES, SWAP)  5.12 us
    ppermute x1, starting transfers between devices, on_device(): other_weights = lax.ppermute(other_weights, AXES, SWAP)  4.27 us
    pallas_call x1, Pallas kernels, message_parts(): pl.pallas_call(message_kernel, out_shape=(jax.ShapeDtypeStruct((half, F),...  3.72 us
  transfers between devices with their start and end apart: 4, of which 3 were waited for; matrix products, arithmetic and copies ran while one was open for 0% of the time, Pallas kernels for 7%

profile of v1, /device:TPU:33, one launch (start us, length us, event | category | flops | bytes accessed | tf_op | source)
XLA Modules:
  0.0 109.0 jit_solution(492247042149051160)
XLA Ops:
  0.0 0.6 stack.23.place_ref
  0.6 6.6 %factors.1 = bf16[640,256]{1,0:T(8,128)(2,1)} custom-call(s32[5]{0:T(128)} %stack.23.place_ref, f32[8,8,640]{2,1,0:T(8,128)} %constant.73.clone.steps_ref, s32[3,2048]{1,0:T(4,128)} %coords_ref.2, bf16[2048,256]{1,0:T(8,128)(2,1)} %features_ref.3), custom_call_target="tpu_custom_call" | custom-call | flops 671088640 | bytes 1048576 | tf_op jit(solution)/shard_map/factors/pallas_call | solution.py:129
  7.3 15.4 %all_to_all.20.arrived_ref = bf16[16,40,256]{2,1,0:T(8,128)(2,1)} all-to-all(bf16[16,40,256]{2,1,0:T(8,128)(2,1)} %bitcast.11), channel_id=1, replica_groups={{0,8,16,24,128,136,144,152,256,264,272,280,384,392,400,408},{1,9,17,25,..., dimensions={0} | all-to-all | bytes 655360 | tf_op jit(solution)/shard_map/all_to_all | solution.py:392
  22.6 1.7 %plane_sum.1 = bf16[4,10,256]{2,1,0:T(8,128)(2,1)} custom-call(bf16[16,40,256]{2,1,0:T(8,128)(2,1)} %all_to_all.20.arrived_ref), custom_call_target="tpu_custom_call" | custom-call | tf_op jit(solution)/shard_map/plane_sum/pallas_call | solution.py:219
  24.3 5.4 %all-to-all-start.1 = ((bf16[4,10,256]{2,1,0:T(8,128)(2,1)}), bf16[4,10,256]{2,1,0:T(8,128)(2,1)S(1)}, u32[]{:S(2)}, u32[]{:S(2)}) async-start(bf16[4,10,256]{2,1,0:T(8,128)(2,1)} %plane_sum.1), calls=%async_computation.1 | async-start | bytes 65536 | tf_op jit(solution)/shard_map/all_to_all | solution.py:392
  29.7 2.0 %grid_weights.1 = (bf16[32,256]{1,0:T(8,128)(2,1)}, bf16[32,256]{1,0:T(8,128)(2,1)}) custom-call(s32[5]{0:T(128)} %stack.23.place_ref, s32[3,512]{1,0:T(4,128)} %miller_ref, f32[512,256]{1,0:T(8,128)} %weights_ref.1), custom_call_target="tpu_custom_call" | custom-call | flops 33554432 | bytes 524288 | tf_op jit(solution)/shard_map/grid_weights/pallas_call | solution.py:194
  31.7 4.3 %collective-permute-start = (bf16[32,256]{1,0:T(8,128)(2,1)}, bf16[32,256]{1,0:T(8,128)(2,1)S(1)}, u32[]{:S(2)}, u32[]{:S(2)}) collective-permute-start(bf16[32,256]{1,0:T(8,128)(2,1)} %get-tuple-element.16), channel_id=1, source_target_pairs={{0,1},{1,0},{2,3},{3,2},{4,5},{5,4},{6,7},{7,6},{8,9},{9,8},{10,11... | collective-permute-start | bytes 49160 | tf_op jit(solution)/shard_map/ppermute | solution.py:422
  36.0 1.0 collective-permute-done.other_ref
  37.0 0.0 copy-start.3
  37.0 0.0 all-to-all-done.1.arrived_ref
  37.0 0.0 copy-start.1
  37.0 0.6 copy-done.3
  37.6 0.0 copy-done.1
  37.6 1.6 %scale_factors.1 = bf16[16,32,256]{2,1,0:T(8,128)(2,1)} custom-call(bf16[4,10,256]{2,1,0:T(8,128)(2,1)} %copy-done.1, bf16[32,256]{1,0:T(8,128)(2,1)} %get-tuple-element.15.own_ref, bf16[32,256]{1,0:T(8,128)(2,1)} %copy-done.3), custom_call_target="tpu_custom_call" | custom-call | tf_op jit(solution)/shard_map/scale_factors/pallas_call | solution.py:248
  39.2 30.5 %all_to_all.21 = bf16[16,32,256]{2,1,0:T(8,128)(2,1)} all-to-all(bf16[16,32,256]{2,1,0:T(8,128)(2,1)} %scale_factors.1), channel_id=1, replica_groups={{0,32,64,96,2,34,66,98,4,36,68,100,6,38,70,102},{1,33,65,97,3,35,67,99,..., dimensions={0} | all-to-all | bytes 524288 | tf_op jit(solution)/shard_map/all_to_all | solution.py:392
  69.8 2.5 %filter_column.1 = bf16[16,160,256]{2,1,0:T(8,128)(2,1)} custom-call(bf16[512,256]{1,0:T(8,128)(2,1)} %bitcast.10, bf16[160,512]{1,0:T(8,128)(2,1)} %constant.75.clone.factor_ref, bf16[160,512]{1,0:T(8,128)(2,1)} %constant.76.clone.weight_ref), custom_call_target="tpu_custom_call" | custom-call | tf_op jit(solution)/shard_map/filter_column/pallas_call | solution.py:284
  72.2 3.7 %all-to-all-start.3 = ((bf16[16,160,256]{2,1,0:T(8,128)(2,1)}), bf16[16,160,256]{2,1,0:T(8,128)(2,1)S(1)}, u32[]{:S(2)}, u32[]{:S(2)}) async-start(bf16[16,160,256]{2,1,0:T(8,128)(2,1)} %filter_column.1), calls=%async_computation.3 | async-start | bytes 2621440 | tf_op jit(solution)/shard_map/all_to_all | solution.py:392
  75.9 6.2 %message_tables.1.tables_ref = bf16[512,2560]{1,0:T(8,128)(2,1)} custom-call(s32[5]{0:T(128)} %stack.23.place_ref, f32[2,8,2560]{2,1,0:T(8,128)} %constant.74.clone.steps_ref, s32[3,2048]{1,0:T(4,128)} %coords_ref.2), custom_call_target="tpu_custom_call" | custom-call | flops 20971520 | bytes 2621440 | tf_op jit(solution)/shard_map/message_tables/pallas_call | solution.py:309
  82.1 12.3 %all-to-all-done.3 = bf16[16,160,256]{2,1,0:T(8,128)(2,1)S(1)} async-done(((bf16[16,160,256]{2,1,0:T(8,128)(2,1)}), bf16[16,160,256]{2,1,0:T(8,128)(2,1)S(1)}, u32[]{:S(2)}, u32[]{:S(2)}) %all-to-all-start.3) | async-done | bytes 1310752 | tf_op jit(solution)/shard_map/all_to_all | solution.py:392
  94.4 0.0 copy-start
  94.4 1.1 copy-done
  95.5 3.7 %message.1 = (f32[256,256]{1,0:T(8,128)}, bf16[256,256]{1,0:T(8,128)(2,1)}) custom-call(s32[5]{0:T(128)} %stack.23.place_ref, bf16[512,2560]{1,0:T(8,128)(2,1)} %message_tables.1.tables_ref, bf16[2560,256]{1,0:T(8,128)(2,1)} %bitcast.9), custom_call_target="tpu_custom_call" | custom-call | tf_op jit(solution)/shard_map/message/pallas_call | solution.py:339
  99.2 5.1 %collective-permute-start.1 = (bf16[256,256]{1,0:T(8,128)(2,1)}, bf16[256,256]{1,0:T(8,128)(2,1)S(1)}, u32[]{:S(2)}, u32[]{:S(2)}) collective-permute-start(bf16[256,256]{1,0:T(8,128)(2,1)} %get-tuple-element.18), channel_id=1, source_target_pairs={{0,1},{1,0},{2,3},{3,2},{4,5},{5,4},{6,7},{7,6},{8,9},{9,8},{10,11... | collective-permute-start | bytes 393224 | tf_op jit(solution)/shard_map/ppermute | solution.py:433
  104.3 1.2 %collective-permute-done.1.other_ref = bf16[256,256]{1,0:T(8,128)(2,1)S(1)} collective-permute-done((bf16[256,256]{1,0:T(8,128)(2,1)}, bf16[256,256]{1,0:T(8,128)(2,1)S(1)}, u32[]{:S(2)}, u32[]{:S(2)}) %collective-permute-start.1) | collective-permute-done | bytes 131104 | tf_op jit(solution)/shard_map/ppermute | solution.py:433
  105.5 0.0 copy-start.2
  105.5 0.6 copy-done.2
  106.1 2.9 %update.1 = bf16[256,256]{1,0:T(8,128)(2,1)} custom-call(s32[5]{0:T(128)} %stack.23.place_ref, bf16[2048,256]{1,0:T(8,128)(2,1)} %features_ref.3, f32[256,256]{1,0:T(8,128)} %get-tuple-element.17.own_ref, bf16[256,256]{1,0:T(8,128)(2,1)} %copy-done.2, f32[1,256]{1,0:T(1,128)} %bitcast.12, bf16[256,256]{1,0:T(8,128)(2,1)} %w_in_ref.1, bf16[256,256]{1,0:T(8,128)(2,1)} %w_out_ref.1), custom_call_target="tpu_custom_call" | custom-call | tf_op jit(solution)/shard_map/update/pallas_call | solution.py:371
Async XLA Ops:
  24.3 12.7 %all-to-all-start.1 = ((bf16[4,10,256]{2,1,0:T(8,128)(2,1)}), bf16[4,10,256]{2,1,0:T(8,128)(2,1)S(1)}, u32[]{:S(2)}, u32[]{:S(2)}) async-start(bf16[4,10,256]{2,1,0:T(8,128)(2,1)} %plane_sum.1), calls=%async_computation.1 | async-start | bytes 65536 | tf_op jit(solution)/shard_map/all_to_all | solution.py:392
  31.7 5.3 %collective-permute-start = (bf16[32,256]{1,0:T(8,128)(2,1)}, bf16[32,256]{1,0:T(8,128)(2,1)S(1)}, u32[]{:S(2)}, u32[]{:S(2)}) collective-permute-start(bf16[32,256]{1,0:T(8,128)(2,1)} %get-tuple-element.16), channel_id=1, source_target_pairs={{0,1},{1,0},{2,3},{3,2},{4,5},{5,4},{6,7},{7,6},{8,9},{9,8},{10,11... | collective-permute-start | bytes 49160 | tf_op jit(solution)/shard_map/ppermute | solution.py:422
  37.0 0.6 copy-start.3
  37.0 0.6 copy-start.1
  72.2 22.2 %all-to-all-start.3 = ((bf16[16,160,256]{2,1,0:T(8,128)(2,1)}), bf16[16,160,256]{2,1,0:T(8,128)(2,1)S(1)}, u32[]{:S(2)}, u32[]{:S(2)}) async-start(bf16[16,160,256]{2,1,0:T(8,128)(2,1)} %filter_column.1), calls=%async_computation.3 | async-start | bytes 2621440 | tf_op jit(solution)/shard_map/all_to_all | solution.py:392
  94.4 1.1 copy-start
  99.2 6.3 %collective-permute-start.1 = (bf16[256,256]{1,0:T(8,128)(2,1)}, bf16[256,256]{1,0:T(8,128)(2,1)S(1)}, u32[]{:S(2)}, u32[]{:S(2)}) collective-permute-start(bf16[256,256]{1,0:T(8,128)(2,1)} %get-tuple-element.18), channel_id=1, source_target_pairs={{0,1},{1,0},{2,3},{3,2},{4,5},{5,4},{6,7},{7,6},{8,9},{9,8},{10,11... | collective-permute-start | bytes 393224 | tf_op jit(solution)/shard_map/ppermute | solution.py:433
  105.5 0.6 copy-start.2

commit v2 on v1

--- a/solution.py
+++ b/solution.py
@@ -18,8 +18,9 @@
 SHARDS = 8
 POINTS = 320
 PLANES = 16
-LAYERS = 4
-OWN = POINTS // (PLANES * LAYERS)
+OWN = POINTS // PLANES
+CHUNK = 2 * OWN
+PADDED = 24
 ROWS = 2 * POINTS
 F = 256
 TILE = 512
@@ -40,8 +41,8 @@
 GROUPS_LO = [
     [device(y, l, x, h, c) for l in FOUR] for y in FOUR for x in FOUR for h in FOUR for c in TWO
 ]
-GROUPS_Z = [
-    [device(y, l, x, h, c) for h in FOUR for l in FOUR] for y in FOUR for x in FOUR for c in TWO
+GROUPS_HI = [
+    [device(y, l, x, h, c) for h in FOUR] for y in FOUR for x in FOUR for l in FOUR for c in TWO
 ]
 SWAP = [
     (device(y, l, x, h, c), device(y, l, x, h, 1 - c))
@@ -61,7 +62,7 @@
 def row_steps(shard):
     steps = np.zeros((8, ROWS), np.float32)
     for row in range(ROWS):
-        chunk, part, own = row // (2 * OWN), row % (2 * OWN) // OWN, row % OWN
+        chunk, part, own = row // CHUNK, row % CHUNK // OWN, row % OWN
         vector = wavevector(shard, chunk * OWN + own)
         if vector is None:
             steps[6, row] = -0.25
@@ -143,6 +144,7 @@
                 pltpu.VMEM((ROWS, F), jnp.float32),
             ],
         ),
+        compiler_params=pltpu.CompilerParams(vmem_limit_bytes=16 << 20),
         cost_estimate=pl.CostEstimate(
             flops=2 * ROWS * atoms * F, bytes_accessed=atoms * F * 2, transcendentals=0
         ),
@@ -150,144 +152,110 @@
     )(place, steps, coords, features)
 
 
-WROWS = 32
-
-
-def weights_kernel(place_ref, miller_ref, weights_ref, own_ref, other_ref):
-    core, plane, layer = place_ref[1], place_ref[2], place_ref[3]
+def weights_kernel(place_ref, miller_ref, weights_ref, out_ref):
+    plane = place_ref[4] * 4 + place_ref[3]
     m0, m1, m2 = miller_ref[0:1, :], miller_ref[1:2, :], miller_ref[2:3, :]
     flat = (m0 + KMAX) * SIDE + (m1 + KMAX)
     flip = (m2 < 0) | ((m2 == 0) & (flat < HALF))
     flat = jnp.where(flip, 2 * HALF - flat, flat)
     strip = flat - HALF
-    strip_shard = (
-        (strip >= STRIP).astype(jnp.int32)
-        + (strip >= 2 * STRIP).astype(jnp.int32)
-        + (strip >= 3 * STRIP).astype(jnp.int32)
-        + (strip >= 4 * STRIP).astype(jnp.int32)
-        + (strip >= 5 * STRIP).astype(jnp.int32)
-        + (strip >= 6 * STRIP).astype(jnp.int32)
-    )
+    strip_shard = (strip >= STRIP).astype(jnp.int32)
+    for bound in range(2, 7):
+        strip_shard += (strip >= bound * STRIP).astype(jnp.int32)
     shard = jnp.where(m2 == 0, strip_shard, jnp.abs(m2) - 1)
     point = jnp.where(m2 == 0, PLANE + strip - strip_shard * STRIP, flat)
     spot = shard * POINTS + point
-    row = lax.broadcasted_iota(jnp.int32, (WROWS, miller_ref.shape[1]), 0)
-    high = (
-        (row >= OWN).astype(jnp.int32)
-        + (row >= 2 * OWN).astype(jnp.int32)
-        + (row >= 3 * OWN).astype(jnp.int32)
-    )
-    base = (plane * LAYERS + layer) * OWN + row - high * OWN
+    row = lax.broadcasted_iota(jnp.int32, (SHARDS * PADDED, miller_ref.shape[1]), 0)
+    owner = (row * 171) >> 12
+    own = row - owner * PADDED
+    wanted = owner * POINTS + plane * OWN + own
+    match = jnp.where((wanted == spot) & (own < OWN), 1.0, 0.0).astype(jnp.bfloat16)
     weights = weights_ref[...]
     upper = weights.astype(jnp.bfloat16)
     lower = (weights - upper.astype(jnp.float32)).astype(jnp.bfloat16)
-    for held, out_ref in ((core, own_ref), (1 - core, other_ref)):
-        wanted = (high * 2 + held) * POINTS + base
-        match = jnp.where((wanted == spot) & (row < 4 * OWN), 1.0, 0.0).astype(jnp.bfloat16)
-        summed = jnp.dot(match, upper, preferred_element_type=jnp.float32)
-        summed += jnp.dot(match, lower, preferred_element_type=jnp.float32)
-        out_ref[...] = summed.astype(jnp.bfloat16)
+    summed = jnp.dot(match, upper, preferred_element_type=jnp.float32)
+    summed += jnp.dot(match, lower, preferred_element_type=jnp.float32)
+    out_ref[...] = summed.astype(jnp.bfloat16)
 
 
 def grid_weights(place, miller, weights):
-    shape = jax.ShapeDtypeStruct((WROWS, F), jnp.bfloat16)
     return pl.pallas_call(
         weights_kernel,
-        out_shape=(shape, shape),
+        out_shape=jax.ShapeDtypeStruct((SHARDS * PADDED, F), jnp.bfloat16),
         in_specs=[
             pl.BlockSpec(memory_space=pltpu.SMEM),
             pl.BlockSpec(memory_space=pltpu.VMEM),
             pl.BlockSpec(memory_space=pltpu.VMEM),
         ],
-        out_specs=(pl.BlockSpec(memory_space=pltpu.VMEM),) * 2,
+        out_specs=pl.BlockSpec(memory_space=pltpu.VMEM),
+        compiler_params=pltpu.CompilerParams(vmem_limit_bytes=8 << 20),
         cost_estimate=pl.CostEstimate(
-            flops=8 * WROWS * 512 * F, bytes_accessed=512 * F * 4, transcendentals=0
+            flops=4 * SHARDS * PADDED * 512 * F, bytes_accessed=512 * F * 4, transcendentals=0
         ),
         name="grid_weights",
     )(place, miller, weights)
 
 
-def plane_sum_kernel(arrived_ref, out_ref, total):
-    total[...] = jnp.sum(arrived_ref[...].astype(jnp.float32), axis=0)
-    for layer in range(LAYERS):
-        rows = total[layer * 2 * OWN : (layer + 1) * 2 * OWN, :]
-        out_ref[layer] = rows.astype(jnp.bfloat16)
+def plane_sum_kernel(arrived_ref, out_ref):
+    total = jnp.sum(arrived_ref[...].astype(jnp.float32), axis=0).astype(jnp.bfloat16)
+    for peer in range(4):
+        out_ref[peer] = total
 
 
 def plane_sum(arrived):
-    rows = 2 * OWN * LAYERS
     return pl.pallas_call(
         plane_sum_kernel,
-        out_shape=jax.ShapeDtypeStruct((LAYERS, 2 * OWN, F), jnp.bfloat16),
+        out_shape=jax.ShapeDtypeStruct((4, CHUNK, F), jnp.bfloat16),
         in_specs=[pl.BlockSpec(memory_space=pltpu.VMEM)],
         out_specs=pl.BlockSpec(memory_space=pltpu.VMEM),
-        scratch_shapes=[pltpu.VMEM((rows, F), jnp.float32)],
+        compiler_params=pltpu.CompilerParams(vmem_limit_bytes=8 << 20),
         name="plane_sum",
     )(arrived)
 
 
-PACKED = 32
-
-
-def scale_kernel(arrived_ref, own_ref, other_ref, out_ref, packed):
+def filter_kernel(arrived_ref, weights_ref, out_ref, filtered):
     total = jnp.sum(arrived_ref[...].astype(jnp.float32), axis=0)
     cosines, sines = total[:OWN], total[OWN:]
     power = jnp.sum(cosines * cosines + sines * sines, axis=1, keepdims=True) * (1.0 / (2 * F))
-    scale = 1.0 / jnp.sqrt(power + 1e-05)
-    packed[0:OWN, :] = cosines * scale
-    packed[OWN : 2 * OWN, :] = sines * scale
-    weights = own_ref[...].astype(jnp.float32) + other_ref[...].astype(jnp.float32)
-    packed[2 * OWN : 6 * OWN, :] = weights[: 4 * OWN]
-    packed[6 * OWN :, :] = jnp.zeros((PACKED - 6 * OWN, F), jnp.float32)
-    sent = packed[...].astype(jnp.bfloat16)
+    weights = jnp.sum(weights_ref[...].astype(jnp.float32), axis=0)[:OWN]
+    scaled = weights * (1.0 / jnp.sqrt(power + 1e-05))
+    filtered[:OWN, :] = cosines * scaled
+    filtered[OWN:, :] = sines * scaled
+    sent = filtered[...].astype(jnp.bfloat16)
+    for peer in range(4):
+        out_ref[peer] = sent
+
+
+def filter_factors(arrived, weights):
+    return pl.pallas_call(
+        filter_kernel,
+        out_shape=jax.ShapeDtypeStruct((4, CHUNK, F), jnp.bfloat16),
+        in_specs=[pl.BlockSpec(memory_space=pltpu.VMEM)] * 2,
+        out_specs=pl.BlockSpec(memory_space=pltpu.VMEM),
+        scratch_shapes=[pltpu.VMEM((CHUNK, F), jnp.float32)],
+        compiler_params=pltpu.CompilerParams(vmem_limit_bytes=8 << 20),
+        name="filter_factors",
+    )(arrived, weights)
+
+
+COLUMN = 4 * CHUNK
+
+
+def copies_kernel(column_ref, out_ref):
+    column = column_ref[...]
     for peer in range(PLANES):
-        out_ref[peer] = sent
-
-
-def scale_factors(arrived, own, other):
-    return pl.pallas_call(
-        scale_kernel,
-        out_shape=jax.ShapeDtypeStruct((PLANES, PACKED, F), jnp.bfloat16),
-        in_specs=[pl.BlockSpec(memory_space=pltpu.VMEM)] * 3,
+        out_ref[peer] = column
+
+
+def copies(column):
+    return pl.pallas_call(
+        copies_kernel,
+        out_shape=jax.ShapeDtypeStruct((PLANES, COLUMN, F), jnp.bfloat16),
+        in_specs=[pl.BlockSpec(memory_space=pltpu.VMEM)],
         out_specs=pl.BlockSpec(memory_space=pltpu.VMEM),
-        scratch_shapes=[pltpu.VMEM((PACKED, F), jnp.float32)],
-        name="scale_factors",
-    )(arrived, own, other)
-
-
-COLUMN = 2 * OWN * PLANES
-
-
-def column_picks():
-    factor = np.zeros((COLUMN, PLANES * PACKED), np.float32)
-    weight = np.zeros((COLUMN, PLANES * PACKED), np.float32)
-    for row in range(COLUMN):
-        rank, spot = row // (2 * OWN), row % (2 * OWN)
-        high, low = rank // LAYERS, rank % LAYERS
-        factor[row, rank * PACKED + spot] = 1
-        for source in range(4):
-            at = (source * LAYERS + low) * PACKED + 2 * OWN + high * OWN + spot % OWN
-            weight[row, at] = 1
-    return factor, weight
-
-
-def filter_kernel(arrived_ref, factor_ref, weight_ref, out_ref):
-    arrived = arrived_ref[...]
-    factors = jnp.dot(factor_ref[...], arrived, preferred_element_type=jnp.float32)
-    weights = jnp.dot(weight_ref[...], arrived, preferred_element_type=jnp.float32)
-    filtered = (factors * weights).astype(jnp.bfloat16)
-    for peer in range(PLANES):
-        out_ref[peer] = filtered
-
-
-def filter_column(arrived, factor, weight):
-    return pl.pallas_call(
-        filter_kernel,
-        out_shape=jax.ShapeDtypeStruct((PLANES, COLUMN, F), jnp.bfloat16),
-        in_specs=[pl.BlockSpec(memory_space=pltpu.VMEM)] * 3,
-        out_specs=pl.BlockSpec(memory_space=pltpu.VMEM),
-        name="filter_column",
-    )(arrived, factor, weight)
+        compiler_params=pltpu.CompilerParams(vmem_limit_bytes=8 << 20),
+        name="copies",
+    )(column)
 
 
 ALL_ROWS = COLUMN * PLANES
@@ -314,10 +282,11 @@
             grid=(ALL_ROWS // width,),
             in_specs=[
                 pl.BlockSpec((1, 8, width), lambda t, place: (place[1], 0, t)),
-                pl.BlockSpec((3, TILE), lambda t, place: (0, place[4])),
+                pl.BlockSpec((3, TILE), lambda t, place: (0, place[2])),
             ],
             out_specs=pl.BlockSpec((TILE, width), lambda t, place: (0, t)),
         ),
+        compiler_params=pltpu.CompilerParams(vmem_limit_bytes=16 << 20),
         cost_estimate=pl.CostEstimate(
             flops=16 * TILE * ALL_ROWS, bytes_accessed=TILE * ALL_ROWS * 2, transcendentals=0
         ),
@@ -349,6 +318,7 @@
         ],
         out_specs=(pl.BlockSpec(memory_space=pltpu.VMEM),) * 2,
         scratch_shapes=[pltpu.VMEM((TILE, F), jnp.float32)],
+        compiler_params=pltpu.CompilerParams(vmem_limit_bytes=16 << 20),
         name="message",
     )(place, tables, filtered)
 
@@ -384,6 +354,7 @@
             ],
             out_specs=pl.BlockSpec((half, F), lambda t, place: (0, 0)),
         ),
+        compiler_params=pltpu.CompilerParams(vmem_limit_bytes=8 << 20),
         name="update",
     )(place, features, own, other, gain, w_in, w_out)
 
@@ -399,36 +370,27 @@
 
 
 def column_steps(steps):
-    by_core = steps.reshape(4, 2, 8, PLANES, 2 * OWN * LAYERS)
+    by_core = steps.reshape(4, 2, 8, PLANES, CHUNK)
     return by_core.transpose(1, 2, 3, 0, 4).reshape(2, 8, ALL_ROWS)
 
 
 STEPS = shard_steps()
 COLUMN_STEPS = column_steps(STEPS)
-PICK_FACTOR, PICK_WEIGHT = column_picks()
 
 
 def on_device(features, coords, miller, filter_weights, norm_gain, w_in, w_out):
-    atom, wave = lax.axis_index("atom"), lax.axis_index("wave")
-    core, high = wave % 2, wave // 2
-    plane = atom // 16 * 4 + atom % 4
-    layer = atom // 4 % 4
-    place = jnp.stack([wave, core, plane, layer, high]).astype(jnp.int32)
+    number = lax.axis_index("atom") * 8 + lax.axis_index("wave")
+    place = number // np.array([1, 1, 2, 8, 128], np.int32) % np.array([8, 2, 4, 4, 4], np.int32)
 
     factors = partial_factors(place, jnp.asarray(STEPS), coords, features)
     factors, coords, miller = lax.optimization_barrier((factors, coords, miller))
-    arrived = exchange(factors.reshape(PLANES, 2 * OWN * LAYERS, F), GROUPS_XY)
-    own_weights, other_weights = grid_weights(place, miller, filter_weights)
-    other_weights = lax.ppermute(other_weights, AXES, SWAP)
+    arrived = exchange(factors.reshape(PLANES, CHUNK, F), GROUPS_XY)
+    weights = grid_weights(place, miller, filter_weights).reshape(SHARDS, PADDED, F)
+    weights = lax.all_to_all(weights, "wave", split_axis=0, concat_axis=0, tiled=True)
     tables = message_tables(place, jnp.asarray(COLUMN_STEPS), coords)
     shares = exchange(plane_sum(arrived), GROUPS_LO)
-    packed = exchange(scale_factors(shares, own_weights, other_weights), GROUPS_Z)
-    filtered = filter_column(
-        packed.reshape(PLANES * PACKED, F),
-        jnp.asarray(PICK_FACTOR, jnp.bfloat16),
-        jnp.asarray(PICK_WEIGHT, jnp.bfloat16),
-    )
-    filtered = exchange(filtered, GROUPS_XY).reshape(ALL_ROWS, F)
+    filtered = exchange(filter_factors(shares, weights), GROUPS_HI)
+    filtered = exchange(copies(filtered.reshape(COLUMN, F)), GROUPS_XY).reshape(ALL_ROWS, F)
     own, other = message_parts(place, tables, filtered)
     other = lax.ppermute(other, AXES, SWAP)
     return update(place, features, own, other, norm_gain.reshape(1, F), w_in, w_out)

time: 110 us -> 113 us (1.027)
  the two profiles are of different devices: /device:TPU:33 before, /device:TPU:1 now
where the time goes in v2:
time: 113 us
  starting transfers between devices  36.9 us (33%)
  waiting for transfers between devices  31.9 us (28%)
  blocking collectives  23.4 us (21%)
  Pallas kernels  16.7 us (15%)
  local copies, waits for them, and re-layouts  2.92 us (3%)
    all_to_all x2, blocking collectives, exchange(): lax.all_to_all(pieces, AXES, split_axis=0, concat_axis=0, tiled=True, axi...  23.4 us
    all_to_all x2, waiting for transfers between devices, exchange(): lax.all_to_all(pieces, AXES, split_axis=0, concat_axis=0, tiled=True, axi...  18.4 us
    all_to_all x1, starting transfers between devices, on_device(): lax.all_to_all(weights, 'wave', split_axis=0, concat_axis=0, tiled=True)  17.5 us
    all_to_all x1, waiting for transfers between devices, on_device(): lax.all_to_all(weights, 'wave', split_axis=0, concat_axis=0, tiled=True)  12.5 us
    all_to_all x2, starting transfers between devices, exchange(): lax.all_to_all(pieces, AXES, split_axis=0, concat_axis=0, tiled=True, axi...  12.1 us
    ppermute x1, starting transfers between devices, on_device(): other = lax.ppermute(other, AXES, SWAP)  7.2 us
    pallas_call x1, Pallas kernels, partial_factors(): pl.pallas_call(factors_kernel, out_shape=jax.ShapeDtypeStruct((ROWS, F),...  5.54 us
    pallas_call x1, Pallas kernels, message_tables(): pl.pallas_call(tables_kernel, out_shape=jax.ShapeDtypeStruct((TILE, ALL_R...  4.35 us
  transfers between devices with their start and end apart: 4, of which 4 were waited for; matrix products, arithmetic and copies ran while one was open for 0% of the time, Pallas kernels for 5%

profile of v2, /device:TPU:1, one launch (start us, length us, event | category | flops | bytes accessed | tf_op | source)
XLA Modules:
  0.0 112.7 jit_solution(6563240464944362252)
XLA Ops:
  0.0 0.9 and_select_fusion.place_ref
  0.9 0.0 copy-start
  0.9 1.2 %copy-done = bf16[2048,256]{1,0:T(8,128)(2,1)S(1)} copy-done((bf16[2048,256]{1,0:T(8,128)(2,1)S(1)}, bf16[2048,256]{1,0:T(8,128)(2,1)}, u32[]{:S(2)}) %copy-start) | copy-done | bytes 1048600
  2.1 0.0 copy-start.6
  2.2 0.8 copy-done.6
  2.9 0.0 copy-start.10
  2.9 0.9 copy-done.10
  3.8 0.0 copy-start.2
  3.8 0.0 copy-start.8
  3.8 5.5 %factors.1 = bf16[640,256]{1,0:T(8,128)(2,1)} custom-call(s32[5]{0:T(128)S(1)} %and_select_fusion.place_ref, f32[8,8,640]{2,1,0:T(8,128)S(1)} %copy-done.10, s32[3,2048]{1,0:T(4,128)S(1)} %copy-done.6, bf16[2048,256]{1,0:T(8,128)(2,1)S(1)} %copy-done), custom_call_target="tpu_custom_call" | custom-call | flops 671088640 | bytes 1048576 | tf_op jit(solution)/shard_map/factors/pallas_call | solution.py:130
  9.4 7.6 %all-to-all-start = ((bf16[16,40,256]{2,1,0:T(8,128)(2,1)}), bf16[16,40,256]{2,1,0:T(8,128)(2,1)S(1)}, u32[]{:S(2)}, u32[]{:S(2)}) async-start(bf16[16,40,256]{2,1,0:T(8,128)(2,1)} %bitcast), calls=%async_computation | async-start | bytes 655360 | tf_op jit(solution)/shard_map/all_to_all | solution.py:363
  17.0 0.0 copy-done.2
  17.0 0.0 copy-done.8
  17.0 1.5 %grid_weights.1 = bf16[192,256]{1,0:T(8,128)(2,1)} custom-call(s32[5]{0:T(128)S(1)} %and_select_fusion.place_ref, s32[3,512]{1,0:T(4,128)S(1)} %copy-done.8, f32[512,256]{1,0:T(8,128)S(1)} %copy-done.2), custom_call_target="tpu_custom_call" | custom-call | flops 100663296 | bytes 524288 | tf_op jit(solution)/shard_map/grid_weights/pallas_call | solution.py:182
  18.4 6.4 %all-to-all-done.arrived_ref = bf16[16,40,256]{2,1,0:T(8,128)(2,1)S(1)} async-done(((bf16[16,40,256]{2,1,0:T(8,128)(2,1)}), bf16[16,40,256]{2,1,0:T(8,128)(2,1)S(1)}, u32[]{:S(2)}, u32[]{:S(2)}) %all-to-all-start) | async-done | bytes 327712 | tf_op jit(solution)/shard_map/all_to_all | solution.py:363
  24.8 17.5 %all-to-all-start.2 = ((bf16[8,24,256]{2,1,0:T(8,128)(2,1)}), bf16[8,24,256]{2,1,0:T(8,128)(2,1)S(1)}, u32[]{:S(2)}, u32[]{:S(2)}) async-start(bf16[8,24,256]{2,1,0:T(8,128)(2,1)} %bitcast.1), calls=%async_computation.2 | async-start | bytes 196608 | tf_op jit(solution)/shard_map/all_to_all | solution.py:389
  42.4 0.1 plane_sum.1
  42.4 12.5 %all-to-all-done.2.weights_ref = bf16[8,24,256]{2,1,0:T(8,128)(2,1)S(1)} async-done(((bf16[8,24,256]{2,1,0:T(8,128)(2,1)}), bf16[8,24,256]{2,1,0:T(8,128)(2,1)S(1)}, u32[]{:S(2)}, u32[]{:S(2)}) %all-to-all-start.2) | async-done | bytes 98336 | tf_op jit(solution)/shard_map/all_to_all | solution.py:389
  54.9 8.2 %all_to_all.25.arrived_ref = bf16[4,40,256]{2,1,0:T(8,128)(2,1)S(1)} all-to-all(bf16[4,40,256]{2,1,0:T(8,128)(2,1)S(1)} %plane_sum.1), channel_id=1, replica_groups={{0,32,64,96},{1,33,65,97},{2,34,66,98},{3,35,67,99},{4,36,68,100},{5,37..., dimensions={0} | all-to-all | bytes 163840 | tf_op jit(solution)/shard_map/all_to_all | solution.py:363
  63.2 0.1 filter_factors.1
  63.3 15.1 %all_to_all.26 = bf16[4,40,256]{2,1,0:T(8,128)(2,1)S(1)} all-to-all(bf16[4,40,256]{2,1,0:T(8,128)(2,1)S(1)} %filter_factors.1), channel_id=1, replica_groups={{0,2,4,6},{1,3,5,7},{32,34,36,38},{33,35,37,39},{64,66,68,70},{65,67,69..., dimensions={0} | all-to-all | bytes 163840 | tf_op jit(solution)/shard_map/all_to_all | solution.py:363
  78.4 1.2 %copies.1 = bf16[16,160,256]{2,1,0:T(8,128)(2,1)} custom-call(bf16[160,256]{1,0:T(8,128)(2,1)S(1)} %bitcast.5), custom_call_target="tpu_custom_call" | custom-call | tf_op jit(solution)/shard_map/copies/pallas_call | solution.py:251
  79.6 0.0 copy-start.3
  79.6 0.0 copy-start.7
  79.6 4.5 %all-to-all-start.4 = ((bf16[16,160,256]{2,1,0:T(8,128)(2,1)}), bf16[16,160,256]{2,1,0:T(8,128)(2,1)}, u32[]{:S(2)}, u32[]{:S(2)}) async-start(bf16[16,160,256]{2,1,0:T(8,128)(2,1)} %copies.1), calls=%async_computation.4 | async-start | bytes 2621440 | tf_op jit(solution)/shard_map/all_to_all | solution.py:363
  84.2 0.0 copy-done.3
  84.2 0.0 copy-done.7
  84.2 4.4 %message_tables.1.tables_ref = bf16[512,2560]{1,0:T(8,128)(2,1)S(1)} custom-call(s32[5]{0:T(128)S(1)} %and_select_fusion.place_ref, f32[2,8,2560]{2,1,0:T(8,128)S(1)} %copy-done.3, s32[3,2048]{1,0:T(4,128)S(1)} %copy-done.7), custom_call_target="tpu_custom_call" | custom-call | flops 20971520 | bytes 2621440 | tf_op jit(solution)/shard_map/message_tables/pallas_call | solution.py:277
  88.6 12.0 %all-to-all-done.4 = bf16[16,160,256]{2,1,0:T(8,128)(2,1)} async-done(((bf16[16,160,256]{2,1,0:T(8,128)(2,1)}), bf16[16,160,256]{2,1,0:T(8,128)(2,1)}, u32[]{:S(2)}, u32[]{:S(2)}) %all-to-all-start.4) | async-done | bytes 1310752 | tf_op jit(solution)/shard_map/all_to_all | solution.py:363
  100.6 0.0 copy-start.1
  100.6 0.0 copy-start.4
  100.6 0.0 copy-start.5
  100.6 0.0 copy-start.9
  100.6 2.3 %message.1 = (f32[256,256]{1,0:T(8,128)S(1)}, bf16[256,256]{1,0:T(8,128)(2,1)S(1)}) custom-call(s32[5]{0:T(128)S(1)} %and_select_fusion.place_ref, bf16[512,2560]{1,0:T(8,128)(2,1)S(1)} %message_tables.1.tables_ref, bf16[2560,256]{1,0:T(8,128)(2,1)} %bitcast.3.filtered_ref), custom_call_target="tpu_custom_call" | custom-call | tf_op jit(solution)/shard_map/message/pallas_call | solution.py:308
  102.9 7.2 %collective-permute-start = (bf16[256,256]{1,0:T(8,128)(2,1)S(1)}, bf16[256,256]{1,0:T(8,128)(2,1)S(1)}, u32[]{:S(2)}, u32[]{:S(2)}) collective-permute-start(bf16[256,256]{1,0:T(8,128)(2,1)S(1)} %get-tuple-element.14), channel_id=1, source_target_pairs={{0,1},{1,0},{2,3},{3,2},{4,5},{5,4},{6,7},{7,6},{8,9},{9,8},{10,11... | collective-permute-start | bytes 393224 | tf_op jit(solution)/shard_map/ppermute | solution.py:395
  110.1 1.0 collective-permute-done.other_ref
  111.1 0.0 copy-done.1
  111.1 0.0 copy-done.4
  111.1 0.0 copy-done.5
  111.1 0.0 copy-done.9
  111.1 1.6 %update.1 = bf16[256,256]{1,0:T(8,128)(2,1)} custom-call(s32[5]{0:T(128)S(1)} %and_select_fusion.place_ref, bf16[2048,256]{1,0:T(8,128)(2,1)S(1)} %copy-done.1, f32[256,256]{1,0:T(8,128)S(1)} %get-tuple-element.13.own_ref, bf16[256,256]{1,0:T(8,128)(2,1)S(1)} %collective-permute-done.other_ref, f32[1,256]{1,0:T(1,128)S(1)} %bitcast.6, ...), custom_call_target="tpu_custom_call" | custom-call | tf_op jit(solution)/shard_map/update/pallas_call | solution.py:341
Async XLA Ops:
  0.9 1.2 %copy-start = (bf16[2048,256]{1,0:T(8,128)(2,1)S(1)}, bf16[2048,256]{1,0:T(8,128)(2,1)}, u32[]{:S(2)}) copy-start(bf16[2048,256]{1,0:T(8,128)(2,1)} %features_ref.3) | copy-start | bytes 3145732
  2.1 0.8 copy-start.6
  2.9 0.9 copy-start.10
  3.8 13.1 %copy-start.2 = (f32[512,256]{1,0:T(8,128)S(1)}, f32[512,256]{1,0:T(8,128)}, u32[]{:S(2)}) copy-start(f32[512,256]{1,0:T(8,128)} %weights_ref.1) | copy-start | bytes 1572868
  3.8 13.1 %copy-start.8 = (s32[3,512]{1,0:T(4,128)S(1)}, s32[3,512]{1,0:T(4,128)}, u32[]{:S(2)}) copy-start(s32[3,512]{1,0:T(4,128)} %miller_ref) | copy-start | bytes 18436
  9.4 15.5 %all-to-all-start = ((bf16[16,40,256]{2,1,0:T(8,128)(2,1)}), bf16[16,40,256]{2,1,0:T(8,128)(2,1)S(1)}, u32[]{:S(2)}, u32[]{:S(2)}) async-start(bf16[16,40,256]{2,1,0:T(8,128)(2,1)} %bitcast), calls=%async_computation | async-start | bytes 655360 | tf_op jit(solution)/shard_map/all_to_all | solution.py:363
  24.8 30.1 %all-to-all-start.2 = ((bf16[8,24,256]{2,1,0:T(8,128)(2,1)}), bf16[8,24,256]{2,1,0:T(8,128)(2,1)S(1)}, u32[]{:S(2)}, u32[]{:S(2)}) async-start(bf16[8,24,256]{2,1,0:T(8,128)(2,1)} %bitcast.1), calls=%async_computation.2 | async-start | bytes 196608 | tf_op jit(solution)/shard_map/all_to_all | solution.py:389
  79.6 4.6 %copy-start.3 = (f32[2,8,2560]{2,1,0:T(8,128)S(1)}, f32[2,8,2560]{2,1,0:T(8,128)}, u32[]{:S(2)}) copy-start(f32[2,8,2560]{2,1,0:T(8,128)} %constant.34.clone.steps_ref) | copy-start | bytes 491524
  79.6 4.6 %copy-start.7 = (s32[3,2048]{1,0:T(4,128)S(1)}, s32[3,2048]{1,0:T(4,128)}, u32[]{:S(2)}) copy-start(s32[3,2048]{1,0:T(4,128)} %coords_ref.2) | copy-start | bytes 73732
  79.6 21.0 %all-to-all-start.4 = ((bf16[16,160,256]{2,1,0:T(8,128)(2,1)}), bf16[16,160,256]{2,1,0:T(8,128)(2,1)}, u32[]{:S(2)}, u32[]{:S(2)}) async-start(bf16[16,160,256]{2,1,0:T(8,128)(2,1)} %copies.1), calls=%async_computation.4 | async-start | bytes 2621440 | tf_op jit(solution)/shard_map/all_to_all | solution.py:363
  100.6 10.5 %copy-start.1 = (bf16[2048,256]{1,0:T(8,128)(2,1)S(1)}, bf16[2048,256]{1,0:T(8,128)(2,1)}, u32[]{:S(2)}) copy-start(bf16[2048,256]{1,0:T(8,128)(2,1)} %features_ref.3) | copy-start | bytes 3145732
  100.6 10.5 %copy-start.4 = (bf16[256,256]{1,0:T(8,128)(2,1)S(1)}, bf16[256,256]{1,0:T(8,128)(2,1)}, u32[]{:S(2)}) copy-start(bf16[256,256]{1,0:T(8,128)(2,1)} %w_in_ref.1) | copy-start | bytes 393220
  100.6 10.5 %copy-start.5 = (bf16[256,256]{1,0:T(8,128)(2,1)S(1)}, bf16[256,256]{1,0:T(8,128)(2,1)}, u32[]{:S(2)}) copy-start(bf16[256,256]{1,0:T(8,128)(2,1)} %w_out_ref.1) | copy-start | bytes 393220
  100.6 10.5 %copy-start.9 = (f32[256]{0:T(256)S(1)}, f32[256]{0:T(256)}, u32[]{:S(2)}) copy-start(f32[256]{0:T(256)} %param.15) | copy-start | bytes 3076
  102.9 8.2 %collective-permute-start = (bf16[256,256]{1,0:T(8,128)(2,1)S(1)}, bf16[256,256]{1,0:T(8,128)(2,1)S(1)}, u32[]{:S(2)}, u32[]{:S(2)}) collective-permute-start(bf16[256,256]{1,0:T(8,128)(2,1)S(1)} %get-tuple-element.14), channel_id=1, source_target_pairs={{0,1},{1,0},{2,3},{3,2},{4,5},{5,4},{6,7},{7,6},{8,9},{9,8},{10,11... | collective-permute-start | bytes 393224 | tf_op jit(solution)/shard_map/ppermute | solution.py:395

commit v3 on v2

--- a/solution.py
+++ b/solution.py
@@ -20,7 +20,6 @@
 PLANES = 16
 OWN = POINTS // PLANES
 CHUNK = 2 * OWN
-PADDED = 24
 ROWS = 2 * POINTS
 F = 256
 TILE = 512
@@ -144,7 +143,6 @@
                 pltpu.VMEM((ROWS, F), jnp.float32),
             ],
         ),
-        compiler_params=pltpu.CompilerParams(vmem_limit_bytes=16 << 20),
         cost_estimate=pl.CostEstimate(
             flops=2 * ROWS * atoms * F, bytes_accessed=atoms * F * 2, transcendentals=0
         ),
@@ -152,8 +150,11 @@
     )(place, steps, coords, features)
 
 
-def weights_kernel(place_ref, miller_ref, weights_ref, out_ref):
-    plane = place_ref[4] * 4 + place_ref[3]
+SPOTS = 4 * OWN
+
+
+def weights_kernel(place_ref, miller_ref, weights_ref, own_ref, other_ref):
+    core, plane = place_ref[1], place_ref[4] * 4 + place_ref[3]
     m0, m1, m2 = miller_ref[0:1, :], miller_ref[1:2, :], miller_ref[2:3, :]
     flat = (m0 + KMAX) * SIDE + (m1 + KMAX)
     flip = (m2 < 0) | ((m2 == 0) & (flat < HALF))
@@ -165,32 +166,36 @@
     shard = jnp.where(m2 == 0, strip_shard, jnp.abs(m2) - 1)
     point = jnp.where(m2 == 0, PLANE + strip - strip_shard * STRIP, flat)
     spot = shard * POINTS + point
-    row = lax.broadcasted_iota(jnp.int32, (SHARDS * PADDED, miller_ref.shape[1]), 0)
-    owner = (row * 171) >> 12
-    own = row - owner * PADDED
-    wanted = owner * POINTS + plane * OWN + own
-    match = jnp.where((wanted == spot) & (own < OWN), 1.0, 0.0).astype(jnp.bfloat16)
+    row = lax.broadcasted_iota(jnp.int32, (SPOTS, miller_ref.shape[1]), 0)
+    high = (row >= OWN).astype(jnp.int32)
+    for bound in range(2, 4):
+        high += (row >= bound * OWN).astype(jnp.int32)
+    base = plane * OWN + row - high * OWN
     weights = weights_ref[...]
     upper = weights.astype(jnp.bfloat16)
     lower = (weights - upper.astype(jnp.float32)).astype(jnp.bfloat16)
-    summed = jnp.dot(match, upper, preferred_element_type=jnp.float32)
-    summed += jnp.dot(match, lower, preferred_element_type=jnp.float32)
-    out_ref[...] = summed.astype(jnp.bfloat16)
+    for held, out_ref in ((core, own_ref), (1 - core, other_ref)):
+        wanted = (high * 2 + held) * POINTS + base
+        match = jnp.where(wanted == spot, 1.0, 0.0).astype(jnp.bfloat16)
+        summed = jnp.dot(match, upper, preferred_element_type=jnp.float32)
+        summed += jnp.dot(match, lower, preferred_element_type=jnp.float32)
+        out_ref[...] = summed.astype(jnp.bfloat16)
 
 
 def grid_weights(place, miller, weights):
+    shape = jax.ShapeDtypeStruct((SPOTS, F), jnp.bfloat16)
     return pl.pallas_call(
         weights_kernel,
-        out_shape=jax.ShapeDtypeStruct((SHARDS * PADDED, F), jnp.bfloat16),
+        out_shape=(shape, shape),
         in_specs=[
             pl.BlockSpec(memory_space=pltpu.SMEM),
             pl.BlockSpec(memory_space=pltpu.VMEM),
             pl.BlockSpec(memory_space=pltpu.VMEM),
         ],
-        out_specs=pl.BlockSpec(memory_space=pltpu.VMEM),
+        out_specs=(pl.BlockSpec(memory_space=pltpu.VMEM),) * 2,
         compiler_params=pltpu.CompilerParams(vmem_limit_bytes=8 << 20),
         cost_estimate=pl.CostEstimate(
-            flops=4 * SHARDS * PADDED * 512 * F, bytes_accessed=512 * F * 4, transcendentals=0
+            flops=8 * SPOTS * 512 * F, bytes_accessed=512 * F * 4, transcendentals=0
         ),
         name="grid_weights",
     )(place, miller, weights)
@@ -213,49 +218,59 @@
     )(arrived)
 
 
-def filter_kernel(arrived_ref, weights_ref, out_ref, filtered):
+PACKED = CHUNK + SPOTS
+
+
+def scale_kernel(arrived_ref, own_ref, other_ref, out_ref, packed):
     total = jnp.sum(arrived_ref[...].astype(jnp.float32), axis=0)
     cosines, sines = total[:OWN], total[OWN:]
     power = jnp.sum(cosines * cosines + sines * sines, axis=1, keepdims=True) * (1.0 / (2 * F))
-    weights = jnp.sum(weights_ref[...].astype(jnp.float32), axis=0)[:OWN]
-    scaled = weights * (1.0 / jnp.sqrt(power + 1e-05))
-    filtered[:OWN, :] = cosines * scaled
-    filtered[OWN:, :] = sines * scaled
-    sent = filtered[...].astype(jnp.bfloat16)
+    scale = 1.0 / jnp.sqrt(power + 1e-05)
+    packed[:OWN, :] = cosines * scale
+    packed[OWN:CHUNK, :] = sines * scale
+    packed[CHUNK:, :] = own_ref[...].astype(jnp.float32) + other_ref[...].astype(jnp.float32)
+    sent = packed[...].astype(jnp.bfloat16)
     for peer in range(4):
         out_ref[peer] = sent
 
 
-def filter_factors(arrived, weights):
-    return pl.pallas_call(
-        filter_kernel,
-        out_shape=jax.ShapeDtypeStruct((4, CHUNK, F), jnp.bfloat16),
-        in_specs=[pl.BlockSpec(memory_space=pltpu.VMEM)] * 2,
+def scale_factors(arrived, own, other):
+    return pl.pallas_call(
+        scale_kernel,
+        out_shape=jax.ShapeDtypeStruct((4, PACKED, F), jnp.bfloat16),
+        in_specs=[pl.BlockSpec(memory_space=pltpu.VMEM)] * 3,
         out_specs=pl.BlockSpec(memory_space=pltpu.VMEM),
-        scratch_shapes=[pltpu.VMEM((CHUNK, F), jnp.float32)],
+        scratch_shapes=[pltpu.VMEM((PACKED, F), jnp.float32)],
         compiler_params=pltpu.CompilerParams(vmem_limit_bytes=8 << 20),
-        name="filter_factors",
-    )(arrived, weights)
+        name="scale_factors",
+    )(arrived, own, other)
 
 
 COLUMN = 4 * CHUNK
 
 
-def copies_kernel(column_ref, out_ref):
-    column = column_ref[...]
+def filter_kernel(arrived_ref, out_ref, filtered):
+    weights = jnp.sum(arrived_ref[:, CHUNK:, :].astype(jnp.float32), axis=0)
+    for high in range(4):
+        weight = weights[high * OWN : (high + 1) * OWN]
+        factors = arrived_ref[high, :CHUNK, :].astype(jnp.float32)
+        filtered[high * CHUNK : high * CHUNK + OWN, :] = factors[:OWN] * weight
+        filtered[high * CHUNK + OWN : (high + 1) * CHUNK, :] = factors[OWN:] * weight
+    column = filtered[...].astype(jnp.bfloat16)
     for peer in range(PLANES):
         out_ref[peer] = column
 
 
-def copies(column):
-    return pl.pallas_call(
-        copies_kernel,
+def filter_column(arrived):
+    return pl.pallas_call(
+        filter_kernel,
         out_shape=jax.ShapeDtypeStruct((PLANES, COLUMN, F), jnp.bfloat16),
         in_specs=[pl.BlockSpec(memory_space=pltpu.VMEM)],
         out_specs=pl.BlockSpec(memory_space=pltpu.VMEM),
+        scratch_shapes=[pltpu.VMEM((COLUMN, F), jnp.float32)],
         compiler_params=pltpu.CompilerParams(vmem_limit_bytes=8 << 20),
-        name="copies",
-    )(column)
+        name="filter_column",
+    )(arrived)
 
 
 ALL_ROWS = COLUMN * PLANES
@@ -385,12 +400,12 @@
     factors = partial_factors(place, jnp.asarray(STEPS), coords, features)
     factors, coords, miller = lax.optimization_barrier((factors, coords, miller))
     arrived = exchange(factors.reshape(PLANES, CHUNK, F), GROUPS_XY)
-    weights = grid_weights(place, miller, filter_weights).reshape(SHARDS, PADDED, F)
-    weights = lax.all_to_all(weights, "wave", split_axis=0, concat_axis=0, tiled=True)
+    own_weights, other_weights = grid_weights(place, miller, filter_weights)
+    other_weights = lax.ppermute(other_weights, AXES, SWAP)
     tables = message_tables(place, jnp.asarray(COLUMN_STEPS), coords)
     shares = exchange(plane_sum(arrived), GROUPS_LO)
-    filtered = exchange(filter_factors(shares, weights), GROUPS_HI)
-    filtered = exchange(copies(filtered.reshape(COLUMN, F)), GROUPS_XY).reshape(ALL_ROWS, F)
+    packed = exchange(scale_factors(shares, own_weights, other_weights), GROUPS_HI)
+    filtered = exchange(filter_column(packed), GROUPS_XY).reshape(ALL_ROWS, F)
     own, other = message_parts(place, tables, filtered)
     other = lax.ppermute(other, AXES, SWAP)
     return update(place, features, own, other, norm_gain.reshape(1, F), w_in, w_out)

time: 113 us -> 104 us (0.920)
  the two profiles are of different devices: /device:TPU:1 before, /device:TPU:65 now
where the time goes in v3:
time: 104 us; the launch traced here: 103 us
  blocking collectives  48.1 us (46%)
  Pallas kernels  17.9 us (17%)
  waiting for transfers between devices  17.9 us (17%)
  starting transfers between devices  17.6 us (17%)
  other arithmetic  1.49 us (1%)
    all_to_all x2, blocking collectives, exchange(): lax.all_to_all(pieces, AXES, split_axis=0, concat_axis=0, tiled=True, axi...  48.1 us
    all_to_all x2, waiting for transfers between devices, exchange(): lax.all_to_all(pieces, AXES, split_axis=0, concat_axis=0, tiled=True, axi...  16.1 us
    all_to_all x2, starting transfers between devices, exchange(): lax.all_to_all(pieces, AXES, split_axis=0, concat_axis=0, tiled=True, axi...  9.52 us
    pallas_call x1, Pallas kernels, partial_factors(): pl.pallas_call(factors_kernel, out_shape=jax.ShapeDtypeStruct((ROWS, F),...  6.78 us
    pallas_call x1, Pallas kernels, message_tables(): pl.pallas_call(tables_kernel, out_shape=jax.ShapeDtypeStruct((TILE, ALL_R...  4.36 us
    ppermute x1, starting transfers between devices, on_device(): other_weights = lax.ppermute(other_weights, AXES, SWAP)  4.28 us
    ppermute x1, starting transfers between devices, on_device(): other = lax.ppermute(other, AXES, SWAP)  3.79 us
    pallas_call x1, Pallas kernels, message_parts(): pl.pallas_call(message_kernel, out_shape=(jax.ShapeDtypeStruct((half, F),...  2.3 us
  transfers between devices with their start and end apart: 4, of which 3 were waited for; matrix products, arithmetic and copies ran while one was open for 0% of the time, Pallas kernels for 5%

profile of v3, /device:TPU:65, one launch (start us, length us, event | category | flops | bytes accessed | tf_op | source)
XLA Modules:
  0.0 103.0 jit_solution(5571302944375836751)
XLA Ops:
  0.0 1.5 %and_select_fusion.place_ref = s32[5]{0:T(128)} fusion(s32[5]{0:T(128)} %constant.37, s32[5]{0:T(128)} %constant.31.clone, pred[]{:T(512)S(6)} %ne.25, s32[]{:T(128)S(6)} %add.8), kind=kLoop, calls=%fused_computation | loop fusion | flops 60 | bytes 65 | tf_op jit(solution)/shard_map/jit(remainder)/select_n | solution.py:398
  1.5 0.0 copy-start.1
  1.5 0.0 copy-start.6
  1.5 0.0 copy-start.7
  1.5 6.8 %factors.1 = bf16[640,256]{1,0:T(8,128)(2,1)} custom-call(s32[5]{0:T(128)} %and_select_fusion.place_ref, f32[8,8,640]{2,1,0:T(8,128)} %constant.33.clone.steps_ref, s32[3,2048]{1,0:T(4,128)} %coords_ref.2, bf16[2048,256]{1,0:T(8,128)(2,1)} %features_ref.3), custom_call_target="tpu_custom_call" | custom-call | flops 671088640 | bytes 1048576 | tf_op jit(solution)/shard_map/factors/pallas_call | solution.py:129
  8.3 15.3 %all_to_all.20.arrived_ref = bf16[16,40,256]{2,1,0:T(8,128)(2,1)S(1)} all-to-all(bf16[16,40,256]{2,1,0:T(8,128)(2,1)} %bitcast.4), channel_id=1, replica_groups={{0,8,16,24,128,136,144,152,256,264,272,280,384,392,400,408},{1,9,17,25,..., dimensions={0} | all-to-all | bytes 655360 | tf_op jit(solution)/shard_map/all_to_all | solution.py:378
  23.6 0.7 plane_sum.1
  24.2 5.0 %all-to-all-start.1 = ((bf16[4,40,256]{2,1,0:T(8,128)(2,1)}), bf16[4,40,256]{2,1,0:T(8,128)(2,1)S(1)}, u32[]{:S(2)}, u32[]{:S(2)}) async-start(bf16[4,40,256]{2,1,0:T(8,128)(2,1)} %plane_sum.1), calls=%async_computation.1 | async-start | bytes 163840 | tf_op jit(solution)/shard_map/all_to_all | solution.py:378
  29.2 0.0 copy-done.1
  29.2 0.0 copy-done.6
  29.2 0.0 copy-done.7
  29.2 0.8 grid_weights.1
  30.1 4.3 %collective-permute-start = (bf16[80,256]{1,0:T(8,128)(2,1)S(1)}, bf16[80,256]{1,0:T(8,128)(2,1)S(1)}, u32[]{:S(2)}, u32[]{:S(2)}) collective-permute-start(bf16[80,256]{1,0:T(8,128)(2,1)S(1)} %get-tuple-element.16), channel_id=1, source_target_pairs={{0,1},{1,0},{2,3},{3,2},{4,5},{5,4},{6,7},{7,6},{8,9},{9,8},{10,11... | collective-permute-start | bytes 122888 | tf_op jit(solution)/shard_map/ppermute | solution.py:404
  34.4 0.8 collective-permute-done.other_ref
  35.2 0.0 all-to-all-done.1.arrived_ref
  35.2 0.1 scale_factors.1
  35.3 32.8 %all_to_all.21.arrived_ref = bf16[4,120,256]{2,1,0:T(8,128)(2,1)S(1)} all-to-all(bf16[4,120,256]{2,1,0:T(8,128)(2,1)S(1)} %scale_factors.1), channel_id=1, replica_groups={{0,2,4,6},{1,3,5,7},{32,34,36,38},{33,35,37,39},{64,66,68,70},{65,67,69..., dimensions={0} | all-to-all | bytes 491520 | tf_op jit(solution)/shard_map/all_to_all | solution.py:378
  68.1 1.2 %filter_column.1 = bf16[16,160,256]{2,1,0:T(8,128)(2,1)} custom-call(bf16[4,120,256]{2,1,0:T(8,128)(2,1)S(1)} %all_to_all.21.arrived_ref), custom_call_target="tpu_custom_call" | custom-call | tf_op jit(solution)/shard_map/filter_column/pallas_call | solution.py:265
  69.3 0.0 copy-start.2
  69.3 0.0 copy-start.5
  69.3 4.5 %all-to-all-start.3 = ((bf16[16,160,256]{2,1,0:T(8,128)(2,1)}), bf16[16,160,256]{2,1,0:T(8,128)(2,1)}, u32[]{:S(2)}, u32[]{:S(2)}) async-start(bf16[16,160,256]{2,1,0:T(8,128)(2,1)} %filter_column.1), calls=%async_computation.3 | async-start | bytes 2621440 | tf_op jit(solution)/shard_map/all_to_all | solution.py:378
  73.9 0.0 copy-done.2
  73.9 0.0 copy-done.5
  73.9 4.4 %message_tables.1.tables_ref = bf16[512,2560]{1,0:T(8,128)(2,1)S(1)} custom-call(s32[5]{0:T(128)S(1)} %copy-done.6, f32[2,8,2560]{2,1,0:T(8,128)S(1)} %copy-done.2, s32[3,2048]{1,0:T(4,128)S(1)} %copy-done.5), custom_call_target="tpu_custom_call" | custom-call | flops 20971520 | bytes 2621440 | tf_op jit(solution)/shard_map/message_tables/pallas_call | solution.py:292
  78.3 16.1 %all-to-all-done.3 = bf16[16,160,256]{2,1,0:T(8,128)(2,1)} async-done(((bf16[16,160,256]{2,1,0:T(8,128)(2,1)}), bf16[16,160,256]{2,1,0:T(8,128)(2,1)}, u32[]{:S(2)}, u32[]{:S(2)}) %all-to-all-start.3) | async-done | bytes 1310752 | tf_op jit(solution)/shard_map/all_to_all | solution.py:378
  94.3 0.0 copy-start
  94.3 0.0 copy-start.3
  94.3 0.0 copy-start.4
  94.3 0.0 copy-start.8
  94.3 2.3 %message.1 = (f32[256,256]{1,0:T(8,128)S(1)}, bf16[256,256]{1,0:T(8,128)(2,1)S(1)}) custom-call(s32[5]{0:T(128)S(1)} %copy-done.6, bf16[512,2560]{1,0:T(8,128)(2,1)S(1)} %message_tables.1.tables_ref, bf16[2560,256]{1,0:T(8,128)(2,1)} %bitcast.1.filtered_ref), custom_call_target="tpu_custom_call" | custom-call | tf_op jit(solution)/shard_map/message/pallas_call | solution.py:323
  96.6 3.8 %collective-permute-start.1 = (bf16[256,256]{1,0:T(8,128)(2,1)S(1)}, bf16[256,256]{1,0:T(8,128)(2,1)S(1)}, u32[]{:S(2)}, u32[]{:S(2)}) collective-permute-start(bf16[256,256]{1,0:T(8,128)(2,1)S(1)} %get-tuple-element.18), channel_id=1, source_target_pairs={{0,1},{1,0},{2,3},{3,2},{4,5},{5,4},{6,7},{7,6},{8,9},{9,8},{10,11... | collective-permute-start | bytes 393224 | tf_op jit(solution)/shard_map/ppermute | solution.py:410
  100.4 1.0 collective-permute-done.1.other_ref
  101.4 0.0 copy-done
  101.4 0.0 copy-done.3
  101.4 0.0 copy-done.4
  101.4 0.0 copy-done.8
  101.4 1.6 %update.1 = bf16[256,256]{1,0:T(8,128)(2,1)} custom-call(s32[5]{0:T(128)S(1)} %copy-done.6, bf16[2048,256]{1,0:T(8,128)(2,1)S(1)} %copy-done, f32[256,256]{1,0:T(8,128)S(1)} %get-tuple-element.17.own_ref, bf16[256,256]{1,0:T(8,128)(2,1)S(1)} %collective-permute-done.1.other_ref, f32[1,256]{1,0:T(1,128)S(1)} %bitcast.3, bf16[256,256]{1,0:T(8,128)(2,1)S(1)} %copy-done.3, ...), custom_call_target="tpu_custom_call" | custom-call | tf_op jit(solution)/shard_map/update/pallas_call | solution.py:356
Async XLA Ops:
  1.5 27.7 %copy-start.1 = (f32[512,256]{1,0:T(8,128)S(1)}, f32[512,256]{1,0:T(8,128)}, u32[]{:S(2)}) copy-start(f32[512,256]{1,0:T(8,128)} %weights_ref.1) | copy-start | bytes 1572868
  1.5 27.7 %copy-start.6 = (s32[5]{0:T(128)S(1)}, s32[5]{0:T(128)}, u32[]{:S(2)}) copy-start(s32[5]{0:T(128)} %and_select_fusion.place_ref) | copy-start | bytes 64
  1.5 27.7 %copy-start.7 = (s32[3,512]{1,0:T(4,128)S(1)}, s32[3,512]{1,0:T(4,128)}, u32[]{:S(2)}) copy-start(s32[3,512]{1,0:T(4,128)} %miller_ref) | copy-start | bytes 18436
  24.2 11.0 %all-to-all-start.1 = ((bf16[4,40,256]{2,1,0:T(8,128)(2,1)}), bf16[4,40,256]{2,1,0:T(8,128)(2,1)S(1)}, u32[]{:S(2)}, u32[]{:S(2)}) async-start(bf16[4,40,256]{2,1,0:T(8,128)(2,1)} %plane_sum.1), calls=%async_computation.1 | async-start | bytes 163840 | tf_op jit(solution)/shard_map/all_to_all | solution.py:378
  30.1 5.1 %collective-permute-start = (bf16[80,256]{1,0:T(8,128)(2,1)S(1)}, bf16[80,256]{1,0:T(8,128)(2,1)S(1)}, u32[]{:S(2)}, u32[]{:S(2)}) collective-permute-start(bf16[80,256]{1,0:T(8,128)(2,1)S(1)} %get-tuple-element.16), channel_id=1, source_target_pairs={{0,1},{1,0},{2,3},{3,2},{4,5},{5,4},{6,7},{7,6},{8,9},{9,8},{10,11... | collective-permute-start | bytes 122888 | tf_op jit(solution)/shard_map/ppermute | solution.py:404
  69.3 4.5 %copy-start.2 = (f32[2,8,2560]{2,1,0:T(8,128)S(1)}, f32[2,8,2560]{2,1,0:T(8,128)}, u32[]{:S(2)}) copy-start(f32[2,8,2560]{2,1,0:T(8,128)} %constant.34.clone.steps_ref) | copy-start | bytes 491524
  69.3 4.6 %copy-start.5 = (s32[3,2048]{1,0:T(4,128)S(1)}, s32[3,2048]{1,0:T(4,128)}, u32[]{:S(2)}) copy-start(s32[3,2048]{1,0:T(4,128)} %coords_ref.2) | copy-start | bytes 73732
  69.3 25.0 %all-to-all-start.3 = ((bf16[16,160,256]{2,1,0:T(8,128)(2,1)}), bf16[16,160,256]{2,1,0:T(8,128)(2,1)}, u32[]{:S(2)}, u32[]{:S(2)}) async-start(bf16[16,160,256]{2,1,0:T(8,128)(2,1)} %filter_column.1), calls=%async_computation.3 | async-start | bytes 2621440 | tf_op jit(solution)/shard_map/all_to_all | solution.py:378
  94.3 7.1 %copy-start = (bf16[2048,256]{1,0:T(8,128)(2,1)S(1)}, bf16[2048,256]{1,0:T(8,128)(2,1)}, u32[]{:S(2)}) copy-start(bf16[2048,256]{1,0:T(8,128)(2,1)} %features_ref.3) | copy-start | bytes 3145732
  94.3 7.1 %copy-start.3 = (bf16[256,256]{1,0:T(8,128)(2,1)S(1)}, bf16[256,256]{1,0:T(8,128)(2,1)}, u32[]{:S(2)}) copy-start(bf16[256,256]{1,0:T(8,128)(2,1)} %w_in_ref.1) | copy-start | bytes 393220
  94.3 7.1 %copy-start.4 = (bf16[256,256]{1,0:T(8,128)(2,1)S(1)}, bf16[256,256]{1,0:T(8,128)(2,1)}, u32[]{:S(2)}) copy-start(bf16[256,256]{1,0:T(8,128)(2,1)} %w_out_ref.1) | copy-start | bytes 393220
  94.3 7.1 %copy-start.8 = (f32[256]{0:T(256)S(1)}, f32[256]{0:T(256)}, u32[]{:S(2)}) copy-start(f32[256]{0:T(256)} %param.15) | copy-start | bytes 3076
  96.6 4.8 %collective-permute-start.1 = (bf16[256,256]{1,0:T(8,128)(2,1)S(1)}, bf16[256,256]{1,0:T(8,128)(2,1)S(1)}, u32[]{:S(2)}, u32[]{:S(2)}) collective-permute-start(bf16[256,256]{1,0:T(8,128)(2,1)S(1)} %get-tuple-element.18), channel_id=1, source_target_pairs={{0,1},{1,0},{2,3},{3,2},{4,5},{5,4},{6,7},{7,6},{8,9},{9,8},{10,11... | collective-permute-start | bytes 393224 | tf_op jit(solution)/shard_map/ppermute | solution.py:410

commit v4 on v3

--- a/solution.py
+++ b/solution.py
@@ -18,10 +18,12 @@
 SHARDS = 8
 POINTS = 320
 PLANES = 16
-OWN = POINTS // PLANES
+PEERS = 64
+OWN = POINTS // PEERS
 CHUNK = 2 * OWN
 ROWS = 2 * POINTS
 F = 256
+LANES = 128
 TILE = 512
 AXES = ("atom", "wave")
 BOTH = (((1,), (0,)), ((), ()))
@@ -121,14 +123,17 @@
 
     @pl.when(tile == pl.num_programs(0) - 1)
     def _():
-        out_ref[...] = total[...].astype(jnp.bfloat16)
+        for peer in range(PEERS):
+            for side in range(2):
+                piece = total[peer * CHUNK : (peer + 1) * CHUNK, side * LANES : (side + 1) * LANES]
+                out_ref[peer, side * CHUNK : (side + 1) * CHUNK, :] = piece.astype(jnp.bfloat16)
 
 
 def partial_factors(place, steps, coords, features):
     atoms = features.shape[0]
     return pl.pallas_call(
         factors_kernel,
-        out_shape=jax.ShapeDtypeStruct((ROWS, F), jnp.bfloat16),
+        out_shape=jax.ShapeDtypeStruct((PEERS, 2 * CHUNK, LANES), jnp.bfloat16),
         grid_spec=pltpu.PrefetchScalarGridSpec(
             num_scalar_prefetch=1,
             grid=(atoms // TILE,),
@@ -137,7 +142,7 @@
                 pl.BlockSpec((3, TILE), lambda t, place: (0, t)),
                 pl.BlockSpec((TILE, F), lambda t, place: (t, 0)),
             ],
-            out_specs=pl.BlockSpec((ROWS, F), lambda t, place: (0, 0)),
+            out_specs=pl.BlockSpec((PEERS, 2 * CHUNK, LANES), lambda t, place: (0, 0, 0)),
             scratch_shapes=[
                 pltpu.VMEM((ROWS, TILE), jnp.bfloat16),
                 pltpu.VMEM((ROWS, F), jnp.float32),
@@ -150,11 +155,11 @@
     )(place, steps, coords, features)
 
 
-SPOTS = 4 * OWN
+SPOTS = 32
 
 
 def weights_kernel(place_ref, miller_ref, weights_ref, own_ref, other_ref):
-    core, plane = place_ref[1], place_ref[4] * 4 + place_ref[3]
+    core, atom = place_ref[1], place_ref[3]
     m0, m1, m2 = miller_ref[0:1, :], miller_ref[1:2, :], miller_ref[2:3, :]
     flat = (m0 + KMAX) * SIDE + (m1 + KMAX)
     flip = (m2 < 0) | ((m2 == 0) & (flat < HALF))
@@ -168,9 +173,9 @@
     spot = shard * POINTS + point
     row = lax.broadcasted_iota(jnp.int32, (SPOTS, miller_ref.shape[1]), 0)
     high = (row >= OWN).astype(jnp.int32)
-    for bound in range(2, 4):
+    for bound in range(2, 7):
         high += (row >= bound * OWN).astype(jnp.int32)
-    base = plane * OWN + row - high * OWN
+    base = atom * OWN + row - high * OWN
     weights = weights_ref[...]
     upper = weights.astype(jnp.bfloat16)
     lower = (weights - upper.astype(jnp.float32)).astype(jnp.bfloat16)
@@ -201,37 +206,26 @@
     )(place, miller, weights)
 
 
-def plane_sum_kernel(arrived_ref, out_ref):
-    total = jnp.sum(arrived_ref[...].astype(jnp.float32), axis=0).astype(jnp.bfloat16)
-    for peer in range(4):
-        out_ref[peer] = total
-
-
-def plane_sum(arrived):
-    return pl.pallas_call(
-        plane_sum_kernel,
-        out_shape=jax.ShapeDtypeStruct((4, CHUNK, F), jnp.bfloat16),
-        in_specs=[pl.BlockSpec(memory_space=pltpu.VMEM)],
-        out_specs=pl.BlockSpec(memory_space=pltpu.VMEM),
-        compiler_params=pltpu.CompilerParams(vmem_limit_bytes=8 << 20),
-        name="plane_sum",
-    )(arrived)
-
-
-PACKED = CHUNK + SPOTS
-
-
-def scale_kernel(arrived_ref, own_ref, other_ref, out_ref, packed):
-    total = jnp.sum(arrived_ref[...].astype(jnp.float32), axis=0)
-    cosines, sines = total[:OWN], total[OWN:]
-    power = jnp.sum(cosines * cosines + sines * sines, axis=1, keepdims=True) * (1.0 / (2 * F))
+def scale_kernel(arrived_ref, own_ref, other_ref, out_ref, total, packed):
+    total[...] = jnp.sum(arrived_ref[...].astype(jnp.float32), axis=0)
+    halves = total[...] * total[...]
+    squares = halves[:CHUNK] + halves[CHUNK:]
+    power = jnp.sum(squares[:OWN] + squares[OWN:], axis=1, keepdims=True) * (1.0 / (2 * F))
     scale = 1.0 / jnp.sqrt(power + 1e-05)
-    packed[:OWN, :] = cosines * scale
-    packed[OWN:CHUNK, :] = sines * scale
-    packed[CHUNK:, :] = own_ref[...].astype(jnp.float32) + other_ref[...].astype(jnp.float32)
+    for part in range(2):
+        for side in range(2):
+            start = side * CHUNK + part * OWN
+            packed[part * OWN : (part + 1) * OWN, side * LANES : (side + 1) * LANES] = (
+                total[start : start + OWN, :] * scale
+            )
+    weights = own_ref[...].astype(jnp.float32) + other_ref[...].astype(jnp.float32)
+    packed[CHUNK:, :] = weights[: PACKED - CHUNK]
     sent = packed[...].astype(jnp.bfloat16)
     for peer in range(4):
         out_ref[peer] = sent
+
+
+PACKED = 32
 
 
 def scale_factors(arrived, own, other):
@@ -240,37 +234,61 @@
         out_shape=jax.ShapeDtypeStruct((4, PACKED, F), jnp.bfloat16),
         in_specs=[pl.BlockSpec(memory_space=pltpu.VMEM)] * 3,
         out_specs=pl.BlockSpec(memory_space=pltpu.VMEM),
-        scratch_shapes=[pltpu.VMEM((PACKED, F), jnp.float32)],
+        scratch_shapes=[
+            pltpu.VMEM((2 * CHUNK, LANES), jnp.float32),
+            pltpu.VMEM((PACKED, F), jnp.float32),
+        ],
         compiler_params=pltpu.CompilerParams(vmem_limit_bytes=8 << 20),
         name="scale_factors",
     )(arrived, own, other)
 
 
-COLUMN = 4 * CHUNK
+LINE = 4 * CHUNK
 
 
 def filter_kernel(arrived_ref, out_ref, filtered):
-    weights = jnp.sum(arrived_ref[:, CHUNK:, :].astype(jnp.float32), axis=0)
+    weights = jnp.sum(arrived_ref[...].astype(jnp.float32), axis=0)
     for high in range(4):
-        weight = weights[high * OWN : (high + 1) * OWN]
-        factors = arrived_ref[high, :CHUNK, :].astype(jnp.float32)
-        filtered[high * CHUNK : high * CHUNK + OWN, :] = factors[:OWN] * weight
-        filtered[high * CHUNK + OWN : (high + 1) * CHUNK, :] = factors[OWN:] * weight
-    column = filtered[...].astype(jnp.bfloat16)
+        weight = weights[CHUNK + high * OWN : CHUNK + (high + 1) * OWN]
+        factors = arrived_ref[high].astype(jnp.float32)
+        for part in range(2):
+            start = high * CHUNK + part * OWN
+            filtered[start : start + OWN, :] = factors[part * OWN : (part + 1) * OWN] * weight
+    line = filtered[...].astype(jnp.bfloat16)
+    for peer in range(4):
+        out_ref[peer] = line
+
+
+def filter_line(arrived):
+    return pl.pallas_call(
+        filter_kernel,
+        out_shape=jax.ShapeDtypeStruct((4, LINE, F), jnp.bfloat16),
+        in_specs=[pl.BlockSpec(memory_space=pltpu.VMEM)],
+        out_specs=pl.BlockSpec(memory_space=pltpu.VMEM),
+        scratch_shapes=[pltpu.VMEM((LINE, F), jnp.float32)],
+        compiler_params=pltpu.CompilerParams(vmem_limit_bytes=8 << 20),
+        name="filter_line",
+    )(arrived)
+
+
+COLUMN = 4 * LINE
+
+
+def copies_kernel(column_ref, out_ref):
+    column = column_ref[...]
     for peer in range(PLANES):
         out_ref[peer] = column
 
 
-def filter_column(arrived):
-    return pl.pallas_call(
-        filter_kernel,
+def copies(column):
+    return pl.pallas_call(
+        copies_kernel,
         out_shape=jax.ShapeDtypeStruct((PLANES, COLUMN, F), jnp.bfloat16),
         in_specs=[pl.BlockSpec(memory_space=pltpu.VMEM)],
         out_specs=pl.BlockSpec(memory_space=pltpu.VMEM),
-        scratch_shapes=[pltpu.VMEM((COLUMN, F), jnp.float32)],
         compiler_params=pltpu.CompilerParams(vmem_limit_bytes=8 << 20),
-        name="filter_column",
-    )(arrived)
+        name="copies",
+    )(column)
 
 
 ALL_ROWS = COLUMN * PLANES
@@ -385,8 +403,8 @@
 
 
 def column_steps(steps):
-    by_core = steps.reshape(4, 2, 8, PLANES, CHUNK)
-    return by_core.transpose(1, 2, 3, 0, 4).reshape(2, 8, ALL_ROWS)
+    by_core = steps.reshape(4, 2, 8, 4, 4, 4, CHUNK)
+    return by_core.transpose(1, 2, 3, 5, 4, 0, 6).reshape(2, 8, ALL_ROWS)
 
 
 STEPS = shard_steps()
@@ -395,17 +413,17 @@
 
 def on_device(features, coords, miller, filter_weights, norm_gain, w_in, w_out):
     number = lax.axis_index("atom") * 8 + lax.axis_index("wave")
-    place = number // np.array([1, 1, 2, 8, 128], np.int32) % np.array([8, 2, 4, 4, 4], np.int32)
+    place = number // np.array([1, 1, 2, 8], np.int32) % np.array([8, 2, 4, 64], np.int32)
 
     factors = partial_factors(place, jnp.asarray(STEPS), coords, features)
     factors, coords, miller = lax.optimization_barrier((factors, coords, miller))
-    arrived = exchange(factors.reshape(PLANES, CHUNK, F), GROUPS_XY)
+    arrived = lax.all_to_all(factors, "atom", split_axis=0, concat_axis=0, tiled=True)
     own_weights, other_weights = grid_weights(place, miller, filter_weights)
     other_weights = lax.ppermute(other_weights, AXES, SWAP)
     tables = message_tables(place, jnp.asarray(COLUMN_STEPS), coords)
-    shares = exchange(plane_sum(arrived), GROUPS_LO)
-    packed = exchange(scale_factors(shares, own_weights, other_weights), GROUPS_HI)
-    filtered = exchange(filter_column(packed), GROUPS_XY).reshape(ALL_ROWS, F)
+    packed = exchange(scale_factors(arrived, own_weights, other_weights), GROUPS_HI)
+    line = exchange(filter_line(packed), GROUPS_LO)
+    filtered = exchange(copies(line.reshape(COLUMN, F)), GROUPS_XY).reshape(ALL_ROWS, F)
     own, other = message_parts(place, tables, filtered)
     other = lax.ppermute(other, AXES, SWAP)
     return update(place, features, own, other, norm_gain.reshape(1, F), w_in, w_out)

time: 104 us -> 101 us (0.971)
  the two profiles are of different devices: /device:TPU:65 before, /device:TPU:1 now
where the time goes in v4:
time: 101 us
  blocking collectives  30.7 us (30%)
  starting transfers between devices  28.3 us (28%)
  waiting for transfers between devices  22.7 us (22%)
  Pallas kernels  17.4 us (17%)
  other arithmetic  1.43 us (1%)
    all_to_all x2, blocking collectives, exchange(): lax.all_to_all(pieces, AXES, split_axis=0, concat_axis=0, tiled=True, axi...  30.7 us
    all_to_all x1, starting transfers between devices, on_device(): lax.all_to_all(factors, 'atom', split_axis=0, concat_axis=0, tiled=True)  12.5 us
    all_to_all x1, waiting for transfers between devices, exchange(): lax.all_to_all(pieces, AXES, split_axis=0, concat_axis=0, tiled=True, axi...  11.1 us
    all_to_all x1, waiting for transfers between devices, on_device(): lax.all_to_all(factors, 'atom', split_axis=0, concat_axis=0, tiled=True)  9.76 us
    ppermute x1, starting transfers between devices, on_device(): other = lax.ppermute(other, AXES, SWAP)  8.33 us
    pallas_call x1, Pallas kernels, partial_factors(): pl.pallas_call(factors_kernel, out_shape=jax.ShapeDtypeStruct((PEERS, 2 *...  6.9 us
    all_to_all x1, starting transfers between devices, exchange(): lax.all_to_all(pieces, AXES, split_axis=0, concat_axis=0, tiled=True, axi...  4.53 us
    pallas_call x1, Pallas kernels, message_tables(): pl.pallas_call(tables_kernel, out_shape=jax.ShapeDtypeStruct((TILE, ALL_R...  4.35 us
  transfers between devices with their start and end apart: 4, of which 4 were waited for; matrix products, arithmetic and copies ran while one was open for 0% of the time, Pallas kernels for 5%

profile of v4, /device:TPU:1, one launch (start us, length us, event | category | flops | bytes accessed | tf_op | source)
XLA Modules:
  0.0 100.7 jit_solution(58394607895117801)
XLA Ops:
  0.0 1.4 %and_select_fusion.place_ref = s32[4]{0:T(128)} fusion(s32[4]{0:T(128)} %constant.37, s32[4]{0:T(128)} %constant.31.clone, pred[]{:T(512)S(6)} %ne.25, s32[]{:T(128)S(6)} %add.8), kind=kLoop, calls=%fused_computation | loop fusion | flops 48 | bytes 53 | tf_op jit(solution)/shard_map/jit(remainder)/select_n | solution.py:416
  1.4 0.0 copy-start.1
  1.4 0.0 copy-start.6
  1.4 0.0 copy-start.7
  1.4 6.9 %factors.1 = bf16[64,20,128]{2,1,0:T(8,128)(2,1)} custom-call(s32[4]{0:T(128)} %and_select_fusion.place_ref, f32[8,8,640]{2,1,0:T(8,128)} %constant.33.clone.steps_ref, s32[3,2048]{1,0:T(4,128)} %coords_ref.2, bf16[2048,256]{1,0:T(8,128)(2,1)} %features_ref.3), custom_call_target="tpu_custom_call" | custom-call | flops 671088640 | bytes 1048576 | tf_op jit(solution)/shard_map/factors/pallas_call | solution.py:134
  8.3 12.5 %all-to-all-start = ((bf16[64,20,128]{2,1,0:T(8,128)(2,1)}), bf16[64,20,128]{2,1,0:T(8,128)(2,1)S(1)}, u32[]{:S(2)}, u32[]{:S(2)}) async-start(bf16[64,20,128]{2,1,0:T(8,128)(2,1)} %factors.1), calls=%async_computation | async-start | bytes 786432 | tf_op jit(solution)/shard_map/all_to_all | solution.py:420
  20.9 0.0 copy-done.1
  20.9 0.0 copy-done.6
  20.9 0.0 copy-done.7
  20.9 0.8 grid_weights.1
  21.7 2.9 %collective-permute-start = (bf16[32,256]{1,0:T(8,128)(2,1)S(1)}, bf16[32,256]{1,0:T(8,128)(2,1)S(1)}, u32[]{:S(2)}, u32[]{:S(2)}) collective-permute-start(bf16[32,256]{1,0:T(8,128)(2,1)S(1)} %get-tuple-element.16), channel_id=1, source_target_pairs={{0,1},{1,0},{2,3},{3,2},{4,5},{5,4},{6,7},{7,6},{8,9},{9,8},{10,11... | collective-permute-start | bytes 49160 | tf_op jit(solution)/shard_map/ppermute | solution.py:422
  24.6 0.8 collective-permute-done.other_ref
  25.4 9.8 %all-to-all-done.arrived_ref = bf16[64,20,128]{2,1,0:T(8,128)(2,1)S(1)} async-done(((bf16[64,20,128]{2,1,0:T(8,128)(2,1)}), bf16[64,20,128]{2,1,0:T(8,128)(2,1)S(1)}, u32[]{:S(2)}, u32[]{:S(2)}) %all-to-all-start) | async-done | bytes 327712 | tf_op jit(solution)/shard_map/all_to_all | solution.py:420
  35.2 0.2 scale_factors.1
  35.4 23.7 %all_to_all.20.arrived_ref = bf16[4,32,256]{2,1,0:T(8,128)(2,1)S(1)} all-to-all(bf16[4,32,256]{2,1,0:T(8,128)(2,1)S(1)} %scale_factors.1), channel_id=1, replica_groups={{0,2,4,6},{1,3,5,7},{32,34,36,38},{33,35,37,39},{64,66,68,70},{65,67,69..., dimensions={0} | all-to-all | bytes 131072 | tf_op jit(solution)/shard_map/all_to_all | solution.py:396
  59.1 7.0 %all_to_all.21 = bf16[4,40,256]{2,1,0:T(8,128)(2,1)S(1)} all-to-all(bf16[4,40,256]{2,1,0:T(8,128)(2,1)S(1)} %filter_line.1), channel_id=1, replica_groups={{0,32,64,96},{1,33,65,97},{2,34,66,98},{3,35,67,99},{4,36,68,100},{5,37..., dimensions={0} | all-to-all | bytes 163840 | tf_op jit(solution)/shard_map/all_to_all | solution.py:396
  66.1 1.2 %copies.1 = bf16[16,160,256]{2,1,0:T(8,128)(2,1)} custom-call(bf16[160,256]{1,0:T(8,128)(2,1)S(1)} %bitcast.3), custom_call_target="tpu_custom_call" | custom-call | tf_op jit(solution)/shard_map/copies/pallas_call | solution.py:284
  67.3 0.0 copy-start.2
  67.3 0.0 copy-start.5
  67.3 4.5 %all-to-all-start.3 = ((bf16[16,160,256]{2,1,0:T(8,128)(2,1)}), bf16[16,160,256]{2,1,0:T(8,128)(2,1)}, u32[]{:S(2)}, u32[]{:S(2)}) async-start(bf16[16,160,256]{2,1,0:T(8,128)(2,1)} %copies.1), calls=%async_computation.3 | async-start | bytes 2621440 | tf_op jit(solution)/shard_map/all_to_all | solution.py:396
  71.9 0.0 copy-done.2
  71.9 0.0 copy-done.5
  71.9 4.4 %message_tables.1.tables_ref = bf16[512,2560]{1,0:T(8,128)(2,1)S(1)} custom-call(s32[4]{0:T(128)S(1)} %copy-done.6, f32[2,8,2560]{2,1,0:T(8,128)S(1)} %copy-done.2, s32[3,2048]{1,0:T(4,128)S(1)} %copy-done.5), custom_call_target="tpu_custom_call" | custom-call | flops 20971520 | bytes 2621440 | tf_op jit(solution)/shard_map/message_tables/pallas_call | solution.py:310
  76.3 11.1 %all-to-all-done.3 = bf16[16,160,256]{2,1,0:T(8,128)(2,1)} async-done(((bf16[16,160,256]{2,1,0:T(8,128)(2,1)}), bf16[16,160,256]{2,1,0:T(8,128)(2,1)}, u32[]{:S(2)}, u32[]{:S(2)}) %all-to-all-start.3) | async-done | bytes 1310752 | tf_op jit(solution)/shard_map/all_to_all | solution.py:396
  87.4 0.0 copy-start
  87.4 0.0 copy-start.3
  87.4 0.0 copy-start.4
  87.4 0.0 copy-start.8
  87.4 2.3 %message.1 = (f32[256,256]{1,0:T(8,128)S(1)}, bf16[256,256]{1,0:T(8,128)(2,1)S(1)}) custom-call(s32[4]{0:T(128)S(1)} %copy-done.6, bf16[512,2560]{1,0:T(8,128)(2,1)S(1)} %message_tables.1.tables_ref, bf16[2560,256]{1,0:T(8,128)(2,1)} %bitcast.1.filtered_ref), custom_call_target="tpu_custom_call" | custom-call | tf_op jit(solution)/shard_map/message/pallas_call | solution.py:341
  89.7 8.3 %collective-permute-start.1 = (bf16[256,256]{1,0:T(8,128)(2,1)S(1)}, bf16[256,256]{1,0:T(8,128)(2,1)S(1)}, u32[]{:S(2)}, u32[]{:S(2)}) collective-permute-start(bf16[256,256]{1,0:T(8,128)(2,1)S(1)} %get-tuple-element.18), channel_id=1, source_target_pairs={{0,1},{1,0},{2,3},{3,2},{4,5},{5,4},{6,7},{7,6},{8,9},{9,8},{10,11... | collective-permute-start | bytes 393224 | tf_op jit(solution)/shard_map/ppermute | solution.py:428
  98.1 1.0 collective-permute-done.1.other_ref
  99.0 0.0 copy-done
  99.0 0.0 copy-done.3
  99.0 0.0 copy-done.4
  99.0 0.0 copy-done.8
  99.1 1.6 %update.1 = bf16[256,256]{1,0:T(8,128)(2,1)} custom-call(s32[4]{0:T(128)S(1)} %copy-done.6, bf16[2048,256]{1,0:T(8,128)(2,1)S(1)} %copy-done, f32[256,256]{1,0:T(8,128)S(1)} %get-tuple-element.17.own_ref, bf16[256,256]{1,0:T(8,128)(2,1)S(1)} %collective-permute-done.1.other_ref, f32[1,256]{1,0:T(1,128)S(1)} %bitcast.4, bf16[256,256]{1,0:T(8,128)(2,1)S(1)} %copy-done.3, ...), custom_call_target="tpu_custom_call" | custom-call | tf_op jit(solution)/shard_map/update/pallas_call | solution.py:374
  (1 shorter events, 0.0 us)
Async XLA Ops:
  1.4 19.5 %copy-start.1 = (f32[512,256]{1,0:T(8,128)S(1)}, f32[512,256]{1,0:T(8,128)}, u32[]{:S(2)}) copy-start(f32[512,256]{1,0:T(8,128)} %weights_ref.1) | copy-start | bytes 1572868
  1.4 19.5 %copy-start.6 = (s32[4]{0:T(128)S(1)}, s32[4]{0:T(128)}, u32[]{:S(2)}) copy-start(s32[4]{0:T(128)} %and_select_fusion.place_ref) | copy-start | bytes 52
  1.4 19.5 %copy-start.7 = (s32[3,512]{1,0:T(4,128)S(1)}, s32[3,512]{1,0:T(4,128)}, u32[]{:S(2)}) copy-start(s32[3,512]{1,0:T(4,128)} %miller_ref) | copy-start | bytes 18436
  8.3 26.8 %all-to-all-start = ((bf16[64,20,128]{2,1,0:T(8,128)(2,1)}), bf16[64,20,128]{2,1,0:T(8,128)(2,1)S(1)}, u32[]{:S(2)}, u32[]{:S(2)}) async-start(bf16[64,20,128]{2,1,0:T(8,128)(2,1)} %factors.1), calls=%async_computation | async-start | bytes 786432 | tf_op jit(solution)/shard_map/all_to_all | solution.py:420
  21.7 3.7 %collective-permute-start = (bf16[32,256]{1,0:T(8,128)(2,1)S(1)}, bf16[32,256]{1,0:T(8,128)(2,1)S(1)}, u32[]{:S(2)}, u32[]{:S(2)}) collective-permute-start(bf16[32,256]{1,0:T(8,128)(2,1)S(1)} %get-tuple-element.16), channel_id=1, source_target_pairs={{0,1},{1,0},{2,3},{3,2},{4,5},{5,4},{6,7},{7,6},{8,9},{9,8},{10,11... | collective-permute-start | bytes 49160 | tf_op jit(solution)/shard_map/ppermute | solution.py:422
  67.3 4.5 %copy-start.2 = (f32[2,8,2560]{2,1,0:T(8,128)S(1)}, f32[2,8,2560]{2,1,0:T(8,128)}, u32[]{:S(2)}) copy-start(f32[2,8,2560]{2,1,0:T(8,128)} %constant.34.clone.steps_ref) | copy-start | bytes 491524
  67.3 4.6 %copy-start.5 = (s32[3,2048]{1,0:T(4,128)S(1)}, s32[3,2048]{1,0:T(4,128)}, u32[]{:S(2)}) copy-start(s32[3,2048]{1,0:T(4,128)} %coords_ref.2) | copy-start | bytes 73732
  67.3 20.1 %all-to-all-start.3 = ((bf16[16,160,256]{2,1,0:T(8,128)(2,1)}), bf16[16,160,256]{2,1,0:T(8,128)(2,1)}, u32[]{:S(2)}, u32[]{:S(2)}) async-start(bf16[16,160,256]{2,1,0:T(8,128)(2,1)} %copies.1), calls=%async_computation.3 | async-start | bytes 2621440 | tf_op jit(solution)/shard_map/all_to_all | solution.py:396
  87.4 11.6 %copy-start = (bf16[2048,256]{1,0:T(8,128)(2,1)S(1)}, bf16[2048,256]{1,0:T(8,128)(2,1)}, u32[]{:S(2)}) copy-start(bf16[2048,256]{1,0:T(8,128)(2,1)} %features_ref.3) | copy-start | bytes 3145732
  87.4 11.6 %copy-start.3 = (bf16[256,256]{1,0:T(8,128)(2,1)S(1)}, bf16[256,256]{1,0:T(8,128)(2,1)}, u32[]{:S(2)}) copy-start(bf16[256,256]{1,0:T(8,128)(2,1)} %w_in_ref.1) | copy-start | bytes 393220
  87.4 11.6 %copy-start.4 = (bf16[256,256]{1,0:T(8,128)(2,1)S(1)}, bf16[256,256]{1,0:T(8,128)(2,1)}, u32[]{:S(2)}) copy-start(bf16[256,256]{1,0:T(8,128)(2,1)} %w_out_ref.1) | copy-start | bytes 393220
  87.4 11.6 %copy-start.8 = (f32[256]{0:T(256)S(1)}, f32[256]{0:T(256)}, u32[]{:S(2)}) copy-start(f32[256]{0:T(256)} %param.15) | copy-start | bytes 3076
  89.7 9.3 %collective-permute-start.1 = (bf16[256,256]{1,0:T(8,128)(2,1)S(1)}, bf16[256,256]{1,0:T(8,128)(2,1)S(1)}, u32[]{:S(2)}, u32[]{:S(2)}) collective-permute-start(bf16[256,256]{1,0:T(8,128)(2,1)S(1)} %get-tuple-element.18), channel_id=1, source_target_pairs={{0,1},{1,0},{2,3},{3,2},{4,5},{5,4},{6,7},{7,6},{8,9},{9,8},{10,11... | collective-permute-start | bytes 393224 | tf_op jit(solution)/shard_map/ppermute | solution.py:428

commit v5 on v3

v5 whole, which is shorter than its diff:
```python
import itertools
import math

import jax
import jax.numpy as jnp
import numpy as np
from jax import lax
from jax.experimental import pallas as pl
from jax.experimental.pallas import tpu as pltpu
from jax.sharding import PartitionSpec as P

K = 4096
KMAX = 8
SIDE = 2 * KMAX + 1
PLANES = 16
BLOCKS = 4
OWN = 20
BLOCK = 2 * OWN
COLUMN = BLOCKS * BLOCK
ALL_ROWS = PLANES * COLUMN
MIDDLE = 8
POINTS = BLOCKS * OWN
F = 256
HALVES = 256
TILE = 512
AXES = ("atom", "wave")
BOTH = (((1,), (0,)), ((), ()))
OUTER = (((0,), (0,)), ((), ()))


def device(y, z_lo, x, z_hi, core):
    return (((y * 4 + z_lo) * 4 + x) * 4 + z_hi) * 2 + core


FOUR = range(4)
TWO = range(2)
GROUPS_XY = [
    [device(y, l, x, h, c) for y in FOUR for x in FOUR] for l in FOUR for h in FOUR for c in TWO
]
GROUPS_LO = [
    [device(y, l, x, h, c) for l in FOUR] for y in FOUR for x in FOUR for h in FOUR for c in TWO
]
SWAP = [
    (device(y, l, x, h, c), device(y, l, x, h, 1 - c))
    for y, l, x, h, c in itertools.product(FOUR, FOUR, FOUR, FOUR, TWO)
]
OUTER_PAIRS = [
    (device(y, l, x, h, c), device(y, l, x, 3 - h, c))
    for y, l, x, h, c in itertools.product(FOUR, FOUR, FOUR, FOUR, TWO)
]
INNER_PAIRS = [
    (device(y, l, x, h, c), device(y, l, x, h ^ 1, c))
    for y, l, x, h, c in itertools.product(FOUR, FOUR, FOUR, FOUR, TWO)
]


def row_line(core, block, spot):
    third = 2 * block + core + 1
    if spot < SIDE:
        return (spot - KMAX, 0, third), 1
    if spot == SIDE:
        return (4 * core + block + 1, 0, 0), 1
    if spot == SIDE + 1:
        return (0, KMAX, third), 0
    if (core, block) == (0, 0):
        return (0, MIDDLE, 0), 1
    if (core, block) == (0, 1):
        return (MIDDLE + 1, KMAX, 0), 0
    if (core, block) == (0, 2):
        return (KMAX, KMAX, MIDDLE + 1), 2
    return None


def column_of(vector, part):
    steps = np.zeros(8, np.float32)
    steps[0:3] = vector
    steps[3:6] = vector
    steps[6] = -0.25 * part
    return steps


def row_steps(core, block, row, peer):
    line = row_line(core, block, row % OWN)
    if line is None:
        return column_of((0, 0, 0), 1)
    vector = list(line[0])
    vector[line[1]] += peer - MIDDLE
    return column_of(vector, row // OWN)


def stride_steps(core, block, row):
    line = row_line(core, block, row % OWN)
    vector = [0, 0, 0]
    vector[1 if line is None else line[1]] = 1
    return column_of(vector, 0)


MIXED = list(range(16, 24)) + list(range(32, 40))
FIRST = 2 * BLOCK + len(MIXED)


def first_steps():
    out = np.zeros((2, 8, BLOCKS * FIRST), np.float32)
    for core in range(2):
        columns = []
        for block in range(BLOCKS):
            columns += [row_steps(core, block, row, MIDDLE) for row in range(BLOCK)]
            columns += [row_steps(core, block, row, MIDDLE + 1) for row in range(BLOCK)]
            columns += [stride_steps(core, block, row) for row in MIXED]
        out[core] = np.stack(columns, axis=1)
    return out


def all_steps():
    rows = list(itertools.product(range(PLANES), range(BLOCKS), range(BLOCK)))
    return np.stack(
        [np.stack([row_steps(c, b, r, q) for q, b, r in rows], axis=1) for c in range(2)]
    )


def split_coords(coords):
    high = (coords >> 8).astype(jnp.float32) * (1.0 / 256.0)
    low = (coords & 255).astype(jnp.float32) * (1.0 / 65536.0)
    ones = jnp.ones((2, coords.shape[1]), jnp.float32)
    return jnp.concatenate([high, low, ones], axis=0).astype(jnp.bfloat16)


def cosine_coefficients():
    nodes = 0.125 + 0.125 * np.cos(np.pi * (np.arange(400) + 0.5) / 400)
    fit = np.polynomial.chebyshev.Chebyshev.fit(
        nodes, np.cos(2 * np.pi * np.sqrt(nodes)), 6, domain=[0, 0.25]
    )
    return [float(c) for c in fit.convert(kind=np.polynomial.Polynomial).coef]


COSINE = cosine_coefficients()


def cosine_of_turns(turns):
    left = turns - jnp.round(turns)
    square = left * left
    total = jnp.full_like(square, COSINE[-1])
    for c in COSINE[-2::-1]:
        total = total * square + c
    return total


def factors_kernel(steps_ref, coords_ref, features_ref, out_ref, first, tables, total):
    tile = pl.program_id(0)
    core = lax.axis_index("wave") % 2
    parts = split_coords(coords_ref[...])
    steps = steps_ref[core].astype(jnp.bfloat16)
    for block in range(BLOCKS):
        turns = lax.dot_general(
            steps[:, block * FIRST : (block + 1) * FIRST],
            parts,
            OUTER,
            preferred_element_type=jnp.float32,
        )
        first[block] = cosine_of_turns(turns)
    features = features_ref[...]
    for block in range(BLOCKS):
        for start in range(0, TILE, HALVES):
            lanes = pl.ds(start, HALVES)
            at = first[block, :BLOCK, lanes]
            after = first[block, BLOCK : 2 * BLOCK, lanes]
            mixed = 2.0 * first[block, 2 * BLOCK :, lanes]
            common = jnp.broadcast_to(mixed[0:1, :], (16, HALVES))
            stride = jnp.concatenate([common, mixed[:8], common[:8], mixed[8:]], axis=0)
            held = {MIDDLE: at, MIDDLE + 1: after}
            for peer in range(MIDDLE, PLANES, 2):
                for later in (peer, peer + 1):
                    if later not in held:
                        held[later] = stride * held[later - 1] - held[later - 2]
                pair = jnp.concatenate([held[peer], held[peer + 1]], axis=0)
                tables[block, peer * BLOCK : (peer + 2) * BLOCK, lanes] = pair.astype(jnp.bfloat16)
            for peer in range(MIDDLE - 2, -1, -2):
                for earlier in (peer + 1, peer):
                    held[earlier] = stride * held[earlier + 1] - held[earlier + 2]
                pair = jnp.concatenate([held[peer], held[peer + 1]], axis=0)
                tables[block, peer * BLOCK : (peer + 2) * BLOCK, lanes] = pair.astype(jnp.bfloat16)
        added = jnp.dot(tables[block], features, preferred_element_type=jnp.float32)

        @pl.when(tile == 0)
        def _():
            total[block] = added

        @pl.when(tile > 0)
        def _():
            total[block] += added

    @pl.when(tile == pl.num_programs(0) - 1)
    def _():
        for block in range(BLOCKS):
            for peer in range(PLANES):
                piece = total[block, peer * BLOCK : (peer + 1) * BLOCK, :]
                out_ref[peer, block * BLOCK : (block + 1) * BLOCK, :] = piece.astype(jnp.bfloat16)


def partial_factors(steps, coords, features):
    atoms = features.shape[0]
    return pl.pallas_call(
        factors_kernel,
        out_shape=jax.ShapeDtypeStruct((PLANES, COLUMN, F), jnp.bfloat16),
        grid=(atoms // TILE,),
        in_specs=[
            pl.BlockSpec((2, 8, BLOCKS * FIRST), lambda t: (0, 0, 0)),
            pl.BlockSpec((3, TILE), lambda t: (0, t)),
            pl.BlockSpec((TILE, F), lambda t: (t, 0)),
        ],
        out_specs=pl.BlockSpec((PLANES, COLUMN, F), lambda t: (0, 0, 0)),
        scratch_shapes=[
            pltpu.VMEM((BLOCKS, FIRST, TILE), jnp.float32),
            pltpu.VMEM((BLOCKS, PLANES * BLOCK, TILE), jnp.bfloat16),
            pltpu.VMEM((BLOCKS, PLANES * BLOCK, F), jnp.float32),
        ],
        cost_estimate=pl.CostEstimate(
            flops=2 * ALL_ROWS * atoms * F, bytes_accessed=atoms * F * 2, transcendentals=0
        ),
        name="factors",
    )(steps, coords, features)


def grid_spots(m0, m1, m2):
    flip = (m2 < 0) | ((m2 == 0) & ((m0 < 0) | ((m0 == 0) & (m1 < 0))))
    m0, m1, m2 = (jnp.where(flip, -m, m) for m in (m0, m1, m2))
    zero, last = m2 == 0, m1 == KMAX
    corner = last & (m0 == KMAX) & (m2 > 0)
    edge = zero & last & (m0 > 0)
    axis = zero & (m0 == 0)
    sheet = zero & (m0 > 0) & (m1 < KMAX)
    rim = last & (m0 < KMAX) & (m2 > 0)
    core = jnp.where(sheet, (m0 - 1) >> 2, (m2 - 1) & 1)
    block = jnp.where(sheet, (m0 - 1) & 3, (m2 - 1) >> 1)
    block = jnp.where(corner, 2, jnp.where(edge, 1, jnp.where(axis, 0, block)))
    core = jnp.where(corner | edge | axis, 0, core)
    peer = jnp.where(rim, m0 + KMAX, m1 + KMAX)
    peer = jnp.where(corner, m2 - 1, jnp.where(edge, m0 - 1, jnp.where(axis, m1, peer)))
    spot = jnp.where(sheet, SIDE, jnp.where(rim, SIDE + 1, m0 + KMAX))
    spot = jnp.where(corner | edge | axis, SIDE + 2, spot)
    return ((core * PLANES + peer) * BLOCKS + block) * OWN + spot


def weights_kernel(miller_ref, weights_ref, own_ref, other_ref):
    core, atom = lax.axis_index("wave") % 2, lax.axis_index("atom")
    plane = atom // 16 * 4 + atom % 4
    spots = grid_spots(miller_ref[0:1, :], miller_ref[1:2, :], miller_ref[2:3, :])
    row = lax.broadcasted_iota(jnp.int32, (POINTS, miller_ref.shape[1]), 0)
    weights = weights_ref[...]
    upper = weights.astype(jnp.bfloat16)
    lower = (weights - upper.astype(jnp.float32)).astype(jnp.bfloat16)
    for held, out_ref in ((core, own_ref), (1 - core, other_ref)):
        wanted = row + (held * PLANES + plane) * POINTS
        match = jnp.where(wanted == spots, 1.0, 0.0).astype(jnp.bfloat16)
        summed = jnp.dot(match, upper, preferred_element_type=jnp.float32)
        summed += jnp.dot(match, lower, preferred_element_type=jnp.float32)
        out_ref[...] = summed.astype(jnp.bfloat16)


def grid_weights(miller, weights):
    shape = jax.ShapeDtypeStruct((POINTS, F), jnp.bfloat16)
    return pl.pallas_call(
        weights_kernel,
        out_shape=(shape, shape),
        in_specs=[pl.BlockSpec(memory_space=pltpu.VMEM)] * 2,
        out_specs=(pl.BlockSpec(memory_space=pltpu.VMEM),) * 2,
        compiler_params=pltpu.CompilerParams(vmem_limit_bytes=8 << 20),
        cost_estimate=pl.CostEstimate(
            flops=8 * POINTS * 512 * F, bytes_accessed=512 * F * 4, transcendentals=0
        ),
        name="grid_weights",
    )(miller, weights)


def plane_sum_kernel(arrived_ref, out_ref):
    total = arrived_ref[0].astype(jnp.float32)
    for peer in range(1, PLANES):
        total += arrived_ref[peer].astype(jnp.float32)
    sent = total.astype(jnp.bfloat16)
    for peer in range(4):
        out_ref[peer] = sent


def plane_sum(arrived):
    return pl.pallas_call(
        plane_sum_kernel,
        out_shape=jax.ShapeDtypeStruct((4, COLUMN, F), jnp.bfloat16),
        in_specs=[pl.BlockSpec(memory_space=pltpu.VMEM)],
        out_specs=pl.BlockSpec(memory_space=pltpu.VMEM),
        compiler_params=pltpu.CompilerParams(vmem_limit_bytes=8 << 20),
        name="plane_sum",
    )(arrived)


def filter_kernel(arrived_ref, near_ref, far_ref, out_ref, total, filtered):
    total[...] = jnp.sum(arrived_ref[...].astype(jnp.float32), axis=0)
    weights = near_ref[...].astype(jnp.float32) + far_ref[...].astype(jnp.float32)
    for block in range(BLOCKS):
        start = block * BLOCK
        cosines, sines = total[start : start + OWN, :], total[start + OWN : start + BLOCK, :]
        power = jnp.sum(cosines * cosines + sines * sines, axis=1, keepdims=True) * (0.5 / F)
        scaled = weights[block * OWN : (block + 1) * OWN] * (1.0 / jnp.sqrt(power + 1e-05))
        filtered[start : start + OWN, :] = cosines * scaled
        filtered[start + OWN : start + BLOCK, :] = sines * scaled
    column = filtered[...].astype(jnp.bfloat16)
    for peer in range(PLANES):
        out_ref[peer] = column


def filter_column(arrived, near, far):
    return pl.pallas_call(
        filter_kernel,
        out_shape=jax.ShapeDtypeStruct((PLANES, COLUMN, F), jnp.bfloat16),
        in_specs=[pl.BlockSpec(memory_space=pltpu.VMEM)] * 3,
        out_specs=pl.BlockSpec(memory_space=pltpu.VMEM),
        scratch_shapes=[pltpu.VMEM((COLUMN, F), jnp.float32)] * 2,
        compiler_params=pltpu.CompilerParams(vmem_limit_bytes=8 << 20),
        name="filter_column",
    )(arrived, near, far)


def tables_kernel(place_ref, steps_ref, coords_ref, out_ref):
    parts = split_coords(coords_ref[...])
    steps = steps_ref[0].astype(jnp.bfloat16)
    block = 128
    for start in range(0, TILE, block):
        turns = lax.dot_general(
            parts[:, start : start + block], steps, OUTER, preferred_element_type=jnp.float32
        )
        out_ref[start : start + block, :] = cosine_of_turns(turns).astype(jnp.bfloat16)


def message_tables(place, steps, coords):
    width = 512
    return pl.pallas_call(
        tables_kernel,
        out_shape=jax.ShapeDtypeStruct((TILE, ALL_ROWS), jnp.bfloat16),
        grid_spec=pltpu.PrefetchScalarGridSpec(
            num_scalar_prefetch=1,
            grid=(ALL_ROWS // width,),
            in_specs=[
                pl.BlockSpec((1, 8, width), lambda t, place: (place[1], 0, t)),
                pl.BlockSpec((3, TILE), lambda t, place: (0, place[2])),
            ],
            out_specs=pl.BlockSpec((TILE, width), lambda t, place: (0, t)),
        ),
        compiler_params=pltpu.CompilerParams(vmem_limit_bytes=16 << 20),
        cost_estimate=pl.CostEstimate(
            flops=16 * TILE * ALL_ROWS, bytes_accessed=TILE * ALL_ROWS * 2, transcendentals=0
        ),
        name="message_tables",
    )(place, steps, coords)


def message_kernel(place_ref, tables_ref, filtered_ref, own_ref, other_ref, total):
    core = place_ref[1]
    total[...] = jnp.dot(tables_ref[...], filtered_ref[...], preferred_element_type=jnp.float32)
    half = TILE // 2
    own_ref[...] = total[pl.ds(pl.multiple_of(core * half, half), half), :]
    other = total[pl.ds(pl.multiple_of((1 - core) * half, half), half), :]
    other_ref[...] = other.astype(jnp.bfloat16)


def message_parts(place, tables, filtered):
    half = TILE // 2
    return pl.pallas_call(
        message_kernel,
        out_shape=(
            jax.ShapeDtypeStruct((half, F), jnp.float32),
            jax.ShapeDtypeStruct((half, F), jnp.bfloat16),
        ),
        in_specs=[
            pl.BlockSpec(memory_space=pltpu.SMEM),
            pl.BlockSpec(memory_space=pltpu.VMEM),
            pl.BlockSpec(memory_space=pltpu.VMEM),
        ],
        out_specs=(pl.BlockSpec(memory_space=pltpu.VMEM),) * 2,
        scratch_shapes=[pltpu.VMEM((TILE, F), jnp.float32)],
        compiler_params=pltpu.CompilerParams(vmem_limit_bytes=16 << 20),
        name="message",
    )(place, tables, filtered)


def update_kernel(
    place_ref, features_ref, own_ref, other_ref, gain_ref, w_in_ref, w_out_ref, out_ref
):
    message = own_ref[...] + other_ref[...].astype(jnp.float32)
    updated = features_ref[...].astype(jnp.float32) + message * (1.0 / math.sqrt(K))
    power = jnp.mean(updated * updated, axis=1, keepdims=True)
    normed = (updated / jnp.sqrt(power + 1e-06) * gain_ref[...]).astype(jnp.bfloat16)
    hidden = jnp.dot(normed, w_in_ref[...], preferred_element_type=jnp.float32)
    hidden = (hidden / (1.0 + jnp.exp(-hidden))).astype(jnp.bfloat16)
    added = jnp.dot(hidden, w_out_ref[...], preferred_element_type=jnp.float32)
    out_ref[...] = (updated + added).astype(jnp.bfloat16)


def update(place, features, own, other, gain, w_in, w_out):
    half = TILE // 2
    return pl.pallas_call(
        update_kernel,
        out_shape=jax.ShapeDtypeStruct((half, F), jnp.bfloat16),
        grid_spec=pltpu.PrefetchScalarGridSpec(
            num_scalar_prefetch=1,
            grid=(1,),
            in_specs=[
                pl.BlockSpec((half, F), lambda t, place: (place[0], 0)),
                pl.BlockSpec((half, F), lambda t, place: (0, 0)),
                pl.BlockSpec((half, F), lambda t, place: (0, 0)),
                pl.BlockSpec((1, F), lambda t, place: (0, 0)),
                pl.BlockSpec((F, F), lambda t, place: (0, 0)),
                pl.BlockSpec((F, F), lambda t, place: (0, 0)),
            ],
            out_specs=pl.BlockSpec((half, F), lambda t, place: (0, 0)),
        ),
        compiler_params=pltpu.CompilerParams(vmem_limit_bytes=8 << 20),
        name="update",
    )(place, features, own, other, gain, w_in, w_out)


def exchange(pieces, groups):
    return lax.all_to_all(
        pieces, AXES, split_axis=0, concat_axis=0, tiled=True, axis_index_groups=groups
    )


FIRST_STEPS = first_steps()
ALL_STEPS = all_steps()


def on_device(features, coords, miller, filter_weights, norm_gain, w_in, w_out):
    factors = partial_factors(jnp.asarray(FIRST_STEPS), coords, features)
    factors, coords, miller = lax.optimization_barrier((factors, coords, miller))
    number = lax.axis_index("atom") * 8 + lax.axis_index("wave")
    place = number // np.array([1, 1, 2], np.int32) % np.array([8, 2, 4], np.int32)
    arrived = exchange(factors, GROUPS_XY)
    weights, swapped = grid_weights(miller, filter_weights)
    weights += lax.ppermute(swapped, AXES, SWAP)
    weights += lax.ppermute(weights, AXES, OUTER_PAIRS)
    tables = message_tables(place, jnp.asarray(ALL_STEPS), coords)
    sums = plane_sum(arrived)
    sums, weights = lax.optimization_barrier((sums, weights))
    shares = exchange(sums, GROUPS_LO)
    filtered = filter_column(shares, weights, lax.ppermute(weights, AXES, INNER_PAIRS))
    filtered = exchange(filtered, GROUPS_XY).reshape(ALL_ROWS, F)
    own, other = message_parts(place, tables, filtered)
    other = lax.ppermute(other, AXES, SWAP)
    return update(place, features, own, other, norm_gain.reshape(1, F), w_in, w_out)


def solution(mesh):
    in_specs = (P("atom", None), P(None, "atom"), P(None, "wave"), P("wave", None), P(), P(), P())
    out_specs = P(("atom", "wave"), None)
    return jax.shard_map(
        on_device, mesh=mesh, in_specs=in_specs, out_specs=out_specs, check_vma=False
    )
```

time: 104 us -> 96.2 us (0.925)
  blocking collectives: 48.1 us -> 0 us
  starting transfers between devices: 17.6 us -> 47.4 us
  waiting for transfers between devices: 17.9 us -> 24.2 us
  Pallas kernels: 17.9 us -> 23.7 us
  other arithmetic: 1.49 us -> 0.27 us
    all_to_all x2 -> x0, blocking collectives: 48.1 us -> none  [exchange(): lax.all_to_all(pieces, AXES, split_axis=0, concat_axis=0, tiled=True, axi...]
    ppermute x1 -> x3, starting transfers between devices: 4.28 us -> 22.3 us  [the longest x1 10.7 us: on_device(): weights += lax.ppermute(weights, AXES, OUTER_PAIRS)]
    all_to_all x2 -> x3, starting transfers between devices: 9.52 us -> 19.5 us  [exchange(): lax.all_to_all(pieces, AXES, split_axis=0, concat_axis=0, tiled=True, axi...]
    ppermute x1 -> x3, waiting for transfers between devices: 0.85 us -> 7.19 us  [the longest x1 4.93 us: on_device(): lax.ppermute(weights, AXES, INNER_PAIRS)]
    pallas_call x3 -> x2, Pallas kernels: 7.58 us -> 13.8 us  [the longest x1 12.9 us: partial_factors(): pl.pallas_call(factors_kernel, out_shape=jax.ShapeDtypeStruct((PLANES, CO...]
    ppermute x1, starting transfers between devices: 3.79 us -> 5.52 us  [on_device(): other = lax.ppermute(other, AXES, SWAP)]
    select_n x1, other arithmetic: 1.49 us -> 0.25 us  [on_device(): number // np.array([1, 1, 2], np.int32) % np.array([8, 2, 4], np.int32)]
    all_to_all x2 -> x3, waiting for transfers between devices: 16.1 us -> 16.1 us  [exchange(): lax.all_to_all(pieces, AXES, split_axis=0, concat_axis=0, tiled=True, axi...]
  transfers between devices with their start and end apart: 4 -> 7, of which waited for: 3 -> 6; matrix products, arithmetic and copies ran while one was open for 0% -> 0% of each run, Pallas kernels for 5% -> 5%
where the time goes in v5:
time: 96.2 us; the launch traced here: 95.7 us
  starting transfers between devices  47.4 us (49%)
  waiting for transfers between devices  24.2 us (25%)
  Pallas kernels  23.7 us (25%)
    all_to_all x3, starting transfers between devices, exchange(): lax.all_to_all(pieces, AXES, split_axis=0, concat_axis=0, tiled=True, axi...  19.5 us
    all_to_all x3, waiting for transfers between devices, exchange(): lax.all_to_all(pieces, AXES, split_axis=0, concat_axis=0, tiled=True, axi...  16.1 us
    pallas_call x1, Pallas kernels, partial_factors(): pl.pallas_call(factors_kernel, out_shape=jax.ShapeDtypeStruct((PLANES, CO...  12.9 us
    ppermute x1, starting transfers between devices, on_device(): weights += lax.ppermute(weights, AXES, OUTER_PAIRS)  10.7 us
    ppermute x1, starting transfers between devices, on_device(): lax.ppermute(weights, AXES, INNER_PAIRS)  8.8 us
    ppermute x1, starting transfers between devices, on_device(): other = lax.ppermute(other, AXES, SWAP)  5.52 us
    ppermute x1, waiting for transfers between devices, on_device(): lax.ppermute(weights, AXES, INNER_PAIRS)  4.93 us
    pallas_call x1, Pallas kernels, message_tables(): pl.pallas_call(tables_kernel, out_shape=jax.ShapeDtypeStruct((TILE, ALL_R...  4.35 us
  transfers between devices with their start and end apart: 7, of which 6 were waited for; matrix products, arithmetic and copies ran while one was open for 0% of the time, Pallas kernels for 5%

profile of v5, /device:TPU:65, one launch (start us, length us, event | category | flops | bytes accessed | tf_op | source)
XLA Modules:
  0.0 95.7 jit_solution(1600860641452713180)
XLA Ops:
  0.0 12.9 %factors.1 = bf16[16,160,256]{2,1,0:T(8,128)(2,1)} custom-call(f32[2,8,384]{2,1,0:T(8,128)} %constant.31.clone.steps_ref, s32[3,2048]{1,0:T(4,128)} %coords_ref.2, bf16[2048,256]{1,0:T(8,128)(2,1)} %features_ref.3), custom_call_target="tpu_custom_call" | custom-call | flops 2684354560 | bytes 1048576 | tf_op jit(solution)/shard_map/factors/pallas_call | solution.py:202
  12.9 0.0 copy-start.1
  12.9 0.0 copy-start.6
  12.9 6.9 %all-to-all-start = ((bf16[16,160,256]{2,1,0:T(8,128)(2,1)}), bf16[16,160,256]{2,1,0:T(8,128)(2,1)S(1)}, u32[]{:S(2)}, u32[]{:S(2)}) async-start(bf16[16,160,256]{2,1,0:T(8,128)(2,1)} %factors.1), calls=%async_computation | async-start | bytes 2621440 | tf_op jit(solution)/shard_map/all_to_all | solution.py:421
  19.8 0.0 copy-done.1
  19.8 0.0 copy-done.6
  19.8 0.3 grid_weights.1
  20.1 2.9 %collective-permute-start = (bf16[80,256]{1,0:T(8,128)(2,1)S(1)}, bf16[80,256]{1,0:T(8,128)(2,1)S(1)}, u32[]{:S(2)}, u32[]{:S(2)}) collective-permute-start(bf16[80,256]{1,0:T(8,128)(2,1)S(1)} %get-tuple-element.18), channel_id=1, source_target_pairs={{0,1},{1,0},{2,3},{3,2},{4,5},{5,4},{6,7},{7,6},{8,9},{9,8},{10,11... | collective-permute-start | bytes 122888 | tf_op jit(solution)/shard_map/ppermute | solution.py:437
  23.0 0.8 collective-permute-done
  23.9 10.7 %collective-permute-start.1 = (bf16[80,256]{1,0:T(8,128)(2,1)S(1)}, bf16[80,256]{1,0:T(8,128)(2,1)S(1)}, u32[]{:S(2)}, u32[]{:S(2)}) collective-permute-start(bf16[80,256]{1,0:T(8,128)(2,1)S(1)} %add.16), channel_id=1, source_target_pairs={{0,6},{1,7},{2,4},{3,5},{4,2},{5,3},{6,0},{7,1},{8,14},{9,15},{10,... | collective-permute-start | bytes 122888 | tf_op jit(solution)/shard_map/ppermute | solution.py:438
  34.5 1.4 %collective-permute-done.1 = bf16[80,256]{1,0:T(8,128)(2,1)S(1)} collective-permute-done((bf16[80,256]{1,0:T(8,128)(2,1)S(1)}, bf16[80,256]{1,0:T(8,128)(2,1)S(1)}, u32[]{:S(2)}, u32[]{:S(2)}) %collective-permute-start.1) | collective-permute-done | bytes 40992 | tf_op jit(solution)/shard_map/ppermute | solution.py:438
  36.0 2.8 %all-to-all-done.arrived_ref = bf16[16,160,256]{2,1,0:T(8,128)(2,1)S(1)} async-done(((bf16[16,160,256]{2,1,0:T(8,128)(2,1)}), bf16[16,160,256]{2,1,0:T(8,128)(2,1)S(1)}, u32[]{:S(2)}, u32[]{:S(2)}) %all-to-all-start) | async-done | bytes 1310752 | tf_op jit(solution)/shard_map/all_to_all | solution.py:421
  38.8 0.9 plane_sum.1
  39.7 5.0 %all-to-all-start.1 = ((bf16[4,160,256]{2,1,0:T(8,128)(2,1)}), bf16[4,160,256]{2,1,0:T(8,128)(2,1)S(1)}, u32[]{:S(2)}, u32[]{:S(2)}) async-start(bf16[4,160,256]{2,1,0:T(8,128)(2,1)} %plane_sum.1), calls=%async_computation.1 | async-start | bytes 655360 | tf_op jit(solution)/shard_map/all_to_all | solution.py:421
  44.6 8.8 %collective-permute-start.2 = (bf16[80,256]{1,0:T(8,128)(2,1)S(1)}, bf16[80,256]{1,0:T(8,128)(2,1)S(1)}, u32[]{:S(2)}, u32[]{:S(2)}) collective-permute-start(bf16[80,256]{1,0:T(8,128)(2,1)S(1)} %add.17.near_ref), channel_id=1, source_target_pairs={{0,2},{1,3},{2,0},{3,1},{4,6},{5,7},{6,4},{7,5},{8,10},{9,11},{10,... | collective-permute-start | bytes 122888 | tf_op jit(solution)/shard_map/ppermute | solution.py:443
  53.4 4.9 %collective-permute-done.2.far_ref = bf16[80,256]{1,0:T(8,128)(2,1)S(1)} collective-permute-done((bf16[80,256]{1,0:T(8,128)(2,1)S(1)}, bf16[80,256]{1,0:T(8,128)(2,1)S(1)}, u32[]{:S(2)}, u32[]{:S(2)}) %collective-permute-start.2) | collective-permute-done | bytes 40992 | tf_op jit(solution)/shard_map/ppermute | solution.py:443
  58.4 0.0 all-to-all-done.1.arrived_ref
  58.4 1.3 %filter_column.1 = bf16[16,160,256]{2,1,0:T(8,128)(2,1)} custom-call(bf16[4,160,256]{2,1,0:T(8,128)(2,1)S(1)} %all-to-all-done.1.arrived_ref, bf16[80,256]{1,0:T(8,128)(2,1)S(1)} %add.17.near_ref, bf16[80,256]{1,0:T(8,128)(2,1)S(1)} %collective-permute-done.2.far_ref), custom_call_target="tpu_custom_call" | custom-call | tf_op jit(solution)/shard_map/filter_column/pallas_call | solution.py:311
  59.7 0.0 copy-start.8
  59.7 0.0 copy-start.9
  59.7 0.0 copy-start.2
  59.7 0.0 copy-start.5
  59.7 7.7 %all-to-all-start.2 = ((bf16[16,160,256]{2,1,0:T(8,128)(2,1)}), bf16[16,160,256]{2,1,0:T(8,128)(2,1)}, u32[]{:S(2)}, u32[]{:S(2)}) async-start(bf16[16,160,256]{2,1,0:T(8,128)(2,1)} %filter_column.1), calls=%async_computation.2 | async-start | bytes 2621440 | tf_op jit(solution)/shard_map/all_to_all | solution.py:421
  67.4 0.0 copy-done.8
  67.4 0.0 copy-done.9
  67.4 0.2 and_select_fusion.place_ref
  67.6 0.0 copy-done.2
  67.7 0.0 copy-done.5
  67.7 4.4 %message_tables.1.tables_ref = bf16[512,2560]{1,0:T(8,128)(2,1)S(1)} custom-call(s32[3]{0:T(128)S(1)} %and_select_fusion.place_ref, f32[2,8,2560]{2,1,0:T(8,128)S(1)} %copy-done.2, s32[3,2048]{1,0:T(4,128)S(1)} %copy-done.5), custom_call_target="tpu_custom_call" | custom-call | flops 20971520 | bytes 2621440 | tf_op jit(solution)/shard_map/message_tables/pallas_call | solution.py:335
  72.0 13.2 %all-to-all-done.2 = bf16[16,160,256]{2,1,0:T(8,128)(2,1)} async-done(((bf16[16,160,256]{2,1,0:T(8,128)(2,1)}), bf16[16,160,256]{2,1,0:T(8,128)(2,1)}, u32[]{:S(2)}, u32[]{:S(2)}) %all-to-all-start.2) | async-done | bytes 1310752 | tf_op jit(solution)/shard_map/all_to_all | solution.py:421
  85.3 0.0 copy-start
  85.3 0.0 copy-start.3
  85.3 0.0 copy-start.4
  85.3 0.0 copy-start.7
  85.3 2.3 %message.1 = (f32[256,256]{1,0:T(8,128)S(1)}, bf16[256,256]{1,0:T(8,128)(2,1)S(1)}) custom-call(s32[3]{0:T(128)S(1)} %and_select_fusion.place_ref, bf16[512,2560]{1,0:T(8,128)(2,1)S(1)} %message_tables.1.tables_ref, bf16[2560,256]{1,0:T(8,128)(2,1)} %bitcast.filtered_ref), custom_call_target="tpu_custom_call" | custom-call | tf_op jit(solution)/shard_map/message/pallas_call | solution.py:366
  87.6 5.5 %collective-permute-start.3 = (bf16[256,256]{1,0:T(8,128)(2,1)S(1)}, bf16[256,256]{1,0:T(8,128)(2,1)S(1)}, u32[]{:S(2)}, u32[]{:S(2)}) collective-permute-start(bf16[256,256]{1,0:T(8,128)(2,1)S(1)} %get-tuple-element.22), channel_id=1, source_target_pairs={{0,1},{1,0},{2,3},{3,2},{4,5},{5,4},{6,7},{7,6},{8,9},{9,8},{10,11... | collective-permute-start | bytes 393224 | tf_op jit(solution)/shard_map/ppermute | solution.py:446
  93.1 1.0 %collective-permute-done.3.other_ref = bf16[256,256]{1,0:T(8,128)(2,1)S(1)} collective-permute-done((bf16[256,256]{1,0:T(8,128)(2,1)S(1)}, bf16[256,256]{1,0:T(8,128)(2,1)S(1)}, u32[]{:S(2)}, u32[]{:S(2)}) %collective-permute-start.3) | collective-permute-done | bytes 131104 | tf_op jit(solution)/shard_map/ppermute | solution.py:446
  94.1 0.0 copy-done
  94.1 0.0 copy-done.3
  94.1 0.0 copy-done.4
  94.1 0.0 copy-done.7
  94.1 1.6 %update.1 = bf16[256,256]{1,0:T(8,128)(2,1)} custom-call(s32[3]{0:T(128)S(1)} %and_select_fusion.place_ref, bf16[2048,256]{1,0:T(8,128)(2,1)S(1)} %copy-done, f32[256,256]{1,0:T(8,128)S(1)} %get-tuple-element.21.own_ref, bf16[256,256]{1,0:T(8,128)(2,1)S(1)} %collective-permute-done.3.other_ref, f32[1,256]{1,0:T(1,128)S(1)} %bitcast.2, ...), custom_call_target="tpu_custom_call" | custom-call | tf_op jit(solution)/shard_map/update/pallas_call | solution.py:399
  (2 shorter events, 0.0 us)
Async XLA Ops:
  12.9 6.9 %copy-start.1 = (f32[512,256]{1,0:T(8,128)S(1)}, f32[512,256]{1,0:T(8,128)}, u32[]{:S(2)}) copy-start(f32[512,256]{1,0:T(8,128)} %weights_ref.1) | copy-start | bytes 1572868
  12.9 6.9 %copy-start.6 = (s32[3,512]{1,0:T(4,128)S(1)}, s32[3,512]{1,0:T(4,128)}, u32[]{:S(2)}) copy-start(s32[3,512]{1,0:T(4,128)} %miller_ref) | copy-start | bytes 18436
  12.9 25.9 %all-to-all-start = ((bf16[16,160,256]{2,1,0:T(8,128)(2,1)}), bf16[16,160,256]{2,1,0:T(8,128)(2,1)S(1)}, u32[]{:S(2)}, u32[]{:S(2)}) async-start(bf16[16,160,256]{2,1,0:T(8,128)(2,1)} %factors.1), calls=%async_computation | async-start | bytes 2621440 | tf_op jit(solution)/shard_map/all_to_all | solution.py:421
  20.1 3.7 %collective-permute-start = (bf16[80,256]{1,0:T(8,128)(2,1)S(1)}, bf16[80,256]{1,0:T(8,128)(2,1)S(1)}, u32[]{:S(2)}, u32[]{:S(2)}) collective-permute-start(bf16[80,256]{1,0:T(8,128)(2,1)S(1)} %get-tuple-element.18), channel_id=1, source_target_pairs={{0,1},{1,0},{2,3},{3,2},{4,5},{5,4},{6,7},{7,6},{8,9},{9,8},{10,11... | collective-permute-start | bytes 122888 | tf_op jit(solution)/shard_map/ppermute | solution.py:437
  23.9 12.1 %collective-permute-start.1 = (bf16[80,256]{1,0:T(8,128)(2,1)S(1)}, bf16[80,256]{1,0:T(8,128)(2,1)S(1)}, u32[]{:S(2)}, u32[]{:S(2)}) collective-permute-start(bf16[80,256]{1,0:T(8,128)(2,1)S(1)} %add.16), channel_id=1, source_target_pairs={{0,6},{1,7},{2,4},{3,5},{4,2},{5,3},{6,0},{7,1},{8,14},{9,15},{10,... | collective-permute-start | bytes 122888 | tf_op jit(solution)/shard_map/ppermute | solution.py:438
  39.7 18.7 %all-to-all-start.1 = ((bf16[4,160,256]{2,1,0:T(8,128)(2,1)}), bf16[4,160,256]{2,1,0:T(8,128)(2,1)S(1)}, u32[]{:S(2)}, u32[]{:S(2)}) async-start(bf16[4,160,256]{2,1,0:T(8,128)(2,1)} %plane_sum.1), calls=%async_computation.1 | async-start | bytes 655360 | tf_op jit(solution)/shard_map/all_to_all | solution.py:421
  44.6 13.7 %collective-permute-start.2 = (bf16[80,256]{1,0:T(8,128)(2,1)S(1)}, bf16[80,256]{1,0:T(8,128)(2,1)S(1)}, u32[]{:S(2)}, u32[]{:S(2)}) collective-permute-start(bf16[80,256]{1,0:T(8,128)(2,1)S(1)} %add.17.near_ref), channel_id=1, source_target_pairs={{0,2},{1,3},{2,0},{3,1},{4,6},{5,7},{6,4},{7,5},{8,10},{9,11},{10,... | collective-permute-start | bytes 122888 | tf_op jit(solution)/shard_map/ppermute | solution.py:443
  59.7 7.7 %copy-start.8 = (s32[3]{0:T(128)S(1)}, s32[3]{0:T(128)}, u32[]{:S(2)}) copy-start(s32[3]{0:T(128)} %constant.37) | copy-start | bytes 40
  59.7 7.7 %copy-start.9 = (s32[3]{0:T(128)S(1)}, s32[3]{0:T(128)}, u32[]{:S(2)}) copy-start(s32[3]{0:T(128)} %constant.32.clone) | copy-start | bytes 40
  59.7 8.0 %copy-start.2 = (f32[2,8,2560]{2,1,0:T(8,128)S(1)}, f32[2,8,2560]{2,1,0:T(8,128)}, u32[]{:S(2)}) copy-start(f32[2,8,2560]{2,1,0:T(8,128)} %constant.34.clone.steps_ref) | copy-start | bytes 491524
  59.7 8.0 %copy-start.5 = (s32[3,2048]{1,0:T(4,128)S(1)}, s32[3,2048]{1,0:T(4,128)}, u32[]{:S(2)}) copy-start(s32[3,2048]{1,0:T(4,128)} %coords_ref.2) | copy-start | bytes 73732
  59.7 25.6 %all-to-all-start.2 = ((bf16[16,160,256]{2,1,0:T(8,128)(2,1)}), bf16[16,160,256]{2,1,0:T(8,128)(2,1)}, u32[]{:S(2)}, u32[]{:S(2)}) async-start(bf16[16,160,256]{2,1,0:T(8,128)(2,1)} %filter_column.1), calls=%async_computation.2 | async-start | bytes 2621440 | tf_op jit(solution)/shard_map/all_to_all | solution.py:421
  85.3 8.8 %copy-start = (bf16[2048,256]{1,0:T(8,128)(2,1)S(1)}, bf16[2048,256]{1,0:T(8,128)(2,1)}, u32[]{:S(2)}) copy-start(bf16[2048,256]{1,0:T(8,128)(2,1)} %features_ref.3) | copy-start | bytes 3145732
  85.3 8.8 %copy-start.3 = (bf16[256,256]{1,0:T(8,128)(2,1)S(1)}, bf16[256,256]{1,0:T(8,128)(2,1)}, u32[]{:S(2)}) copy-start(bf16[256,256]{1,0:T(8,128)(2,1)} %w_in_ref.1) | copy-start | bytes 393220
  85.3 8.8 %copy-start.4 = (bf16[256,256]{1,0:T(8,128)(2,1)S(1)}, bf16[256,256]{1,0:T(8,128)(2,1)}, u32[]{:S(2)}) copy-start(bf16[256,256]{1,0:T(8,128)(2,1)} %w_out_ref.1) | copy-start | bytes 393220
  85.3 8.8 %copy-start.7 = (f32[256]{0:T(256)S(1)}, f32[256]{0:T(256)}, u32[]{:S(2)}) copy-start(f32[256]{0:T(256)} %param.15) | copy-start | bytes 3076
  87.6 6.5 %collective-permute-start.3 = (bf16[256,256]{1,0:T(8,128)(2,1)S(1)}, bf16[256,256]{1,0:T(8,128)(2,1)S(1)}, u32[]{:S(2)}, u32[]{:S(2)}) collective-permute-start(bf16[256,256]{1,0:T(8,128)(2,1)S(1)} %get-tuple-element.22), channel_id=1, source_target_pairs={{0,1},{1,0},{2,3},{3,2},{4,5},{5,4},{6,7},{7,6},{8,9},{9,8},{10,11... | collective-permute-start | bytes 393224 | tf_op jit(solution)/shard_map/ppermute | solution.py:446

commit v6 on v5

--- a/solution.py
+++ b/solution.py
@@ -1,3 +1,4 @@
+import functools
 import itertools
 import math
 
@@ -24,7 +25,6 @@
 HALVES = 256
 TILE = 512
 AXES = ("atom", "wave")
-BOTH = (((1,), (0,)), ((), ()))
 OUTER = (((0,), (0,)), ((), ()))
 
 
@@ -79,34 +79,49 @@
     return steps
 
 
+def spot_of(row):
+    if row < 2 * SIDE:
+        return row % SIDE, row // SIDE
+    extra = OWN - SIDE
+    return SIDE + (row - 2 * SIDE) % extra, (row - 2 * SIDE) // extra
+
+
 def row_steps(core, block, row, peer):
-    line = row_line(core, block, row % OWN)
+    spot, part = spot_of(row)
+    line = row_line(core, block, spot)
     if line is None:
         return column_of((0, 0, 0), 1)
     vector = list(line[0])
     vector[line[1]] += peer - MIDDLE
-    return column_of(vector, row // OWN)
+    return column_of(vector, part)
 
 
 def stride_steps(core, block, row):
-    line = row_line(core, block, row % OWN)
+    line = row_line(core, block, spot_of(row)[0])
     vector = [0, 0, 0]
     vector[1 if line is None else line[1]] = 1
     return column_of(vector, 0)
 
 
-MIXED = list(range(16, 24)) + list(range(32, 40))
-FIRST = 2 * BLOCK + len(MIXED)
+MAIN = 32
+MIXED = range(MAIN, BLOCK)
+AT = [0, 2 * BLOCK, 4 * BLOCK, 4 * BLOCK + 16]
+STRIDES = 4 * BLOCK + 32
+THIRD = STRIDES + 8 * BLOCKS
+FIRST = THIRD + 8
 
 
 def first_steps():
-    out = np.zeros((2, 8, BLOCKS * FIRST), np.float32)
+    out = np.zeros((2, 8, FIRST), np.float32)
     for core in range(2):
         columns = []
         for block in range(BLOCKS):
-            columns += [row_steps(core, block, row, MIDDLE) for row in range(BLOCK)]
-            columns += [row_steps(core, block, row, MIDDLE + 1) for row in range(BLOCK)]
+            rows = range(BLOCK) if block < 2 else MIXED
+            columns += [row_steps(core, block, row, MIDDLE) for row in rows]
+            columns += [row_steps(core, block, row, MIDDLE + 1) for row in rows]
+        for block in range(BLOCKS):
             columns += [stride_steps(core, block, row) for row in MIXED]
+        columns += [column_of((0, 0, 2), 0)] * 8
         out[core] = np.stack(columns, axis=1)
     return out
 
@@ -128,7 +143,7 @@
 def cosine_coefficients():
     nodes = 0.125 + 0.125 * np.cos(np.pi * (np.arange(400) + 0.5) / 400)
     fit = np.polynomial.chebyshev.Chebyshev.fit(
-        nodes, np.cos(2 * np.pi * np.sqrt(nodes)), 6, domain=[0, 0.25]
+        nodes, np.cos(2 * np.pi * np.sqrt(nodes)), 5, domain=[0, 0.25]
     )
     return [float(c) for c in fit.convert(kind=np.polynomial.Polynomial).coef]
 
@@ -147,26 +162,36 @@
 
 def factors_kernel(steps_ref, coords_ref, features_ref, out_ref, first, tables, total):
     tile = pl.program_id(0)
+
+    @pl.when(tile == 0)
+    def _():
+        total[...] = jnp.zeros_like(total)
+
     core = lax.axis_index("wave") % 2
     parts = split_coords(coords_ref[...])
     steps = steps_ref[core].astype(jnp.bfloat16)
-    for block in range(BLOCKS):
-        turns = lax.dot_general(
-            steps[:, block * FIRST : (block + 1) * FIRST],
-            parts,
-            OUTER,
-            preferred_element_type=jnp.float32,
-        )
-        first[block] = cosine_of_turns(turns)
+    turns = lax.dot_general(steps, parts, OUTER, preferred_element_type=jnp.float32)
+    first[...] = cosine_of_turns(turns)
     features = features_ref[...]
+    mains = {}
     for block in range(BLOCKS):
         for start in range(0, TILE, HALVES):
             lanes = pl.ds(start, HALVES)
-            at = first[block, :BLOCK, lanes]
-            after = first[block, BLOCK : 2 * BLOCK, lanes]
-            mixed = 2.0 * first[block, 2 * BLOCK :, lanes]
-            common = jnp.broadcast_to(mixed[0:1, :], (16, HALVES))
-            stride = jnp.concatenate([common, mixed[:8], common[:8], mixed[8:]], axis=0)
+            if block < 2:
+                at = first[AT[block] : AT[block] + BLOCK, lanes]
+                after = first[AT[block] + BLOCK : AT[block] + 2 * BLOCK, lanes]
+            else:
+                third = 2.0 * first[THIRD : THIRD + 1, lanes]
+                main = [
+                    third * near - far
+                    for near, far in zip(mains[block - 1, start], mains[block - 2, start])
+                ]
+                mixed = [first[AT[block] + 8 * p : AT[block] + 8 * p + 8, lanes] for p in TWO]
+                at, after = (jnp.concatenate([main[p], mixed[p]], axis=0) for p in TWO)
+            mains[block, start] = at[:MAIN], after[:MAIN]
+            mixed = 2.0 * first[STRIDES + 8 * block : STRIDES + 8 * block + 8, lanes]
+            common = jnp.broadcast_to(mixed[0:1, :], (MAIN, HALVES))
+            stride = jnp.concatenate([common, mixed], axis=0)
             held = {MIDDLE: at, MIDDLE + 1: after}
             for peer in range(MIDDLE, PLANES, 2):
                 for later in (peer, peer + 1):
@@ -179,15 +204,7 @@
                     held[earlier] = stride * held[earlier + 1] - held[earlier + 2]
                 pair = jnp.concatenate([held[peer], held[peer + 1]], axis=0)
                 tables[block, peer * BLOCK : (peer + 2) * BLOCK, lanes] = pair.astype(jnp.bfloat16)
-        added = jnp.dot(tables[block], features, preferred_element_type=jnp.float32)
-
-        @pl.when(tile == 0)
-        def _():
-            total[block] = added
-
-        @pl.when(tile > 0)
-        def _():
-            total[block] += added
+        total[block] += jnp.dot(tables[block], features, preferred_element_type=jnp.float32)
 
     @pl.when(tile == pl.num_programs(0) - 1)
     def _():
@@ -204,13 +221,13 @@
         out_shape=jax.ShapeDtypeStruct((PLANES, COLUMN, F), jnp.bfloat16),
         grid=(atoms // TILE,),
         in_specs=[
-            pl.BlockSpec((2, 8, BLOCKS * FIRST), lambda t: (0, 0, 0)),
+            pl.BlockSpec((2, 8, FIRST), lambda t: (0, 0, 0)),
             pl.BlockSpec((3, TILE), lambda t: (0, t)),
             pl.BlockSpec((TILE, F), lambda t: (t, 0)),
         ],
         out_specs=pl.BlockSpec((PLANES, COLUMN, F), lambda t: (0, 0, 0)),
         scratch_shapes=[
-            pltpu.VMEM((BLOCKS, FIRST, TILE), jnp.float32),
+            pltpu.VMEM((FIRST, TILE), jnp.float32),
             pltpu.VMEM((BLOCKS, PLANES * BLOCK, TILE), jnp.bfloat16),
             pltpu.VMEM((BLOCKS, PLANES * BLOCK, F), jnp.float32),
         ],
@@ -295,13 +312,15 @@
 def filter_kernel(arrived_ref, near_ref, far_ref, out_ref, total, filtered):
     total[...] = jnp.sum(arrived_ref[...].astype(jnp.float32), axis=0)
     weights = near_ref[...].astype(jnp.float32) + far_ref[...].astype(jnp.float32)
+    extra = OWN - SIDE
     for block in range(BLOCKS):
-        start = block * BLOCK
-        cosines, sines = total[start : start + OWN, :], total[start + OWN : start + BLOCK, :]
-        power = jnp.sum(cosines * cosines + sines * sines, axis=1, keepdims=True) * (0.5 / F)
-        scaled = weights[block * OWN : (block + 1) * OWN] * (1.0 / jnp.sqrt(power + 1e-05))
-        filtered[start : start + OWN, :] = cosines * scaled
-        filtered[start + OWN : start + BLOCK, :] = sines * scaled
+        for row, spot, count in ((0, 0, SIDE), (2 * SIDE, SIDE, extra)):
+            start, weight = block * BLOCK + row, block * OWN + spot
+            cosines, sines = total[start : start + count, :], total[start + count : start + 2 * count, :]
+            power = jnp.sum(cosines * cosines + sines * sines, axis=1, keepdims=True) * (0.5 / F)
+            scaled = weights[weight : weight + count] * (1.0 / jnp.sqrt(power + 1e-05))
+            filtered[start : start + count, :] = cosines * scaled
+            filtered[start + count : start + 2 * count, :] = sines * scaled
     column = filtered[...].astype(jnp.bfloat16)
     for peer in range(PLANES):
         out_ref[peer] = column
@@ -352,32 +371,30 @@
     )(place, steps, coords)
 
 
-def message_kernel(place_ref, tables_ref, filtered_ref, own_ref, other_ref, total):
-    core = place_ref[1]
-    total[...] = jnp.dot(tables_ref[...], filtered_ref[...], preferred_element_type=jnp.float32)
+def message_kernel(place_ref, tables_ref, filtered_ref, out_ref, *, own):
     half = TILE // 2
-    own_ref[...] = total[pl.ds(pl.multiple_of(core * half, half), half), :]
-    other = total[pl.ds(pl.multiple_of((1 - core) * half, half), half), :]
-    other_ref[...] = other.astype(jnp.bfloat16)
-
-
-def message_parts(place, tables, filtered):
+    core = place_ref[1] if own else 1 - place_ref[1]
+    tables = tables_ref[pl.ds(pl.multiple_of(core * half, half), half), :]
+    message = jnp.dot(tables, filtered_ref[...], preferred_element_type=jnp.float32)
+    out_ref[...] = message.astype(out_ref.dtype)
+
+
+def message_half(place, tables, filtered, own):
     half = TILE // 2
     return pl.pallas_call(
-        message_kernel,
-        out_shape=(
-            jax.ShapeDtypeStruct((half, F), jnp.float32),
-            jax.ShapeDtypeStruct((half, F), jnp.bfloat16),
-        ),
+        functools.partial(message_kernel, own=own),
+        out_shape=jax.ShapeDtypeStruct((half, F), jnp.float32 if own else jnp.bfloat16),
         in_specs=[
             pl.BlockSpec(memory_space=pltpu.SMEM),
             pl.BlockSpec(memory_space=pltpu.VMEM),
             pl.BlockSpec(memory_space=pltpu.VMEM),
         ],
-        out_specs=(pl.BlockSpec(memory_space=pltpu.VMEM),) * 2,
-        scratch_shapes=[pltpu.VMEM((TILE, F), jnp.float32)],
+        out_specs=pl.BlockSpec(memory_space=pltpu.VMEM),
         compiler_params=pltpu.CompilerParams(vmem_limit_bytes=16 << 20),
-        name="message",
+        cost_estimate=pl.CostEstimate(
+            flops=2 * half * ALL_ROWS * F, bytes_accessed=4 * half * ALL_ROWS, transcendentals=0
+        ),
+        name="message_own" if own else "message_other",
     )(place, tables, filtered)
 
 
@@ -427,7 +444,7 @@
 ALL_STEPS = all_steps()
 
 
-def on_device(features, coords, miller, filter_weights, norm_gain, w_in, w_out):
+def layer(features, coords, miller, filter_weights, norm_gain, w_in, w_out):
     factors = partial_factors(jnp.asarray(FIRST_STEPS), coords, features)
     factors, coords, miller = lax.optimization_barrier((factors, coords, miller))
     number = lax.axis_index("atom") * 8 + lax.axis_index("wave")
@@ -436,20 +453,19 @@
     weights, swapped = grid_weights(miller, filter_weights)
     weights += lax.ppermute(swapped, AXES, SWAP)
     weights += lax.ppermute(weights, AXES, OUTER_PAIRS)
+    arrived, weights = lax.optimization_barrier((arrived, weights))
+    far_weights = lax.ppermute(weights, AXES, INNER_PAIRS)
     tables = message_tables(place, jnp.asarray(ALL_STEPS), coords)
     sums = plane_sum(arrived)
-    sums, weights = lax.optimization_barrier((sums, weights))
     shares = exchange(sums, GROUPS_LO)
-    filtered = filter_column(shares, weights, lax.ppermute(weights, AXES, INNER_PAIRS))
+    filtered = filter_column(shares, weights, far_weights)
     filtered = exchange(filtered, GROUPS_XY).reshape(ALL_ROWS, F)
-    own, other = message_parts(place, tables, filtered)
-    other = lax.ppermute(other, AXES, SWAP)
+    other = lax.ppermute(message_half(place, tables, filtered, False), AXES, SWAP)
+    own = message_half(place, tables, filtered, True)
     return update(place, features, own, other, norm_gain.reshape(1, F), w_in, w_out)
 
 
 def solution(mesh):
     in_specs = (P("atom", None), P(None, "atom"), P(None, "wave"), P("wave", None), P(), P(), P())
     out_specs = P(("atom", "wave"), None)
-    return jax.shard_map(
-        on_device, mesh=mesh, in_specs=in_specs, out_specs=out_specs, check_vma=False
-    )
+    return jax.shard_map(layer, mesh=mesh, in_specs=in_specs, out_specs=out_specs, check_vma=False)

time: 96.2 us -> 91.6 us (0.952)
  Pallas kernels: 23.7 us -> 19.5 us
    pallas_call x1, Pallas kernels: 12.9 us -> 7.57 us  [partial_factors(): pl.pallas_call(factors_kernel, out_shape=jax.ShapeDtypeStruct((PLANES, CO...]
    pallas_call x1 -> x2, Pallas kernels: 2.3 us -> 3.66 us  [message_half(): pl.pallas_call(functools.partial(message_kernel, own=own), out_shape=jax....]
    ppermute x4, waiting for transfers between devices: 8.15 us -> 7.19 us  [the longest x1 4.93 us: layer(): far_weights = lax.ppermute(weights, AXES, INNER_PAIRS)]
  transfers between devices with their start and end apart: 7 -> 7, of which waited for: 6 -> 5; matrix products, arithmetic and copies ran while one was open for 0% -> 0% of each run, Pallas kernels for 5% -> 7%
where the time goes in v6:
time: 91.6 us; the launch traced here: 91.1 us
  starting transfers between devices  47.5 us (52%)
  waiting for transfers between devices  23.6 us (26%)
  Pallas kernels  19.5 us (21%)
    all_to_all x3, starting transfers between devices, exchange(): lax.all_to_all(pieces, AXES, split_axis=0, concat_axis=0, tiled=True, axi...  19.5 us
    all_to_all x3, waiting for transfers between devices, exchange(): lax.all_to_all(pieces, AXES, split_axis=0, concat_axis=0, tiled=True, axi...  16.4 us
    ppermute x1, starting transfers between devices, layer(): weights += lax.ppermute(weights, AXES, OUTER_PAIRS)  10.7 us
    ppermute x1, starting transfers between devices, layer(): far_weights = lax.ppermute(weights, AXES, INNER_PAIRS)  8.81 us
    pallas_call x1, Pallas kernels, partial_factors(): pl.pallas_call(factors_kernel, out_shape=jax.ShapeDtypeStruct((PLANES, CO...  7.57 us
    ppermute x1, starting transfers between devices, layer(): lax.ppermute(message_half(place, tables, filtered, False), AXES, SWAP)  5.65 us
    ppermute x1, waiting for transfers between devices, layer(): far_weights = lax.ppermute(weights, AXES, INNER_PAIRS)  4.93 us
    pallas_call x1, Pallas kernels, message_tables(): pl.pallas_call(tables_kernel, out_shape=jax.ShapeDtypeStruct((TILE, ALL_R...  4.02 us
  transfers between devices with their start and end apart: 7, of which 5 were waited for; matrix products, arithmetic and copies ran while one was open for 0% of the time, Pallas kernels for 7%

profile of v6, /device:TPU:65, one launch (start us, length us, event | category | flops | bytes accessed | tf_op | source)
XLA Modules:
  0.0 91.1 jit_solution(3733666230621478291)
XLA Ops:
  0.0 7.6 %factors.1 = bf16[16,160,256]{2,1,0:T(8,128)(2,1)} custom-call(f32[2,8,232]{2,1,0:T(8,128)} %constant.31.clone.steps_ref, s32[3,2048]{1,0:T(4,128)} %coords_ref.2, bf16[2048,256]{1,0:T(8,128)(2,1)} %features_ref.3), custom_call_target="tpu_custom_call" | custom-call | flops 2684354560 | bytes 1048576 | tf_op jit(solution)/shard_map/factors/pallas_call | solution.py:219
  7.6 0.0 copy-start.1
  7.6 0.0 copy-start.6
  7.6 6.9 %all-to-all-start = ((bf16[16,160,256]{2,1,0:T(8,128)(2,1)}), bf16[16,160,256]{2,1,0:T(8,128)(2,1)S(1)}, u32[]{:S(2)}, u32[]{:S(2)}) async-start(bf16[16,160,256]{2,1,0:T(8,128)(2,1)} %factors.1), calls=%async_computation | async-start | bytes 2621440 | tf_op jit(solution)/shard_map/all_to_all | solution.py:438
  14.5 0.0 copy-done.1
  14.5 0.0 copy-done.6
  14.5 0.3 grid_weights.1
  14.8 2.9 %collective-permute-start = (bf16[80,256]{1,0:T(8,128)(2,1)S(1)}, bf16[80,256]{1,0:T(8,128)(2,1)S(1)}, u32[]{:S(2)}, u32[]{:S(2)}) collective-permute-start(bf16[80,256]{1,0:T(8,128)(2,1)S(1)} %get-tuple-element.16), channel_id=1, source_target_pairs={{0,1},{1,0},{2,3},{3,2},{4,5},{5,4},{6,7},{7,6},{8,9},{9,8},{10,11... | collective-permute-start | bytes 122888 | tf_op jit(solution)/shard_map/ppermute | solution.py:454
  17.7 0.8 collective-permute-done
  18.5 10.7 %collective-permute-start.1 = (bf16[80,256]{1,0:T(8,128)(2,1)S(1)}, bf16[80,256]{1,0:T(8,128)(2,1)S(1)}, u32[]{:S(2)}, u32[]{:S(2)}) collective-permute-start(bf16[80,256]{1,0:T(8,128)(2,1)S(1)} %add.16), channel_id=1, source_target_pairs={{0,6},{1,7},{2,4},{3,5},{4,2},{5,3},{6,0},{7,1},{8,14},{9,15},{10,... | collective-permute-start | bytes 122888 | tf_op jit(solution)/shard_map/ppermute | solution.py:455
  29.2 1.4 %collective-permute-done.1 = bf16[80,256]{1,0:T(8,128)(2,1)S(1)} collective-permute-done((bf16[80,256]{1,0:T(8,128)(2,1)S(1)}, bf16[80,256]{1,0:T(8,128)(2,1)S(1)}, u32[]{:S(2)}, u32[]{:S(2)}) %collective-permute-start.1) | collective-permute-done | bytes 40992 | tf_op jit(solution)/shard_map/ppermute | solution.py:455
  30.6 2.8 %all-to-all-done.arrived_ref = bf16[16,160,256]{2,1,0:T(8,128)(2,1)S(1)} async-done(((bf16[16,160,256]{2,1,0:T(8,128)(2,1)}), bf16[16,160,256]{2,1,0:T(8,128)(2,1)S(1)}, u32[]{:S(2)}, u32[]{:S(2)}) %all-to-all-start) | async-done | bytes 1310752 | tf_op jit(solution)/shard_map/all_to_all | solution.py:438
  33.4 0.9 plane_sum.1
  34.4 5.0 %all-to-all-start.1 = ((bf16[4,160,256]{2,1,0:T(8,128)(2,1)}), bf16[4,160,256]{2,1,0:T(8,128)(2,1)S(1)}, u32[]{:S(2)}, u32[]{:S(2)}) async-start(bf16[4,160,256]{2,1,0:T(8,128)(2,1)} %plane_sum.1), calls=%async_computation.1 | async-start | bytes 655360 | tf_op jit(solution)/shard_map/all_to_all | solution.py:438
  39.3 8.8 %collective-permute-start.2 = (bf16[80,256]{1,0:T(8,128)(2,1)S(1)}, bf16[80,256]{1,0:T(8,128)(2,1)S(1)}, u32[]{:S(2)}, u32[]{:S(2)}) collective-permute-start(bf16[80,256]{1,0:T(8,128)(2,1)S(1)} %add.17.near_ref), channel_id=1, source_target_pairs={{0,2},{1,3},{2,0},{3,1},{4,6},{5,7},{6,4},{7,5},{8,10},{9,11},{10,... | collective-permute-start | bytes 122888 | tf_op jit(solution)/shard_map/ppermute | solution.py:457
  48.2 4.9 %collective-permute-done.2.far_ref = bf16[80,256]{1,0:T(8,128)(2,1)S(1)} collective-permute-done((bf16[80,256]{1,0:T(8,128)(2,1)S(1)}, bf16[80,256]{1,0:T(8,128)(2,1)S(1)}, u32[]{:S(2)}, u32[]{:S(2)}) %collective-permute-start.2) | collective-permute-done | bytes 40992 | tf_op jit(solution)/shard_map/ppermute | solution.py:457
  53.1 0.0 all-to-all-done.1.arrived_ref
  53.1 1.3 %filter_column.1 = bf16[16,160,256]{2,1,0:T(8,128)(2,1)} custom-call(bf16[4,160,256]{2,1,0:T(8,128)(2,1)S(1)} %all-to-all-done.1.arrived_ref, bf16[80,256]{1,0:T(8,128)(2,1)S(1)} %add.17.near_ref, bf16[80,256]{1,0:T(8,128)(2,1)S(1)} %collective-permute-done.2.far_ref), custom_call_target="tpu_custom_call" | custom-call | tf_op jit(solution)/shard_map/filter_column/pallas_call | solution.py:330
  54.4 0.0 copy-start.8
  54.4 0.0 copy-start.9
  54.4 0.0 copy-start.2
  54.4 0.0 copy-start.5
  54.4 7.7 %all-to-all-start.2 = ((bf16[16,160,256]{2,1,0:T(8,128)(2,1)}), bf16[16,160,256]{2,1,0:T(8,128)(2,1)}, u32[]{:S(2)}, u32[]{:S(2)}) async-start(bf16[16,160,256]{2,1,0:T(8,128)(2,1)} %filter_column.1), calls=%async_computation.2 | async-start | bytes 2621440 | tf_op jit(solution)/shard_map/all_to_all | solution.py:438
  62.1 0.0 copy-done.8
  62.1 0.0 copy-done.9
  62.1 0.2 and_select_fusion.place_ref
  62.4 0.0 copy-done.2
  62.4 0.0 copy-done.5
  62.4 4.0 %message_tables.1.tables_ref = bf16[512,2560]{1,0:T(8,128)(2,1)S(1)} custom-call(s32[3]{0:T(128)S(1)} %and_select_fusion.place_ref, f32[2,8,2560]{2,1,0:T(8,128)S(1)} %copy-done.2, s32[3,2048]{1,0:T(4,128)S(1)} %copy-done.5), custom_call_target="tpu_custom_call" | custom-call | flops 20971520 | bytes 2621440 | tf_op jit(solution)/shard_map/message_tables/pallas_call | solution.py:354
  66.4 13.6 %all-to-all-done.2 = bf16[16,160,256]{2,1,0:T(8,128)(2,1)} async-done(((bf16[16,160,256]{2,1,0:T(8,128)(2,1)}), bf16[16,160,256]{2,1,0:T(8,128)(2,1)}, u32[]{:S(2)}, u32[]{:S(2)}) %all-to-all-start.2) | async-done | bytes 1310752 | tf_op jit(solution)/shard_map/all_to_all | solution.py:438
  80.0 1.8 %message_other.1 = bf16[256,256]{1,0:T(8,128)(2,1)S(1)} custom-call(s32[3]{0:T(128)S(1)} %and_select_fusion.place_ref, bf16[512,2560]{1,0:T(8,128)(2,1)S(1)} %message_tables.1.tables_ref, bf16[2560,256]{1,0:T(8,128)(2,1)} %bitcast.filtered_ref), custom_call_target="tpu_custom_call" | custom-call | flops 335544320 | bytes 2621440 | tf_op jit(solution)/shard_map/message_other/pallas_call | solution.py:384
  81.8 0.0 copy-start
  81.9 0.0 copy-start.3
  81.9 0.0 copy-start.4
  81.9 0.0 copy-start.7
  81.9 5.7 %collective-permute-start.3 = (bf16[256,256]{1,0:T(8,128)(2,1)S(1)}, bf16[256,256]{1,0:T(8,128)(2,1)S(1)}, u32[]{:S(2)}, u32[]{:S(2)}) collective-permute-start(bf16[256,256]{1,0:T(8,128)(2,1)S(1)} %message_other.1), channel_id=1, source_target_pairs={{0,1},{1,0},{2,3},{3,2},{4,5},{5,4},{6,7},{7,6},{8,9},{9,8},{10,11... | collective-permute-start | bytes 393224 | tf_op jit(solution)/shard_map/ppermute | solution.py:463
  87.6 1.8 %message_own.1.own_ref = f32[256,256]{1,0:T(8,128)S(1)} custom-call(s32[3]{0:T(128)S(1)} %and_select_fusion.place_ref, bf16[512,2560]{1,0:T(8,128)(2,1)S(1)} %message_tables.1.tables_ref, bf16[2560,256]{1,0:T(8,128)(2,1)} %bitcast.filtered_ref), custom_call_target="tpu_custom_call" | custom-call | flops 335544320 | bytes 2621440 | tf_op jit(solution)/shard_map/message_own/pallas_call | solution.py:384
  89.4 0.0 collective-permute-done.3.other_ref
  89.4 0.0 copy-done
  89.4 0.0 copy-done.3
  89.4 0.0 copy-done.4
  89.4 0.0 copy-done.7
  89.4 1.6 %update.1 = bf16[256,256]{1,0:T(8,128)(2,1)} custom-call(s32[3]{0:T(128)S(1)} %and_select_fusion.place_ref, bf16[2048,256]{1,0:T(8,128)(2,1)S(1)} %copy-done, f32[256,256]{1,0:T(8,128)S(1)} %message_own.1.own_ref, bf16[256,256]{1,0:T(8,128)(2,1)S(1)} %collective-permute-done.3.other_ref, f32[1,256]{1,0:T(1,128)S(1)} %bitcast.2, ...), custom_call_target="tpu_custom_call" | custom-call | tf_op jit(solution)/shard_map/update/pallas_call | solution.py:416
  (2 shorter events, 0.0 us)
Async XLA Ops:
  7.6 6.9 %copy-start.1 = (f32[512,256]{1,0:T(8,128)S(1)}, f32[512,256]{1,0:T(8,128)}, u32[]{:S(2)}) copy-start(f32[512,256]{1,0:T(8,128)} %weights_ref.1) | copy-start | bytes 1572868
  7.6 6.9 %copy-start.6 = (s32[3,512]{1,0:T(4,128)S(1)}, s32[3,512]{1,0:T(4,128)}, u32[]{:S(2)}) copy-start(s32[3,512]{1,0:T(4,128)} %miller_ref) | copy-start | bytes 18436
  7.6 25.9 %all-to-all-start = ((bf16[16,160,256]{2,1,0:T(8,128)(2,1)}), bf16[16,160,256]{2,1,0:T(8,128)(2,1)S(1)}, u32[]{:S(2)}, u32[]{:S(2)}) async-start(bf16[16,160,256]{2,1,0:T(8,128)(2,1)} %factors.1), calls=%async_computation | async-start | bytes 2621440 | tf_op jit(solution)/shard_map/all_to_all | solution.py:438
  14.8 3.7 %collective-permute-start = (bf16[80,256]{1,0:T(8,128)(2,1)S(1)}, bf16[80,256]{1,0:T(8,128)(2,1)S(1)}, u32[]{:S(2)}, u32[]{:S(2)}) collective-permute-start(bf16[80,256]{1,0:T(8,128)(2,1)S(1)} %get-tuple-element.16), channel_id=1, source_target_pairs={{0,1},{1,0},{2,3},{3,2},{4,5},{5,4},{6,7},{7,6},{8,9},{9,8},{10,11... | collective-permute-start | bytes 122888 | tf_op jit(solution)/shard_map/ppermute | solution.py:454
  18.5 12.1 %collective-permute-start.1 = (bf16[80,256]{1,0:T(8,128)(2,1)S(1)}, bf16[80,256]{1,0:T(8,128)(2,1)S(1)}, u32[]{:S(2)}, u32[]{:S(2)}) collective-permute-start(bf16[80,256]{1,0:T(8,128)(2,1)S(1)} %add.16), channel_id=1, source_target_pairs={{0,6},{1,7},{2,4},{3,5},{4,2},{5,3},{6,0},{7,1},{8,14},{9,15},{10,... | collective-permute-start | bytes 122888 | tf_op jit(solution)/shard_map/ppermute | solution.py:455
  34.4 18.7 %all-to-all-start.1 = ((bf16[4,160,256]{2,1,0:T(8,128)(2,1)}), bf16[4,160,256]{2,1,0:T(8,128)(2,1)S(1)}, u32[]{:S(2)}, u32[]{:S(2)}) async-start(bf16[4,160,256]{2,1,0:T(8,128)(2,1)} %plane_sum.1), calls=%async_computation.1 | async-start | bytes 655360 | tf_op jit(solution)/shard_map/all_to_all | solution.py:438
  39.3 13.7 %collective-permute-start.2 = (bf16[80,256]{1,0:T(8,128)(2,1)S(1)}, bf16[80,256]{1,0:T(8,128)(2,1)S(1)}, u32[]{:S(2)}, u32[]{:S(2)}) collective-permute-start(bf16[80,256]{1,0:T(8,128)(2,1)S(1)} %add.17.near_ref), channel_id=1, source_target_pairs={{0,2},{1,3},{2,0},{3,1},{4,6},{5,7},{6,4},{7,5},{8,10},{9,11},{10,... | collective-permute-start | bytes 122888 | tf_op jit(solution)/shard_map/ppermute | solution.py:457
  54.4 7.7 %copy-start.8 = (s32[3]{0:T(128)S(1)}, s32[3]{0:T(128)}, u32[]{:S(2)}) copy-start(s32[3]{0:T(128)} %constant.37) | copy-start | bytes 40
  54.4 7.7 %copy-start.9 = (s32[3]{0:T(128)S(1)}, s32[3]{0:T(128)}, u32[]{:S(2)}) copy-start(s32[3]{0:T(128)} %constant.32.clone) | copy-start | bytes 40
  54.4 8.0 %copy-start.2 = (f32[2,8,2560]{2,1,0:T(8,128)S(1)}, f32[2,8,2560]{2,1,0:T(8,128)}, u32[]{:S(2)}) copy-start(f32[2,8,2560]{2,1,0:T(8,128)} %constant.34.clone.steps_ref) | copy-start | bytes 491524
  54.4 8.0 %copy-start.5 = (s32[3,2048]{1,0:T(4,128)S(1)}, s32[3,2048]{1,0:T(4,128)}, u32[]{:S(2)}) copy-start(s32[3,2048]{1,0:T(4,128)} %coords_ref.2) | copy-start | bytes 73732
  54.4 25.6 %all-to-all-start.2 = ((bf16[16,160,256]{2,1,0:T(8,128)(2,1)}), bf16[16,160,256]{2,1,0:T(8,128)(2,1)}, u32[]{:S(2)}, u32[]{:S(2)}) async-start(bf16[16,160,256]{2,1,0:T(8,128)(2,1)} %filter_column.1), calls=%async_computation.2 | async-start | bytes 2621440 | tf_op jit(solution)/shard_map/all_to_all | solution.py:438
  81.8 7.6 %copy-start = (bf16[2048,256]{1,0:T(8,128)(2,1)S(1)}, bf16[2048,256]{1,0:T(8,128)(2,1)}, u32[]{:S(2)}) copy-start(bf16[2048,256]{1,0:T(8,128)(2,1)} %features_ref.3) | copy-start | bytes 3145732
  81.9 7.6 %copy-start.3 = (bf16[256,256]{1,0:T(8,128)(2,1)S(1)}, bf16[256,256]{1,0:T(8,128)(2,1)}, u32[]{:S(2)}) copy-start(bf16[256,256]{1,0:T(8,128)(2,1)} %w_in_ref.1) | copy-start | bytes 393220
  81.9 7.6 %copy-start.4 = (bf16[256,256]{1,0:T(8,128)(2,1)S(1)}, bf16[256,256]{1,0:T(8,128)(2,1)}, u32[]{:S(2)}) copy-start(bf16[256,256]{1,0:T(8,128)(2,1)} %w_out_ref.1) | copy-start | bytes 393220
  81.9 7.6 %copy-start.7 = (f32[256]{0:T(256)S(1)}, f32[256]{0:T(256)}, u32[]{:S(2)}) copy-start(f32[256]{0:T(256)} %param.15) | copy-start | bytes 3076
  81.9 7.5 %collective-permute-start.3 = (bf16[256,256]{1,0:T(8,128)(2,1)S(1)}, bf16[256,256]{1,0:T(8,128)(2,1)S(1)}, u32[]{:S(2)}, u32[]{:S(2)}) collective-permute-start(bf16[256,256]{1,0:T(8,128)(2,1)S(1)} %message_other.1), channel_id=1, source_target_pairs={{0,1},{1,0},{2,3},{3,2},{4,5},{5,4},{6,7},{7,6},{8,9},{9,8},{10,11... | collective-permute-start | bytes 393224 | tf_op jit(solution)/shard_map/ppermute | solution.py:463

commit v7 on v6

--- a/solution.py
+++ b/solution.py
@@ -18,9 +18,10 @@
 OWN = 20
 BLOCK = 2 * OWN
 COLUMN = BLOCKS * BLOCK
-ALL_ROWS = PLANES * COLUMN
+HALF = COLUMN // 2
+ALL_ROWS = PLANES * HALF
 MIDDLE = 8
-POINTS = BLOCKS * OWN
+POINTS = BLOCKS * OWN // 2
 F = 256
 HALVES = 256
 TILE = 512
@@ -50,6 +51,16 @@
 ]
 INNER_PAIRS = [
     (device(y, l, x, h, c), device(y, l, x, h ^ 1, c))
+    for y, l, x, h, c in itertools.product(FOUR, FOUR, FOUR, FOUR, TWO)
+]
+
+
+LINE_SAME = [
+    (device(y, l, x, h, c), device(y, l ^ 1, x, h, c))
+    for y, l, x, h, c in itertools.product(FOUR, FOUR, FOUR, FOUR, TWO)
+]
+LINE_CROSS = [
+    (device(y, l, x, h, c), device(y, l ^ 1, x, h, 1 - c))
     for y, l, x, h, c in itertools.product(FOUR, FOUR, FOUR, FOUR, TWO)
 ]
 
@@ -127,10 +138,11 @@
 
 
 def all_steps():
-    rows = list(itertools.product(range(PLANES), range(BLOCKS), range(BLOCK)))
-    return np.stack(
-        [np.stack([row_steps(c, b, r, q) for q, b, r in rows], axis=1) for c in range(2)]
-    )
+    out = []
+    for core, part in itertools.product(TWO, TWO):
+        rows = itertools.product(range(PLANES), (2 * part, 2 * part + 1), range(BLOCK))
+        out.append(np.stack([row_steps(core, b, r, q) for q, b, r in rows], axis=1))
+    return np.stack(out)
 
 
 def split_coords(coords):
@@ -260,14 +272,14 @@
 
 def weights_kernel(miller_ref, weights_ref, own_ref, other_ref):
     core, atom = lax.axis_index("wave") % 2, lax.axis_index("atom")
-    plane = atom // 16 * 4 + atom % 4
+    plane, part = atom // 16 * 4 + atom % 4, atom // 4 % 2
     spots = grid_spots(miller_ref[0:1, :], miller_ref[1:2, :], miller_ref[2:3, :])
     row = lax.broadcasted_iota(jnp.int32, (POINTS, miller_ref.shape[1]), 0)
     weights = weights_ref[...]
     upper = weights.astype(jnp.bfloat16)
     lower = (weights - upper.astype(jnp.float32)).astype(jnp.bfloat16)
     for held, out_ref in ((core, own_ref), (1 - core, other_ref)):
-        wanted = row + (held * PLANES + plane) * POINTS
+        wanted = row + ((held * PLANES + plane) * 2 + part) * POINTS
         match = jnp.where(wanted == spots, 1.0, 0.0).astype(jnp.bfloat16)
         summed = jnp.dot(match, upper, preferred_element_type=jnp.float32)
         summed += jnp.dot(match, lower, preferred_element_type=jnp.float32)
@@ -295,13 +307,13 @@
         total += arrived_ref[peer].astype(jnp.float32)
     sent = total.astype(jnp.bfloat16)
     for peer in range(4):
-        out_ref[peer] = sent
+        out_ref[peer] = sent[peer % 2 * HALF : (peer % 2 + 1) * HALF]
 
 
 def plane_sum(arrived):
     return pl.pallas_call(
         plane_sum_kernel,
-        out_shape=jax.ShapeDtypeStruct((4, COLUMN, F), jnp.bfloat16),
+        out_shape=jax.ShapeDtypeStruct((4, HALF, F), jnp.bfloat16),
         in_specs=[pl.BlockSpec(memory_space=pltpu.VMEM)],
         out_specs=pl.BlockSpec(memory_space=pltpu.VMEM),
         compiler_params=pltpu.CompilerParams(vmem_limit_bytes=8 << 20),
@@ -313,7 +325,7 @@
     total[...] = jnp.sum(arrived_ref[...].astype(jnp.float32), axis=0)
     weights = near_ref[...].astype(jnp.float32) + far_ref[...].astype(jnp.float32)
     extra = OWN - SIDE
-    for block in range(BLOCKS):
+    for block in range(BLOCKS // 2):
         for row, spot, count in ((0, 0, SIDE), (2 * SIDE, SIDE, extra)):
             start, weight = block * BLOCK + row, block * OWN + spot
             cosines, sines = total[start : start + count, :], total[start + count : start + 2 * count, :]
@@ -329,61 +341,66 @@
 def filter_column(arrived, near, far):
     return pl.pallas_call(
         filter_kernel,
-        out_shape=jax.ShapeDtypeStruct((PLANES, COLUMN, F), jnp.bfloat16),
+        out_shape=jax.ShapeDtypeStruct((PLANES, HALF, F), jnp.bfloat16),
         in_specs=[pl.BlockSpec(memory_space=pltpu.VMEM)] * 3,
         out_specs=pl.BlockSpec(memory_space=pltpu.VMEM),
-        scratch_shapes=[pltpu.VMEM((COLUMN, F), jnp.float32)] * 2,
+        scratch_shapes=[pltpu.VMEM((HALF, F), jnp.float32)] * 2,
         compiler_params=pltpu.CompilerParams(vmem_limit_bytes=8 << 20),
         name="filter_column",
     )(arrived, near, far)
 
 
-def tables_kernel(place_ref, steps_ref, coords_ref, out_ref):
-    parts = split_coords(coords_ref[...])
+def tables_kernel(place_ref, steps_ref, own_ref, near_ref, out_ref):
     steps = steps_ref[0].astype(jnp.bfloat16)
     block = 128
-    for start in range(0, TILE, block):
-        turns = lax.dot_general(
-            parts[:, start : start + block], steps, OUTER, preferred_element_type=jnp.float32
-        )
-        out_ref[start : start + block, :] = cosine_of_turns(turns).astype(jnp.bfloat16)
-
-
-def message_tables(place, steps, coords):
-    width = 512
+    for side, coords_ref in enumerate((own_ref, near_ref)):
+        parts = split_coords(coords_ref[...])
+        for start in range(0, TILE, block):
+            turns = lax.dot_general(
+                parts[:, start : start + block], steps, OUTER, preferred_element_type=jnp.float32
+            )
+            rows = side * TILE + start
+            out_ref[rows : rows + block, :] = cosine_of_turns(turns).astype(jnp.bfloat16)
+
+
+def message_tables(place, steps, coords, near):
+    width = 256
     return pl.pallas_call(
         tables_kernel,
-        out_shape=jax.ShapeDtypeStruct((TILE, ALL_ROWS), jnp.bfloat16),
+        out_shape=jax.ShapeDtypeStruct((2 * TILE, ALL_ROWS), jnp.bfloat16),
         grid_spec=pltpu.PrefetchScalarGridSpec(
             num_scalar_prefetch=1,
             grid=(ALL_ROWS // width,),
             in_specs=[
-                pl.BlockSpec((1, 8, width), lambda t, place: (place[1], 0, t)),
+                pl.BlockSpec((1, 8, width), lambda t, place: (place[3], 0, t)),
                 pl.BlockSpec((3, TILE), lambda t, place: (0, place[2])),
+                pl.BlockSpec((3, TILE), lambda t, place: (0, 0)),
             ],
-            out_specs=pl.BlockSpec((TILE, width), lambda t, place: (0, t)),
+            out_specs=pl.BlockSpec((2 * TILE, width), lambda t, place: (0, t)),
         ),
         compiler_params=pltpu.CompilerParams(vmem_limit_bytes=16 << 20),
         cost_estimate=pl.CostEstimate(
-            flops=16 * TILE * ALL_ROWS, bytes_accessed=TILE * ALL_ROWS * 2, transcendentals=0
+            flops=32 * TILE * ALL_ROWS, bytes_accessed=TILE * ALL_ROWS * 4, transcendentals=0
         ),
         name="message_tables",
-    )(place, steps, coords)
-
-
-def message_kernel(place_ref, tables_ref, filtered_ref, out_ref, *, own):
+    )(place, steps, coords, near)
+
+
+def message_kernel(place_ref, tables_ref, filtered_ref, out_ref, *, far, own):
     half = TILE // 2
     core = place_ref[1] if own else 1 - place_ref[1]
-    tables = tables_ref[pl.ds(pl.multiple_of(core * half, half), half), :]
+    start = pl.multiple_of(core * half, half) + far * TILE
+    tables = tables_ref[pl.ds(start, half), :]
     message = jnp.dot(tables, filtered_ref[...], preferred_element_type=jnp.float32)
     out_ref[...] = message.astype(out_ref.dtype)
 
 
-def message_half(place, tables, filtered, own):
+def message_quarter(place, tables, filtered, far, own):
     half = TILE // 2
-    return pl.pallas_call(
-        functools.partial(message_kernel, own=own),
-        out_shape=jax.ShapeDtypeStruct((half, F), jnp.float32 if own else jnp.bfloat16),
+    kept = own and not far
+    return pl.pallas_call(
+        functools.partial(message_kernel, far=far, own=own),
+        out_shape=jax.ShapeDtypeStruct((half, F), jnp.float32 if kept else jnp.bfloat16),
         in_specs=[
             pl.BlockSpec(memory_space=pltpu.SMEM),
             pl.BlockSpec(memory_space=pltpu.VMEM),
@@ -394,14 +411,15 @@
         cost_estimate=pl.CostEstimate(
             flops=2 * half * ALL_ROWS * F, bytes_accessed=4 * half * ALL_ROWS, transcendentals=0
         ),
-        name="message_own" if own else "message_other",
     )(place, tables, filtered)
 
 
 def update_kernel(
-    place_ref, features_ref, own_ref, other_ref, gain_ref, w_in_ref, w_out_ref, out_ref
+    place_ref, features_ref, own_ref, a_ref, b_ref, c_ref, gain_ref, w_in_ref, w_out_ref, out_ref
 ):
-    message = own_ref[...] + other_ref[...].astype(jnp.float32)
+    message = own_ref[...]
+    for part_ref in (a_ref, b_ref, c_ref):
+        message += part_ref[...].astype(jnp.float32)
     updated = features_ref[...].astype(jnp.float32) + message * (1.0 / math.sqrt(K))
     power = jnp.mean(updated * updated, axis=1, keepdims=True)
     normed = (updated / jnp.sqrt(power + 1e-06) * gain_ref[...]).astype(jnp.bfloat16)
@@ -411,7 +429,7 @@
     out_ref[...] = (updated + added).astype(jnp.bfloat16)
 
 
-def update(place, features, own, other, gain, w_in, w_out):
+def update(place, features, own, others, gain, w_in, w_out):
     half = TILE // 2
     return pl.pallas_call(
         update_kernel,
@@ -423,6 +441,8 @@
                 pl.BlockSpec((half, F), lambda t, place: (place[0], 0)),
                 pl.BlockSpec((half, F), lambda t, place: (0, 0)),
                 pl.BlockSpec((half, F), lambda t, place: (0, 0)),
+                pl.BlockSpec((half, F), lambda t, place: (0, 0)),
+                pl.BlockSpec((half, F), lambda t, place: (0, 0)),
                 pl.BlockSpec((1, F), lambda t, place: (0, 0)),
                 pl.BlockSpec((F, F), lambda t, place: (0, 0)),
                 pl.BlockSpec((F, F), lambda t, place: (0, 0)),
@@ -431,7 +451,7 @@
         ),
         compiler_params=pltpu.CompilerParams(vmem_limit_bytes=8 << 20),
         name="update",
-    )(place, features, own, other, gain, w_in, w_out)
+    )(place, features, own, *others, gain, w_in, w_out)
 
 
 def exchange(pieces, groups):
@@ -447,22 +467,29 @@
 def layer(features, coords, miller, filter_weights, norm_gain, w_in, w_out):
     factors = partial_factors(jnp.asarray(FIRST_STEPS), coords, features)
     factors, coords, miller = lax.optimization_barrier((factors, coords, miller))
-    number = lax.axis_index("atom") * 8 + lax.axis_index("wave")
-    place = number // np.array([1, 1, 2], np.int32) % np.array([8, 2, 4], np.int32)
+    atom, wave = lax.axis_index("atom"), lax.axis_index("wave")
+    core, high = wave % 2, wave // 2
+    place = jnp.stack([wave, core, high, core * 2 + atom // 4 % 2]).astype(jnp.int32)
     arrived = exchange(factors, GROUPS_XY)
     weights, swapped = grid_weights(miller, filter_weights)
     weights += lax.ppermute(swapped, AXES, SWAP)
     weights += lax.ppermute(weights, AXES, OUTER_PAIRS)
+    far_weights = lax.ppermute(weights, AXES, INNER_PAIRS)
     arrived, weights = lax.optimization_barrier((arrived, weights))
-    far_weights = lax.ppermute(weights, AXES, INNER_PAIRS)
-    tables = message_tables(place, jnp.asarray(ALL_STEPS), coords)
     sums = plane_sum(arrived)
     shares = exchange(sums, GROUPS_LO)
     filtered = filter_column(shares, weights, far_weights)
     filtered = exchange(filtered, GROUPS_XY).reshape(ALL_ROWS, F)
-    other = lax.ppermute(message_half(place, tables, filtered, False), AXES, SWAP)
-    own = message_half(place, tables, filtered, True)
-    return update(place, features, own, other, norm_gain.reshape(1, F), w_in, w_out)
+    near = lax.dynamic_slice_in_dim(coords, high * TILE, TILE, 1)
+    near = lax.ppermute(near, AXES, LINE_SAME)
+    tables = message_tables(place, jnp.asarray(ALL_STEPS), coords, near)
+    quarter = functools.partial(message_quarter, place, tables, filtered)
+    others = [
+        lax.ppermute(quarter(far, own), AXES, pairs)
+        for far, own, pairs in ((True, True, LINE_SAME), (True, False, LINE_CROSS), (False, False, SWAP))
+    ]
+    own = quarter(False, True)
+    return update(place, features, own, others, norm_gain.reshape(1, F), w_in, w_out)
 
 
 def solution(mesh):

time: 91.6 us -> 85.6 us (0.934)
  the two profiles are of different devices: /device:TPU:65 before, /device:TPU:1 now
where the time goes in v7:
time: 85.6 us; the launch traced here: 85 us
  starting transfers between devices  60 us (70%)
  Pallas kernels  18.9 us (22%)
  waiting for transfers between devices  5.7 us (7%)
    all_to_all x3, starting transfers between devices, exchange(): lax.all_to_all(pieces, AXES, split_axis=0, concat_axis=0, tiled=True, axi...  20.1 us
    ppermute x3, starting transfers between devices, layer(): lax.ppermute(quarter(far, own), AXES, pairs)  11.5 us
    ppermute x1, starting transfers between devices, layer(): weights += lax.ppermute(weights, AXES, OUTER_PAIRS)  10.4 us
    ppermute x1, starting transfers between devices, layer(): far_weights = lax.ppermute(weights, AXES, INNER_PAIRS)  8.81 us
    pallas_call x1, Pallas kernels, partial_factors(): pl.pallas_call(factors_kernel, out_shape=jax.ShapeDtypeStruct((PLANES, CO...  7.57 us
    ppermute x1, starting transfers between devices, layer(): weights += lax.ppermute(swapped, AXES, SWAP)  4.88 us
    ppermute x1, starting transfers between devices, layer(): near = lax.ppermute(near, AXES, LINE_SAME)  4.27 us
    pallas_call x1, Pallas kernels, message_tables(): pl.pallas_call(tables_kernel, out_shape=jax.ShapeDtypeStruct((2 * TILE, A...  4 us
  transfers between devices with their start and end apart: 10, of which 6 were waited for; matrix products, arithmetic and copies ran while one was open for 0% of the time, Pallas kernels for 6%

profile of v7, /device:TPU:1, one launch (start us, length us, event | category | flops | bytes accessed | tf_op | source)
XLA Modules:
  0.0 85.0 jit_solution(3468990122970722911)
XLA Ops:
  0.0 7.6 %factors.1 = bf16[16,160,256]{2,1,0:T(8,128)(2,1)} custom-call(f32[2,8,232]{2,1,0:T(8,128)} %constant.56.clone.steps_ref, s32[3,2048]{1,0:T(4,128)} %own_ref, bf16[2048,256]{1,0:T(8,128)(2,1)} %features_ref.3), custom_call_target="tpu_custom_call" | custom-call | flops 1342177280 | bytes 1048576 | tf_op jit(solution)/shard_map/factors/pallas_call | solution.py:231
  7.6 0.0 copy-start.1
  7.6 0.0 copy-start.6
  7.6 7.7 %all-to-all-start = ((bf16[16,160,256]{2,1,0:T(8,128)(2,1)}), bf16[16,160,256]{2,1,0:T(8,128)(2,1)S(1)}, u32[]{:S(2)}, u32[]{:S(2)}) async-start(bf16[16,160,256]{2,1,0:T(8,128)(2,1)} %factors.1), calls=%async_computation | async-start | bytes 2621440 | tf_op jit(solution)/shard_map/all_to_all | solution.py:458
  15.3 0.0 copy-done.1
  15.3 0.0 copy-done.6
  15.3 0.3 grid_weights.1
  15.6 4.9 %collective-permute-start.1 = (bf16[40,256]{1,0:T(8,128)(2,1)S(1)}, bf16[40,256]{1,0:T(8,128)(2,1)S(1)}, u32[]{:S(2)}, u32[]{:S(2)}) collective-permute-start(bf16[40,256]{1,0:T(8,128)(2,1)S(1)} %get-tuple-element.16), channel_id=1, source_target_pairs={{0,1},{1,0},{2,3},{3,2},{4,5},{5,4},{6,7},{7,6},{8,9},{9,8},{10,11... | collective-permute-start | bytes 61448 | tf_op jit(solution)/shard_map/ppermute | solution.py:475
  20.5 0.8 collective-permute-done.1
  21.3 10.4 %collective-permute-start.2 = (bf16[40,256]{1,0:T(8,128)(2,1)S(1)}, bf16[40,256]{1,0:T(8,128)(2,1)S(1)}, u32[]{:S(2)}, u32[]{:S(2)}) collective-permute-start(bf16[40,256]{1,0:T(8,128)(2,1)S(1)} %add.25), channel_id=1, source_target_pairs={{0,6},{1,7},{2,4},{3,5},{4,2},{5,3},{6,0},{7,1},{8,14},{9,15},{10,... | collective-permute-start | bytes 61448 | tf_op jit(solution)/shard_map/ppermute | solution.py:476
  31.8 1.2 %collective-permute-done.2 = bf16[40,256]{1,0:T(8,128)(2,1)S(1)} collective-permute-done((bf16[40,256]{1,0:T(8,128)(2,1)S(1)}, bf16[40,256]{1,0:T(8,128)(2,1)S(1)}, u32[]{:S(2)}, u32[]{:S(2)}) %collective-permute-start.2) | collective-permute-done | bytes 20512 | tf_op jit(solution)/shard_map/ppermute | solution.py:476
  32.9 0.0 all-to-all-done.arrived_ref
  33.0 0.8 plane_sum.1
  33.8 0.0 copy-start.5
  33.8 0.0 copy-start.2
  33.8 7.0 %all-to-all-start.1 = ((bf16[4,80,256]{2,1,0:T(8,128)(2,1)}), bf16[4,80,256]{2,1,0:T(8,128)(2,1)S(1)}, u32[]{:S(2)}, u32[]{:S(2)}) async-start(bf16[4,80,256]{2,1,0:T(8,128)(2,1)} %plane_sum.1), calls=%async_computation.1 | async-start | bytes 327680 | tf_op jit(solution)/shard_map/all_to_all | solution.py:458
  40.8 8.8 %collective-permute-start.3 = (bf16[40,256]{1,0:T(8,128)(2,1)S(1)}, bf16[40,256]{1,0:T(8,128)(2,1)S(1)}, u32[]{:S(2)}, u32[]{:S(2)}) collective-permute-start(bf16[40,256]{1,0:T(8,128)(2,1)S(1)} %add.26.near_ref), channel_id=1, source_target_pairs={{0,2},{1,3},{2,0},{3,1},{4,6},{5,7},{6,4},{7,5},{8,10},{9,11},{10,... | collective-permute-start | bytes 61448 | tf_op jit(solution)/shard_map/ppermute | solution.py:477
  49.7 1.2 %collective-permute-done.3.far_ref = bf16[40,256]{1,0:T(8,128)(2,1)S(1)} collective-permute-done((bf16[40,256]{1,0:T(8,128)(2,1)S(1)}, bf16[40,256]{1,0:T(8,128)(2,1)S(1)}, u32[]{:S(2)}, u32[]{:S(2)}) %collective-permute-start.3) | collective-permute-done | bytes 20512 | tf_op jit(solution)/shard_map/ppermute | solution.py:477
  50.8 0.0 all-to-all-done.1.arrived_ref
  50.8 1.0 %filter_column.1 = bf16[16,80,256]{2,1,0:T(8,128)(2,1)} custom-call(bf16[4,80,256]{2,1,0:T(8,128)(2,1)S(1)} %all-to-all-done.1.arrived_ref, bf16[40,256]{1,0:T(8,128)(2,1)S(1)} %add.26.near_ref, bf16[40,256]{1,0:T(8,128)(2,1)S(1)} %collective-permute-done.3.far_ref), custom_call_target="tpu_custom_call" | custom-call | tf_op jit(solution)/shard_map/filter_column/pallas_call | solution.py:342
  51.9 5.3 %all-to-all-start.2 = ((bf16[16,80,256]{2,1,0:T(8,128)(2,1)}), bf16[16,80,256]{2,1,0:T(8,128)(2,1)S(1)}, u32[]{:S(2)}, u32[]{:S(2)}) async-start(bf16[16,80,256]{2,1,0:T(8,128)(2,1)} %filter_column.1), calls=%async_computation.2 | async-start | bytes 1310720 | tf_op jit(solution)/shard_map/all_to_all | solution.py:458
  57.2 0.0 copy-done.5
  57.2 4.3 %collective-permute-start = (s32[3,512]{1,0:T(4,128)S(1)}, s32[3,512]{1,0:T(4,128)S(1)}, u32[]{:S(2)}, u32[]{:S(2)}) collective-permute-start(s32[3,512]{1,0:T(4,128)S(1)} %constant_dynamic-slice_fusion), channel_id=1, source_target_pairs={{0,32},{1,33},{2,34},{3,35},{4,36},{5,37},{6,38},{7,39},{8,40},{9,... | collective-permute-start | bytes 18440 | tf_op jit(solution)/shard_map/ppermute | solution.py:484
  61.6 0.1 pad_add_fusion.place_ref
  61.6 0.9 %collective-permute-done.near_ref = s32[3,512]{1,0:T(4,128)S(1)} collective-permute-done((s32[3,512]{1,0:T(4,128)S(1)}, s32[3,512]{1,0:T(4,128)S(1)}, u32[]{:S(2)}, u32[]{:S(2)}) %collective-permute-start) | collective-permute-done | bytes 6176 | tf_op jit(solution)/shard_map/ppermute | solution.py:484
  62.5 0.0 copy-done.2
  62.5 4.0 %message_tables.1.tables_ref = bf16[1024,1280]{1,0:T(8,128)(2,1)S(1)} custom-call(s32[4]{0:T(128)S(1)} %pad_add_fusion.place_ref, f32[4,8,1280]{2,1,0:T(8,128)S(1)} %copy-done.2, s32[3,2048]{1,0:T(4,128)S(1)} %copy-done.5, s32[3,512]{1,0:T(4,128)S(1)} %collective-permute-done.near_ref), custom_call_target="tpu_custom_call" | custom-call | flops 20971520 | bytes 2621440 | tf_op jit(solution)/shard_map/message_tables/pallas_call | solution.py:368
  66.6 1.6 %all-to-all-done.2 = bf16[16,80,256]{2,1,0:T(8,128)(2,1)S(1)} async-done(((bf16[16,80,256]{2,1,0:T(8,128)(2,1)}), bf16[16,80,256]{2,1,0:T(8,128)(2,1)S(1)}, u32[]{:S(2)}, u32[]{:S(2)}) %all-to-all-start.2) | async-done | bytes 655392 | tf_op jit(solution)/shard_map/all_to_all | solution.py:458
  68.1 0.9 %shard_map.94 = bf16[256,256]{1,0:T(8,128)(2,1)S(1)} custom-call(s32[4]{0:T(128)S(1)} %pad_add_fusion.place_ref, bf16[1024,1280]{1,0:T(8,128)(2,1)S(1)} %message_tables.1.tables_ref, bf16[1280,256]{1,0:T(8,128)(2,1)S(1)} %bitcast.6), custom_call_target="tpu_custom_call" | custom-call | flops 167772160 | bytes 1310720 | tf_op jit(solution)/shard_map/pallas_call | solution.py:401
  69.0 0.9 %shard_map.93 = bf16[256,256]{1,0:T(8,128)(2,1)S(1)} custom-call(s32[4]{0:T(128)S(1)} %pad_add_fusion.place_ref, bf16[1024,1280]{1,0:T(8,128)(2,1)S(1)} %message_tables.1.tables_ref, bf16[1280,256]{1,0:T(8,128)(2,1)S(1)} %bitcast.7), custom_call_target="tpu_custom_call" | custom-call | flops 167772160 | bytes 1310720 | tf_op jit(solution)/shard_map/pallas_call | solution.py:401
  69.9 0.9 %shard_map.92 = bf16[256,256]{1,0:T(8,128)(2,1)S(1)} custom-call(s32[4]{0:T(128)S(1)} %pad_add_fusion.place_ref, bf16[1024,1280]{1,0:T(8,128)(2,1)S(1)} %message_tables.1.tables_ref, bf16[1280,256]{1,0:T(8,128)(2,1)S(1)} %bitcast.8), custom_call_target="tpu_custom_call" | custom-call | flops 167772160 | bytes 1310720 | tf_op jit(solution)/shard_map/pallas_call | solution.py:401
  70.8 0.0 copy-start
  70.8 0.0 copy-start.3
  70.8 0.0 copy-start.4
  70.8 0.0 copy-start.7
  70.8 4.4 %collective-permute-start.4 = (bf16[256,256]{1,0:T(8,128)(2,1)S(1)}, bf16[256,256]{1,0:T(8,128)(2,1)S(1)}, u32[]{:S(2)}, u32[]{:S(2)}) collective-permute-start(bf16[256,256]{1,0:T(8,128)(2,1)S(1)} %shard_map.92), channel_id=1, source_target_pairs={{0,32},{1,33},{2,34},{3,35},{4,36},{5,37},{6,38},{7,39},{8,40},{9,... | collective-permute-start | bytes 393224 | tf_op jit(solution)/shard_map/ppermute | solution.py:488
  75.3 4.8 %collective-permute-start.5 = (bf16[256,256]{1,0:T(8,128)(2,1)S(1)}, bf16[256,256]{1,0:T(8,128)(2,1)S(1)}, u32[]{:S(2)}, u32[]{:S(2)}) collective-permute-start(bf16[256,256]{1,0:T(8,128)(2,1)S(1)} %shard_map.93), channel_id=1, source_target_pairs={{0,33},{1,32},{2,35},{3,34},{4,37},{5,36},{6,39},{7,38},{8,41},{9,... | collective-permute-start | bytes 393224 | tf_op jit(solution)/shard_map/ppermute | solution.py:488
  80.1 2.3 %collective-permute-start.6 = (bf16[256,256]{1,0:T(8,128)(2,1)S(1)}, bf16[256,256]{1,0:T(8,128)(2,1)S(1)}, u32[]{:S(2)}, u32[]{:S(2)}) collective-permute-start(bf16[256,256]{1,0:T(8,128)(2,1)S(1)} %shard_map.94), channel_id=1, source_target_pairs={{0,1},{1,0},{2,3},{3,2},{4,5},{5,4},{6,7},{7,6},{8,9},{9,8},{10,11... | collective-permute-start | bytes 393224 | tf_op jit(solution)/shard_map/ppermute | solution.py:488
  82.4 0.9 %shard_map.91.own_ref = f32[256,256]{1,0:T(8,128)S(1)} custom-call(s32[4]{0:T(128)S(1)} %pad_add_fusion.place_ref, bf16[1024,1280]{1,0:T(8,128)(2,1)S(1)} %message_tables.1.tables_ref, bf16[1280,256]{1,0:T(8,128)(2,1)S(1)} %bitcast.9), custom_call_target="tpu_custom_call" | custom-call | flops 167772160 | bytes 1310720 | tf_op jit(solution)/shard_map/pallas_call | solution.py:401
  83.2 0.0 collective-permute-done.4.a_ref
  83.3 0.0 collective-permute-done.5.b_ref
  83.3 0.1 collective-permute-done.6.c_ref
  83.3 0.0 copy-done
  83.3 0.0 copy-done.3
  83.3 0.0 copy-done.4
  83.3 0.0 copy-done.7
  83.3 1.6 %update.1 = bf16[256,256]{1,0:T(8,128)(2,1)} custom-call(s32[4]{0:T(128)S(1)} %pad_add_fusion.place_ref, bf16[2048,256]{1,0:T(8,128)(2,1)S(1)} %copy-done, f32[256,256]{1,0:T(8,128)S(1)} %shard_map.91.own_ref, bf16[256,256]{1,0:T(8,128)(2,1)S(1)} %collective-permute-done.4.a_ref, bf16[256,256]{1,0:T(8,128)(2,1)S(1)} %collective-permute-done.5.b_ref, ...), custom_call_target="tpu_custom_call" | custom-call | tf_op jit(solution)/shard_map/update/pallas_call | solution.py:434
  (3 shorter events, 0.0 us)
Async XLA Ops:
  7.6 7.7 %copy-start.1 = (f32[512,256]{1,0:T(8,128)S(1)}, f32[512,256]{1,0:T(8,128)}, u32[]{:S(2)}) copy-start(f32[512,256]{1,0:T(8,128)} %weights_ref.1) | copy-start | bytes 1572868
  7.6 7.7 %copy-start.6 = (s32[3,512]{1,0:T(4,128)S(1)}, s32[3,512]{1,0:T(4,128)}, u32[]{:S(2)}) copy-start(s32[3,512]{1,0:T(4,128)} %miller_ref) | copy-start | bytes 18436
  7.6 25.4 %all-to-all-start = ((bf16[16,160,256]{2,1,0:T(8,128)(2,1)}), bf16[16,160,256]{2,1,0:T(8,128)(2,1)S(1)}, u32[]{:S(2)}, u32[]{:S(2)}) async-start(bf16[16,160,256]{2,1,0:T(8,128)(2,1)} %factors.1), calls=%async_computation | async-start | bytes 2621440 | tf_op jit(solution)/shard_map/all_to_all | solution.py:458
  15.6 5.7 %collective-permute-start.1 = (bf16[40,256]{1,0:T(8,128)(2,1)S(1)}, bf16[40,256]{1,0:T(8,128)(2,1)S(1)}, u32[]{:S(2)}, u32[]{:S(2)}) collective-permute-start(bf16[40,256]{1,0:T(8,128)(2,1)S(1)} %get-tuple-element.16), channel_id=1, source_target_pairs={{0,1},{1,0},{2,3},{3,2},{4,5},{5,4},{6,7},{7,6},{8,9},{9,8},{10,11... | collective-permute-start | bytes 61448 | tf_op jit(solution)/shard_map/ppermute | solution.py:475
  21.3 11.6 %collective-permute-start.2 = (bf16[40,256]{1,0:T(8,128)(2,1)S(1)}, bf16[40,256]{1,0:T(8,128)(2,1)S(1)}, u32[]{:S(2)}, u32[]{:S(2)}) collective-permute-start(bf16[40,256]{1,0:T(8,128)(2,1)S(1)} %add.25), channel_id=1, source_target_pairs={{0,6},{1,7},{2,4},{3,5},{4,2},{5,3},{6,0},{7,1},{8,14},{9,15},{10,... | collective-permute-start | bytes 61448 | tf_op jit(solution)/shard_map/ppermute | solution.py:476
  33.8 23.4 %copy-start.5 = (s32[3,2048]{1,0:T(4,128)S(1)}, s32[3,2048]{1,0:T(4,128)}, u32[]{:S(2)}) copy-start(s32[3,2048]{1,0:T(4,128)} %own_ref) | copy-start | bytes 73732
  33.8 28.7 %copy-start.2 = (f32[4,8,1280]{2,1,0:T(8,128)S(1)}, f32[4,8,1280]{2,1,0:T(8,128)}, u32[]{:S(2)}) copy-start(f32[4,8,1280]{2,1,0:T(8,128)} %constant.57.clone.steps_ref) | copy-start | bytes 491524
  33.8 17.0 %all-to-all-start.1 = ((bf16[4,80,256]{2,1,0:T(8,128)(2,1)}), bf16[4,80,256]{2,1,0:T(8,128)(2,1)S(1)}, u32[]{:S(2)}, u32[]{:S(2)}) async-start(bf16[4,80,256]{2,1,0:T(8,128)(2,1)} %plane_sum.1), calls=%async_computation.1 | async-start | bytes 327680 | tf_op jit(solution)/shard_map/all_to_all | solution.py:458
  40.8 10.0 %collective-permute-start.3 = (bf16[40,256]{1,0:T(8,128)(2,1)S(1)}, bf16[40,256]{1,0:T(8,128)(2,1)S(1)}, u32[]{:S(2)}, u32[]{:S(2)}) collective-permute-start(bf16[40,256]{1,0:T(8,128)(2,1)S(1)} %add.26.near_ref), channel_id=1, source_target_pairs={{0,2},{1,3},{2,0},{3,1},{4,6},{5,7},{6,4},{7,5},{8,10},{9,11},{10,... | collective-permute-start | bytes 61448 | tf_op jit(solution)/shard_map/ppermute | solution.py:477
  51.9 16.3 %all-to-all-start.2 = ((bf16[16,80,256]{2,1,0:T(8,128)(2,1)}), bf16[16,80,256]{2,1,0:T(8,128)(2,1)S(1)}, u32[]{:S(2)}, u32[]{:S(2)}) async-start(bf16[16,80,256]{2,1,0:T(8,128)(2,1)} %filter_column.1), calls=%async_computation.2 | async-start | bytes 1310720 | tf_op jit(solution)/shard_map/all_to_all | solution.py:458
  57.2 5.3 %collective-permute-start = (s32[3,512]{1,0:T(4,128)S(1)}, s32[3,512]{1,0:T(4,128)S(1)}, u32[]{:S(2)}, u32[]{:S(2)}) collective-permute-start(s32[3,512]{1,0:T(4,128)S(1)} %constant_dynamic-slice_fusion), channel_id=1, source_target_pairs={{0,32},{1,33},{2,34},{3,35},{4,36},{5,37},{6,38},{7,39},{8,40},{9,... | collective-permute-start | bytes 18440 | tf_op jit(solution)/shard_map/ppermute | solution.py:484
  70.8 12.6 %copy-start = (bf16[2048,256]{1,0:T(8,128)(2,1)S(1)}, bf16[2048,256]{1,0:T(8,128)(2,1)}, u32[]{:S(2)}) copy-start(bf16[2048,256]{1,0:T(8,128)(2,1)} %features_ref.3) | copy-start | bytes 3145732
  70.8 12.5 %copy-start.3 = (bf16[256,256]{1,0:T(8,128)(2,1)S(1)}, bf16[256,256]{1,0:T(8,128)(2,1)}, u32[]{:S(2)}) copy-start(bf16[256,256]{1,0:T(8,128)(2,1)} %w_in_ref.1) | copy-start | bytes 393220
  70.8 12.5 %copy-start.4 = (bf16[256,256]{1,0:T(8,128)(2,1)S(1)}, bf16[256,256]{1,0:T(8,128)(2,1)}, u32[]{:S(2)}) copy-start(bf16[256,256]{1,0:T(8,128)(2,1)} %w_out_ref.1) | copy-start | bytes 393220
  70.8 12.5 %copy-start.7 = (f32[256]{0:T(256)S(1)}, f32[256]{0:T(256)}, u32[]{:S(2)}) copy-start(f32[256]{0:T(256)} %param.13) | copy-start | bytes 3076
  70.8 12.4 %collective-permute-start.4 = (bf16[256,256]{1,0:T(8,128)(2,1)S(1)}, bf16[256,256]{1,0:T(8,128)(2,1)S(1)}, u32[]{:S(2)}, u32[]{:S(2)}) collective-permute-start(bf16[256,256]{1,0:T(8,128)(2,1)S(1)} %shard_map.92), channel_id=1, source_target_pairs={{0,32},{1,33},{2,34},{3,35},{4,36},{5,37},{6,38},{7,39},{8,40},{9,... | collective-permute-start | bytes 393224 | tf_op jit(solution)/shard_map/ppermute | solution.py:488
  75.3 8.0 %collective-permute-start.5 = (bf16[256,256]{1,0:T(8,128)(2,1)S(1)}, bf16[256,256]{1,0:T(8,128)(2,1)S(1)}, u32[]{:S(2)}, u32[]{:S(2)}) collective-permute-start(bf16[256,256]{1,0:T(8,128)(2,1)S(1)} %shard_map.93), channel_id=1, source_target_pairs={{0,33},{1,32},{2,35},{3,34},{4,37},{5,36},{6,39},{7,38},{8,41},{9,... | collective-permute-start | bytes 393224 | tf_op jit(solution)/shard_map/ppermute | solution.py:488
  80.1 3.3 %collective-permute-start.6 = (bf16[256,256]{1,0:T(8,128)(2,1)S(1)}, bf16[256,256]{1,0:T(8,128)(2,1)S(1)}, u32[]{:S(2)}, u32[]{:S(2)}) collective-permute-start(bf16[256,256]{1,0:T(8,128)(2,1)S(1)} %shard_map.94), channel_id=1, source_target_pairs={{0,1},{1,0},{2,3},{3,2},{4,5},{5,4},{6,7},{7,6},{8,9},{9,8},{10,11... | collective-permute-start | bytes 393224 | tf_op jit(solution)/shard_map/ppermute | solution.py:488

commit v8 on v7

--- a/solution.py
+++ b/solution.py
@@ -172,22 +172,21 @@
     return total
 
 
-def factors_kernel(steps_ref, coords_ref, features_ref, out_ref, first, tables, total):
-    tile = pl.program_id(0)
-
-    @pl.when(tile == 0)
-    def _():
-        total[...] = jnp.zeros_like(total)
-
+def factors_kernel(
+    steps_ref, coords_ref, features_ref, out_ref, features, first, tables, copied
+):
+    copy = pltpu.make_async_copy(features_ref, features, copied)
+    copy.start()
     core = lax.axis_index("wave") % 2
-    parts = split_coords(coords_ref[...])
     steps = steps_ref[core].astype(jnp.bfloat16)
-    turns = lax.dot_general(steps, parts, OUTER, preferred_element_type=jnp.float32)
-    first[...] = cosine_of_turns(turns)
-    features = features_ref[...]
+    atoms = coords_ref.shape[1]
+    for start in range(0, atoms, TILE):
+        parts = split_coords(coords_ref[:, start : start + TILE])
+        turns = lax.dot_general(steps, parts, OUTER, preferred_element_type=jnp.float32)
+        first[:, start : start + TILE] = cosine_of_turns(turns)
     mains = {}
     for block in range(BLOCKS):
-        for start in range(0, TILE, HALVES):
+        for start in range(0, atoms, HALVES):
             lanes = pl.ds(start, HALVES)
             if block < 2:
                 at = first[AT[block] : AT[block] + BLOCK, lanes]
@@ -216,14 +215,12 @@
                     held[earlier] = stride * held[earlier + 1] - held[earlier + 2]
                 pair = jnp.concatenate([held[peer], held[peer + 1]], axis=0)
                 tables[block, peer * BLOCK : (peer + 2) * BLOCK, lanes] = pair.astype(jnp.bfloat16)
-        total[block] += jnp.dot(tables[block], features, preferred_element_type=jnp.float32)
-
-    @pl.when(tile == pl.num_programs(0) - 1)
-    def _():
-        for block in range(BLOCKS):
-            for peer in range(PLANES):
-                piece = total[block, peer * BLOCK : (peer + 1) * BLOCK, :]
-                out_ref[peer, block * BLOCK : (block + 1) * BLOCK, :] = piece.astype(jnp.bfloat16)
+        if block == 0:
+            copy.wait()
+        summed = jnp.dot(tables[block], features[...], preferred_element_type=jnp.float32)
+        for peer in range(PLANES):
+            piece = summed[peer * BLOCK : (peer + 1) * BLOCK, :].astype(jnp.bfloat16)
+            out_ref[peer, block * BLOCK : (block + 1) * BLOCK, :] = piece
 
 
 def partial_factors(steps, coords, features):
@@ -231,20 +228,20 @@
     return pl.pallas_call(
         factors_kernel,
         out_shape=jax.ShapeDtypeStruct((PLANES, COLUMN, F), jnp.bfloat16),
-        grid=(atoms // TILE,),
         in_specs=[
-            pl.BlockSpec((2, 8, FIRST), lambda t: (0, 0, 0)),
-            pl.BlockSpec((3, TILE), lambda t: (0, t)),
-            pl.BlockSpec((TILE, F), lambda t: (t, 0)),
+            pl.BlockSpec(memory_space=pltpu.VMEM),
+            pl.BlockSpec(memory_space=pltpu.VMEM),
+            pl.BlockSpec(memory_space=pl.ANY),
         ],
-        out_specs=pl.BlockSpec((PLANES, COLUMN, F), lambda t: (0, 0, 0)),
+        out_specs=pl.BlockSpec(memory_space=pltpu.VMEM),
         scratch_shapes=[
-            pltpu.VMEM((FIRST, TILE), jnp.float32),
-            pltpu.VMEM((BLOCKS, PLANES * BLOCK, TILE), jnp.bfloat16),
-            pltpu.VMEM((BLOCKS, PLANES * BLOCK, F), jnp.float32),
+            pltpu.VMEM((atoms, F), jnp.bfloat16),
+            pltpu.VMEM((FIRST, atoms), jnp.float32),
+            pltpu.VMEM((BLOCKS, PLANES * BLOCK, atoms), jnp.bfloat16),
+            pltpu.SemaphoreType.DMA,
         ],
         cost_estimate=pl.CostEstimate(
-            flops=2 * ALL_ROWS * atoms * F, bytes_accessed=atoms * F * 2, transcendentals=0
+            flops=2 * PLANES * COLUMN * atoms * F, bytes_accessed=atoms * F * 2, transcendentals=0
         ),
         name="factors",
     )(steps, coords, features)
@@ -477,17 +474,19 @@
     far_weights = lax.ppermute(weights, AXES, INNER_PAIRS)
     arrived, weights = lax.optimization_barrier((arrived, weights))
     sums = plane_sum(arrived)
+    sums, coords = lax.optimization_barrier((sums, coords))
+    near = lax.dynamic_slice_in_dim(coords, high * TILE, TILE, 1)
     shares = exchange(sums, GROUPS_LO)
+    near = lax.ppermute(near, AXES, LINE_SAME)
+    shares, near = lax.optimization_barrier((shares, near))
     filtered = filter_column(shares, weights, far_weights)
     filtered = exchange(filtered, GROUPS_XY).reshape(ALL_ROWS, F)
-    near = lax.dynamic_slice_in_dim(coords, high * TILE, TILE, 1)
-    near = lax.ppermute(near, AXES, LINE_SAME)
     tables = message_tables(place, jnp.asarray(ALL_STEPS), coords, near)
     quarter = functools.partial(message_quarter, place, tables, filtered)
-    others = [
-        lax.ppermute(quarter(far, own), AXES, pairs)
-        for far, own, pairs in ((True, True, LINE_SAME), (True, False, LINE_CROSS), (False, False, SWAP))
-    ]
+    others = []
+    for far, own, pairs in ((True, True, LINE_SAME), (True, False, LINE_CROSS), (False, False, SWAP)):
+        part = quarter(far, own)
+        others.append(lax.ppermute(part, AXES, pairs))
     own = quarter(False, True)
     return update(place, features, own, others, norm_gain.reshape(1, F), w_in, w_out)
 

time: 85.6 us -> 87 us (1.016)
  waiting for transfers between devices: 5.7 us -> 9.98 us
  starting transfers between devices: 60 us -> 58.3 us
  Pallas kernels: 18.9 us -> 17.5 us
    all_to_all x3, waiting for transfers between devices: 1.58 us -> 6.24 us  [exchange(): lax.all_to_all(pieces, AXES, split_axis=0, concat_axis=0, tiled=True, axi...]
    pallas_call x1, Pallas kernels: 7.57 us -> 6.22 us  [partial_factors(): pl.pallas_call(factors_kernel, out_shape=jax.ShapeDtypeStruct((PLANES, CO...]
    ppermute x1, waiting for transfers between devices: 1.16 us -> 0.01 us  [layer(): far_weights = lax.ppermute(weights, AXES, INNER_PAIRS)]
    ppermute x1, starting transfers between devices: 4.27 us -> 3.37 us  [layer(): near = lax.ppermute(near, AXES, LINE_SAME)]
  transfers between devices with their start and end apart: 10 -> 10, of which waited for: 6 -> 5; matrix products, arithmetic and copies ran while one was open for 0% -> 0% of each run, Pallas kernels for 6% -> 6%
where the time goes in v8:
time: 87 us; the launch traced here: 86.3 us
  starting transfers between devices  58.3 us (67%)
  Pallas kernels  17.5 us (20%)
  waiting for transfers between devices  9.98 us (11%)
    all_to_all x3, starting transfers between devices, exchange(): lax.all_to_all(pieces, AXES, split_axis=0, concat_axis=0, tiled=True, axi...  19.7 us
    ppermute x3, starting transfers between devices, layer(): others.append(lax.ppermute(part, AXES, pairs))  11.2 us
    ppermute x1, starting transfers between devices, layer(): weights += lax.ppermute(weights, AXES, OUTER_PAIRS)  10.4 us
    ppermute x1, starting transfers between devices, layer(): far_weights = lax.ppermute(weights, AXES, INNER_PAIRS)  8.84 us
    all_to_all x3, waiting for transfers between devices, exchange(): lax.all_to_all(pieces, AXES, split_axis=0, concat_axis=0, tiled=True, axi...  6.24 us
    pallas_call x1, Pallas kernels, partial_factors(): pl.pallas_call(factors_kernel, out_shape=jax.ShapeDtypeStruct((PLANES, CO...  6.22 us
    ppermute x1, starting transfers between devices, layer(): weights += lax.ppermute(swapped, AXES, SWAP)  4.87 us
    pallas_call x1, Pallas kernels, message_tables(): pl.pallas_call(tables_kernel, out_shape=jax.ShapeDtypeStruct((2 * TILE, A...  4 us
  transfers between devices with their start and end apart: 10, of which 5 were waited for; matrix products, arithmetic and copies ran while one was open for 0% of the time, Pallas kernels for 6%

profile of v8, /device:TPU:1, one launch (start us, length us, event | category | flops | bytes accessed | tf_op | source)
XLA Modules:
  0.0 86.3 jit_solution(15686897059326951979)
XLA Ops:
  0.0 6.2 %factors.1 = bf16[16,160,256]{2,1,0:T(8,128)(2,1)} custom-call(f32[2,8,232]{2,1,0:T(8,128)} %constant.56.clone.steps_ref, s32[3,2048]{1,0:T(4,128)} %own_ref, bf16[2048,256]{1,0:T(8,128)(2,1)} %features_ref.3), custom_call_target="tpu_custom_call" | custom-call | flops 2684354560 | bytes 1048576 | tf_op jit(solution)/shard_map/factors/pallas_call | solution.py:228
  6.2 0.0 copy-start.1
  6.2 0.0 copy-start.6
  6.3 7.7 %all-to-all-start = ((bf16[16,160,256]{2,1,0:T(8,128)(2,1)}), bf16[16,160,256]{2,1,0:T(8,128)(2,1)S(1)}, u32[]{:S(2)}, u32[]{:S(2)}) async-start(bf16[16,160,256]{2,1,0:T(8,128)(2,1)} %factors.1), calls=%async_computation | async-start | bytes 2621440 | tf_op jit(solution)/shard_map/all_to_all | solution.py:455
  14.0 0.0 copy-done.1
  14.0 0.0 copy-done.6
  14.0 0.0 copy-start.5
  14.0 0.3 grid_weights.1
  14.3 4.9 %collective-permute-start = (bf16[40,256]{1,0:T(8,128)(2,1)S(1)}, bf16[40,256]{1,0:T(8,128)(2,1)S(1)}, u32[]{:S(2)}, u32[]{:S(2)}) collective-permute-start(bf16[40,256]{1,0:T(8,128)(2,1)S(1)} %get-tuple-element.19), channel_id=1, source_target_pairs={{0,1},{1,0},{2,3},{3,2},{4,5},{5,4},{6,7},{7,6},{8,9},{9,8},{10,11... | collective-permute-start | bytes 61448 | tf_op jit(solution)/shard_map/ppermute | solution.py:472
  19.2 0.8 collective-permute-done
  20.0 10.4 %collective-permute-start.1 = (bf16[40,256]{1,0:T(8,128)(2,1)S(1)}, bf16[40,256]{1,0:T(8,128)(2,1)S(1)}, u32[]{:S(2)}, u32[]{:S(2)}) collective-permute-start(bf16[40,256]{1,0:T(8,128)(2,1)S(1)} %add.24), channel_id=1, source_target_pairs={{0,6},{1,7},{2,4},{3,5},{4,2},{5,3},{6,0},{7,1},{8,14},{9,15},{10,... | collective-permute-start | bytes 61448 | tf_op jit(solution)/shard_map/ppermute | solution.py:473
  30.5 1.2 %collective-permute-done.1 = bf16[40,256]{1,0:T(8,128)(2,1)S(1)} collective-permute-done((bf16[40,256]{1,0:T(8,128)(2,1)S(1)}, bf16[40,256]{1,0:T(8,128)(2,1)S(1)}, u32[]{:S(2)}, u32[]{:S(2)}) %collective-permute-start.1) | collective-permute-done | bytes 20512 | tf_op jit(solution)/shard_map/ppermute | solution.py:473
  31.6 0.0 all-to-all-done.arrived_ref
  31.7 0.8 plane_sum.1
  32.5 0.0 copy-start.2
  32.5 7.0 %all-to-all-start.1 = ((bf16[4,80,256]{2,1,0:T(8,128)(2,1)}), bf16[4,80,256]{2,1,0:T(8,128)(2,1)S(1)}, u32[]{:S(2)}, u32[]{:S(2)}) async-start(bf16[4,80,256]{2,1,0:T(8,128)(2,1)} %plane_sum.1), calls=%async_computation.1 | async-start | bytes 327680 | tf_op jit(solution)/shard_map/all_to_all | solution.py:455
  39.5 8.8 %collective-permute-start.3 = (bf16[40,256]{1,0:T(8,128)(2,1)S(1)}, bf16[40,256]{1,0:T(8,128)(2,1)S(1)}, u32[]{:S(2)}, u32[]{:S(2)}) collective-permute-start(bf16[40,256]{1,0:T(8,128)(2,1)S(1)} %add.25.near_ref), channel_id=1, source_target_pairs={{0,2},{1,3},{2,0},{3,1},{4,6},{5,7},{6,4},{7,5},{8,10},{9,11},{10,... | collective-permute-start | bytes 61448 | tf_op jit(solution)/shard_map/ppermute | solution.py:474
  48.4 0.0 copy-done.5
  48.4 3.4 %collective-permute-start.2 = (s32[3,512]{1,0:T(4,128)S(1)}, s32[3,512]{1,0:T(4,128)S(1)}, u32[]{:S(2)}, u32[]{:S(2)}) collective-permute-start(s32[3,512]{1,0:T(4,128)S(1)} %constant_dynamic-slice_fusion), channel_id=1, source_target_pairs={{0,32},{1,33},{2,34},{3,35},{4,36},{5,37},{6,38},{7,39},{8,40},{9,... | collective-permute-start | bytes 18440 | tf_op jit(solution)/shard_map/ppermute | solution.py:480
  51.8 1.4 %collective-permute-done.2.near_ref = s32[3,512]{1,0:T(4,128)S(1)} collective-permute-done((s32[3,512]{1,0:T(4,128)S(1)}, s32[3,512]{1,0:T(4,128)S(1)}, u32[]{:S(2)}, u32[]{:S(2)}) %collective-permute-start.2) | collective-permute-done | bytes 6176 | tf_op jit(solution)/shard_map/ppermute | solution.py:480
  53.2 0.0 all-to-all-done.1.arrived_ref
  53.2 0.0 collective-permute-done.3.far_ref
  53.2 1.0 %filter_column.1 = bf16[16,80,256]{2,1,0:T(8,128)(2,1)} custom-call(bf16[4,80,256]{2,1,0:T(8,128)(2,1)S(1)} %all-to-all-done.1.arrived_ref, bf16[40,256]{1,0:T(8,128)(2,1)S(1)} %add.25.near_ref, bf16[40,256]{1,0:T(8,128)(2,1)S(1)} %collective-permute-done.3.far_ref), custom_call_target="tpu_custom_call" | custom-call | tf_op jit(solution)/shard_map/filter_column/pallas_call | solution.py:339
  54.2 4.9 %all-to-all-start.2 = ((bf16[16,80,256]{2,1,0:T(8,128)(2,1)}), bf16[16,80,256]{2,1,0:T(8,128)(2,1)S(1)}, u32[]{:S(2)}, u32[]{:S(2)}) async-start(bf16[16,80,256]{2,1,0:T(8,128)(2,1)} %filter_column.1), calls=%async_computation.2 | async-start | bytes 1310720 | tf_op jit(solution)/shard_map/all_to_all | solution.py:455
  59.2 0.1 pad_add_fusion.place_ref
  59.3 0.0 copy-done.2
  59.3 4.0 %message_tables.1.tables_ref = bf16[1024,1280]{1,0:T(8,128)(2,1)S(1)} custom-call(s32[4]{0:T(128)S(1)} %pad_add_fusion.place_ref, f32[4,8,1280]{2,1,0:T(8,128)S(1)} %copy-done.2, s32[3,2048]{1,0:T(4,128)S(1)} %copy-done.5, s32[3,512]{1,0:T(4,128)S(1)} %collective-permute-done.2.near_ref), custom_call_target="tpu_custom_call" | custom-call | flops 20971520 | bytes 2621440 | tf_op jit(solution)/shard_map/message_tables/pallas_call | solution.py:365
  63.3 6.2 %all-to-all-done.2 = bf16[16,80,256]{2,1,0:T(8,128)(2,1)S(1)} async-done(((bf16[16,80,256]{2,1,0:T(8,128)(2,1)}), bf16[16,80,256]{2,1,0:T(8,128)(2,1)S(1)}, u32[]{:S(2)}, u32[]{:S(2)}) %all-to-all-start.2) | async-done | bytes 655392 | tf_op jit(solution)/shard_map/all_to_all | solution.py:455
  69.5 0.9 %shard_map.94 = bf16[256,256]{1,0:T(8,128)(2,1)S(1)} custom-call(s32[4]{0:T(128)S(1)} %pad_add_fusion.place_ref, bf16[1024,1280]{1,0:T(8,128)(2,1)S(1)} %message_tables.1.tables_ref, bf16[1280,256]{1,0:T(8,128)(2,1)S(1)} %bitcast.6), custom_call_target="tpu_custom_call" | custom-call | flops 167772160 | bytes 1310720 | tf_op jit(solution)/shard_map/pallas_call | solution.py:398
  70.4 0.9 %shard_map.93 = bf16[256,256]{1,0:T(8,128)(2,1)S(1)} custom-call(s32[4]{0:T(128)S(1)} %pad_add_fusion.place_ref, bf16[1024,1280]{1,0:T(8,128)(2,1)S(1)} %message_tables.1.tables_ref, bf16[1280,256]{1,0:T(8,128)(2,1)S(1)} %bitcast.7), custom_call_target="tpu_custom_call" | custom-call | flops 167772160 | bytes 1310720 | tf_op jit(solution)/shard_map/pallas_call | solution.py:398
  71.3 0.9 %shard_map.92 = bf16[256,256]{1,0:T(8,128)(2,1)S(1)} custom-call(s32[4]{0:T(128)S(1)} %pad_add_fusion.place_ref, bf16[1024,1280]{1,0:T(8,128)(2,1)S(1)} %message_tables.1.tables_ref, bf16[1280,256]{1,0:T(8,128)(2,1)S(1)} %bitcast.8), custom_call_target="tpu_custom_call" | custom-call | flops 167772160 | bytes 1310720 | tf_op jit(solution)/shard_map/pallas_call | solution.py:398
  72.2 0.0 copy-start
  72.2 0.0 copy-start.3
  72.2 0.0 copy-start.4
  72.2 0.0 copy-start.7
  72.2 3.0 %collective-permute-start.4 = (bf16[256,256]{1,0:T(8,128)(2,1)S(1)}, bf16[256,256]{1,0:T(8,128)(2,1)S(1)}, u32[]{:S(2)}, u32[]{:S(2)}) collective-permute-start(bf16[256,256]{1,0:T(8,128)(2,1)S(1)} %shard_map.92), channel_id=1, source_target_pairs={{0,32},{1,33},{2,34},{3,35},{4,36},{5,37},{6,38},{7,39},{8,40},{9,... | collective-permute-start | bytes 393224 | tf_op jit(solution)/shard_map/ppermute | solution.py:489
  75.2 6.2 %collective-permute-start.5 = (bf16[256,256]{1,0:T(8,128)(2,1)S(1)}, bf16[256,256]{1,0:T(8,128)(2,1)S(1)}, u32[]{:S(2)}, u32[]{:S(2)}) collective-permute-start(bf16[256,256]{1,0:T(8,128)(2,1)S(1)} %shard_map.93), channel_id=1, source_target_pairs={{0,33},{1,32},{2,35},{3,34},{4,37},{5,36},{6,39},{7,38},{8,41},{9,... | collective-permute-start | bytes 393224 | tf_op jit(solution)/shard_map/ppermute | solution.py:489
  81.4 2.0 %collective-permute-start.6 = (bf16[256,256]{1,0:T(8,128)(2,1)S(1)}, bf16[256,256]{1,0:T(8,128)(2,1)S(1)}, u32[]{:S(2)}, u32[]{:S(2)}) collective-permute-start(bf16[256,256]{1,0:T(8,128)(2,1)S(1)} %shard_map.94), channel_id=1, source_target_pairs={{0,1},{1,0},{2,3},{3,2},{4,5},{5,4},{6,7},{7,6},{8,9},{9,8},{10,11... | collective-permute-start | bytes 393224 | tf_op jit(solution)/shard_map/ppermute | solution.py:489
  83.4 0.9 %shard_map.91.own_ref = f32[256,256]{1,0:T(8,128)S(1)} custom-call(s32[4]{0:T(128)S(1)} %pad_add_fusion.place_ref, bf16[1024,1280]{1,0:T(8,128)(2,1)S(1)} %message_tables.1.tables_ref, bf16[1280,256]{1,0:T(8,128)(2,1)S(1)} %bitcast.9), custom_call_target="tpu_custom_call" | custom-call | flops 167772160 | bytes 1310720 | tf_op jit(solution)/shard_map/pallas_call | solution.py:398
  84.3 0.0 collective-permute-done.4.a_ref
  84.3 0.3 collective-permute-done.5.b_ref
  84.6 0.0 collective-permute-done.6.c_ref
  84.6 0.0 copy-done
  84.6 0.0 copy-done.3
  84.6 0.0 copy-done.4
  84.7 0.0 copy-done.7
  84.7 1.6 %update.1 = bf16[256,256]{1,0:T(8,128)(2,1)} custom-call(s32[4]{0:T(128)S(1)} %pad_add_fusion.place_ref, bf16[2048,256]{1,0:T(8,128)(2,1)S(1)} %copy-done, f32[256,256]{1,0:T(8,128)S(1)} %shard_map.91.own_ref, bf16[256,256]{1,0:T(8,128)(2,1)S(1)} %collective-permute-done.4.a_ref, bf16[256,256]{1,0:T(8,128)(2,1)S(1)} %collective-permute-done.5.b_ref, ...), custom_call_target="tpu_custom_call" | custom-call | tf_op jit(solution)/shard_map/update/pallas_call | solution.py:431
  (3 shorter events, 0.0 us)
Async XLA Ops:
  6.2 7.8 %copy-start.1 = (f32[512,256]{1,0:T(8,128)S(1)}, f32[512,256]{1,0:T(8,128)}, u32[]{:S(2)}) copy-start(f32[512,256]{1,0:T(8,128)} %weights_ref.1) | copy-start | bytes 1572868
  6.2 7.8 %copy-start.6 = (s32[3,512]{1,0:T(4,128)S(1)}, s32[3,512]{1,0:T(4,128)}, u32[]{:S(2)}) copy-start(s32[3,512]{1,0:T(4,128)} %miller_ref) | copy-start | bytes 18436
  6.3 25.4 %all-to-all-start = ((bf16[16,160,256]{2,1,0:T(8,128)(2,1)}), bf16[16,160,256]{2,1,0:T(8,128)(2,1)S(1)}, u32[]{:S(2)}, u32[]{:S(2)}) async-start(bf16[16,160,256]{2,1,0:T(8,128)(2,1)} %factors.1), calls=%async_computation | async-start | bytes 2621440 | tf_op jit(solution)/shard_map/all_to_all | solution.py:455
  14.0 34.4 %copy-start.5 = (s32[3,2048]{1,0:T(4,128)S(1)}, s32[3,2048]{1,0:T(4,128)}, u32[]{:S(2)}) copy-start(s32[3,2048]{1,0:T(4,128)} %own_ref) | copy-start | bytes 73732
  14.3 5.7 %collective-permute-start = (bf16[40,256]{1,0:T(8,128)(2,1)S(1)}, bf16[40,256]{1,0:T(8,128)(2,1)S(1)}, u32[]{:S(2)}, u32[]{:S(2)}) collective-permute-start(bf16[40,256]{1,0:T(8,128)(2,1)S(1)} %get-tuple-element.19), channel_id=1, source_target_pairs={{0,1},{1,0},{2,3},{3,2},{4,5},{5,4},{6,7},{7,6},{8,9},{9,8},{10,11... | collective-permute-start | bytes 61448 | tf_op jit(solution)/shard_map/ppermute | solution.py:472
  20.0 11.6 %collective-permute-start.1 = (bf16[40,256]{1,0:T(8,128)(2,1)S(1)}, bf16[40,256]{1,0:T(8,128)(2,1)S(1)}, u32[]{:S(2)}, u32[]{:S(2)}) collective-permute-start(bf16[40,256]{1,0:T(8,128)(2,1)S(1)} %add.24), channel_id=1, source_target_pairs={{0,6},{1,7},{2,4},{3,5},{4,2},{5,3},{6,0},{7,1},{8,14},{9,15},{10,... | collective-permute-start | bytes 61448 | tf_op jit(solution)/shard_map/ppermute | solution.py:473
  32.5 26.8 %copy-start.2 = (f32[4,8,1280]{2,1,0:T(8,128)S(1)}, f32[4,8,1280]{2,1,0:T(8,128)}, u32[]{:S(2)}) copy-start(f32[4,8,1280]{2,1,0:T(8,128)} %constant.57.clone.steps_ref) | copy-start | bytes 491524
  32.5 20.7 %all-to-all-start.1 = ((bf16[4,80,256]{2,1,0:T(8,128)(2,1)}), bf16[4,80,256]{2,1,0:T(8,128)(2,1)S(1)}, u32[]{:S(2)}, u32[]{:S(2)}) async-start(bf16[4,80,256]{2,1,0:T(8,128)(2,1)} %plane_sum.1), calls=%async_computation.1 | async-start | bytes 327680 | tf_op jit(solution)/shard_map/all_to_all | solution.py:455
  39.5 13.7 %collective-permute-start.3 = (bf16[40,256]{1,0:T(8,128)(2,1)S(1)}, bf16[40,256]{1,0:T(8,128)(2,1)S(1)}, u32[]{:S(2)}, u32[]{:S(2)}) collective-permute-start(bf16[40,256]{1,0:T(8,128)(2,1)S(1)} %add.25.near_ref), channel_id=1, source_target_pairs={{0,2},{1,3},{2,0},{3,1},{4,6},{5,7},{6,4},{7,5},{8,10},{9,11},{10,... | collective-permute-start | bytes 61448 | tf_op jit(solution)/shard_map/ppermute | solution.py:474
  48.4 4.8 %collective-permute-start.2 = (s32[3,512]{1,0:T(4,128)S(1)}, s32[3,512]{1,0:T(4,128)S(1)}, u32[]{:S(2)}, u32[]{:S(2)}) collective-permute-start(s32[3,512]{1,0:T(4,128)S(1)} %constant_dynamic-slice_fusion), channel_id=1, source_target_pairs={{0,32},{1,33},{2,34},{3,35},{4,36},{5,37},{6,38},{7,39},{8,40},{9,... | collective-permute-start | bytes 18440 | tf_op jit(solution)/shard_map/ppermute | solution.py:480
  54.2 15.3 %all-to-all-start.2 = ((bf16[16,80,256]{2,1,0:T(8,128)(2,1)}), bf16[16,80,256]{2,1,0:T(8,128)(2,1)S(1)}, u32[]{:S(2)}, u32[]{:S(2)}) async-start(bf16[16,80,256]{2,1,0:T(8,128)(2,1)} %filter_column.1), calls=%async_computation.2 | async-start | bytes 1310720 | tf_op jit(solution)/shard_map/all_to_all | solution.py:455
  72.2 12.5 %copy-start = (bf16[2048,256]{1,0:T(8,128)(2,1)S(1)}, bf16[2048,256]{1,0:T(8,128)(2,1)}, u32[]{:S(2)}) copy-start(bf16[2048,256]{1,0:T(8,128)(2,1)} %features_ref.3) | copy-start | bytes 3145732
  72.2 12.5 %copy-start.3 = (bf16[256,256]{1,0:T(8,128)(2,1)S(1)}, bf16[256,256]{1,0:T(8,128)(2,1)}, u32[]{:S(2)}) copy-start(bf16[256,256]{1,0:T(8,128)(2,1)} %w_in_ref.1) | copy-start | bytes 393220
  72.2 12.4 %copy-start.4 = (bf16[256,256]{1,0:T(8,128)(2,1)S(1)}, bf16[256,256]{1,0:T(8,128)(2,1)}, u32[]{:S(2)}) copy-start(bf16[256,256]{1,0:T(8,128)(2,1)} %w_out_ref.1) | copy-start | bytes 393220
  72.2 12.4 %copy-start.7 = (f32[256]{0:T(256)S(1)}, f32[256]{0:T(256)}, u32[]{:S(2)}) copy-start(f32[256]{0:T(256)} %param.13) | copy-start | bytes 3076
  72.2 12.1 %collective-permute-start.4 = (bf16[256,256]{1,0:T(8,128)(2,1)S(1)}, bf16[256,256]{1,0:T(8,128)(2,1)S(1)}, u32[]{:S(2)}, u32[]{:S(2)}) collective-permute-start(bf16[256,256]{1,0:T(8,128)(2,1)S(1)} %shard_map.92), channel_id=1, source_target_pairs={{0,32},{1,33},{2,34},{3,35},{4,36},{5,37},{6,38},{7,39},{8,40},{9,... | collective-permute-start | bytes 393224 | tf_op jit(solution)/shard_map/ppermute | solution.py:489
  75.2 9.4 %collective-permute-start.5 = (bf16[256,256]{1,0:T(8,128)(2,1)S(1)}, bf16[256,256]{1,0:T(8,128)(2,1)S(1)}, u32[]{:S(2)}, u32[]{:S(2)}) collective-permute-start(bf16[256,256]{1,0:T(8,128)(2,1)S(1)} %shard_map.93), channel_id=1, source_target_pairs={{0,33},{1,32},{2,35},{3,34},{4,37},{5,36},{6,39},{7,38},{8,41},{9,... | collective-permute-start | bytes 393224 | tf_op jit(solution)/shard_map/ppermute | solution.py:489
  81.4 3.2 %collective-permute-start.6 = (bf16[256,256]{1,0:T(8,128)(2,1)S(1)}, bf16[256,256]{1,0:T(8,128)(2,1)S(1)}, u32[]{:S(2)}, u32[]{:S(2)}) collective-permute-start(bf16[256,256]{1,0:T(8,128)(2,1)S(1)} %shard_map.94), channel_id=1, source_target_pairs={{0,1},{1,0},{2,3},{3,2},{4,5},{5,4},{6,7},{7,6},{8,9},{9,8},{10,11... | collective-permute-start | bytes 393224 | tf_op jit(solution)/shard_map/ppermute | solution.py:489

commit v9 on v8

--- a/solution.py
+++ b/solution.py
@@ -267,7 +267,7 @@
     return ((core * PLANES + peer) * BLOCKS + block) * OWN + spot
 
 
-def weights_kernel(miller_ref, weights_ref, own_ref, other_ref):
+def weights_kernel(miller_ref, weights_ref, out_ref):
     core, atom = lax.axis_index("wave") % 2, lax.axis_index("atom")
     plane, part = atom // 16 * 4 + atom % 4, atom // 4 % 2
     spots = grid_spots(miller_ref[0:1, :], miller_ref[1:2, :], miller_ref[2:3, :])
@@ -275,21 +275,20 @@
     weights = weights_ref[...]
     upper = weights.astype(jnp.bfloat16)
     lower = (weights - upper.astype(jnp.float32)).astype(jnp.bfloat16)
-    for held, out_ref in ((core, own_ref), (1 - core, other_ref)):
+    for turn, held in enumerate((core, 1 - core)):
         wanted = row + ((held * PLANES + plane) * 2 + part) * POINTS
         match = jnp.where(wanted == spots, 1.0, 0.0).astype(jnp.bfloat16)
         summed = jnp.dot(match, upper, preferred_element_type=jnp.float32)
         summed += jnp.dot(match, lower, preferred_element_type=jnp.float32)
-        out_ref[...] = summed.astype(jnp.bfloat16)
+        out_ref[turn * POINTS : (turn + 1) * POINTS, :] = summed.astype(jnp.bfloat16)
 
 
 def grid_weights(miller, weights):
-    shape = jax.ShapeDtypeStruct((POINTS, F), jnp.bfloat16)
     return pl.pallas_call(
         weights_kernel,
-        out_shape=(shape, shape),
+        out_shape=jax.ShapeDtypeStruct((2 * POINTS, F), jnp.bfloat16),
         in_specs=[pl.BlockSpec(memory_space=pltpu.VMEM)] * 2,
-        out_specs=(pl.BlockSpec(memory_space=pltpu.VMEM),) * 2,
+        out_specs=pl.BlockSpec(memory_space=pltpu.VMEM),
         compiler_params=pltpu.CompilerParams(vmem_limit_bytes=8 << 20),
         cost_estimate=pl.CostEstimate(
             flops=8 * POINTS * 512 * F, bytes_accessed=512 * F * 4, transcendentals=0
@@ -414,16 +413,20 @@
 def update_kernel(
     place_ref, features_ref, own_ref, a_ref, b_ref, c_ref, gain_ref, w_in_ref, w_out_ref, out_ref
 ):
-    message = own_ref[...]
-    for part_ref in (a_ref, b_ref, c_ref):
-        message += part_ref[...].astype(jnp.float32)
-    updated = features_ref[...].astype(jnp.float32) + message * (1.0 / math.sqrt(K))
-    power = jnp.mean(updated * updated, axis=1, keepdims=True)
-    normed = (updated / jnp.sqrt(power + 1e-06) * gain_ref[...]).astype(jnp.bfloat16)
-    hidden = jnp.dot(normed, w_in_ref[...], preferred_element_type=jnp.float32)
-    hidden = (hidden / (1.0 + jnp.exp(-hidden))).astype(jnp.bfloat16)
-    added = jnp.dot(hidden, w_out_ref[...], preferred_element_type=jnp.float32)
-    out_ref[...] = (updated + added).astype(jnp.bfloat16)
+    gain, w_in, w_out = gain_ref[...], w_in_ref[...], w_out_ref[...]
+    chunk = own_ref.shape[0] // 4
+    for start in range(0, own_ref.shape[0], chunk):
+        rows = pl.ds(start, chunk)
+        message = own_ref[rows, :]
+        for part_ref in (a_ref, b_ref, c_ref):
+            message += part_ref[rows, :].astype(jnp.float32)
+        updated = features_ref[rows, :].astype(jnp.float32) + message * (1.0 / math.sqrt(K))
+        power = jnp.mean(updated * updated, axis=1, keepdims=True)
+        normed = (updated / jnp.sqrt(power + 1e-06) * gain).astype(jnp.bfloat16)
+        hidden = jnp.dot(normed, w_in, preferred_element_type=jnp.float32)
+        hidden = (hidden / (1.0 + jnp.exp(-hidden))).astype(jnp.bfloat16)
+        added = jnp.dot(hidden, w_out, preferred_element_type=jnp.float32)
+        out_ref[rows, :] = (updated + added).astype(jnp.bfloat16)
 
 
 def update(place, features, own, others, gain, w_in, w_out):
@@ -468,18 +471,18 @@
     core, high = wave % 2, wave // 2
     place = jnp.stack([wave, core, high, core * 2 + atom // 4 % 2]).astype(jnp.int32)
     arrived = exchange(factors, GROUPS_XY)
-    weights, swapped = grid_weights(miller, filter_weights)
-    weights += lax.ppermute(swapped, AXES, SWAP)
+    weights = grid_weights(miller, filter_weights)
     weights += lax.ppermute(weights, AXES, OUTER_PAIRS)
     far_weights = lax.ppermute(weights, AXES, INNER_PAIRS)
     arrived, weights = lax.optimization_barrier((arrived, weights))
     sums = plane_sum(arrived)
-    sums, coords = lax.optimization_barrier((sums, coords))
+    shares = exchange(sums, GROUPS_LO)
+    weights += far_weights
+    swapped = lax.ppermute(weights[POINTS:], AXES, SWAP)
+    filtered = filter_column(shares, weights[:POINTS], swapped)
+    filtered, coords = lax.optimization_barrier((filtered, coords))
     near = lax.dynamic_slice_in_dim(coords, high * TILE, TILE, 1)
-    shares = exchange(sums, GROUPS_LO)
     near = lax.ppermute(near, AXES, LINE_SAME)
-    shares, near = lax.optimization_barrier((shares, near))
-    filtered = filter_column(shares, weights, far_weights)
     filtered = exchange(filtered, GROUPS_XY).reshape(ALL_ROWS, F)
     tables = message_tables(place, jnp.asarray(ALL_STEPS), coords, near)
     quarter = functools.partial(message_quarter, place, tables, filtered)

time: 87 us -> 90 us (1.034)
  starting transfers between devices: 58.3 us -> 60.2 us
    ppermute x1, starting transfers between devices: 10.4 us -> 12.5 us  [layer(): weights += lax.ppermute(weights, AXES, OUTER_PAIRS)]
    ppermute x1, waiting for transfers between devices: 0.01 us -> 1.38 us  [layer(): far_weights = lax.ppermute(weights, AXES, INNER_PAIRS)]
    ppermute x3, starting transfers between devices: 11.2 us -> 9.92 us  [layer(): others.append(lax.ppermute(part, AXES, pairs))]
    ppermute x1, starting transfers between devices: 4.87 us -> 6.05 us  [layer(): swapped = lax.ppermute(weights[POINTS:], AXES, SWAP)]
    all_to_all x3, starting transfers between devices: 19.7 us -> 18.6 us  [exchange(): lax.all_to_all(pieces, AXES, split_axis=0, concat_axis=0, tiled=True, axi...]
  transfers between devices with their start and end apart: 10 -> 10, of which waited for: 5 -> 7; matrix products, arithmetic and copies ran while one was open for 0% -> 0% of each run, Pallas kernels for 6% -> 6%
where the time goes in v9:
time: 90 us; the launch traced here: 89 us
  starting transfers between devices  60.2 us (67%)
  Pallas kernels  17.6 us (20%)
  waiting for transfers between devices  10.7 us (12%)
    all_to_all x3, starting transfers between devices, exchange(): lax.all_to_all(pieces, AXES, split_axis=0, concat_axis=0, tiled=True, axi...  18.6 us
    ppermute x1, starting transfers between devices, layer(): weights += lax.ppermute(weights, AXES, OUTER_PAIRS)  12.5 us
    ppermute x3, starting transfers between devices, layer(): others.append(lax.ppermute(part, AXES, pairs))  9.92 us
    ppermute x1, starting transfers between devices, layer(): far_weights = lax.ppermute(weights, AXES, INNER_PAIRS)  8.97 us
    pallas_call x1, Pallas kernels, partial_factors(): pl.pallas_call(factors_kernel, out_shape=jax.ShapeDtypeStruct((PLANES, CO...  6.22 us
    ppermute x1, starting transfers between devices, layer(): swapped = lax.ppermute(weights[POINTS:], AXES, SWAP)  6.05 us
    all_to_all x3, waiting for transfers between devices, exchange(): lax.all_to_all(pieces, AXES, split_axis=0, concat_axis=0, tiled=True, axi...  5.57 us
    ppermute x1, starting transfers between devices, layer(): near = lax.ppermute(near, AXES, LINE_SAME)  4.15 us
  transfers between devices with their start and end apart: 10, of which 7 were waited for; matrix products, arithmetic and copies ran while one was open for 0% of the time, Pallas kernels for 6%

profile of v9, /device:TPU:1, one launch (start us, length us, event | category | flops | bytes accessed | tf_op | source)
XLA Modules:
  0.0 89.0 jit_solution(7249705223164834571)
XLA Ops:
  0.0 6.2 %factors.1 = bf16[16,160,256]{2,1,0:T(8,128)(2,1)} custom-call(f32[2,8,232]{2,1,0:T(8,128)} %constant.56.clone.steps_ref, s32[3,2048]{1,0:T(4,128)} %own_ref, bf16[2048,256]{1,0:T(8,128)(2,1)} %features_ref.3), custom_call_target="tpu_custom_call" | custom-call | flops 2684354560 | bytes 1048576 | tf_op jit(solution)/shard_map/factors/pallas_call | solution.py:228
  6.2 0.0 copy-start.1
  6.2 0.0 copy-start.6
  6.3 7.7 %all-to-all-start = ((bf16[16,160,256]{2,1,0:T(8,128)(2,1)}), bf16[16,160,256]{2,1,0:T(8,128)(2,1)S(1)}, u32[]{:S(2)}, u32[]{:S(2)}) async-start(bf16[16,160,256]{2,1,0:T(8,128)(2,1)} %factors.1), calls=%async_computation | async-start | bytes 2621440 | tf_op jit(solution)/shard_map/all_to_all | solution.py:458
  14.0 0.0 copy-done.1
  14.0 0.0 copy-done.6
  14.0 0.3 grid_weights.1
  14.3 12.5 %collective-permute-start = (bf16[80,256]{1,0:T(8,128)(2,1)S(1)}, bf16[80,256]{1,0:T(8,128)(2,1)S(1)}, u32[]{:S(2)}, u32[]{:S(2)}) collective-permute-start(bf16[80,256]{1,0:T(8,128)(2,1)S(1)} %grid_weights.1), channel_id=1, source_target_pairs={{0,6},{1,7},{2,4},{3,5},{4,2},{5,3},{6,0},{7,1},{8,14},{9,15},{10,... | collective-permute-start | bytes 122888 | tf_op jit(solution)/shard_map/ppermute | solution.py:475
  26.8 1.7 %collective-permute-done = bf16[80,256]{1,0:T(8,128)(2,1)S(1)} collective-permute-done((bf16[80,256]{1,0:T(8,128)(2,1)S(1)}, bf16[80,256]{1,0:T(8,128)(2,1)S(1)}, u32[]{:S(2)}, u32[]{:S(2)}) %collective-permute-start) | collective-permute-done | bytes 40992 | tf_op jit(solution)/shard_map/ppermute | solution.py:475
  28.5 2.8 %all-to-all-done.arrived_ref = bf16[16,160,256]{2,1,0:T(8,128)(2,1)S(1)} async-done(((bf16[16,160,256]{2,1,0:T(8,128)(2,1)}), bf16[16,160,256]{2,1,0:T(8,128)(2,1)S(1)}, u32[]{:S(2)}, u32[]{:S(2)}) %all-to-all-start) | async-done | bytes 1310752 | tf_op jit(solution)/shard_map/all_to_all | solution.py:458
  31.2 0.8 plane_sum.1
  32.1 7.3 %all-to-all-start.1 = ((bf16[4,80,256]{2,1,0:T(8,128)(2,1)}), bf16[4,80,256]{2,1,0:T(8,128)(2,1)S(1)}, u32[]{:S(2)}, u32[]{:S(2)}) async-start(bf16[4,80,256]{2,1,0:T(8,128)(2,1)} %plane_sum.1), calls=%async_computation.1 | async-start | bytes 327680 | tf_op jit(solution)/shard_map/all_to_all | solution.py:458
  39.4 0.0 copy-start.5
  39.4 0.0 copy-start.2
  39.4 9.0 %collective-permute-start.1 = (bf16[80,256]{1,0:T(8,128)(2,1)S(1)}, bf16[80,256]{1,0:T(8,128)(2,1)S(1)}, u32[]{:S(2)}, u32[]{:S(2)}) collective-permute-start(bf16[80,256]{1,0:T(8,128)(2,1)S(1)} %add.24), channel_id=1, source_target_pairs={{0,2},{1,3},{2,0},{3,1},{4,6},{5,7},{6,4},{7,5},{8,10},{9,11},{10,... | collective-permute-start | bytes 122888 | tf_op jit(solution)/shard_map/ppermute | solution.py:476
  48.4 1.4 %collective-permute-done.1 = bf16[80,256]{1,0:T(8,128)(2,1)S(1)} collective-permute-done((bf16[80,256]{1,0:T(8,128)(2,1)S(1)}, bf16[80,256]{1,0:T(8,128)(2,1)S(1)}, u32[]{:S(2)}, u32[]{:S(2)}) %collective-permute-start.1) | collective-permute-done | bytes 40992 | tf_op jit(solution)/shard_map/ppermute | solution.py:476
  49.8 6.0 %collective-permute-start.2 = (bf16[40,256]{1,0:T(8,128)(2,1)S(1)}, bf16[40,256]{1,0:T(8,128)(2,1)S(1)}, u32[]{:S(2)}, u32[]{:S(2)}) collective-permute-start(bf16[40,256]{1,0:T(8,128)(2,1)S(1)} %get-tuple-element.19), channel_id=1, source_target_pairs={{0,1},{1,0},{2,3},{3,2},{4,5},{5,4},{6,7},{7,6},{8,9},{9,8},{10,11... | collective-permute-start | bytes 61448 | tf_op jit(solution)/shard_map/ppermute | solution.py:481
  55.8 0.8 collective-permute-done.2.far_ref
  56.6 0.0 all-to-all-done.1.arrived_ref
  56.6 1.0 %filter_column.1 = bf16[16,80,256]{2,1,0:T(8,128)(2,1)} custom-call(bf16[4,80,256]{2,1,0:T(8,128)(2,1)S(1)} %all-to-all-done.1.arrived_ref, bf16[40,256]{1,0:T(8,128)(2,1)S(1)} %get-tuple-element.20.near_ref, bf16[40,256]{1,0:T(8,128)(2,1)S(1)} %collective-permute-done.2.far_ref), custom_call_target="tpu_custom_call" | custom-call | tf_op jit(solution)/shard_map/filter_column/pallas_call | solution.py:338
  57.7 3.6 %all-to-all-start.2 = ((bf16[16,80,256]{2,1,0:T(8,128)(2,1)}), bf16[16,80,256]{2,1,0:T(8,128)(2,1)S(1)}, u32[]{:S(2)}, u32[]{:S(2)}) async-start(bf16[16,80,256]{2,1,0:T(8,128)(2,1)} %filter_column.1), calls=%async_computation.2 | async-start | bytes 1310720 | tf_op jit(solution)/shard_map/all_to_all | solution.py:458
  61.3 0.0 copy-done.5
  61.4 4.1 %collective-permute-start.3 = (s32[3,512]{1,0:T(4,128)S(1)}, s32[3,512]{1,0:T(4,128)S(1)}, u32[]{:S(2)}, u32[]{:S(2)}) collective-permute-start(s32[3,512]{1,0:T(4,128)S(1)} %constant_dynamic-slice_fusion), channel_id=1, source_target_pairs={{0,32},{1,33},{2,34},{3,35},{4,36},{5,37},{6,38},{7,39},{8,40},{9,... | collective-permute-start | bytes 18440 | tf_op jit(solution)/shard_map/ppermute | solution.py:485
  65.5 0.1 pad_add_fusion.place_ref
  65.6 1.2 %collective-permute-done.3.near_ref = s32[3,512]{1,0:T(4,128)S(1)} collective-permute-done((s32[3,512]{1,0:T(4,128)S(1)}, s32[3,512]{1,0:T(4,128)S(1)}, u32[]{:S(2)}, u32[]{:S(2)}) %collective-permute-start.3) | collective-permute-done | bytes 6176 | tf_op jit(solution)/shard_map/ppermute | solution.py:485
  66.8 0.0 copy-done.2
  66.8 4.0 %message_tables.1.tables_ref = bf16[1024,1280]{1,0:T(8,128)(2,1)S(1)} custom-call(s32[4]{0:T(128)S(1)} %pad_add_fusion.place_ref, f32[4,8,1280]{2,1,0:T(8,128)S(1)} %copy-done.2, s32[3,2048]{1,0:T(4,128)S(1)} %copy-done.5, s32[3,512]{1,0:T(4,128)S(1)} %collective-permute-done.3.near_ref), custom_call_target="tpu_custom_call" | custom-call | flops 20971520 | bytes 2621440 | tf_op jit(solution)/shard_map/message_tables/pallas_call | solution.py:364
  70.8 2.8 %all-to-all-done.2 = bf16[16,80,256]{2,1,0:T(8,128)(2,1)S(1)} async-done(((bf16[16,80,256]{2,1,0:T(8,128)(2,1)}), bf16[16,80,256]{2,1,0:T(8,128)(2,1)S(1)}, u32[]{:S(2)}, u32[]{:S(2)}) %all-to-all-start.2) | async-done | bytes 655392 | tf_op jit(solution)/shard_map/all_to_all | solution.py:458
  73.6 0.9 shard_map.94
  74.5 0.9 shard_map.93
  75.4 0.9 shard_map.92
  76.3 0.0 copy-start
  76.3 0.0 copy-start.3
  76.3 0.0 copy-start.4
  76.3 0.0 copy-start.7
  76.3 4.1 %collective-permute-start.4 = (bf16[256,256]{1,0:T(8,128)(2,1)S(1)}, bf16[256,256]{1,0:T(8,128)(2,1)S(1)}, u32[]{:S(2)}, u32[]{:S(2)}) collective-permute-start(bf16[256,256]{1,0:T(8,128)(2,1)S(1)} %shard_map.92), channel_id=1, source_target_pairs={{0,32},{1,33},{2,34},{3,35},{4,36},{5,37},{6,38},{7,39},{8,40},{9,... | collective-permute-start | bytes 393224 | tf_op jit(solution)/shard_map/ppermute | solution.py:492
  80.4 3.5 %collective-permute-start.5 = (bf16[256,256]{1,0:T(8,128)(2,1)S(1)}, bf16[256,256]{1,0:T(8,128)(2,1)S(1)}, u32[]{:S(2)}, u32[]{:S(2)}) collective-permute-start(bf16[256,256]{1,0:T(8,128)(2,1)S(1)} %shard_map.93), channel_id=1, source_target_pairs={{0,33},{1,32},{2,35},{3,34},{4,37},{5,36},{6,39},{7,38},{8,41},{9,... | collective-permute-start | bytes 393224 | tf_op jit(solution)/shard_map/ppermute | solution.py:492
  84.0 2.3 %collective-permute-start.6 = (bf16[256,256]{1,0:T(8,128)(2,1)S(1)}, bf16[256,256]{1,0:T(8,128)(2,1)S(1)}, u32[]{:S(2)}, u32[]{:S(2)}) collective-permute-start(bf16[256,256]{1,0:T(8,128)(2,1)S(1)} %shard_map.94), channel_id=1, source_target_pairs={{0,1},{1,0},{2,3},{3,2},{4,5},{5,4},{6,7},{7,6},{8,9},{9,8},{10,11... | collective-permute-start | bytes 393224 | tf_op jit(solution)/shard_map/ppermute | solution.py:492
  86.3 0.9 shard_map.91.own_ref
  87.2 0.0 collective-permute-done.4.a_ref
  87.2 0.0 collective-permute-done.5.b_ref
  87.2 0.1 collective-permute-done.6.c_ref
  87.2 0.0 copy-done
  87.3 0.0 copy-done.3
  87.3 0.0 copy-done.4
  87.3 0.0 copy-done.7
  87.3 1.7 %update.1 = bf16[256,256]{1,0:T(8,128)(2,1)} custom-call(s32[4]{0:T(128)S(1)} %pad_add_fusion.place_ref, bf16[2048,256]{1,0:T(8,128)(2,1)S(1)} %copy-done, f32[256,256]{1,0:T(8,128)S(1)} %shard_map.91.own_ref, bf16[256,256]{1,0:T(8,128)(2,1)S(1)} %collective-permute-done.4.a_ref, bf16[256,256]{1,0:T(8,128)(2,1)S(1)} %collective-permute-done.5.b_ref, ...), custom_call_target="tpu_custom_call" | custom-call | tf_op jit(solution)/shard_map/update/pallas_call | solution.py:434
  (4 shorter events, 0.0 us)
Async XLA Ops:
  6.2 7.8 %copy-start.1 = (f32[512,256]{1,0:T(8,128)S(1)}, f32[512,256]{1,0:T(8,128)}, u32[]{:S(2)}) copy-start(f32[512,256]{1,0:T(8,128)} %weights_ref.1) | copy-start | bytes 1572868
  6.2 7.8 %copy-start.6 = (s32[3,512]{1,0:T(4,128)S(1)}, s32[3,512]{1,0:T(4,128)}, u32[]{:S(2)}) copy-start(s32[3,512]{1,0:T(4,128)} %miller_ref) | copy-start | bytes 18436
  6.3 25.0 %all-to-all-start = ((bf16[16,160,256]{2,1,0:T(8,128)(2,1)}), bf16[16,160,256]{2,1,0:T(8,128)(2,1)S(1)}, u32[]{:S(2)}, u32[]{:S(2)}) async-start(bf16[16,160,256]{2,1,0:T(8,128)(2,1)} %factors.1), calls=%async_computation | async-start | bytes 2621440 | tf_op jit(solution)/shard_map/all_to_all | solution.py:458
  14.3 14.1 %collective-permute-start = (bf16[80,256]{1,0:T(8,128)(2,1)S(1)}, bf16[80,256]{1,0:T(8,128)(2,1)S(1)}, u32[]{:S(2)}, u32[]{:S(2)}) collective-permute-start(bf16[80,256]{1,0:T(8,128)(2,1)S(1)} %grid_weights.1), channel_id=1, source_target_pairs={{0,6},{1,7},{2,4},{3,5},{4,2},{5,3},{6,0},{7,1},{8,14},{9,15},{10,... | collective-permute-start | bytes 122888 | tf_op jit(solution)/shard_map/ppermute | solution.py:475
  32.1 24.6 %all-to-all-start.1 = ((bf16[4,80,256]{2,1,0:T(8,128)(2,1)}), bf16[4,80,256]{2,1,0:T(8,128)(2,1)S(1)}, u32[]{:S(2)}, u32[]{:S(2)}) async-start(bf16[4,80,256]{2,1,0:T(8,128)(2,1)} %plane_sum.1), calls=%async_computation.1 | async-start | bytes 327680 | tf_op jit(solution)/shard_map/all_to_all | solution.py:458
  39.4 22.0 %copy-start.5 = (s32[3,2048]{1,0:T(4,128)S(1)}, s32[3,2048]{1,0:T(4,128)}, u32[]{:S(2)}) copy-start(s32[3,2048]{1,0:T(4,128)} %own_ref) | copy-start | bytes 73732
  39.4 27.5 %copy-start.2 = (f32[4,8,1280]{2,1,0:T(8,128)S(1)}, f32[4,8,1280]{2,1,0:T(8,128)}, u32[]{:S(2)}) copy-start(f32[4,8,1280]{2,1,0:T(8,128)} %constant.57.clone.steps_ref) | copy-start | bytes 491524
  39.4 10.4 %collective-permute-start.1 = (bf16[80,256]{1,0:T(8,128)(2,1)S(1)}, bf16[80,256]{1,0:T(8,128)(2,1)S(1)}, u32[]{:S(2)}, u32[]{:S(2)}) collective-permute-start(bf16[80,256]{1,0:T(8,128)(2,1)S(1)} %add.24), channel_id=1, source_target_pairs={{0,2},{1,3},{2,0},{3,1},{4,6},{5,7},{6,4},{7,5},{8,10},{9,11},{10,... | collective-permute-start | bytes 122888 | tf_op jit(solution)/shard_map/ppermute | solution.py:476
  49.8 6.9 %collective-permute-start.2 = (bf16[40,256]{1,0:T(8,128)(2,1)S(1)}, bf16[40,256]{1,0:T(8,128)(2,1)S(1)}, u32[]{:S(2)}, u32[]{:S(2)}) collective-permute-start(bf16[40,256]{1,0:T(8,128)(2,1)S(1)} %get-tuple-element.19), channel_id=1, source_target_pairs={{0,1},{1,0},{2,3},{3,2},{4,5},{5,4},{6,7},{7,6},{8,9},{9,8},{10,11... | collective-permute-start | bytes 61448 | tf_op jit(solution)/shard_map/ppermute | solution.py:481
  57.7 16.0 %all-to-all-start.2 = ((bf16[16,80,256]{2,1,0:T(8,128)(2,1)}), bf16[16,80,256]{2,1,0:T(8,128)(2,1)S(1)}, u32[]{:S(2)}, u32[]{:S(2)}) async-start(bf16[16,80,256]{2,1,0:T(8,128)(2,1)} %filter_column.1), calls=%async_computation.2 | async-start | bytes 1310720 | tf_op jit(solution)/shard_map/all_to_all | solution.py:458
  61.4 5.5 %collective-permute-start.3 = (s32[3,512]{1,0:T(4,128)S(1)}, s32[3,512]{1,0:T(4,128)S(1)}, u32[]{:S(2)}, u32[]{:S(2)}) collective-permute-start(s32[3,512]{1,0:T(4,128)S(1)} %constant_dynamic-slice_fusion), channel_id=1, source_target_pairs={{0,32},{1,33},{2,34},{3,35},{4,36},{5,37},{6,38},{7,39},{8,40},{9,... | collective-permute-start | bytes 18440 | tf_op jit(solution)/shard_map/ppermute | solution.py:485
  76.3 11.0 %copy-start = (bf16[2048,256]{1,0:T(8,128)(2,1)S(1)}, bf16[2048,256]{1,0:T(8,128)(2,1)}, u32[]{:S(2)}) copy-start(bf16[2048,256]{1,0:T(8,128)(2,1)} %features_ref.3) | copy-start | bytes 3145732
  76.3 11.0 %copy-start.3 = (bf16[256,256]{1,0:T(8,128)(2,1)S(1)}, bf16[256,256]{1,0:T(8,128)(2,1)}, u32[]{:S(2)}) copy-start(bf16[256,256]{1,0:T(8,128)(2,1)} %w_in_ref.1) | copy-start | bytes 393220
  76.3 10.9 %copy-start.4 = (bf16[256,256]{1,0:T(8,128)(2,1)S(1)}, bf16[256,256]{1,0:T(8,128)(2,1)}, u32[]{:S(2)}) copy-start(bf16[256,256]{1,0:T(8,128)(2,1)} %w_out_ref.1) | copy-start | bytes 393220
  76.3 10.9 %copy-start.7 = (f32[256]{0:T(256)S(1)}, f32[256]{0:T(256)}, u32[]{:S(2)}) copy-start(f32[256]{0:T(256)} %param.13) | copy-start | bytes 3076
  76.3 10.8 %collective-permute-start.4 = (bf16[256,256]{1,0:T(8,128)(2,1)S(1)}, bf16[256,256]{1,0:T(8,128)(2,1)S(1)}, u32[]{:S(2)}, u32[]{:S(2)}) collective-permute-start(bf16[256,256]{1,0:T(8,128)(2,1)S(1)} %shard_map.92), channel_id=1, source_target_pairs={{0,32},{1,33},{2,34},{3,35},{4,36},{5,37},{6,38},{7,39},{8,40},{9,... | collective-permute-start | bytes 393224 | tf_op jit(solution)/shard_map/ppermute | solution.py:492
  80.4 6.8 %collective-permute-start.5 = (bf16[256,256]{1,0:T(8,128)(2,1)S(1)}, bf16[256,256]{1,0:T(8,128)(2,1)S(1)}, u32[]{:S(2)}, u32[]{:S(2)}) collective-permute-start(bf16[256,256]{1,0:T(8,128)(2,1)S(1)} %shard_map.93), channel_id=1, source_target_pairs={{0,33},{1,32},{2,35},{3,34},{4,37},{5,36},{6,39},{7,38},{8,41},{9,... | collective-permute-start | bytes 393224 | tf_op jit(solution)/shard_map/ppermute | solution.py:492
  84.0 3.3 %collective-permute-start.6 = (bf16[256,256]{1,0:T(8,128)(2,1)S(1)}, bf16[256,256]{1,0:T(8,128)(2,1)S(1)}, u32[]{:S(2)}, u32[]{:S(2)}) collective-permute-start(bf16[256,256]{1,0:T(8,128)(2,1)S(1)} %shard_map.94), channel_id=1, source_target_pairs={{0,1},{1,0},{2,3},{3,2},{4,5},{5,4},{6,7},{7,6},{8,9},{9,8},{10,11... | collective-permute-start | bytes 393224 | tf_op jit(solution)/shard_map/ppermute | solution.py:492

commit v10 on v9

--- a/solution.py
+++ b/solution.py
@@ -173,54 +173,70 @@
 
 
 def factors_kernel(
-    steps_ref, coords_ref, features_ref, out_ref, features, first, tables, copied
+    steps_ref, coords_ref, features_ref, out_ref, features, first, tables, total, copied
 ):
     copy = pltpu.make_async_copy(features_ref, features, copied)
     copy.start()
     core = lax.axis_index("wave") % 2
     steps = steps_ref[core].astype(jnp.bfloat16)
-    atoms = coords_ref.shape[1]
-    for start in range(0, atoms, TILE):
+    part = coords_ref.shape[1] // 2
+    for half in TWO:
+        first_half(half, part, steps, coords_ref, first)
+        mains = {}
+        for block in range(BLOCKS):
+            for start in range(half * part, (half + 1) * part, HALVES):
+                fill_tables(block, start, first, mains, tables)
+            if half == 0 and block == 0:
+                copy.wait()
+            atoms = pl.ds(half * part, part)
+            added = jnp.dot(
+                tables[block, :, atoms], features[atoms, :], preferred_element_type=jnp.float32
+            )
+            if half == 0:
+                total[block] = added
+                continue
+            summed = total[block] + added
+            for peer in range(PLANES):
+                piece = summed[peer * BLOCK : (peer + 1) * BLOCK, :].astype(jnp.bfloat16)
+                out_ref[peer, block * BLOCK : (block + 1) * BLOCK, :] = piece
+
+
+def first_half(half, part, steps, coords_ref, first):
+    for start in range(half * part, (half + 1) * part, TILE):
         parts = split_coords(coords_ref[:, start : start + TILE])
         turns = lax.dot_general(steps, parts, OUTER, preferred_element_type=jnp.float32)
         first[:, start : start + TILE] = cosine_of_turns(turns)
-    mains = {}
-    for block in range(BLOCKS):
-        for start in range(0, atoms, HALVES):
-            lanes = pl.ds(start, HALVES)
-            if block < 2:
-                at = first[AT[block] : AT[block] + BLOCK, lanes]
-                after = first[AT[block] + BLOCK : AT[block] + 2 * BLOCK, lanes]
-            else:
-                third = 2.0 * first[THIRD : THIRD + 1, lanes]
-                main = [
-                    third * near - far
-                    for near, far in zip(mains[block - 1, start], mains[block - 2, start])
-                ]
-                mixed = [first[AT[block] + 8 * p : AT[block] + 8 * p + 8, lanes] for p in TWO]
-                at, after = (jnp.concatenate([main[p], mixed[p]], axis=0) for p in TWO)
-            mains[block, start] = at[:MAIN], after[:MAIN]
-            mixed = 2.0 * first[STRIDES + 8 * block : STRIDES + 8 * block + 8, lanes]
-            common = jnp.broadcast_to(mixed[0:1, :], (MAIN, HALVES))
-            stride = jnp.concatenate([common, mixed], axis=0)
-            held = {MIDDLE: at, MIDDLE + 1: after}
-            for peer in range(MIDDLE, PLANES, 2):
-                for later in (peer, peer + 1):
-                    if later not in held:
-                        held[later] = stride * held[later - 1] - held[later - 2]
-                pair = jnp.concatenate([held[peer], held[peer + 1]], axis=0)
-                tables[block, peer * BLOCK : (peer + 2) * BLOCK, lanes] = pair.astype(jnp.bfloat16)
-            for peer in range(MIDDLE - 2, -1, -2):
-                for earlier in (peer + 1, peer):
-                    held[earlier] = stride * held[earlier + 1] - held[earlier + 2]
-                pair = jnp.concatenate([held[peer], held[peer + 1]], axis=0)
-                tables[block, peer * BLOCK : (peer + 2) * BLOCK, lanes] = pair.astype(jnp.bfloat16)
-        if block == 0:
-            copy.wait()
-        summed = jnp.dot(tables[block], features[...], preferred_element_type=jnp.float32)
-        for peer in range(PLANES):
-            piece = summed[peer * BLOCK : (peer + 1) * BLOCK, :].astype(jnp.bfloat16)
-            out_ref[peer, block * BLOCK : (block + 1) * BLOCK, :] = piece
+
+
+def fill_tables(block, start, first, mains, tables):
+    lanes = pl.ds(start, HALVES)
+    if block < 2:
+        at = first[AT[block] : AT[block] + BLOCK, lanes]
+        after = first[AT[block] + BLOCK : AT[block] + 2 * BLOCK, lanes]
+    else:
+        third = 2.0 * first[THIRD : THIRD + 1, lanes]
+        main = [
+            third * near - far
+            for near, far in zip(mains[block - 1, start], mains[block - 2, start])
+        ]
+        mixed = [first[AT[block] + 8 * p : AT[block] + 8 * p + 8, lanes] for p in TWO]
+        at, after = (jnp.concatenate([main[p], mixed[p]], axis=0) for p in TWO)
+    mains[block, start] = at[:MAIN], after[:MAIN]
+    mixed = 2.0 * first[STRIDES + 8 * block : STRIDES + 8 * block + 8, lanes]
+    common = jnp.broadcast_to(mixed[0:1, :], (MAIN, HALVES))
+    stride = jnp.concatenate([common, mixed], axis=0)
+    held = {MIDDLE: at, MIDDLE + 1: after}
+    for peer in range(MIDDLE, PLANES, 2):
+        for later in (peer, peer + 1):
+            if later not in held:
+                held[later] = stride * held[later - 1] - held[later - 2]
+        pair = jnp.concatenate([held[peer], held[peer + 1]], axis=0)
+        tables[block, peer * BLOCK : (peer + 2) * BLOCK, lanes] = pair.astype(jnp.bfloat16)
+    for peer in range(MIDDLE - 2, -1, -2):
+        for earlier in (peer + 1, peer):
+            held[earlier] = stride * held[earlier + 1] - held[earlier + 2]
+        pair = jnp.concatenate([held[peer], held[peer + 1]], axis=0)
+        tables[block, peer * BLOCK : (peer + 2) * BLOCK, lanes] = pair.astype(jnp.bfloat16)
 
 
 def partial_factors(steps, coords, features):
@@ -238,6 +254,7 @@
             pltpu.VMEM((atoms, F), jnp.bfloat16),
             pltpu.VMEM((FIRST, atoms), jnp.float32),
             pltpu.VMEM((BLOCKS, PLANES * BLOCK, atoms), jnp.bfloat16),
+            pltpu.VMEM((BLOCKS, PLANES * BLOCK, F), jnp.float32),
             pltpu.SemaphoreType.DMA,
         ],
         cost_estimate=pl.CostEstimate(
@@ -382,21 +399,23 @@
     )(place, steps, coords, near)
 
 
-def message_kernel(place_ref, tables_ref, filtered_ref, out_ref, *, far, own):
+def message_kernel(place_ref, tables_ref, filtered_ref, out_ref, *, own):
     half = TILE // 2
     core = place_ref[1] if own else 1 - place_ref[1]
-    start = pl.multiple_of(core * half, half) + far * TILE
-    tables = tables_ref[pl.ds(start, half), :]
-    message = jnp.dot(tables, filtered_ref[...], preferred_element_type=jnp.float32)
-    out_ref[...] = message.astype(out_ref.dtype)
-
-
-def message_quarter(place, tables, filtered, far, own):
+    start = pl.multiple_of(core * half, half)
+    filtered = filtered_ref[...]
+    for side in TWO:
+        tables = tables_ref[pl.ds(start + side * TILE, half), :]
+        message = jnp.dot(tables, filtered, preferred_element_type=jnp.float32)
+        out_ref[side] = message.astype(out_ref.dtype)
+
+
+def message_halves(place, tables, filtered, own):
     half = TILE // 2
-    kept = own and not far
-    return pl.pallas_call(
-        functools.partial(message_kernel, far=far, own=own),
-        out_shape=jax.ShapeDtypeStruct((half, F), jnp.float32 if kept else jnp.bfloat16),
+    dtype = jnp.float32 if own else jnp.bfloat16
+    return pl.pallas_call(
+        functools.partial(message_kernel, own=own),
+        out_shape=jax.ShapeDtypeStruct((2, half, F), dtype),
         in_specs=[
             pl.BlockSpec(memory_space=pltpu.SMEM),
             pl.BlockSpec(memory_space=pltpu.VMEM),
@@ -405,22 +424,25 @@
         out_specs=pl.BlockSpec(memory_space=pltpu.VMEM),
         compiler_params=pltpu.CompilerParams(vmem_limit_bytes=16 << 20),
         cost_estimate=pl.CostEstimate(
-            flops=2 * half * ALL_ROWS * F, bytes_accessed=4 * half * ALL_ROWS, transcendentals=0
+            flops=4 * half * ALL_ROWS * F, bytes_accessed=8 * half * ALL_ROWS, transcendentals=0
         ),
+        name="message_own" if own else "message_other",
     )(place, tables, filtered)
 
 
 def update_kernel(
-    place_ref, features_ref, own_ref, a_ref, b_ref, c_ref, gain_ref, w_in_ref, w_out_ref, out_ref
+    place_ref, features_ref, owns_ref, others_ref, far_ref, gain_ref, w_in_ref, w_out_ref, out_ref
 ):
     gain, w_in, w_out = gain_ref[...], w_in_ref[...], w_out_ref[...]
-    chunk = own_ref.shape[0] // 4
-    for start in range(0, own_ref.shape[0], chunk):
+    half = TILE // 2
+    base = pl.multiple_of(place_ref[0] * half, half)
+    chunk = half // 2
+    for start in range(0, half, chunk):
         rows = pl.ds(start, chunk)
-        message = own_ref[rows, :]
-        for part_ref in (a_ref, b_ref, c_ref):
-            message += part_ref[rows, :].astype(jnp.float32)
-        updated = features_ref[rows, :].astype(jnp.float32) + message * (1.0 / math.sqrt(K))
+        message = owns_ref[0, rows, :] + others_ref[0, rows, :].astype(jnp.float32)
+        message += far_ref[rows, :].astype(jnp.float32)
+        features = features_ref[pl.ds(base + start, chunk), :].astype(jnp.float32)
+        updated = features + message * (1.0 / math.sqrt(K))
         power = jnp.mean(updated * updated, axis=1, keepdims=True)
         normed = (updated / jnp.sqrt(power + 1e-06) * gain).astype(jnp.bfloat16)
         hidden = jnp.dot(normed, w_in, preferred_element_type=jnp.float32)
@@ -429,29 +451,16 @@
         out_ref[rows, :] = (updated + added).astype(jnp.bfloat16)
 
 
-def update(place, features, own, others, gain, w_in, w_out):
-    half = TILE // 2
+def update(place, features, owns, others, far, gain, w_in, w_out):
     return pl.pallas_call(
         update_kernel,
-        out_shape=jax.ShapeDtypeStruct((half, F), jnp.bfloat16),
-        grid_spec=pltpu.PrefetchScalarGridSpec(
-            num_scalar_prefetch=1,
-            grid=(1,),
-            in_specs=[
-                pl.BlockSpec((half, F), lambda t, place: (place[0], 0)),
-                pl.BlockSpec((half, F), lambda t, place: (0, 0)),
-                pl.BlockSpec((half, F), lambda t, place: (0, 0)),
-                pl.BlockSpec((half, F), lambda t, place: (0, 0)),
-                pl.BlockSpec((half, F), lambda t, place: (0, 0)),
-                pl.BlockSpec((1, F), lambda t, place: (0, 0)),
-                pl.BlockSpec((F, F), lambda t, place: (0, 0)),
-                pl.BlockSpec((F, F), lambda t, place: (0, 0)),
-            ],
-            out_specs=pl.BlockSpec((half, F), lambda t, place: (0, 0)),
-        ),
+        out_shape=jax.ShapeDtypeStruct((TILE // 2, F), jnp.bfloat16),
+        in_specs=[pl.BlockSpec(memory_space=pltpu.SMEM)]
+        + [pl.BlockSpec(memory_space=pltpu.VMEM)] * 7,
+        out_specs=pl.BlockSpec(memory_space=pltpu.VMEM),
         compiler_params=pltpu.CompilerParams(vmem_limit_bytes=8 << 20),
         name="update",
-    )(place, features, own, *others, gain, w_in, w_out)
+    )(place, features, owns, others, far, gain, w_in, w_out)
 
 
 def exchange(pieces, groups):
@@ -485,13 +494,12 @@
     near = lax.ppermute(near, AXES, LINE_SAME)
     filtered = exchange(filtered, GROUPS_XY).reshape(ALL_ROWS, F)
     tables = message_tables(place, jnp.asarray(ALL_STEPS), coords, near)
-    quarter = functools.partial(message_quarter, place, tables, filtered)
-    others = []
-    for far, own, pairs in ((True, True, LINE_SAME), (True, False, LINE_CROSS), (False, False, SWAP)):
-        part = quarter(far, own)
-        others.append(lax.ppermute(part, AXES, pairs))
-    own = quarter(False, True)
-    return update(place, features, own, others, norm_gain.reshape(1, F), w_in, w_out)
+    others = message_halves(place, tables, filtered, False)
+    others = lax.ppermute(others, AXES, SWAP)
+    owns = message_halves(place, tables, filtered, True)
+    far = (owns[1] + others[1].astype(jnp.float32)).astype(jnp.bfloat16)
+    far = lax.ppermute(far, AXES, LINE_SAME)
+    return update(place, features, owns, others, far, norm_gain.reshape(1, F), w_in, w_out)
 
 
 def solution(mesh):

time: 90 us -> 89.8 us (level)
  waiting for transfers between devices: 10.7 us -> 14.3 us
  starting transfers between devices: 60.2 us -> 58 us
  Pallas kernels: 17.6 us -> 16.5 us
    ppermute x3 -> x2, waiting for transfers between devices: 0.06 us -> 3.58 us  [the longest x1 3.49 us: layer(): far = lax.ppermute(far, AXES, LINE_SAME)]
    ppermute x3 -> x2, starting transfers between devices: 9.92 us -> 7.73 us  [the longest x1 4.19 us: layer(): far = lax.ppermute(far, AXES, LINE_SAME)]
    pallas_call x5 -> x3, Pallas kernels: 5.2 us -> 3.72 us  [the longest x2 2.09 us: message_halves(): pl.pallas_call(functools.partial(message_kernel, own=own), out_shape=jax....]
  transfers between devices with their start and end apart: 10 -> 9, of which waited for: 7 -> 8; matrix products, arithmetic and copies ran while one was open for 0% -> 0% of each run, Pallas kernels for 6% -> 6%
where the time goes in v10:
time: 89.8 us; the launch traced here: 89.2 us
  starting transfers between devices  58 us (65%)
  Pallas kernels  16.5 us (18%)
  waiting for transfers between devices  14.3 us (16%)
    all_to_all x3, starting transfers between devices, exchange(): lax.all_to_all(pieces, AXES, split_axis=0, concat_axis=0, tiled=True, axi...  18.6 us
    ppermute x1, starting transfers between devices, layer(): weights += lax.ppermute(weights, AXES, OUTER_PAIRS)  12.5 us
    ppermute x1, starting transfers between devices, layer(): far_weights = lax.ppermute(weights, AXES, INNER_PAIRS)  8.94 us
    pallas_call x1, Pallas kernels, partial_factors(): pl.pallas_call(factors_kernel, out_shape=jax.ShapeDtypeStruct((PLANES, CO...  6.63 us
    ppermute x1, starting transfers between devices, layer(): swapped = lax.ppermute(weights[POINTS:], AXES, SWAP)  6.05 us
    all_to_all x3, waiting for transfers between devices, exchange(): lax.all_to_all(pieces, AXES, split_axis=0, concat_axis=0, tiled=True, axi...  5.57 us
    ppermute x1, starting transfers between devices, layer(): far = lax.ppermute(far, AXES, LINE_SAME)  4.19 us
    ppermute x1, starting transfers between devices, layer(): near = lax.ppermute(near, AXES, LINE_SAME)  4.15 us
  transfers between devices with their start and end apart: 9, of which 8 were waited for; matrix products, arithmetic and copies ran while one was open for 0% of the time, Pallas kernels for 6%

profile of v10, /device:TPU:1, one launch (start us, length us, event | category | flops | bytes accessed | tf_op | source)
XLA Modules:
  0.0 89.2 jit_solution(335979188936049876)
XLA Ops:
  0.0 6.6 %factors.1 = bf16[16,160,256]{2,1,0:T(8,128)(2,1)} custom-call(f32[2,8,232]{2,1,0:T(8,128)} %constant.56.clone.steps_ref, s32[3,2048]{1,0:T(4,128)} %own_ref, bf16[2048,256]{1,0:T(8,128)(2,1)} %features_ref.3), custom_call_target="tpu_custom_call" | custom-call | flops 2684354560 | bytes 1048576 | tf_op jit(solution)/shard_map/factors/pallas_call | solution.py:244
  6.6 0.0 copy-start.1
  6.7 0.0 copy-start.6
  6.7 7.7 %all-to-all-start = ((bf16[16,160,256]{2,1,0:T(8,128)(2,1)}), bf16[16,160,256]{2,1,0:T(8,128)(2,1)S(1)}, u32[]{:S(2)}, u32[]{:S(2)}) async-start(bf16[16,160,256]{2,1,0:T(8,128)(2,1)} %factors.1), calls=%async_computation | async-start | bytes 2621440 | tf_op jit(solution)/shard_map/all_to_all | solution.py:467
  14.4 0.0 copy-done.1
  14.4 0.0 copy-done.6
  14.4 0.3 grid_weights.1
  14.7 12.5 %collective-permute-start = (bf16[80,256]{1,0:T(8,128)(2,1)S(1)}, bf16[80,256]{1,0:T(8,128)(2,1)S(1)}, u32[]{:S(2)}, u32[]{:S(2)}) collective-permute-start(bf16[80,256]{1,0:T(8,128)(2,1)S(1)} %grid_weights.1), channel_id=1, source_target_pairs={{0,6},{1,7},{2,4},{3,5},{4,2},{5,3},{6,0},{7,1},{8,14},{9,15},{10,... | collective-permute-start | bytes 122888 | tf_op jit(solution)/shard_map/ppermute | solution.py:484
  27.2 1.7 %collective-permute-done = bf16[80,256]{1,0:T(8,128)(2,1)S(1)} collective-permute-done((bf16[80,256]{1,0:T(8,128)(2,1)S(1)}, bf16[80,256]{1,0:T(8,128)(2,1)S(1)}, u32[]{:S(2)}, u32[]{:S(2)}) %collective-permute-start) | collective-permute-done | bytes 40992 | tf_op jit(solution)/shard_map/ppermute | solution.py:484
  28.9 2.8 %all-to-all-done.arrived_ref = bf16[16,160,256]{2,1,0:T(8,128)(2,1)S(1)} async-done(((bf16[16,160,256]{2,1,0:T(8,128)(2,1)}), bf16[16,160,256]{2,1,0:T(8,128)(2,1)S(1)}, u32[]{:S(2)}, u32[]{:S(2)}) %all-to-all-start) | async-done | bytes 1310752 | tf_op jit(solution)/shard_map/all_to_all | solution.py:467
  31.6 0.8 plane_sum.1
  32.5 7.3 %all-to-all-start.1 = ((bf16[4,80,256]{2,1,0:T(8,128)(2,1)}), bf16[4,80,256]{2,1,0:T(8,128)(2,1)S(1)}, u32[]{:S(2)}, u32[]{:S(2)}) async-start(bf16[4,80,256]{2,1,0:T(8,128)(2,1)} %plane_sum.1), calls=%async_computation.1 | async-start | bytes 327680 | tf_op jit(solution)/shard_map/all_to_all | solution.py:467
  39.8 0.0 copy-start.5
  39.8 0.0 copy-start.2
  39.8 8.9 %collective-permute-start.1 = (bf16[80,256]{1,0:T(8,128)(2,1)S(1)}, bf16[80,256]{1,0:T(8,128)(2,1)S(1)}, u32[]{:S(2)}, u32[]{:S(2)}) collective-permute-start(bf16[80,256]{1,0:T(8,128)(2,1)S(1)} %add.28), channel_id=1, source_target_pairs={{0,2},{1,3},{2,0},{3,1},{4,6},{5,7},{6,4},{7,5},{8,10},{9,11},{10,... | collective-permute-start | bytes 122888 | tf_op jit(solution)/shard_map/ppermute | solution.py:485
  48.8 1.4 %collective-permute-done.1 = bf16[80,256]{1,0:T(8,128)(2,1)S(1)} collective-permute-done((bf16[80,256]{1,0:T(8,128)(2,1)S(1)}, bf16[80,256]{1,0:T(8,128)(2,1)S(1)}, u32[]{:S(2)}, u32[]{:S(2)}) %collective-permute-start.1) | collective-permute-done | bytes 40992 | tf_op jit(solution)/shard_map/ppermute | solution.py:485
  50.2 6.0 %collective-permute-start.2 = (bf16[40,256]{1,0:T(8,128)(2,1)S(1)}, bf16[40,256]{1,0:T(8,128)(2,1)S(1)}, u32[]{:S(2)}, u32[]{:S(2)}) collective-permute-start(bf16[40,256]{1,0:T(8,128)(2,1)S(1)} %get-tuple-element.19), channel_id=1, source_target_pairs={{0,1},{1,0},{2,3},{3,2},{4,5},{5,4},{6,7},{7,6},{8,9},{9,8},{10,11... | collective-permute-start | bytes 61448 | tf_op jit(solution)/shard_map/ppermute | solution.py:490
  56.2 0.8 collective-permute-done.2.far_ref
  57.0 0.0 all-to-all-done.1.arrived_ref
  57.0 1.0 %filter_column.1 = bf16[16,80,256]{2,1,0:T(8,128)(2,1)} custom-call(bf16[4,80,256]{2,1,0:T(8,128)(2,1)S(1)} %all-to-all-done.1.arrived_ref, bf16[40,256]{1,0:T(8,128)(2,1)S(1)} %get-tuple-element.20.near_ref, bf16[40,256]{1,0:T(8,128)(2,1)S(1)} %collective-permute-done.2.far_ref), custom_call_target="tpu_custom_call" | custom-call | tf_op jit(solution)/shard_map/filter_column/pallas_call | solution.py:355
  58.1 3.6 %all-to-all-start.2 = ((bf16[16,80,256]{2,1,0:T(8,128)(2,1)}), bf16[16,80,256]{2,1,0:T(8,128)(2,1)S(1)}, u32[]{:S(2)}, u32[]{:S(2)}) async-start(bf16[16,80,256]{2,1,0:T(8,128)(2,1)} %filter_column.1), calls=%async_computation.2 | async-start | bytes 1310720 | tf_op jit(solution)/shard_map/all_to_all | solution.py:467
  61.7 0.0 copy-done.5
  61.7 4.2 %collective-permute-start.3 = (s32[3,512]{1,0:T(4,128)S(1)}, s32[3,512]{1,0:T(4,128)S(1)}, u32[]{:S(2)}, u32[]{:S(2)}) collective-permute-start(s32[3,512]{1,0:T(4,128)S(1)} %constant_dynamic-slice_fusion), channel_id=1, source_target_pairs={{0,32},{1,33},{2,34},{3,35},{4,36},{5,37},{6,38},{7,39},{8,40},{9,... | collective-permute-start | bytes 18440 | tf_op jit(solution)/shard_map/ppermute | solution.py:494
  65.9 0.1 pad_add_fusion.place_ref
  66.0 1.2 %collective-permute-done.3.near_ref = s32[3,512]{1,0:T(4,128)S(1)} collective-permute-done((s32[3,512]{1,0:T(4,128)S(1)}, s32[3,512]{1,0:T(4,128)S(1)}, u32[]{:S(2)}, u32[]{:S(2)}) %collective-permute-start.3) | collective-permute-done | bytes 6176 | tf_op jit(solution)/shard_map/ppermute | solution.py:494
  67.2 0.0 copy-done.2
  67.2 4.0 %message_tables.1.tables_ref = bf16[1024,1280]{1,0:T(8,128)(2,1)S(1)} custom-call(s32[4]{0:T(128)S(1)} %pad_add_fusion.place_ref, f32[4,8,1280]{2,1,0:T(8,128)S(1)} %copy-done.2, s32[3,2048]{1,0:T(4,128)S(1)} %copy-done.5, s32[3,512]{1,0:T(4,128)S(1)} %collective-permute-done.3.near_ref), custom_call_target="tpu_custom_call" | custom-call | flops 20971520 | bytes 2621440 | tf_op jit(solution)/shard_map/message_tables/pallas_call | solution.py:381
  71.2 2.8 %all-to-all-done.2 = bf16[16,80,256]{2,1,0:T(8,128)(2,1)S(1)} async-done(((bf16[16,80,256]{2,1,0:T(8,128)(2,1)}), bf16[16,80,256]{2,1,0:T(8,128)(2,1)S(1)}, u32[]{:S(2)}, u32[]{:S(2)}) %all-to-all-start.2) | async-done | bytes 655392 | tf_op jit(solution)/shard_map/all_to_all | solution.py:467
  74.0 1.0 %message_other.1 = bf16[2,256,256]{2,1,0:T(8,128)(2,1)S(1)} custom-call(s32[4]{0:T(128)S(1)} %pad_add_fusion.place_ref, bf16[1024,1280]{1,0:T(8,128)(2,1)S(1)} %message_tables.1.tables_ref, bf16[1280,256]{1,0:T(8,128)(2,1)S(1)} %bitcast.8), custom_call_target="tpu_custom_call" | custom-call | flops 335544320 | bytes 2621440 | tf_op jit(solution)/shard_map/message_other/pallas_call | solution.py:416
  75.1 0.0 copy-start
  75.1 0.0 copy-start.3
  75.1 0.0 copy-start.4
  75.1 0.0 copy-start.7
  75.1 3.5 %collective-permute-start.4 = (bf16[2,256,256]{2,1,0:T(8,128)(2,1)S(1)}, bf16[2,256,256]{2,1,0:T(8,128)(2,1)S(1)}, u32[]{:S(2)}, u32[]{:S(2)}) collective-permute-start(bf16[2,256,256]{2,1,0:T(8,128)(2,1)S(1)} %message_other.1), channel_id=1, source_target_pairs={{0,1},{1,0},{2,3},{3,2},{4,5},{5,4},{6,7},{7,6},{8,9},{9,8},{10,11... | collective-permute-start | bytes 786440 | tf_op jit(solution)/shard_map/ppermute | solution.py:498
  78.7 1.0 %message_own.1.owns_ref = f32[2,256,256]{2,1,0:T(8,128)S(1)} custom-call(s32[4]{0:T(128)S(1)} %pad_add_fusion.place_ref, bf16[1024,1280]{1,0:T(8,128)(2,1)S(1)} %message_tables.1.tables_ref, bf16[1280,256]{1,0:T(8,128)(2,1)S(1)} %bitcast.9), custom_call_target="tpu_custom_call" | custom-call | flops 335544320 | bytes 2621440 | tf_op jit(solution)/shard_map/message_own/pallas_call | solution.py:416
  79.7 0.1 collective-permute-done.4.others_ref
  79.8 4.2 %collective-permute-start.5 = (bf16[256,256]{1,0:T(8,128)(2,1)S(1)}, bf16[256,256]{1,0:T(8,128)(2,1)S(1)}, u32[]{:S(2)}, u32[]{:S(2)}) collective-permute-start(bf16[256,256]{1,0:T(8,128)(2,1)S(1)} %fusion.1), channel_id=1, source_target_pairs={{0,32},{1,33},{2,34},{3,35},{4,36},{5,37},{6,38},{7,39},{8,40},{9,... | collective-permute-start | bytes 393224 | tf_op jit(solution)/shard_map/ppermute | solution.py:501
  84.0 3.5 %collective-permute-done.5.far_ref = bf16[256,256]{1,0:T(8,128)(2,1)S(1)} collective-permute-done((bf16[256,256]{1,0:T(8,128)(2,1)S(1)}, bf16[256,256]{1,0:T(8,128)(2,1)S(1)}, u32[]{:S(2)}, u32[]{:S(2)}) %collective-permute-start.5) | collective-permute-done | bytes 131104 | tf_op jit(solution)/shard_map/ppermute | solution.py:501
  87.5 0.0 copy-done
  87.5 0.0 copy-done.3
  87.5 0.0 copy-done.4
  87.5 0.0 copy-done.7
  87.6 1.6 %update.1 = bf16[256,256]{1,0:T(8,128)(2,1)} custom-call(s32[4]{0:T(128)S(1)} %pad_add_fusion.place_ref, bf16[2048,256]{1,0:T(8,128)(2,1)S(1)} %copy-done, f32[2,256,256]{2,1,0:T(8,128)S(1)} %message_own.1.owns_ref, bf16[2,256,256]{2,1,0:T(8,128)(2,1)S(1)} %collective-permute-done.4.others_ref, bf16[256,256]{1,0:T(8,128)(2,1)S(1)} %collective-permute-done.5.far_ref, ...), custom_call_target="tpu_custom_call" | custom-call | tf_op jit(solution)/shard_map/update/pallas_call | solution.py:455
  (5 shorter events, 0.1 us)
Async XLA Ops:
  6.6 7.8 %copy-start.1 = (f32[512,256]{1,0:T(8,128)S(1)}, f32[512,256]{1,0:T(8,128)}, u32[]{:S(2)}) copy-start(f32[512,256]{1,0:T(8,128)} %weights_ref.1) | copy-start | bytes 1572868
  6.7 7.8 %copy-start.6 = (s32[3,512]{1,0:T(4,128)S(1)}, s32[3,512]{1,0:T(4,128)}, u32[]{:S(2)}) copy-start(s32[3,512]{1,0:T(4,128)} %miller_ref) | copy-start | bytes 18436
  6.7 25.0 %all-to-all-start = ((bf16[16,160,256]{2,1,0:T(8,128)(2,1)}), bf16[16,160,256]{2,1,0:T(8,128)(2,1)S(1)}, u32[]{:S(2)}, u32[]{:S(2)}) async-start(bf16[16,160,256]{2,1,0:T(8,128)(2,1)} %factors.1), calls=%async_computation | async-start | bytes 2621440 | tf_op jit(solution)/shard_map/all_to_all | solution.py:467
  14.7 14.1 %collective-permute-start = (bf16[80,256]{1,0:T(8,128)(2,1)S(1)}, bf16[80,256]{1,0:T(8,128)(2,1)S(1)}, u32[]{:S(2)}, u32[]{:S(2)}) collective-permute-start(bf16[80,256]{1,0:T(8,128)(2,1)S(1)} %grid_weights.1), channel_id=1, source_target_pairs={{0,6},{1,7},{2,4},{3,5},{4,2},{5,3},{6,0},{7,1},{8,14},{9,15},{10,... | collective-permute-start | bytes 122888 | tf_op jit(solution)/shard_map/ppermute | solution.py:484
  32.5 24.6 %all-to-all-start.1 = ((bf16[4,80,256]{2,1,0:T(8,128)(2,1)}), bf16[4,80,256]{2,1,0:T(8,128)(2,1)S(1)}, u32[]{:S(2)}, u32[]{:S(2)}) async-start(bf16[4,80,256]{2,1,0:T(8,128)(2,1)} %plane_sum.1), calls=%async_computation.1 | async-start | bytes 327680 | tf_op jit(solution)/shard_map/all_to_all | solution.py:467
  39.8 21.9 %copy-start.5 = (s32[3,2048]{1,0:T(4,128)S(1)}, s32[3,2048]{1,0:T(4,128)}, u32[]{:S(2)}) copy-start(s32[3,2048]{1,0:T(4,128)} %own_ref) | copy-start | bytes 73732
  39.8 27.4 %copy-start.2 = (f32[4,8,1280]{2,1,0:T(8,128)S(1)}, f32[4,8,1280]{2,1,0:T(8,128)}, u32[]{:S(2)}) copy-start(f32[4,8,1280]{2,1,0:T(8,128)} %constant.57.clone.steps_ref) | copy-start | bytes 491524
  39.8 10.3 %collective-permute-start.1 = (bf16[80,256]{1,0:T(8,128)(2,1)S(1)}, bf16[80,256]{1,0:T(8,128)(2,1)S(1)}, u32[]{:S(2)}, u32[]{:S(2)}) collective-permute-start(bf16[80,256]{1,0:T(8,128)(2,1)S(1)} %add.28), channel_id=1, source_target_pairs={{0,2},{1,3},{2,0},{3,1},{4,6},{5,7},{6,4},{7,5},{8,10},{9,11},{10,... | collective-permute-start | bytes 122888 | tf_op jit(solution)/shard_map/ppermute | solution.py:485
  50.2 6.9 %collective-permute-start.2 = (bf16[40,256]{1,0:T(8,128)(2,1)S(1)}, bf16[40,256]{1,0:T(8,128)(2,1)S(1)}, u32[]{:S(2)}, u32[]{:S(2)}) collective-permute-start(bf16[40,256]{1,0:T(8,128)(2,1)S(1)} %get-tuple-element.19), channel_id=1, source_target_pairs={{0,1},{1,0},{2,3},{3,2},{4,5},{5,4},{6,7},{7,6},{8,9},{9,8},{10,11... | collective-permute-start | bytes 61448 | tf_op jit(solution)/shard_map/ppermute | solution.py:490
  58.1 16.0 %all-to-all-start.2 = ((bf16[16,80,256]{2,1,0:T(8,128)(2,1)}), bf16[16,80,256]{2,1,0:T(8,128)(2,1)S(1)}, u32[]{:S(2)}, u32[]{:S(2)}) async-start(bf16[16,80,256]{2,1,0:T(8,128)(2,1)} %filter_column.1), calls=%async_computation.2 | async-start | bytes 1310720 | tf_op jit(solution)/shard_map/all_to_all | solution.py:467
  61.7 5.5 %collective-permute-start.3 = (s32[3,512]{1,0:T(4,128)S(1)}, s32[3,512]{1,0:T(4,128)S(1)}, u32[]{:S(2)}, u32[]{:S(2)}) collective-permute-start(s32[3,512]{1,0:T(4,128)S(1)} %constant_dynamic-slice_fusion), channel_id=1, source_target_pairs={{0,32},{1,33},{2,34},{3,35},{4,36},{5,37},{6,38},{7,39},{8,40},{9,... | collective-permute-start | bytes 18440 | tf_op jit(solution)/shard_map/ppermute | solution.py:494
  75.1 12.5 %copy-start = (bf16[2048,256]{1,0:T(8,128)(2,1)S(1)}, bf16[2048,256]{1,0:T(8,128)(2,1)}, u32[]{:S(2)}) copy-start(bf16[2048,256]{1,0:T(8,128)(2,1)} %features_ref.3) | copy-start | bytes 3145732
  75.1 12.4 %copy-start.3 = (bf16[256,256]{1,0:T(8,128)(2,1)S(1)}, bf16[256,256]{1,0:T(8,128)(2,1)}, u32[]{:S(2)}) copy-start(bf16[256,256]{1,0:T(8,128)(2,1)} %w_in_ref.1) | copy-start | bytes 393220
  75.1 12.4 %copy-start.4 = (bf16[256,256]{1,0:T(8,128)(2,1)S(1)}, bf16[256,256]{1,0:T(8,128)(2,1)}, u32[]{:S(2)}) copy-start(bf16[256,256]{1,0:T(8,128)(2,1)} %w_out_ref.1) | copy-start | bytes 393220
  75.1 12.4 %copy-start.7 = (f32[256]{0:T(256)S(1)}, f32[256]{0:T(256)}, u32[]{:S(2)}) copy-start(f32[256]{0:T(256)} %param.13) | copy-start | bytes 3076
  75.1 4.7 %collective-permute-start.4 = (bf16[2,256,256]{2,1,0:T(8,128)(2,1)S(1)}, bf16[2,256,256]{2,1,0:T(8,128)(2,1)S(1)}, u32[]{:S(2)}, u32[]{:S(2)}) collective-permute-start(bf16[2,256,256]{2,1,0:T(8,128)(2,1)S(1)} %message_other.1), channel_id=1, source_target_pairs={{0,1},{1,0},{2,3},{3,2},{4,5},{5,4},{6,7},{7,6},{8,9},{9,8},{10,11... | collective-permute-start | bytes 786440 | tf_op jit(solution)/shard_map/ppermute | solution.py:498
  79.8 7.7 %collective-permute-start.5 = (bf16[256,256]{1,0:T(8,128)(2,1)S(1)}, bf16[256,256]{1,0:T(8,128)(2,1)S(1)}, u32[]{:S(2)}, u32[]{:S(2)}) collective-permute-start(bf16[256,256]{1,0:T(8,128)(2,1)S(1)} %fusion.1), channel_id=1, source_target_pairs={{0,32},{1,33},{2,34},{3,35},{4,36},{5,37},{6,38},{7,39},{8,40},{9,... | collective-permute-start | bytes 393224 | tf_op jit(solution)/shard_map/ppermute | solution.py:501

commit v11 on v9

--- a/solution.py
+++ b/solution.py
@@ -382,45 +382,47 @@
     )(place, steps, coords, near)
 
 
-def message_kernel(place_ref, tables_ref, filtered_ref, out_ref, *, far, own):
+def message_kernel(tables_ref, filtered_ref, out_ref, *, own):
     half = TILE // 2
-    core = place_ref[1] if own else 1 - place_ref[1]
-    start = pl.multiple_of(core * half, half) + far * TILE
-    tables = tables_ref[pl.ds(start, half), :]
-    message = jnp.dot(tables, filtered_ref[...], preferred_element_type=jnp.float32)
-    out_ref[...] = message.astype(out_ref.dtype)
-
-
-def message_quarter(place, tables, filtered, far, own):
+    core = lax.axis_index("wave") % 2
+    core = core if own else 1 - core
+    start = pl.multiple_of(core * half, half)
+    filtered = filtered_ref[...]
+    for side in TWO:
+        tables = tables_ref[pl.ds(start + side * TILE, half), :]
+        message = jnp.dot(tables, filtered, preferred_element_type=jnp.float32)
+        out_ref[side] = message.astype(out_ref.dtype)
+
+
+def message_halves(tables, filtered, own):
     half = TILE // 2
-    kept = own and not far
-    return pl.pallas_call(
-        functools.partial(message_kernel, far=far, own=own),
-        out_shape=jax.ShapeDtypeStruct((half, F), jnp.float32 if kept else jnp.bfloat16),
-        in_specs=[
-            pl.BlockSpec(memory_space=pltpu.SMEM),
-            pl.BlockSpec(memory_space=pltpu.VMEM),
-            pl.BlockSpec(memory_space=pltpu.VMEM),
-        ],
+    dtype = jnp.float32 if own else jnp.bfloat16
+    return pl.pallas_call(
+        functools.partial(message_kernel, own=own),
+        out_shape=jax.ShapeDtypeStruct((2, half, F), dtype),
+        in_specs=[pl.BlockSpec(memory_space=pltpu.VMEM)] * 2,
         out_specs=pl.BlockSpec(memory_space=pltpu.VMEM),
         compiler_params=pltpu.CompilerParams(vmem_limit_bytes=16 << 20),
         cost_estimate=pl.CostEstimate(
-            flops=2 * half * ALL_ROWS * F, bytes_accessed=4 * half * ALL_ROWS, transcendentals=0
+            flops=4 * half * ALL_ROWS * F, bytes_accessed=8 * half * ALL_ROWS, transcendentals=0
         ),
-    )(place, tables, filtered)
+        name="message_own" if own else "message_other",
+    )(tables, filtered)
 
 
 def update_kernel(
-    place_ref, features_ref, own_ref, a_ref, b_ref, c_ref, gain_ref, w_in_ref, w_out_ref, out_ref
+    features_ref, owns_ref, others_ref, far_ref, gain_ref, w_in_ref, w_out_ref, out_ref
 ):
     gain, w_in, w_out = gain_ref[...], w_in_ref[...], w_out_ref[...]
-    chunk = own_ref.shape[0] // 4
-    for start in range(0, own_ref.shape[0], chunk):
+    half = TILE // 2
+    base = pl.multiple_of(lax.axis_index("wave") * half, half)
+    chunk = half // 2
+    for start in range(0, half, chunk):
         rows = pl.ds(start, chunk)
-        message = own_ref[rows, :]
-        for part_ref in (a_ref, b_ref, c_ref):
-            message += part_ref[rows, :].astype(jnp.float32)
-        updated = features_ref[rows, :].astype(jnp.float32) + message * (1.0 / math.sqrt(K))
+        message = owns_ref[0, rows, :] + others_ref[0, rows, :].astype(jnp.float32)
+        message += far_ref[rows, :].astype(jnp.float32)
+        features = features_ref[pl.ds(base + start, chunk), :].astype(jnp.float32)
+        updated = features + message * (1.0 / math.sqrt(K))
         power = jnp.mean(updated * updated, axis=1, keepdims=True)
         normed = (updated / jnp.sqrt(power + 1e-06) * gain).astype(jnp.bfloat16)
         hidden = jnp.dot(normed, w_in, preferred_element_type=jnp.float32)
@@ -429,29 +431,15 @@
         out_ref[rows, :] = (updated + added).astype(jnp.bfloat16)
 
 
-def update(place, features, own, others, gain, w_in, w_out):
-    half = TILE // 2
+def update(features, owns, others, far, gain, w_in, w_out):
     return pl.pallas_call(
         update_kernel,
-        out_shape=jax.ShapeDtypeStruct((half, F), jnp.bfloat16),
-        grid_spec=pltpu.PrefetchScalarGridSpec(
-            num_scalar_prefetch=1,
-            grid=(1,),
-            in_specs=[
-                pl.BlockSpec((half, F), lambda t, place: (place[0], 0)),
-                pl.BlockSpec((half, F), lambda t, place: (0, 0)),
-                pl.BlockSpec((half, F), lambda t, place: (0, 0)),
-                pl.BlockSpec((half, F), lambda t, place: (0, 0)),
-                pl.BlockSpec((half, F), lambda t, place: (0, 0)),
-                pl.BlockSpec((1, F), lambda t, place: (0, 0)),
-                pl.BlockSpec((F, F), lambda t, place: (0, 0)),
-                pl.BlockSpec((F, F), lambda t, place: (0, 0)),
-            ],
-            out_specs=pl.BlockSpec((half, F), lambda t, place: (0, 0)),
-        ),
+        out_shape=jax.ShapeDtypeStruct((TILE // 2, F), jnp.bfloat16),
+        in_specs=[pl.BlockSpec(memory_space=pltpu.VMEM)] * 7,
+        out_specs=pl.BlockSpec(memory_space=pltpu.VMEM),
         compiler_params=pltpu.CompilerParams(vmem_limit_bytes=8 << 20),
         name="update",
-    )(place, features, own, *others, gain, w_in, w_out)
+    )(features, owns, others, far, gain, w_in, w_out)
 
 
 def exchange(pieces, groups):
@@ -485,13 +473,12 @@
     near = lax.ppermute(near, AXES, LINE_SAME)
     filtered = exchange(filtered, GROUPS_XY).reshape(ALL_ROWS, F)
     tables = message_tables(place, jnp.asarray(ALL_STEPS), coords, near)
-    quarter = functools.partial(message_quarter, place, tables, filtered)
-    others = []
-    for far, own, pairs in ((True, True, LINE_SAME), (True, False, LINE_CROSS), (False, False, SWAP)):
-        part = quarter(far, own)
-        others.append(lax.ppermute(part, AXES, pairs))
-    own = quarter(False, True)
-    return update(place, features, own, others, norm_gain.reshape(1, F), w_in, w_out)
+    others = message_halves(tables, filtered, False)
+    others = lax.ppermute(others, AXES, SWAP)
+    owns = message_halves(tables, filtered, True)
+    far = (owns[1] + others[1].astype(jnp.float32)).astype(jnp.bfloat16)
+    far = lax.ppermute(far, AXES, LINE_SAME)
+    return update(features, owns, others, far, norm_gain.reshape(1, F), w_in, w_out)
 
 
 def solution(mesh):

time: 90 us -> 88.3 us (0.981)
  waiting for transfers between devices: 10.7 us -> 14.8 us
  Pallas kernels: 17.6 us -> 14.5 us
  starting transfers between devices: 60.2 us -> 58 us
    ppermute x3 -> x2, waiting for transfers between devices: 0.06 us -> 4.12 us  [the longest x1 3.49 us: layer(): far = lax.ppermute(far, AXES, LINE_SAME)]
    pallas_call x5 -> x3, Pallas kernels: 5.2 us -> 2.09 us  [the longest x1 1.1 us: update(): pl.pallas_call(update_kernel, out_shape=jax.ShapeDtypeStruct((TILE // 2,...]
    ppermute x3 -> x2, starting transfers between devices: 9.92 us -> 7.72 us  [the longest x1 4.19 us: layer(): far = lax.ppermute(far, AXES, LINE_SAME)]
  transfers between devices with their start and end apart: 10 -> 9, of which waited for: 7 -> 8; matrix products, arithmetic and copies ran while one was open for 0% -> 0% of each run, Pallas kernels for 6% -> 5%
where the time goes in v11:
time: 88.3 us; the launch traced here: 87.7 us
  starting transfers between devices  58 us (66%)
  waiting for transfers between devices  14.8 us (17%)
  Pallas kernels  14.5 us (16%)
    all_to_all x3, starting transfers between devices, exchange(): lax.all_to_all(pieces, AXES, split_axis=0, concat_axis=0, tiled=True, axi...  18.6 us
    ppermute x1, starting transfers between devices, layer(): weights += lax.ppermute(weights, AXES, OUTER_PAIRS)  12.5 us
    ppermute x1, starting transfers between devices, layer(): far_weights = lax.ppermute(weights, AXES, INNER_PAIRS)  8.97 us
    pallas_call x1, Pallas kernels, partial_factors(): pl.pallas_call(factors_kernel, out_shape=jax.ShapeDtypeStruct((PLANES, CO...  6.22 us
    ppermute x1, starting transfers between devices, layer(): swapped = lax.ppermute(weights[POINTS:], AXES, SWAP)  6.05 us
    all_to_all x3, waiting for transfers between devices, exchange(): lax.all_to_all(pieces, AXES, split_axis=0, concat_axis=0, tiled=True, axi...  5.57 us
    ppermute x1, starting transfers between devices, layer(): far = lax.ppermute(far, AXES, LINE_SAME)  4.19 us
    ppermute x1, starting transfers between devices, layer(): near = lax.ppermute(near, AXES, LINE_SAME)  4.15 us
  transfers between devices with their start and end apart: 9, of which 8 were waited for; matrix products, arithmetic and copies ran while one was open for 0% of the time, Pallas kernels for 5%

profile of v11, /device:TPU:1, one launch (start us, length us, event | category | flops | bytes accessed | tf_op | source)
XLA Modules:
  0.0 87.7 jit_solution(15957299249326325813)
XLA Ops:
  0.0 6.2 %factors.1 = bf16[16,160,256]{2,1,0:T(8,128)(2,1)} custom-call(f32[2,8,232]{2,1,0:T(8,128)} %constant.56.clone.steps_ref, s32[3,2048]{1,0:T(4,128)} %own_ref, bf16[2048,256]{1,0:T(8,128)(2,1)} %features_ref.3), custom_call_target="tpu_custom_call" | custom-call | flops 2684354560 | bytes 1048576 | tf_op jit(solution)/shard_map/factors/pallas_call | solution.py:228
  6.2 0.0 copy-start.1
  6.2 0.0 copy-start.6
  6.3 7.7 %all-to-all-start = ((bf16[16,160,256]{2,1,0:T(8,128)(2,1)}), bf16[16,160,256]{2,1,0:T(8,128)(2,1)S(1)}, u32[]{:S(2)}, u32[]{:S(2)}) async-start(bf16[16,160,256]{2,1,0:T(8,128)(2,1)} %factors.1), calls=%async_computation | async-start | bytes 2621440 | tf_op jit(solution)/shard_map/all_to_all | solution.py:446
  14.0 0.0 copy-done.1
  14.0 0.0 copy-done.6
  14.0 0.3 grid_weights.1
  14.3 12.5 %collective-permute-start = (bf16[80,256]{1,0:T(8,128)(2,1)S(1)}, bf16[80,256]{1,0:T(8,128)(2,1)S(1)}, u32[]{:S(2)}, u32[]{:S(2)}) collective-permute-start(bf16[80,256]{1,0:T(8,128)(2,1)S(1)} %grid_weights.1), channel_id=1, source_target_pairs={{0,6},{1,7},{2,4},{3,5},{4,2},{5,3},{6,0},{7,1},{8,14},{9,15},{10,... | collective-permute-start | bytes 122888 | tf_op jit(solution)/shard_map/ppermute | solution.py:463
  26.8 1.7 %collective-permute-done = bf16[80,256]{1,0:T(8,128)(2,1)S(1)} collective-permute-done((bf16[80,256]{1,0:T(8,128)(2,1)S(1)}, bf16[80,256]{1,0:T(8,128)(2,1)S(1)}, u32[]{:S(2)}, u32[]{:S(2)}) %collective-permute-start) | collective-permute-done | bytes 40992 | tf_op jit(solution)/shard_map/ppermute | solution.py:463
  28.5 2.8 %all-to-all-done.arrived_ref = bf16[16,160,256]{2,1,0:T(8,128)(2,1)S(1)} async-done(((bf16[16,160,256]{2,1,0:T(8,128)(2,1)}), bf16[16,160,256]{2,1,0:T(8,128)(2,1)S(1)}, u32[]{:S(2)}, u32[]{:S(2)}) %all-to-all-start) | async-done | bytes 1310752 | tf_op jit(solution)/shard_map/all_to_all | solution.py:446
  31.2 0.8 plane_sum.1
  32.1 7.3 %all-to-all-start.1 = ((bf16[4,80,256]{2,1,0:T(8,128)(2,1)}), bf16[4,80,256]{2,1,0:T(8,128)(2,1)S(1)}, u32[]{:S(2)}, u32[]{:S(2)}) async-start(bf16[4,80,256]{2,1,0:T(8,128)(2,1)} %plane_sum.1), calls=%async_computation.1 | async-start | bytes 327680 | tf_op jit(solution)/shard_map/all_to_all | solution.py:446
  39.4 0.0 copy-start.5
  39.4 0.0 copy-start.2
  39.4 9.0 %collective-permute-start.1 = (bf16[80,256]{1,0:T(8,128)(2,1)S(1)}, bf16[80,256]{1,0:T(8,128)(2,1)S(1)}, u32[]{:S(2)}, u32[]{:S(2)}) collective-permute-start(bf16[80,256]{1,0:T(8,128)(2,1)S(1)} %add.28), channel_id=1, source_target_pairs={{0,2},{1,3},{2,0},{3,1},{4,6},{5,7},{6,4},{7,5},{8,10},{9,11},{10,... | collective-permute-start | bytes 122888 | tf_op jit(solution)/shard_map/ppermute | solution.py:464
  48.4 1.4 %collective-permute-done.1 = bf16[80,256]{1,0:T(8,128)(2,1)S(1)} collective-permute-done((bf16[80,256]{1,0:T(8,128)(2,1)S(1)}, bf16[80,256]{1,0:T(8,128)(2,1)S(1)}, u32[]{:S(2)}, u32[]{:S(2)}) %collective-permute-start.1) | collective-permute-done | bytes 40992 | tf_op jit(solution)/shard_map/ppermute | solution.py:464
  49.8 6.0 %collective-permute-start.2 = (bf16[40,256]{1,0:T(8,128)(2,1)S(1)}, bf16[40,256]{1,0:T(8,128)(2,1)S(1)}, u32[]{:S(2)}, u32[]{:S(2)}) collective-permute-start(bf16[40,256]{1,0:T(8,128)(2,1)S(1)} %get-tuple-element.19), channel_id=1, source_target_pairs={{0,1},{1,0},{2,3},{3,2},{4,5},{5,4},{6,7},{7,6},{8,9},{9,8},{10,11... | collective-permute-start | bytes 61448 | tf_op jit(solution)/shard_map/ppermute | solution.py:469
  55.8 0.8 collective-permute-done.2.far_ref
  56.6 0.0 all-to-all-done.1.arrived_ref
  56.6 1.0 %filter_column.1 = bf16[16,80,256]{2,1,0:T(8,128)(2,1)} custom-call(bf16[4,80,256]{2,1,0:T(8,128)(2,1)S(1)} %all-to-all-done.1.arrived_ref, bf16[40,256]{1,0:T(8,128)(2,1)S(1)} %get-tuple-element.20.near_ref, bf16[40,256]{1,0:T(8,128)(2,1)S(1)} %collective-permute-done.2.far_ref), custom_call_target="tpu_custom_call" | custom-call | tf_op jit(solution)/shard_map/filter_column/pallas_call | solution.py:338
  57.7 3.6 %all-to-all-start.2 = ((bf16[16,80,256]{2,1,0:T(8,128)(2,1)}), bf16[16,80,256]{2,1,0:T(8,128)(2,1)S(1)}, u32[]{:S(2)}, u32[]{:S(2)}) async-start(bf16[16,80,256]{2,1,0:T(8,128)(2,1)} %filter_column.1), calls=%async_computation.2 | async-start | bytes 1310720 | tf_op jit(solution)/shard_map/all_to_all | solution.py:446
  61.3 0.0 copy-done.5
  61.4 4.1 %collective-permute-start.3 = (s32[3,512]{1,0:T(4,128)S(1)}, s32[3,512]{1,0:T(4,128)S(1)}, u32[]{:S(2)}, u32[]{:S(2)}) collective-permute-start(s32[3,512]{1,0:T(4,128)S(1)} %constant_dynamic-slice_fusion), channel_id=1, source_target_pairs={{0,32},{1,33},{2,34},{3,35},{4,36},{5,37},{6,38},{7,39},{8,40},{9,... | collective-permute-start | bytes 18440 | tf_op jit(solution)/shard_map/ppermute | solution.py:473
  65.5 0.1 pad_add_fusion.place_ref
  65.6 1.2 %collective-permute-done.3.near_ref = s32[3,512]{1,0:T(4,128)S(1)} collective-permute-done((s32[3,512]{1,0:T(4,128)S(1)}, s32[3,512]{1,0:T(4,128)S(1)}, u32[]{:S(2)}, u32[]{:S(2)}) %collective-permute-start.3) | collective-permute-done | bytes 6176 | tf_op jit(solution)/shard_map/ppermute | solution.py:473
  66.8 0.0 copy-done.2
  66.8 4.0 %message_tables.1.tables_ref = bf16[1024,1280]{1,0:T(8,128)(2,1)S(1)} custom-call(s32[4]{0:T(128)S(1)} %pad_add_fusion.place_ref, f32[4,8,1280]{2,1,0:T(8,128)S(1)} %copy-done.2, s32[3,2048]{1,0:T(4,128)S(1)} %copy-done.5, s32[3,512]{1,0:T(4,128)S(1)} %collective-permute-done.3.near_ref), custom_call_target="tpu_custom_call" | custom-call | flops 20971520 | bytes 2621440 | tf_op jit(solution)/shard_map/message_tables/pallas_call | solution.py:364
  70.8 2.8 %all-to-all-done.2 = bf16[16,80,256]{2,1,0:T(8,128)(2,1)S(1)} async-done(((bf16[16,80,256]{2,1,0:T(8,128)(2,1)}), bf16[16,80,256]{2,1,0:T(8,128)(2,1)S(1)}, u32[]{:S(2)}, u32[]{:S(2)}) %all-to-all-start.2) | async-done | bytes 655392 | tf_op jit(solution)/shard_map/all_to_all | solution.py:446
  73.6 0.5 message_other.1
  74.1 0.0 copy-start
  74.2 0.0 copy-start.3
  74.2 0.0 copy-start.4
  74.2 0.0 copy-start.7
  74.2 3.5 %collective-permute-start.4 = (bf16[2,256,256]{2,1,0:T(8,128)(2,1)S(1)}, bf16[2,256,256]{2,1,0:T(8,128)(2,1)S(1)}, u32[]{:S(2)}, u32[]{:S(2)}) collective-permute-start(bf16[2,256,256]{2,1,0:T(8,128)(2,1)S(1)} %message_other.1), channel_id=1, source_target_pairs={{0,1},{1,0},{2,3},{3,2},{4,5},{5,4},{6,7},{7,6},{8,9},{9,8},{10,11... | collective-permute-start | bytes 786440 | tf_op jit(solution)/shard_map/ppermute | solution.py:477
  77.7 0.5 message_own.1.owns_ref
  78.2 0.6 collective-permute-done.4.others_ref
  78.9 4.2 %collective-permute-start.5 = (bf16[256,256]{1,0:T(8,128)(2,1)S(1)}, bf16[256,256]{1,0:T(8,128)(2,1)S(1)}, u32[]{:S(2)}, u32[]{:S(2)}) collective-permute-start(bf16[256,256]{1,0:T(8,128)(2,1)S(1)} %fusion.1), channel_id=1, source_target_pairs={{0,32},{1,33},{2,34},{3,35},{4,36},{5,37},{6,38},{7,39},{8,40},{9,... | collective-permute-start | bytes 393224 | tf_op jit(solution)/shard_map/ppermute | solution.py:480
  83.1 3.5 %collective-permute-done.5.far_ref = bf16[256,256]{1,0:T(8,128)(2,1)S(1)} collective-permute-done((bf16[256,256]{1,0:T(8,128)(2,1)S(1)}, bf16[256,256]{1,0:T(8,128)(2,1)S(1)}, u32[]{:S(2)}, u32[]{:S(2)}) %collective-permute-start.5) | collective-permute-done | bytes 131104 | tf_op jit(solution)/shard_map/ppermute | solution.py:480
  86.6 0.0 copy-done
  86.6 0.0 copy-done.3
  86.6 0.0 copy-done.4
  86.6 0.0 copy-done.7
  86.6 1.1 %update.1 = bf16[256,256]{1,0:T(8,128)(2,1)} custom-call(bf16[2048,256]{1,0:T(8,128)(2,1)S(1)} %copy-done, f32[2,256,256]{2,1,0:T(8,128)S(1)} %message_own.1.owns_ref, bf16[2,256,256]{2,1,0:T(8,128)(2,1)S(1)} %collective-permute-done.4.others_ref, bf16[256,256]{1,0:T(8,128)(2,1)S(1)} %collective-permute-done.5.far_ref, f32[1,256]{1,0:T(1,128)S(1)} %bitcast.10, ...), custom_call_target="tpu_custom_call" | custom-call | tf_op jit(solution)/shard_map/update/pallas_call | solution.py:435
  (5 shorter events, 0.1 us)
Async XLA Ops:
  6.2 7.8 %copy-start.1 = (f32[512,256]{1,0:T(8,128)S(1)}, f32[512,256]{1,0:T(8,128)}, u32[]{:S(2)}) copy-start(f32[512,256]{1,0:T(8,128)} %weights_ref.1) | copy-start | bytes 1572868
  6.2 7.8 %copy-start.6 = (s32[3,512]{1,0:T(4,128)S(1)}, s32[3,512]{1,0:T(4,128)}, u32[]{:S(2)}) copy-start(s32[3,512]{1,0:T(4,128)} %miller_ref) | copy-start | bytes 18436
  6.3 25.0 %all-to-all-start = ((bf16[16,160,256]{2,1,0:T(8,128)(2,1)}), bf16[16,160,256]{2,1,0:T(8,128)(2,1)S(1)}, u32[]{:S(2)}, u32[]{:S(2)}) async-start(bf16[16,160,256]{2,1,0:T(8,128)(2,1)} %factors.1), calls=%async_computation | async-start | bytes 2621440 | tf_op jit(solution)/shard_map/all_to_all | solution.py:446
  14.3 14.1 %collective-permute-start = (bf16[80,256]{1,0:T(8,128)(2,1)S(1)}, bf16[80,256]{1,0:T(8,128)(2,1)S(1)}, u32[]{:S(2)}, u32[]{:S(2)}) collective-permute-start(bf16[80,256]{1,0:T(8,128)(2,1)S(1)} %grid_weights.1), channel_id=1, source_target_pairs={{0,6},{1,7},{2,4},{3,5},{4,2},{5,3},{6,0},{7,1},{8,14},{9,15},{10,... | collective-permute-start | bytes 122888 | tf_op jit(solution)/shard_map/ppermute | solution.py:463
  32.1 24.6 %all-to-all-start.1 = ((bf16[4,80,256]{2,1,0:T(8,128)(2,1)}), bf16[4,80,256]{2,1,0:T(8,128)(2,1)S(1)}, u32[]{:S(2)}, u32[]{:S(2)}) async-start(bf16[4,80,256]{2,1,0:T(8,128)(2,1)} %plane_sum.1), calls=%async_computation.1 | async-start | bytes 327680 | tf_op jit(solution)/shard_map/all_to_all | solution.py:446
  39.4 21.9 %copy-start.5 = (s32[3,2048]{1,0:T(4,128)S(1)}, s32[3,2048]{1,0:T(4,128)}, u32[]{:S(2)}) copy-start(s32[3,2048]{1,0:T(4,128)} %own_ref) | copy-start | bytes 73732
  39.4 27.5 %copy-start.2 = (f32[4,8,1280]{2,1,0:T(8,128)S(1)}, f32[4,8,1280]{2,1,0:T(8,128)}, u32[]{:S(2)}) copy-start(f32[4,8,1280]{2,1,0:T(8,128)} %constant.57.clone.steps_ref) | copy-start | bytes 491524
  39.4 10.4 %collective-permute-start.1 = (bf16[80,256]{1,0:T(8,128)(2,1)S(1)}, bf16[80,256]{1,0:T(8,128)(2,1)S(1)}, u32[]{:S(2)}, u32[]{:S(2)}) collective-permute-start(bf16[80,256]{1,0:T(8,128)(2,1)S(1)} %add.28), channel_id=1, source_target_pairs={{0,2},{1,3},{2,0},{3,1},{4,6},{5,7},{6,4},{7,5},{8,10},{9,11},{10,... | collective-permute-start | bytes 122888 | tf_op jit(solution)/shard_map/ppermute | solution.py:464
  49.8 6.9 %collective-permute-start.2 = (bf16[40,256]{1,0:T(8,128)(2,1)S(1)}, bf16[40,256]{1,0:T(8,128)(2,1)S(1)}, u32[]{:S(2)}, u32[]{:S(2)}) collective-permute-start(bf16[40,256]{1,0:T(8,128)(2,1)S(1)} %get-tuple-element.19), channel_id=1, source_target_pairs={{0,1},{1,0},{2,3},{3,2},{4,5},{5,4},{6,7},{7,6},{8,9},{9,8},{10,11... | collective-permute-start | bytes 61448 | tf_op jit(solution)/shard_map/ppermute | solution.py:469
  57.7 16.0 %all-to-all-start.2 = ((bf16[16,80,256]{2,1,0:T(8,128)(2,1)}), bf16[16,80,256]{2,1,0:T(8,128)(2,1)S(1)}, u32[]{:S(2)}, u32[]{:S(2)}) async-start(bf16[16,80,256]{2,1,0:T(8,128)(2,1)} %filter_column.1), calls=%async_computation.2 | async-start | bytes 1310720 | tf_op jit(solution)/shard_map/all_to_all | solution.py:446
  61.4 5.5 %collective-permute-start.3 = (s32[3,512]{1,0:T(4,128)S(1)}, s32[3,512]{1,0:T(4,128)S(1)}, u32[]{:S(2)}, u32[]{:S(2)}) collective-permute-start(s32[3,512]{1,0:T(4,128)S(1)} %constant_dynamic-slice_fusion), channel_id=1, source_target_pairs={{0,32},{1,33},{2,34},{3,35},{4,36},{5,37},{6,38},{7,39},{8,40},{9,... | collective-permute-start | bytes 18440 | tf_op jit(solution)/shard_map/ppermute | solution.py:473
  74.1 12.4 %copy-start = (bf16[2048,256]{1,0:T(8,128)(2,1)S(1)}, bf16[2048,256]{1,0:T(8,128)(2,1)}, u32[]{:S(2)}) copy-start(bf16[2048,256]{1,0:T(8,128)(2,1)} %features_ref.3) | copy-start | bytes 3145732
  74.2 12.4 %copy-start.3 = (bf16[256,256]{1,0:T(8,128)(2,1)S(1)}, bf16[256,256]{1,0:T(8,128)(2,1)}, u32[]{:S(2)}) copy-start(bf16[256,256]{1,0:T(8,128)(2,1)} %w_in_ref.1) | copy-start | bytes 393220
  74.2 12.4 %copy-start.4 = (bf16[256,256]{1,0:T(8,128)(2,1)S(1)}, bf16[256,256]{1,0:T(8,128)(2,1)}, u32[]{:S(2)}) copy-start(bf16[256,256]{1,0:T(8,128)(2,1)} %w_out_ref.1) | copy-start | bytes 393220
  74.2 12.4 %copy-start.7 = (f32[256]{0:T(256)S(1)}, f32[256]{0:T(256)}, u32[]{:S(2)}) copy-start(f32[256]{0:T(256)} %param.13) | copy-start | bytes 3076
  74.2 4.7 %collective-permute-start.4 = (bf16[2,256,256]{2,1,0:T(8,128)(2,1)S(1)}, bf16[2,256,256]{2,1,0:T(8,128)(2,1)S(1)}, u32[]{:S(2)}, u32[]{:S(2)}) collective-permute-start(bf16[2,256,256]{2,1,0:T(8,128)(2,1)S(1)} %message_other.1), channel_id=1, source_target_pairs={{0,1},{1,0},{2,3},{3,2},{4,5},{5,4},{6,7},{7,6},{8,9},{9,8},{10,11... | collective-permute-start | bytes 786440 | tf_op jit(solution)/shard_map/ppermute | solution.py:477
  78.9 7.7 %collective-permute-start.5 = (bf16[256,256]{1,0:T(8,128)(2,1)S(1)}, bf16[256,256]{1,0:T(8,128)(2,1)S(1)}, u32[]{:S(2)}, u32[]{:S(2)}) collective-permute-start(bf16[256,256]{1,0:T(8,128)(2,1)S(1)} %fusion.1), channel_id=1, source_target_pairs={{0,32},{1,33},{2,34},{3,35},{4,36},{5,37},{6,38},{7,39},{8,40},{9,... | collective-permute-start | bytes 393224 | tf_op jit(solution)/shard_map/ppermute | solution.py:480

commit v12 on v11

--- a/solution.py
+++ b/solution.py
@@ -173,7 +173,7 @@
 
 
 def factors_kernel(
-    steps_ref, coords_ref, features_ref, out_ref, features, first, tables, copied
+    steps_ref, coords_ref, features_ref, out_ref, features, first, tables, made, copied, sent
 ):
     copy = pltpu.make_async_copy(features_ref, features, copied)
     copy.start()
@@ -184,7 +184,7 @@
         parts = split_coords(coords_ref[:, start : start + TILE])
         turns = lax.dot_general(steps, parts, OUTER, preferred_element_type=jnp.float32)
         first[:, start : start + TILE] = cosine_of_turns(turns)
-    mains = {}
+    mains, sends = {}, []
     for block in range(BLOCKS):
         for start in range(0, atoms, HALVES):
             lanes = pl.ds(start, HALVES)
@@ -220,7 +220,18 @@
         summed = jnp.dot(tables[block], features[...], preferred_element_type=jnp.float32)
         for peer in range(PLANES):
             piece = summed[peer * BLOCK : (peer + 1) * BLOCK, :].astype(jnp.bfloat16)
-            out_ref[peer, block * BLOCK : (block + 1) * BLOCK, :] = piece
+            made[block, peer] = piece
+        for group in range(4):
+            sends.append(
+                pltpu.make_async_copy(
+                    made.at[block, pl.ds(4 * group, 4)],
+                    out_ref.at[pl.ds(4 * group, 4), pl.ds(block * BLOCK, BLOCK), :],
+                    sent.at[block, group],
+                )
+            )
+            sends[-1].start()
+    for send in sends:
+        send.wait()
 
 
 def partial_factors(steps, coords, features):
@@ -233,12 +244,14 @@
             pl.BlockSpec(memory_space=pltpu.VMEM),
             pl.BlockSpec(memory_space=pl.ANY),
         ],
-        out_specs=pl.BlockSpec(memory_space=pltpu.VMEM),
+        out_specs=pl.BlockSpec(memory_space=pl.ANY),
         scratch_shapes=[
             pltpu.VMEM((atoms, F), jnp.bfloat16),
             pltpu.VMEM((FIRST, atoms), jnp.float32),
             pltpu.VMEM((BLOCKS, PLANES * BLOCK, atoms), jnp.bfloat16),
+            pltpu.VMEM((BLOCKS, PLANES, BLOCK, F), jnp.bfloat16),
             pltpu.SemaphoreType.DMA,
+            pltpu.SemaphoreType.DMA((BLOCKS, 4)),
         ],
         cost_estimate=pl.CostEstimate(
             flops=2 * PLANES * COLUMN * atoms * F, bytes_accessed=atoms * F * 2, transcendentals=0
@@ -317,7 +330,7 @@
     )(arrived)
 
 
-def filter_kernel(arrived_ref, near_ref, far_ref, out_ref, total, filtered):
+def filter_kernel(arrived_ref, near_ref, far_ref, out_ref, total, filtered, column, sent):
     total[...] = jnp.sum(arrived_ref[...].astype(jnp.float32), axis=0)
     weights = near_ref[...].astype(jnp.float32) + far_ref[...].astype(jnp.float32)
     extra = OWN - SIDE
@@ -329,9 +342,14 @@
             scaled = weights[weight : weight + count] * (1.0 / jnp.sqrt(power + 1e-05))
             filtered[start : start + count, :] = cosines * scaled
             filtered[start + count : start + 2 * count, :] = sines * scaled
-    column = filtered[...].astype(jnp.bfloat16)
-    for peer in range(PLANES):
-        out_ref[peer] = column
+    column[...] = filtered[...].astype(jnp.bfloat16)
+    sends = [
+        pltpu.make_async_copy(column, out_ref.at[peer], sent.at[peer]) for peer in range(PLANES)
+    ]
+    for send in sends:
+        send.start()
+    for send in sends:
+        send.wait()
 
 
 def filter_column(arrived, near, far):
@@ -339,8 +357,13 @@
         filter_kernel,
         out_shape=jax.ShapeDtypeStruct((PLANES, HALF, F), jnp.bfloat16),
         in_specs=[pl.BlockSpec(memory_space=pltpu.VMEM)] * 3,
-        out_specs=pl.BlockSpec(memory_space=pltpu.VMEM),
-        scratch_shapes=[pltpu.VMEM((HALF, F), jnp.float32)] * 2,
+        out_specs=pl.BlockSpec(memory_space=pl.ANY),
+        scratch_shapes=[
+            pltpu.VMEM((HALF, F), jnp.float32),
+            pltpu.VMEM((HALF, F), jnp.float32),
+            pltpu.VMEM((HALF, F), jnp.bfloat16),
+            pltpu.SemaphoreType.DMA((PLANES,)),
+        ],
         compiler_params=pltpu.CompilerParams(vmem_limit_bytes=8 << 20),
         name="filter_column",
     )(arrived, near, far)
@@ -382,36 +405,38 @@
     )(place, steps, coords, near)
 
 
-def message_kernel(tables_ref, filtered_ref, out_ref, *, own):
+def message_kernel(tables_ref, filtered_ref, own_ref, other_ref, *, side):
     half = TILE // 2
     core = lax.axis_index("wave") % 2
-    core = core if own else 1 - core
-    start = pl.multiple_of(core * half, half)
     filtered = filtered_ref[...]
-    for side in TWO:
-        tables = tables_ref[pl.ds(start + side * TILE, half), :]
-        message = jnp.dot(tables, filtered, preferred_element_type=jnp.float32)
-        out_ref[side] = message.astype(out_ref.dtype)
-
-
-def message_halves(tables, filtered, own):
+    for held, out_ref in ((core, own_ref), (1 - core, other_ref)):
+        start = pl.multiple_of(held * half, half) + side * TILE
+        message = jnp.dot(
+            tables_ref[pl.ds(start, half), :], filtered, preferred_element_type=jnp.float32
+        )
+        out_ref[...] = message.astype(out_ref.dtype)
+
+
+def message_halves(tables, filtered, side):
     half = TILE // 2
-    dtype = jnp.float32 if own else jnp.bfloat16
-    return pl.pallas_call(
-        functools.partial(message_kernel, own=own),
-        out_shape=jax.ShapeDtypeStruct((2, half, F), dtype),
+    return pl.pallas_call(
+        functools.partial(message_kernel, side=side),
+        out_shape=(
+            jax.ShapeDtypeStruct((half, F), jnp.bfloat16 if side else jnp.float32),
+            jax.ShapeDtypeStruct((half, F), jnp.bfloat16),
+        ),
         in_specs=[pl.BlockSpec(memory_space=pltpu.VMEM)] * 2,
-        out_specs=pl.BlockSpec(memory_space=pltpu.VMEM),
+        out_specs=(pl.BlockSpec(memory_space=pltpu.VMEM),) * 2,
         compiler_params=pltpu.CompilerParams(vmem_limit_bytes=16 << 20),
         cost_estimate=pl.CostEstimate(
             flops=4 * half * ALL_ROWS * F, bytes_accessed=8 * half * ALL_ROWS, transcendentals=0
         ),
-        name="message_own" if own else "message_other",
+        name="message_far" if side else "message_near",
     )(tables, filtered)
 
 
 def update_kernel(
-    features_ref, owns_ref, others_ref, far_ref, gain_ref, w_in_ref, w_out_ref, out_ref
+    features_ref, own_ref, a_ref, b_ref, c_ref, gain_ref, w_in_ref, w_out_ref, out_ref
 ):
     gain, w_in, w_out = gain_ref[...], w_in_ref[...], w_out_ref[...]
     half = TILE // 2
@@ -419,8 +444,9 @@
     chunk = half // 2
     for start in range(0, half, chunk):
         rows = pl.ds(start, chunk)
-        message = owns_ref[0, rows, :] + others_ref[0, rows, :].astype(jnp.float32)
-        message += far_ref[rows, :].astype(jnp.float32)
+        message = own_ref[rows, :]
+        for part_ref in (a_ref, b_ref, c_ref):
+            message += part_ref[rows, :].astype(jnp.float32)
         features = features_ref[pl.ds(base + start, chunk), :].astype(jnp.float32)
         updated = features + message * (1.0 / math.sqrt(K))
         power = jnp.mean(updated * updated, axis=1, keepdims=True)
@@ -431,15 +457,15 @@
         out_ref[rows, :] = (updated + added).astype(jnp.bfloat16)
 
 
-def update(features, owns, others, far, gain, w_in, w_out):
+def update(features, own, other, far, cross, gain, w_in, w_out):
     return pl.pallas_call(
         update_kernel,
         out_shape=jax.ShapeDtypeStruct((TILE // 2, F), jnp.bfloat16),
-        in_specs=[pl.BlockSpec(memory_space=pltpu.VMEM)] * 7,
+        in_specs=[pl.BlockSpec(memory_space=pltpu.VMEM)] * 8,
         out_specs=pl.BlockSpec(memory_space=pltpu.VMEM),
         compiler_params=pltpu.CompilerParams(vmem_limit_bytes=8 << 20),
         name="update",
-    )(features, owns, others, far, gain, w_in, w_out)
+    )(features, own, other, far, cross, gain, w_in, w_out)
 
 
 def exchange(pieces, groups):
@@ -473,12 +499,13 @@
     near = lax.ppermute(near, AXES, LINE_SAME)
     filtered = exchange(filtered, GROUPS_XY).reshape(ALL_ROWS, F)
     tables = message_tables(place, jnp.asarray(ALL_STEPS), coords, near)
-    others = message_halves(tables, filtered, False)
-    others = lax.ppermute(others, AXES, SWAP)
-    owns = message_halves(tables, filtered, True)
-    far = (owns[1] + others[1].astype(jnp.float32)).astype(jnp.bfloat16)
+    far, cross = message_halves(tables, filtered, 1)
     far = lax.ppermute(far, AXES, LINE_SAME)
-    return update(features, owns, others, far, norm_gain.reshape(1, F), w_in, w_out)
+    cross = lax.ppermute(cross, AXES, LINE_CROSS)
+    own, other = message_halves(tables, filtered, 0)
+    other = lax.ppermute(other, AXES, SWAP)
+    gain = norm_gain.reshape(1, F)
+    return update(features, own, other, far, cross, gain, w_in, w_out)
 
 
 def solution(mesh):

time: 88.3 us -> 87.7 us (level)
  waiting for transfers between devices: 14.8 us -> 11.6 us
  starting transfers between devices: 58 us -> 60 us
    ppermute x1, waiting for transfers between devices: 3.49 us -> 0.01 us  [layer(): far = lax.ppermute(far, AXES, LINE_SAME)]
    ppermute x1 -> x2, starting transfers between devices: 3.54 us -> 5.84 us  [the longest x1 3.54 us: layer(): cross = lax.ppermute(cross, AXES, LINE_CROSS)]
  transfers between devices with their start and end apart: 9 -> 10, of which waited for: 8 -> 8; matrix products, arithmetic and copies ran while one was open for 0% -> 0% of each run, Pallas kernels for 5% -> 5%
where the time goes in v12:
time: 87.7 us; the launch traced here: 86.7 us
  starting transfers between devices  60 us (68%)
  Pallas kernels  14.6 us (17%)
  waiting for transfers between devices  11.6 us (13%)
    all_to_all x3, starting transfers between devices, exchange(): lax.all_to_all(pieces, AXES, split_axis=0, concat_axis=0, tiled=True, axi...  18.6 us
    ppermute x1, starting transfers between devices, layer(): weights += lax.ppermute(weights, AXES, OUTER_PAIRS)  12.5 us
    ppermute x1, starting transfers between devices, layer(): far_weights = lax.ppermute(weights, AXES, INNER_PAIRS)  8.97 us
    pallas_call x1, Pallas kernels, partial_factors(): pl.pallas_call(factors_kernel, out_shape=jax.ShapeDtypeStruct((PLANES, CO...  6.19 us
    ppermute x1, starting transfers between devices, layer(): swapped = lax.ppermute(weights[POINTS:], AXES, SWAP)  6.05 us
    all_to_all x3, waiting for transfers between devices, exchange(): lax.all_to_all(pieces, AXES, split_axis=0, concat_axis=0, tiled=True, axi...  5.58 us
    ppermute x1, starting transfers between devices, layer(): near = lax.ppermute(near, AXES, LINE_SAME)  4.15 us
    pallas_call x1, Pallas kernels, message_tables(): pl.pallas_call(tables_kernel, out_shape=jax.ShapeDtypeStruct((2 * TILE, A...  4 us
  transfers between devices with their start and end apart: 10, of which 8 were waited for; matrix products, arithmetic and copies ran while one was open for 0% of the time, Pallas kernels for 5%

profile of v12, /device:TPU:1, one launch (start us, length us, event | category | flops | bytes accessed | tf_op | source)
XLA Modules:
  0.0 86.7 jit_solution(5091081589028881668)
XLA Ops:
  0.0 6.2 %factors.1 = bf16[16,160,256]{2,1,0:T(8,128)(2,1)} custom-call(f32[2,8,232]{2,1,0:T(8,128)} %constant.56.clone.steps_ref, s32[3,2048]{1,0:T(4,128)} %own_ref, bf16[2048,256]{1,0:T(8,128)(2,1)} %features_ref.3), custom_call_target="tpu_custom_call" | custom-call | flops 2684354560 | bytes 1048576 | tf_op jit(solution)/shard_map/factors/pallas_call | solution.py:239
  6.2 0.0 copy-start.1
  6.2 0.0 copy-start.6
  6.2 7.7 %all-to-all-start = ((bf16[16,160,256]{2,1,0:T(8,128)(2,1)}), bf16[16,160,256]{2,1,0:T(8,128)(2,1)S(1)}, u32[]{:S(2)}, u32[]{:S(2)}) async-start(bf16[16,160,256]{2,1,0:T(8,128)(2,1)} %factors.1), calls=%async_computation | async-start | bytes 2621440 | tf_op jit(solution)/shard_map/all_to_all | solution.py:472
  14.0 0.0 copy-done.1
  14.0 0.0 copy-done.6
  14.0 0.3 grid_weights.1
  14.3 12.5 %collective-permute-start = (bf16[80,256]{1,0:T(8,128)(2,1)S(1)}, bf16[80,256]{1,0:T(8,128)(2,1)S(1)}, u32[]{:S(2)}, u32[]{:S(2)}) collective-permute-start(bf16[80,256]{1,0:T(8,128)(2,1)S(1)} %grid_weights.1), channel_id=1, source_target_pairs={{0,6},{1,7},{2,4},{3,5},{4,2},{5,3},{6,0},{7,1},{8,14},{9,15},{10,... | collective-permute-start | bytes 122888 | tf_op jit(solution)/shard_map/ppermute | solution.py:489
  26.7 1.7 %collective-permute-done = bf16[80,256]{1,0:T(8,128)(2,1)S(1)} collective-permute-done((bf16[80,256]{1,0:T(8,128)(2,1)S(1)}, bf16[80,256]{1,0:T(8,128)(2,1)S(1)}, u32[]{:S(2)}, u32[]{:S(2)}) %collective-permute-start) | collective-permute-done | bytes 40992 | tf_op jit(solution)/shard_map/ppermute | solution.py:489
  28.4 2.8 %all-to-all-done.arrived_ref = bf16[16,160,256]{2,1,0:T(8,128)(2,1)S(1)} async-done(((bf16[16,160,256]{2,1,0:T(8,128)(2,1)}), bf16[16,160,256]{2,1,0:T(8,128)(2,1)S(1)}, u32[]{:S(2)}, u32[]{:S(2)}) %all-to-all-start) | async-done | bytes 1310752 | tf_op jit(solution)/shard_map/all_to_all | solution.py:472
  31.2 0.8 plane_sum.1
  32.0 7.3 %all-to-all-start.1 = ((bf16[4,80,256]{2,1,0:T(8,128)(2,1)}), bf16[4,80,256]{2,1,0:T(8,128)(2,1)S(1)}, u32[]{:S(2)}, u32[]{:S(2)}) async-start(bf16[4,80,256]{2,1,0:T(8,128)(2,1)} %plane_sum.1), calls=%async_computation.1 | async-start | bytes 327680 | tf_op jit(solution)/shard_map/all_to_all | solution.py:472
  39.3 0.0 copy-start.5
  39.3 0.0 copy-start.2
  39.3 9.0 %collective-permute-start.1 = (bf16[80,256]{1,0:T(8,128)(2,1)S(1)}, bf16[80,256]{1,0:T(8,128)(2,1)S(1)}, u32[]{:S(2)}, u32[]{:S(2)}) collective-permute-start(bf16[80,256]{1,0:T(8,128)(2,1)S(1)} %add.24), channel_id=1, source_target_pairs={{0,2},{1,3},{2,0},{3,1},{4,6},{5,7},{6,4},{7,5},{8,10},{9,11},{10,... | collective-permute-start | bytes 122888 | tf_op jit(solution)/shard_map/ppermute | solution.py:490
  48.3 1.4 %collective-permute-done.1 = bf16[80,256]{1,0:T(8,128)(2,1)S(1)} collective-permute-done((bf16[80,256]{1,0:T(8,128)(2,1)S(1)}, bf16[80,256]{1,0:T(8,128)(2,1)S(1)}, u32[]{:S(2)}, u32[]{:S(2)}) %collective-permute-start.1) | collective-permute-done | bytes 40992 | tf_op jit(solution)/shard_map/ppermute | solution.py:490
  49.7 6.0 %collective-permute-start.2 = (bf16[40,256]{1,0:T(8,128)(2,1)S(1)}, bf16[40,256]{1,0:T(8,128)(2,1)S(1)}, u32[]{:S(2)}, u32[]{:S(2)}) collective-permute-start(bf16[40,256]{1,0:T(8,128)(2,1)S(1)} %get-tuple-element.27), channel_id=1, source_target_pairs={{0,1},{1,0},{2,3},{3,2},{4,5},{5,4},{6,7},{7,6},{8,9},{9,8},{10,11... | collective-permute-start | bytes 61448 | tf_op jit(solution)/shard_map/ppermute | solution.py:495
  55.8 0.8 collective-permute-done.2.far_ref
  56.6 0.0 all-to-all-done.1.arrived_ref
  56.6 1.2 %filter_column.1 = bf16[16,80,256]{2,1,0:T(8,128)(2,1)} custom-call(bf16[4,80,256]{2,1,0:T(8,128)(2,1)S(1)} %all-to-all-done.1.arrived_ref, bf16[40,256]{1,0:T(8,128)(2,1)S(1)} %get-tuple-element.28.near_ref, bf16[40,256]{1,0:T(8,128)(2,1)S(1)} %collective-permute-done.2.far_ref), custom_call_target="tpu_custom_call" | custom-call | tf_op jit(solution)/shard_map/filter_column/pallas_call | solution.py:356
  57.8 3.6 %all-to-all-start.2 = ((bf16[16,80,256]{2,1,0:T(8,128)(2,1)}), bf16[16,80,256]{2,1,0:T(8,128)(2,1)S(1)}, u32[]{:S(2)}, u32[]{:S(2)}) async-start(bf16[16,80,256]{2,1,0:T(8,128)(2,1)} %filter_column.1), calls=%async_computation.2 | async-start | bytes 1310720 | tf_op jit(solution)/shard_map/all_to_all | solution.py:472
  61.4 0.0 copy-done.5
  61.5 4.1 %collective-permute-start.3 = (s32[3,512]{1,0:T(4,128)S(1)}, s32[3,512]{1,0:T(4,128)S(1)}, u32[]{:S(2)}, u32[]{:S(2)}) collective-permute-start(s32[3,512]{1,0:T(4,128)S(1)} %constant_dynamic-slice_fusion), channel_id=1, source_target_pairs={{0,32},{1,33},{2,34},{3,35},{4,36},{5,37},{6,38},{7,39},{8,40},{9,... | collective-permute-start | bytes 18440 | tf_op jit(solution)/shard_map/ppermute | solution.py:499
  65.6 0.1 pad_add_fusion.place_ref
  65.7 1.2 %collective-permute-done.3.near_ref = s32[3,512]{1,0:T(4,128)S(1)} collective-permute-done((s32[3,512]{1,0:T(4,128)S(1)}, s32[3,512]{1,0:T(4,128)S(1)}, u32[]{:S(2)}, u32[]{:S(2)}) %collective-permute-start.3) | collective-permute-done | bytes 6176 | tf_op jit(solution)/shard_map/ppermute | solution.py:499
  67.0 0.0 copy-done.2
  67.0 4.0 %message_tables.1.tables_ref = bf16[1024,1280]{1,0:T(8,128)(2,1)S(1)} custom-call(s32[4]{0:T(128)S(1)} %pad_add_fusion.place_ref, f32[4,8,1280]{2,1,0:T(8,128)S(1)} %copy-done.2, s32[3,2048]{1,0:T(4,128)S(1)} %copy-done.5, s32[3,512]{1,0:T(4,128)S(1)} %collective-permute-done.3.near_ref), custom_call_target="tpu_custom_call" | custom-call | flops 20971520 | bytes 2621440 | tf_op jit(solution)/shard_map/message_tables/pallas_call | solution.py:387
  71.0 2.8 %all-to-all-done.2 = bf16[16,80,256]{2,1,0:T(8,128)(2,1)S(1)} async-done(((bf16[16,80,256]{2,1,0:T(8,128)(2,1)}), bf16[16,80,256]{2,1,0:T(8,128)(2,1)S(1)}, u32[]{:S(2)}, u32[]{:S(2)}) %all-to-all-start.2) | async-done | bytes 655392 | tf_op jit(solution)/shard_map/all_to_all | solution.py:472
  73.8 0.5 message_far.1
  74.3 0.0 copy-start
  74.3 0.0 copy-start.3
  74.3 0.0 copy-start.4
  74.3 0.0 copy-start.7
  74.3 0.5 message_near.1
  74.8 3.9 %collective-permute-start.5 = (bf16[256,256]{1,0:T(8,128)(2,1)S(1)}, bf16[256,256]{1,0:T(8,128)(2,1)S(1)}, u32[]{:S(2)}, u32[]{:S(2)}) collective-permute-start(bf16[256,256]{1,0:T(8,128)(2,1)S(1)} %get-tuple-element.25), channel_id=1, source_target_pairs={{0,32},{1,33},{2,34},{3,35},{4,36},{5,37},{6,38},{7,39},{8,40},{9,... | collective-permute-start | bytes 393224 | tf_op jit(solution)/shard_map/ppermute | solution.py:503
  78.8 3.5 %collective-permute-start.6 = (bf16[256,256]{1,0:T(8,128)(2,1)S(1)}, bf16[256,256]{1,0:T(8,128)(2,1)S(1)}, u32[]{:S(2)}, u32[]{:S(2)}) collective-permute-start(bf16[256,256]{1,0:T(8,128)(2,1)S(1)} %get-tuple-element.26), channel_id=1, source_target_pairs={{0,33},{1,32},{2,35},{3,34},{4,37},{5,36},{6,39},{7,38},{8,41},{9,... | collective-permute-start | bytes 393224 | tf_op jit(solution)/shard_map/ppermute | solution.py:504
  82.3 2.3 %collective-permute-start.4 = (bf16[256,256]{1,0:T(8,128)(2,1)S(1)}, bf16[256,256]{1,0:T(8,128)(2,1)S(1)}, u32[]{:S(2)}, u32[]{:S(2)}) collective-permute-start(bf16[256,256]{1,0:T(8,128)(2,1)S(1)} %get-tuple-element.24), channel_id=1, source_target_pairs={{0,1},{1,0},{2,3},{3,2},{4,5},{5,4},{6,7},{7,6},{8,9},{9,8},{10,11... | collective-permute-start | bytes 393224 | tf_op jit(solution)/shard_map/ppermute | solution.py:506
  84.6 0.0 collective-permute-done.5.b_ref
  84.6 0.8 collective-permute-done.6.c_ref
  85.4 0.2 collective-permute-done.4.a_ref
  85.6 0.0 copy-done
  85.6 0.0 copy-done.3
  85.6 0.0 copy-done.4
  85.6 0.0 copy-done.7
  85.6 1.1 %update.1 = bf16[256,256]{1,0:T(8,128)(2,1)} custom-call(bf16[2048,256]{1,0:T(8,128)(2,1)S(1)} %copy-done, f32[256,256]{1,0:T(8,128)S(1)} %get-tuple-element.23.own_ref, bf16[256,256]{1,0:T(8,128)(2,1)S(1)} %collective-permute-done.4.a_ref, bf16[256,256]{1,0:T(8,128)(2,1)S(1)} %collective-permute-done.5.b_ref, ...), custom_call_target="tpu_custom_call" | custom-call | tf_op jit(solution)/shard_map/update/pallas_call | solution.py:461
  (4 shorter events, 0.0 us)
Async XLA Ops:
  6.2 7.8 %copy-start.1 = (f32[512,256]{1,0:T(8,128)S(1)}, f32[512,256]{1,0:T(8,128)}, u32[]{:S(2)}) copy-start(f32[512,256]{1,0:T(8,128)} %weights_ref.1) | copy-start | bytes 1572868
  6.2 7.7 %copy-start.6 = (s32[3,512]{1,0:T(4,128)S(1)}, s32[3,512]{1,0:T(4,128)}, u32[]{:S(2)}) copy-start(s32[3,512]{1,0:T(4,128)} %miller_ref) | copy-start | bytes 18436
  6.2 25.0 %all-to-all-start = ((bf16[16,160,256]{2,1,0:T(8,128)(2,1)}), bf16[16,160,256]{2,1,0:T(8,128)(2,1)S(1)}, u32[]{:S(2)}, u32[]{:S(2)}) async-start(bf16[16,160,256]{2,1,0:T(8,128)(2,1)} %factors.1), calls=%async_computation | async-start | bytes 2621440 | tf_op jit(solution)/shard_map/all_to_all | solution.py:472
  14.3 14.1 %collective-permute-start = (bf16[80,256]{1,0:T(8,128)(2,1)S(1)}, bf16[80,256]{1,0:T(8,128)(2,1)S(1)}, u32[]{:S(2)}, u32[]{:S(2)}) collective-permute-start(bf16[80,256]{1,0:T(8,128)(2,1)S(1)} %grid_weights.1), channel_id=1, source_target_pairs={{0,6},{1,7},{2,4},{3,5},{4,2},{5,3},{6,0},{7,1},{8,14},{9,15},{10,... | collective-permute-start | bytes 122888 | tf_op jit(solution)/shard_map/ppermute | solution.py:489
  32.0 24.6 %all-to-all-start.1 = ((bf16[4,80,256]{2,1,0:T(8,128)(2,1)}), bf16[4,80,256]{2,1,0:T(8,128)(2,1)S(1)}, u32[]{:S(2)}, u32[]{:S(2)}) async-start(bf16[4,80,256]{2,1,0:T(8,128)(2,1)} %plane_sum.1), calls=%async_computation.1 | async-start | bytes 327680 | tf_op jit(solution)/shard_map/all_to_all | solution.py:472
  39.3 22.1 %copy-start.5 = (s32[3,2048]{1,0:T(4,128)S(1)}, s32[3,2048]{1,0:T(4,128)}, u32[]{:S(2)}) copy-start(s32[3,2048]{1,0:T(4,128)} %own_ref) | copy-start | bytes 73732
  39.3 27.6 %copy-start.2 = (f32[4,8,1280]{2,1,0:T(8,128)S(1)}, f32[4,8,1280]{2,1,0:T(8,128)}, u32[]{:S(2)}) copy-start(f32[4,8,1280]{2,1,0:T(8,128)} %constant.57.clone.steps_ref) | copy-start | bytes 491524
  39.3 10.4 %collective-permute-start.1 = (bf16[80,256]{1,0:T(8,128)(2,1)S(1)}, bf16[80,256]{1,0:T(8,128)(2,1)S(1)}, u32[]{:S(2)}, u32[]{:S(2)}) collective-permute-start(bf16[80,256]{1,0:T(8,128)(2,1)S(1)} %add.24), channel_id=1, source_target_pairs={{0,2},{1,3},{2,0},{3,1},{4,6},{5,7},{6,4},{7,5},{8,10},{9,11},{10,... | collective-permute-start | bytes 122888 | tf_op jit(solution)/shard_map/ppermute | solution.py:490
  49.7 6.9 %collective-permute-start.2 = (bf16[40,256]{1,0:T(8,128)(2,1)S(1)}, bf16[40,256]{1,0:T(8,128)(2,1)S(1)}, u32[]{:S(2)}, u32[]{:S(2)}) collective-permute-start(bf16[40,256]{1,0:T(8,128)(2,1)S(1)} %get-tuple-element.27), channel_id=1, source_target_pairs={{0,1},{1,0},{2,3},{3,2},{4,5},{5,4},{6,7},{7,6},{8,9},{9,8},{10,11... | collective-permute-start | bytes 61448 | tf_op jit(solution)/shard_map/ppermute | solution.py:495
  57.8 16.0 %all-to-all-start.2 = ((bf16[16,80,256]{2,1,0:T(8,128)(2,1)}), bf16[16,80,256]{2,1,0:T(8,128)(2,1)S(1)}, u32[]{:S(2)}, u32[]{:S(2)}) async-start(bf16[16,80,256]{2,1,0:T(8,128)(2,1)} %filter_column.1), calls=%async_computation.2 | async-start | bytes 1310720 | tf_op jit(solution)/shard_map/all_to_all | solution.py:472
  61.5 5.5 %collective-permute-start.3 = (s32[3,512]{1,0:T(4,128)S(1)}, s32[3,512]{1,0:T(4,128)S(1)}, u32[]{:S(2)}, u32[]{:S(2)}) collective-permute-start(s32[3,512]{1,0:T(4,128)S(1)} %constant_dynamic-slice_fusion), channel_id=1, source_target_pairs={{0,32},{1,33},{2,34},{3,35},{4,36},{5,37},{6,38},{7,39},{8,40},{9,... | collective-permute-start | bytes 18440 | tf_op jit(solution)/shard_map/ppermute | solution.py:499
  74.3 11.3 %copy-start = (bf16[2048,256]{1,0:T(8,128)(2,1)S(1)}, bf16[2048,256]{1,0:T(8,128)(2,1)}, u32[]{:S(2)}) copy-start(bf16[2048,256]{1,0:T(8,128)(2,1)} %features_ref.3) | copy-start | bytes 3145732
  74.3 11.3 %copy-start.3 = (bf16[256,256]{1,0:T(8,128)(2,1)S(1)}, bf16[256,256]{1,0:T(8,128)(2,1)}, u32[]{:S(2)}) copy-start(bf16[256,256]{1,0:T(8,128)(2,1)} %w_in_ref.1) | copy-start | bytes 393220
  74.3 11.3 %copy-start.4 = (bf16[256,256]{1,0:T(8,128)(2,1)S(1)}, bf16[256,256]{1,0:T(8,128)(2,1)}, u32[]{:S(2)}) copy-start(bf16[256,256]{1,0:T(8,128)(2,1)} %w_out_ref.1) | copy-start | bytes 393220
  74.3 11.3 %copy-start.7 = (f32[256]{0:T(256)S(1)}, f32[256]{0:T(256)}, u32[]{:S(2)}) copy-start(f32[256]{0:T(256)} %param.13) | copy-start | bytes 3076
  74.8 9.8 %collective-permute-start.5 = (bf16[256,256]{1,0:T(8,128)(2,1)S(1)}, bf16[256,256]{1,0:T(8,128)(2,1)S(1)}, u32[]{:S(2)}, u32[]{:S(2)}) collective-permute-start(bf16[256,256]{1,0:T(8,128)(2,1)S(1)} %get-tuple-element.25), channel_id=1, source_target_pairs={{0,32},{1,33},{2,34},{3,35},{4,36},{5,37},{6,38},{7,39},{8,40},{9,... | collective-permute-start | bytes 393224 | tf_op jit(solution)/shard_map/ppermute | solution.py:503
  78.8 6.7 %collective-permute-start.6 = (bf16[256,256]{1,0:T(8,128)(2,1)S(1)}, bf16[256,256]{1,0:T(8,128)(2,1)S(1)}, u32[]{:S(2)}, u32[]{:S(2)}) collective-permute-start(bf16[256,256]{1,0:T(8,128)(2,1)S(1)} %get-tuple-element.26), channel_id=1, source_target_pairs={{0,33},{1,32},{2,35},{3,34},{4,37},{5,36},{6,39},{7,38},{8,41},{9,... | collective-permute-start | bytes 393224 | tf_op jit(solution)/shard_map/ppermute | solution.py:504
  82.3 3.3 %collective-permute-start.4 = (bf16[256,256]{1,0:T(8,128)(2,1)S(1)}, bf16[256,256]{1,0:T(8,128)(2,1)S(1)}, u32[]{:S(2)}, u32[]{:S(2)}) collective-permute-start(bf16[256,256]{1,0:T(8,128)(2,1)S(1)} %get-tuple-element.24), channel_id=1, source_target_pairs={{0,1},{1,0},{2,3},{3,2},{4,5},{5,4},{6,7},{7,6},{8,9},{9,8},{10,11... | collective-permute-start | bytes 393224 | tf_op jit(solution)/shard_map/ppermute | solution.py:506

commit v13 on v12

--- a/solution.py
+++ b/solution.py
@@ -311,12 +311,14 @@
 
 
 def plane_sum_kernel(arrived_ref, out_ref):
-    total = arrived_ref[0].astype(jnp.float32)
-    for peer in range(1, PLANES):
-        total += arrived_ref[peer].astype(jnp.float32)
-    sent = total.astype(jnp.bfloat16)
-    for peer in range(4):
-        out_ref[peer] = sent[peer % 2 * HALF : (peer % 2 + 1) * HALF]
+    for part in TWO:
+        rows = pl.ds(part * HALF, HALF)
+        total = arrived_ref[0, rows, :].astype(jnp.float32)
+        for peer in range(1, PLANES):
+            total += arrived_ref[peer, rows, :].astype(jnp.float32)
+        sent = total.astype(jnp.bfloat16)
+        for peer in (part, part + 2):
+            out_ref[peer] = sent
 
 
 def plane_sum(arrived):
@@ -330,7 +332,7 @@
     )(arrived)
 
 
-def filter_kernel(arrived_ref, near_ref, far_ref, out_ref, total, filtered, column, sent):
+def filter_kernel(arrived_ref, near_ref, far_ref, out_ref, total, filtered):
     total[...] = jnp.sum(arrived_ref[...].astype(jnp.float32), axis=0)
     weights = near_ref[...].astype(jnp.float32) + far_ref[...].astype(jnp.float32)
     extra = OWN - SIDE
@@ -342,14 +344,9 @@
             scaled = weights[weight : weight + count] * (1.0 / jnp.sqrt(power + 1e-05))
             filtered[start : start + count, :] = cosines * scaled
             filtered[start + count : start + 2 * count, :] = sines * scaled
-    column[...] = filtered[...].astype(jnp.bfloat16)
-    sends = [
-        pltpu.make_async_copy(column, out_ref.at[peer], sent.at[peer]) for peer in range(PLANES)
-    ]
-    for send in sends:
-        send.start()
-    for send in sends:
-        send.wait()
+    column = filtered[...].astype(jnp.bfloat16)
+    for peer in range(PLANES):
+        out_ref[peer] = column
 
 
 def filter_column(arrived, near, far):
@@ -357,13 +354,8 @@
         filter_kernel,
         out_shape=jax.ShapeDtypeStruct((PLANES, HALF, F), jnp.bfloat16),
         in_specs=[pl.BlockSpec(memory_space=pltpu.VMEM)] * 3,
-        out_specs=pl.BlockSpec(memory_space=pl.ANY),
-        scratch_shapes=[
-            pltpu.VMEM((HALF, F), jnp.float32),
-            pltpu.VMEM((HALF, F), jnp.float32),
-            pltpu.VMEM((HALF, F), jnp.bfloat16),
-            pltpu.SemaphoreType.DMA((PLANES,)),
-        ],
+        out_specs=pl.BlockSpec(memory_space=pltpu.VMEM),
+        scratch_shapes=[pltpu.VMEM((HALF, F), jnp.float32)] * 2,
         compiler_params=pltpu.CompilerParams(vmem_limit_bytes=8 << 20),
         name="filter_column",
     )(arrived, near, far)

time: 87.7 us -> 87.6 us (level)
  no operation moved by 1% of the time
where the time goes in v13:
time: 87.6 us; the launch traced here: 86.6 us
  starting transfers between devices  60 us (68%)
  Pallas kernels  14.5 us (17%)
  waiting for transfers between devices  11.6 us (13%)
    all_to_all x3, starting transfers between devices, exchange(): lax.all_to_all(pieces, AXES, split_axis=0, concat_axis=0, tiled=True, axi...  18.6 us
    ppermute x1, starting transfers between devices, layer(): weights += lax.ppermute(weights, AXES, OUTER_PAIRS)  12.5 us
    ppermute x1, starting transfers between devices, layer(): far_weights = lax.ppermute(weights, AXES, INNER_PAIRS)  8.97 us
    pallas_call x1, Pallas kernels, partial_factors(): pl.pallas_call(factors_kernel, out_shape=jax.ShapeDtypeStruct((PLANES, CO...  6.19 us
    ppermute x1, starting transfers between devices, layer(): swapped = lax.ppermute(weights[POINTS:], AXES, SWAP)  6.05 us
    all_to_all x3, waiting for transfers between devices, exchange(): lax.all_to_all(pieces, AXES, split_axis=0, concat_axis=0, tiled=True, axi...  5.58 us
    ppermute x1, starting transfers between devices, layer(): near = lax.ppermute(near, AXES, LINE_SAME)  4.15 us
    pallas_call x1, Pallas kernels, message_tables(): pl.pallas_call(tables_kernel, out_shape=jax.ShapeDtypeStruct((2 * TILE, A...  4 us
  transfers between devices with their start and end apart: 10, of which 8 were waited for; matrix products, arithmetic and copies ran while one was open for 0% of the time, Pallas kernels for 5%

profile of v13, /device:TPU:1, one launch (start us, length us, event | category | flops | bytes accessed | tf_op | source)
XLA Modules:
  0.0 86.6 jit_solution(14071549177597861570)
XLA Ops:
  0.0 6.2 %factors.1 = bf16[16,160,256]{2,1,0:T(8,128)(2,1)} custom-call(f32[2,8,232]{2,1,0:T(8,128)} %constant.56.clone.steps_ref, s32[3,2048]{1,0:T(4,128)} %own_ref, bf16[2048,256]{1,0:T(8,128)(2,1)} %features_ref.3), custom_call_target="tpu_custom_call" | custom-call | flops 2684354560 | bytes 1048576 | tf_op jit(solution)/shard_map/factors/pallas_call | solution.py:239
  6.2 0.0 copy-start.1
  6.2 0.0 copy-start.6
  6.2 7.7 %all-to-all-start = ((bf16[16,160,256]{2,1,0:T(8,128)(2,1)}), bf16[16,160,256]{2,1,0:T(8,128)(2,1)S(1)}, u32[]{:S(2)}, u32[]{:S(2)}) async-start(bf16[16,160,256]{2,1,0:T(8,128)(2,1)} %factors.1), calls=%async_computation | async-start | bytes 2621440 | tf_op jit(solution)/shard_map/all_to_all | solution.py:464
  14.0 0.0 copy-done.1
  14.0 0.0 copy-done.6
  14.0 0.3 grid_weights.1
  14.3 12.5 %collective-permute-start = (bf16[80,256]{1,0:T(8,128)(2,1)S(1)}, bf16[80,256]{1,0:T(8,128)(2,1)S(1)}, u32[]{:S(2)}, u32[]{:S(2)}) collective-permute-start(bf16[80,256]{1,0:T(8,128)(2,1)S(1)} %grid_weights.1), channel_id=1, source_target_pairs={{0,6},{1,7},{2,4},{3,5},{4,2},{5,3},{6,0},{7,1},{8,14},{9,15},{10,... | collective-permute-start | bytes 122888 | tf_op jit(solution)/shard_map/ppermute | solution.py:481
  26.7 1.7 %collective-permute-done = bf16[80,256]{1,0:T(8,128)(2,1)S(1)} collective-permute-done((bf16[80,256]{1,0:T(8,128)(2,1)S(1)}, bf16[80,256]{1,0:T(8,128)(2,1)S(1)}, u32[]{:S(2)}, u32[]{:S(2)}) %collective-permute-start) | collective-permute-done | bytes 40992 | tf_op jit(solution)/shard_map/ppermute | solution.py:481
  28.4 2.8 %all-to-all-done.arrived_ref = bf16[16,160,256]{2,1,0:T(8,128)(2,1)S(1)} async-done(((bf16[16,160,256]{2,1,0:T(8,128)(2,1)}), bf16[16,160,256]{2,1,0:T(8,128)(2,1)S(1)}, u32[]{:S(2)}, u32[]{:S(2)}) %all-to-all-start) | async-done | bytes 1310752 | tf_op jit(solution)/shard_map/all_to_all | solution.py:464
  31.2 0.8 plane_sum.1
  32.0 7.3 %all-to-all-start.1 = ((bf16[4,80,256]{2,1,0:T(8,128)(2,1)}), bf16[4,80,256]{2,1,0:T(8,128)(2,1)S(1)}, u32[]{:S(2)}, u32[]{:S(2)}) async-start(bf16[4,80,256]{2,1,0:T(8,128)(2,1)} %plane_sum.1), calls=%async_computation.1 | async-start | bytes 327680 | tf_op jit(solution)/shard_map/all_to_all | solution.py:464
  39.3 0.0 copy-start.5
  39.3 0.0 copy-start.2
  39.3 9.0 %collective-permute-start.1 = (bf16[80,256]{1,0:T(8,128)(2,1)S(1)}, bf16[80,256]{1,0:T(8,128)(2,1)S(1)}, u32[]{:S(2)}, u32[]{:S(2)}) collective-permute-start(bf16[80,256]{1,0:T(8,128)(2,1)S(1)} %add.24), channel_id=1, source_target_pairs={{0,2},{1,3},{2,0},{3,1},{4,6},{5,7},{6,4},{7,5},{8,10},{9,11},{10,... | collective-permute-start | bytes 122888 | tf_op jit(solution)/shard_map/ppermute | solution.py:482
  48.3 1.4 %collective-permute-done.1 = bf16[80,256]{1,0:T(8,128)(2,1)S(1)} collective-permute-done((bf16[80,256]{1,0:T(8,128)(2,1)S(1)}, bf16[80,256]{1,0:T(8,128)(2,1)S(1)}, u32[]{:S(2)}, u32[]{:S(2)}) %collective-permute-start.1) | collective-permute-done | bytes 40992 | tf_op jit(solution)/shard_map/ppermute | solution.py:482
  49.7 6.0 %collective-permute-start.2 = (bf16[40,256]{1,0:T(8,128)(2,1)S(1)}, bf16[40,256]{1,0:T(8,128)(2,1)S(1)}, u32[]{:S(2)}, u32[]{:S(2)}) collective-permute-start(bf16[40,256]{1,0:T(8,128)(2,1)S(1)} %get-tuple-element.27), channel_id=1, source_target_pairs={{0,1},{1,0},{2,3},{3,2},{4,5},{5,4},{6,7},{7,6},{8,9},{9,8},{10,11... | collective-permute-start | bytes 61448 | tf_op jit(solution)/shard_map/ppermute | solution.py:487
  55.8 0.8 collective-permute-done.2.far_ref
  56.6 0.0 all-to-all-done.1.arrived_ref
  56.6 1.0 %filter_column.1 = bf16[16,80,256]{2,1,0:T(8,128)(2,1)} custom-call(bf16[4,80,256]{2,1,0:T(8,128)(2,1)S(1)} %all-to-all-done.1.arrived_ref, bf16[40,256]{1,0:T(8,128)(2,1)S(1)} %get-tuple-element.28.near_ref, bf16[40,256]{1,0:T(8,128)(2,1)S(1)} %collective-permute-done.2.far_ref), custom_call_target="tpu_custom_call" | custom-call | tf_op jit(solution)/shard_map/filter_column/pallas_call | solution.py:353
  57.7 3.6 %all-to-all-start.2 = ((bf16[16,80,256]{2,1,0:T(8,128)(2,1)}), bf16[16,80,256]{2,1,0:T(8,128)(2,1)S(1)}, u32[]{:S(2)}, u32[]{:S(2)}) async-start(bf16[16,80,256]{2,1,0:T(8,128)(2,1)} %filter_column.1), calls=%async_computation.2 | async-start | bytes 1310720 | tf_op jit(solution)/shard_map/all_to_all | solution.py:464
  61.3 0.0 copy-done.5
  61.3 4.1 %collective-permute-start.3 = (s32[3,512]{1,0:T(4,128)S(1)}, s32[3,512]{1,0:T(4,128)S(1)}, u32[]{:S(2)}, u32[]{:S(2)}) collective-permute-start(s32[3,512]{1,0:T(4,128)S(1)} %constant_dynamic-slice_fusion), channel_id=1, source_target_pairs={{0,32},{1,33},{2,34},{3,35},{4,36},{5,37},{6,38},{7,39},{8,40},{9,... | collective-permute-start | bytes 18440 | tf_op jit(solution)/shard_map/ppermute | solution.py:491
  65.5 0.1 pad_add_fusion.place_ref
  65.6 1.2 %collective-permute-done.3.near_ref = s32[3,512]{1,0:T(4,128)S(1)} collective-permute-done((s32[3,512]{1,0:T(4,128)S(1)}, s32[3,512]{1,0:T(4,128)S(1)}, u32[]{:S(2)}, u32[]{:S(2)}) %collective-permute-start.3) | collective-permute-done | bytes 6176 | tf_op jit(solution)/shard_map/ppermute | solution.py:491
  66.8 0.0 copy-done.2
  66.8 4.0 %message_tables.1.tables_ref = bf16[1024,1280]{1,0:T(8,128)(2,1)S(1)} custom-call(s32[4]{0:T(128)S(1)} %pad_add_fusion.place_ref, f32[4,8,1280]{2,1,0:T(8,128)S(1)} %copy-done.2, s32[3,2048]{1,0:T(4,128)S(1)} %copy-done.5, s32[3,512]{1,0:T(4,128)S(1)} %collective-permute-done.3.near_ref), custom_call_target="tpu_custom_call" | custom-call | flops 20971520 | bytes 2621440 | tf_op jit(solution)/shard_map/message_tables/pallas_call | solution.py:379
  70.8 2.8 %all-to-all-done.2 = bf16[16,80,256]{2,1,0:T(8,128)(2,1)S(1)} async-done(((bf16[16,80,256]{2,1,0:T(8,128)(2,1)}), bf16[16,80,256]{2,1,0:T(8,128)(2,1)S(1)}, u32[]{:S(2)}, u32[]{:S(2)}) %all-to-all-start.2) | async-done | bytes 655392 | tf_op jit(solution)/shard_map/all_to_all | solution.py:464
  73.6 0.5 message_far.1
  74.1 0.0 copy-start
  74.1 0.0 copy-start.3
  74.1 0.0 copy-start.4
  74.2 0.0 copy-start.7
  74.2 0.5 message_near.1
  74.7 3.9 %collective-permute-start.5 = (bf16[256,256]{1,0:T(8,128)(2,1)S(1)}, bf16[256,256]{1,0:T(8,128)(2,1)S(1)}, u32[]{:S(2)}, u32[]{:S(2)}) collective-permute-start(bf16[256,256]{1,0:T(8,128)(2,1)S(1)} %get-tuple-element.25), channel_id=1, source_target_pairs={{0,32},{1,33},{2,34},{3,35},{4,36},{5,37},{6,38},{7,39},{8,40},{9,... | collective-permute-start | bytes 393224 | tf_op jit(solution)/shard_map/ppermute | solution.py:495
  78.6 3.5 %collective-permute-start.6 = (bf16[256,256]{1,0:T(8,128)(2,1)S(1)}, bf16[256,256]{1,0:T(8,128)(2,1)S(1)}, u32[]{:S(2)}, u32[]{:S(2)}) collective-permute-start(bf16[256,256]{1,0:T(8,128)(2,1)S(1)} %get-tuple-element.26), channel_id=1, source_target_pairs={{0,33},{1,32},{2,35},{3,34},{4,37},{5,36},{6,39},{7,38},{8,41},{9,... | collective-permute-start | bytes 393224 | tf_op jit(solution)/shard_map/ppermute | solution.py:496
  82.2 2.3 %collective-permute-start.4 = (bf16[256,256]{1,0:T(8,128)(2,1)S(1)}, bf16[256,256]{1,0:T(8,128)(2,1)S(1)}, u32[]{:S(2)}, u32[]{:S(2)}) collective-permute-start(bf16[256,256]{1,0:T(8,128)(2,1)S(1)} %get-tuple-element.24), channel_id=1, source_target_pairs={{0,1},{1,0},{2,3},{3,2},{4,5},{5,4},{6,7},{7,6},{8,9},{9,8},{10,11... | collective-permute-start | bytes 393224 | tf_op jit(solution)/shard_map/ppermute | solution.py:498
  84.5 0.0 collective-permute-done.5.b_ref
  84.5 0.8 collective-permute-done.6.c_ref
  85.3 0.2 collective-permute-done.4.a_ref
  85.5 0.0 copy-done
  85.5 0.0 copy-done.3
  85.5 0.0 copy-done.4
  85.5 0.0 copy-done.7
  85.5 1.1 %update.1 = bf16[256,256]{1,0:T(8,128)(2,1)} custom-call(bf16[2048,256]{1,0:T(8,128)(2,1)S(1)} %copy-done, f32[256,256]{1,0:T(8,128)S(1)} %get-tuple-element.23.own_ref, bf16[256,256]{1,0:T(8,128)(2,1)S(1)} %collective-permute-done.4.a_ref, bf16[256,256]{1,0:T(8,128)(2,1)S(1)} %collective-permute-done.5.b_ref, ...), custom_call_target="tpu_custom_call" | custom-call | tf_op jit(solution)/shard_map/update/pallas_call | solution.py:453
  (4 shorter events, 0.0 us)
Async XLA Ops:
  6.2 7.8 %copy-start.1 = (f32[512,256]{1,0:T(8,128)S(1)}, f32[512,256]{1,0:T(8,128)}, u32[]{:S(2)}) copy-start(f32[512,256]{1,0:T(8,128)} %weights_ref.1) | copy-start | bytes 1572868
  6.2 7.7 %copy-start.6 = (s32[3,512]{1,0:T(4,128)S(1)}, s32[3,512]{1,0:T(4,128)}, u32[]{:S(2)}) copy-start(s32[3,512]{1,0:T(4,128)} %miller_ref) | copy-start | bytes 18436
  6.2 25.0 %all-to-all-start = ((bf16[16,160,256]{2,1,0:T(8,128)(2,1)}), bf16[16,160,256]{2,1,0:T(8,128)(2,1)S(1)}, u32[]{:S(2)}, u32[]{:S(2)}) async-start(bf16[16,160,256]{2,1,0:T(8,128)(2,1)} %factors.1), calls=%async_computation | async-start | bytes 2621440 | tf_op jit(solution)/shard_map/all_to_all | solution.py:464
  14.3 14.1 %collective-permute-start = (bf16[80,256]{1,0:T(8,128)(2,1)S(1)}, bf16[80,256]{1,0:T(8,128)(2,1)S(1)}, u32[]{:S(2)}, u32[]{:S(2)}) collective-permute-start(bf16[80,256]{1,0:T(8,128)(2,1)S(1)} %grid_weights.1), channel_id=1, source_target_pairs={{0,6},{1,7},{2,4},{3,5},{4,2},{5,3},{6,0},{7,1},{8,14},{9,15},{10,... | collective-permute-start | bytes 122888 | tf_op jit(solution)/shard_map/ppermute | solution.py:481
  32.0 24.6 %all-to-all-start.1 = ((bf16[4,80,256]{2,1,0:T(8,128)(2,1)}), bf16[4,80,256]{2,1,0:T(8,128)(2,1)S(1)}, u32[]{:S(2)}, u32[]{:S(2)}) async-start(bf16[4,80,256]{2,1,0:T(8,128)(2,1)} %plane_sum.1), calls=%async_computation.1 | async-start | bytes 327680 | tf_op jit(solution)/shard_map/all_to_all | solution.py:464
  39.3 22.0 %copy-start.5 = (s32[3,2048]{1,0:T(4,128)S(1)}, s32[3,2048]{1,0:T(4,128)}, u32[]{:S(2)}) copy-start(s32[3,2048]{1,0:T(4,128)} %own_ref) | copy-start | bytes 73732
  39.3 27.5 %copy-start.2 = (f32[4,8,1280]{2,1,0:T(8,128)S(1)}, f32[4,8,1280]{2,1,0:T(8,128)}, u32[]{:S(2)}) copy-start(f32[4,8,1280]{2,1,0:T(8,128)} %constant.57.clone.steps_ref) | copy-start | bytes 491524
  39.3 10.4 %collective-permute-start.1 = (bf16[80,256]{1,0:T(8,128)(2,1)S(1)}, bf16[80,256]{1,0:T(8,128)(2,1)S(1)}, u32[]{:S(2)}, u32[]{:S(2)}) collective-permute-start(bf16[80,256]{1,0:T(8,128)(2,1)S(1)} %add.24), channel_id=1, source_target_pairs={{0,2},{1,3},{2,0},{3,1},{4,6},{5,7},{6,4},{7,5},{8,10},{9,11},{10,... | collective-permute-start | bytes 122888 | tf_op jit(solution)/shard_map/ppermute | solution.py:482
  49.7 6.9 %collective-permute-start.2 = (bf16[40,256]{1,0:T(8,128)(2,1)S(1)}, bf16[40,256]{1,0:T(8,128)(2,1)S(1)}, u32[]{:S(2)}, u32[]{:S(2)}) collective-permute-start(bf16[40,256]{1,0:T(8,128)(2,1)S(1)} %get-tuple-element.27), channel_id=1, source_target_pairs={{0,1},{1,0},{2,3},{3,2},{4,5},{5,4},{6,7},{7,6},{8,9},{9,8},{10,11... | collective-permute-start | bytes 61448 | tf_op jit(solution)/shard_map/ppermute | solution.py:487
  57.7 16.0 %all-to-all-start.2 = ((bf16[16,80,256]{2,1,0:T(8,128)(2,1)}), bf16[16,80,256]{2,1,0:T(8,128)(2,1)S(1)}, u32[]{:S(2)}, u32[]{:S(2)}) async-start(bf16[16,80,256]{2,1,0:T(8,128)(2,1)} %filter_column.1), calls=%async_computation.2 | async-start | bytes 1310720 | tf_op jit(solution)/shard_map/all_to_all | solution.py:464
  61.3 5.5 %collective-permute-start.3 = (s32[3,512]{1,0:T(4,128)S(1)}, s32[3,512]{1,0:T(4,128)S(1)}, u32[]{:S(2)}, u32[]{:S(2)}) collective-permute-start(s32[3,512]{1,0:T(4,128)S(1)} %constant_dynamic-slice_fusion), channel_id=1, source_target_pairs={{0,32},{1,33},{2,34},{3,35},{4,36},{5,37},{6,38},{7,39},{8,40},{9,... | collective-permute-start | bytes 18440 | tf_op jit(solution)/shard_map/ppermute | solution.py:491
  74.1 11.3 %copy-start = (bf16[2048,256]{1,0:T(8,128)(2,1)S(1)}, bf16[2048,256]{1,0:T(8,128)(2,1)}, u32[]{:S(2)}) copy-start(bf16[2048,256]{1,0:T(8,128)(2,1)} %features_ref.3) | copy-start | bytes 3145732
  74.1 11.3 %copy-start.3 = (bf16[256,256]{1,0:T(8,128)(2,1)S(1)}, bf16[256,256]{1,0:T(8,128)(2,1)}, u32[]{:S(2)}) copy-start(bf16[256,256]{1,0:T(8,128)(2,1)} %w_in_ref.1) | copy-start | bytes 393220
  74.1 11.3 %copy-start.4 = (bf16[256,256]{1,0:T(8,128)(2,1)S(1)}, bf16[256,256]{1,0:T(8,128)(2,1)}, u32[]{:S(2)}) copy-start(bf16[256,256]{1,0:T(8,128)(2,1)} %w_out_ref.1) | copy-start | bytes 393220
  74.2 11.3 %copy-start.7 = (f32[256]{0:T(256)S(1)}, f32[256]{0:T(256)}, u32[]{:S(2)}) copy-start(f32[256]{0:T(256)} %param.13) | copy-start | bytes 3076
  74.7 9.8 %collective-permute-start.5 = (bf16[256,256]{1,0:T(8,128)(2,1)S(1)}, bf16[256,256]{1,0:T(8,128)(2,1)S(1)}, u32[]{:S(2)}, u32[]{:S(2)}) collective-permute-start(bf16[256,256]{1,0:T(8,128)(2,1)S(1)} %get-tuple-element.25), channel_id=1, source_target_pairs={{0,32},{1,33},{2,34},{3,35},{4,36},{5,37},{6,38},{7,39},{8,40},{9,... | collective-permute-start | bytes 393224 | tf_op jit(solution)/shard_map/ppermute | solution.py:495
  78.6 6.7 %collective-permute-start.6 = (bf16[256,256]{1,0:T(8,128)(2,1)S(1)}, bf16[256,256]{1,0:T(8,128)(2,1)S(1)}, u32[]{:S(2)}, u32[]{:S(2)}) collective-permute-start(bf16[256,256]{1,0:T(8,128)(2,1)S(1)} %get-tuple-element.26), channel_id=1, source_target_pairs={{0,33},{1,32},{2,35},{3,34},{4,37},{5,36},{6,39},{7,38},{8,41},{9,... | collective-permute-start | bytes 393224 | tf_op jit(solution)/shard_map/ppermute | solution.py:496
  82.2 3.3 %collective-permute-start.4 = (bf16[256,256]{1,0:T(8,128)(2,1)S(1)}, bf16[256,256]{1,0:T(8,128)(2,1)S(1)}, u32[]{:S(2)}, u32[]{:S(2)}) collective-permute-start(bf16[256,256]{1,0:T(8,128)(2,1)S(1)} %get-tuple-element.24), channel_id=1, source_target_pairs={{0,1},{1,0},{2,3},{3,2},{4,5},{5,4},{6,7},{7,6},{8,9},{9,8},{10,11... | collective-permute-start | bytes 393224 | tf_op jit(solution)/shard_map/ppermute | solution.py:498

commit v14 on v13

--- a/solution.py
+++ b/solution.py
@@ -1,4 +1,3 @@
-import functools
 import itertools
 import math
 
@@ -361,48 +360,44 @@
     )(arrived, near, far)
 
 
-def tables_kernel(place_ref, steps_ref, own_ref, near_ref, out_ref):
+def tables_kernel(place_ref, steps_ref, coords_ref, out_ref):
     steps = steps_ref[0].astype(jnp.bfloat16)
+    parts = split_coords(coords_ref[...])
     block = 128
-    for side, coords_ref in enumerate((own_ref, near_ref)):
-        parts = split_coords(coords_ref[...])
-        for start in range(0, TILE, block):
-            turns = lax.dot_general(
-                parts[:, start : start + block], steps, OUTER, preferred_element_type=jnp.float32
-            )
-            rows = side * TILE + start
-            out_ref[rows : rows + block, :] = cosine_of_turns(turns).astype(jnp.bfloat16)
-
-
-def message_tables(place, steps, coords, near):
+    for start in range(0, TILE, block):
+        turns = lax.dot_general(
+            parts[:, start : start + block], steps, OUTER, preferred_element_type=jnp.float32
+        )
+        out_ref[start : start + block, :] = cosine_of_turns(turns).astype(jnp.bfloat16)
+
+
+def message_tables(place, steps, coords):
     width = 256
     return pl.pallas_call(
         tables_kernel,
-        out_shape=jax.ShapeDtypeStruct((2 * TILE, ALL_ROWS), jnp.bfloat16),
+        out_shape=jax.ShapeDtypeStruct((TILE, ALL_ROWS), jnp.bfloat16),
         grid_spec=pltpu.PrefetchScalarGridSpec(
             num_scalar_prefetch=1,
             grid=(ALL_ROWS // width,),
             in_specs=[
-                pl.BlockSpec((1, 8, width), lambda t, place: (place[3], 0, t)),
-                pl.BlockSpec((3, TILE), lambda t, place: (0, place[2])),
+                pl.BlockSpec((1, 8, width), lambda t, place: (place[0], 0, t)),
                 pl.BlockSpec((3, TILE), lambda t, place: (0, 0)),
             ],
-            out_specs=pl.BlockSpec((2 * TILE, width), lambda t, place: (0, t)),
+            out_specs=pl.BlockSpec((TILE, width), lambda t, place: (0, t)),
         ),
         compiler_params=pltpu.CompilerParams(vmem_limit_bytes=16 << 20),
         cost_estimate=pl.CostEstimate(
-            flops=32 * TILE * ALL_ROWS, bytes_accessed=TILE * ALL_ROWS * 4, transcendentals=0
+            flops=600 * TILE * ALL_ROWS, bytes_accessed=TILE * ALL_ROWS * 2, transcendentals=0
         ),
-        name="message_tables",
-    )(place, steps, coords, near)
-
-
-def message_kernel(tables_ref, filtered_ref, own_ref, other_ref, *, side):
+    )(place, steps, coords)
+
+
+def message_kernel(tables_ref, filtered_ref, own_ref, other_ref):
     half = TILE // 2
     core = lax.axis_index("wave") % 2
     filtered = filtered_ref[...]
     for held, out_ref in ((core, own_ref), (1 - core, other_ref)):
-        start = pl.multiple_of(held * half, half) + side * TILE
+        start = pl.multiple_of(held * half, half)
         message = jnp.dot(
             tables_ref[pl.ds(start, half), :], filtered, preferred_element_type=jnp.float32
         )
@@ -412,7 +407,7 @@
 def message_halves(tables, filtered, side):
     half = TILE // 2
     return pl.pallas_call(
-        functools.partial(message_kernel, side=side),
+        message_kernel,
         out_shape=(
             jax.ShapeDtypeStruct((half, F), jnp.bfloat16 if side else jnp.float32),
             jax.ShapeDtypeStruct((half, F), jnp.bfloat16),
@@ -475,7 +470,7 @@
     factors, coords, miller = lax.optimization_barrier((factors, coords, miller))
     atom, wave = lax.axis_index("atom"), lax.axis_index("wave")
     core, high = wave % 2, wave // 2
-    place = jnp.stack([wave, core, high, core * 2 + atom // 4 % 2]).astype(jnp.int32)
+    place = jnp.reshape(core * 2 + atom // 4 % 2, (1,)).astype(jnp.int32)
     arrived = exchange(factors, GROUPS_XY)
     weights = grid_weights(miller, filter_weights)
     weights += lax.ppermute(weights, AXES, OUTER_PAIRS)
@@ -487,14 +482,16 @@
     swapped = lax.ppermute(weights[POINTS:], AXES, SWAP)
     filtered = filter_column(shares, weights[:POINTS], swapped)
     filtered, coords = lax.optimization_barrier((filtered, coords))
-    near = lax.dynamic_slice_in_dim(coords, high * TILE, TILE, 1)
-    near = lax.ppermute(near, AXES, LINE_SAME)
+    mine = lax.dynamic_slice_in_dim(coords, high * TILE, TILE, 1)
+    near = lax.ppermute(mine, AXES, LINE_SAME)
     filtered = exchange(filtered, GROUPS_XY).reshape(ALL_ROWS, F)
-    tables = message_tables(place, jnp.asarray(ALL_STEPS), coords, near)
-    far, cross = message_halves(tables, filtered, 1)
+    steps = jnp.asarray(ALL_STEPS)
+    own_tables = message_tables(place, steps, mine)
+    near_tables = message_tables(place, steps, near)
+    far, cross = message_halves(near_tables, filtered, 1)
     far = lax.ppermute(far, AXES, LINE_SAME)
     cross = lax.ppermute(cross, AXES, LINE_CROSS)
-    own, other = message_halves(tables, filtered, 0)
+    own, other = message_halves(own_tables, filtered, 0)
     other = lax.ppermute(other, AXES, SWAP)
     gain = norm_gain.reshape(1, F)
     return update(features, own, other, far, cross, gain, w_in, w_out)

time: 87.6 us -> 87.4 us (level)
  waiting for transfers between devices: 11.6 us -> 10.7 us
    ppermute x1, waiting for transfers between devices: 1.24 us -> 0.01 us  [layer(): near = lax.ppermute(mine, AXES, LINE_SAME)]
    pallas_call x3 -> x4, Pallas kernels: 4.99 us -> 5.37 us  [the longest x2 4.37 us: message_tables(): pl.pallas_call(tables_kernel, out_shape=jax.ShapeDtypeStruct((TILE, ALL_R...]
  transfers between devices with their start and end apart: 10 -> 10, of which waited for: 8 -> 7; matrix products, arithmetic and copies ran while one was open for 0% -> 1% of each run, Pallas kernels for 5% -> 6%
where the time goes in v14:
time: 87.4 us; the launch traced here: 86.7 us
  starting transfers between devices  60.1 us (69%)
  Pallas kernels  14.8 us (17%)
  waiting for transfers between devices  10.7 us (12%)
    all_to_all x3, starting transfers between devices, exchange(): lax.all_to_all(pieces, AXES, split_axis=0, concat_axis=0, tiled=True, axi...  18.6 us
    ppermute x1, starting transfers between devices, layer(): weights += lax.ppermute(weights, AXES, OUTER_PAIRS)  12.5 us
    ppermute x1, starting transfers between devices, layer(): far_weights = lax.ppermute(weights, AXES, INNER_PAIRS)  8.97 us
    pallas_call x1, Pallas kernels, partial_factors(): pl.pallas_call(factors_kernel, out_shape=jax.ShapeDtypeStruct((PLANES, CO...  6.18 us
    ppermute x1, starting transfers between devices, layer(): swapped = lax.ppermute(weights[POINTS:], AXES, SWAP)  6.05 us
    all_to_all x3, waiting for transfers between devices, exchange(): lax.all_to_all(pieces, AXES, split_axis=0, concat_axis=0, tiled=True, axi...  5.84 us
    pallas_call x2, Pallas kernels, message_tables(): pl.pallas_call(tables_kernel, out_shape=jax.ShapeDtypeStruct((TILE, ALL_R...  4.37 us
    ppermute x1, starting transfers between devices, layer(): near = lax.ppermute(mine, AXES, LINE_SAME)  4.14 us
  transfers between devices with their start and end apart: 10, of which 7 were waited for; matrix products, arithmetic and copies ran while one was open for 1% of the time, Pallas kernels for 6%

profile of v14, /device:TPU:1, one launch (start us, length us, event | category | flops | bytes accessed | tf_op | source)
XLA Modules:
  0.0 86.7 jit_solution(11154720406314757914)
XLA Ops:
  0.0 6.2 %factors.1 = bf16[16,160,256]{2,1,0:T(8,128)(2,1)} custom-call(f32[2,8,232]{2,1,0:T(8,128)} %constant.56.clone.steps_ref, s32[3,2048]{1,0:T(4,128)} %coords_ref.1, bf16[2048,256]{1,0:T(8,128)(2,1)} %features_ref.3), custom_call_target="tpu_custom_call" | custom-call | flops 2684354560 | bytes 1048576 | tf_op jit(solution)/shard_map/factors/pallas_call | solution.py:238
  6.2 0.0 copy-start.2
  6.2 0.0 copy-start.5
  6.2 7.7 %all-to-all-start = ((bf16[16,160,256]{2,1,0:T(8,128)(2,1)}), bf16[16,160,256]{2,1,0:T(8,128)(2,1)S(1)}, u32[]{:S(2)}, u32[]{:S(2)}) async-start(bf16[16,160,256]{2,1,0:T(8,128)(2,1)} %factors.1), calls=%async_computation | async-start | bytes 2621440 | tf_op jit(solution)/shard_map/all_to_all | solution.py:459
  13.9 0.0 copy-done.2
  13.9 0.0 copy-done.5
  14.0 0.3 grid_weights.1
  14.3 12.5 %collective-permute-start = (bf16[80,256]{1,0:T(8,128)(2,1)S(1)}, bf16[80,256]{1,0:T(8,128)(2,1)S(1)}, u32[]{:S(2)}, u32[]{:S(2)}) collective-permute-start(bf16[80,256]{1,0:T(8,128)(2,1)S(1)} %grid_weights.1), channel_id=1, source_target_pairs={{0,6},{1,7},{2,4},{3,5},{4,2},{5,3},{6,0},{7,1},{8,14},{9,15},{10,... | collective-permute-start | bytes 122888 | tf_op jit(solution)/shard_map/ppermute | solution.py:476
  26.7 1.7 %collective-permute-done = bf16[80,256]{1,0:T(8,128)(2,1)S(1)} collective-permute-done((bf16[80,256]{1,0:T(8,128)(2,1)S(1)}, bf16[80,256]{1,0:T(8,128)(2,1)S(1)}, u32[]{:S(2)}, u32[]{:S(2)}) %collective-permute-start) | collective-permute-done | bytes 40992 | tf_op jit(solution)/shard_map/ppermute | solution.py:476
  28.4 2.8 %all-to-all-done.arrived_ref = bf16[16,160,256]{2,1,0:T(8,128)(2,1)S(1)} async-done(((bf16[16,160,256]{2,1,0:T(8,128)(2,1)}), bf16[16,160,256]{2,1,0:T(8,128)(2,1)S(1)}, u32[]{:S(2)}, u32[]{:S(2)}) %all-to-all-start) | async-done | bytes 1310752 | tf_op jit(solution)/shard_map/all_to_all | solution.py:459
  31.2 0.8 plane_sum.1
  32.0 7.3 %all-to-all-start.1 = ((bf16[4,80,256]{2,1,0:T(8,128)(2,1)}), bf16[4,80,256]{2,1,0:T(8,128)(2,1)S(1)}, u32[]{:S(2)}, u32[]{:S(2)}) async-start(bf16[4,80,256]{2,1,0:T(8,128)(2,1)} %plane_sum.1), calls=%async_computation.1 | async-start | bytes 327680 | tf_op jit(solution)/shard_map/all_to_all | solution.py:459
  39.3 0.0 copy-start.1
  39.3 9.0 %collective-permute-start.1 = (bf16[80,256]{1,0:T(8,128)(2,1)S(1)}, bf16[80,256]{1,0:T(8,128)(2,1)S(1)}, u32[]{:S(2)}, u32[]{:S(2)}) collective-permute-start(bf16[80,256]{1,0:T(8,128)(2,1)S(1)} %add.24), channel_id=1, source_target_pairs={{0,2},{1,3},{2,0},{3,1},{4,6},{5,7},{6,4},{7,5},{8,10},{9,11},{10,... | collective-permute-start | bytes 122888 | tf_op jit(solution)/shard_map/ppermute | solution.py:477
  48.3 1.4 %collective-permute-done.1 = bf16[80,256]{1,0:T(8,128)(2,1)S(1)} collective-permute-done((bf16[80,256]{1,0:T(8,128)(2,1)S(1)}, bf16[80,256]{1,0:T(8,128)(2,1)S(1)}, u32[]{:S(2)}, u32[]{:S(2)}) %collective-permute-start.1) | collective-permute-done | bytes 40992 | tf_op jit(solution)/shard_map/ppermute | solution.py:477
  49.7 6.0 %collective-permute-start.2 = (bf16[40,256]{1,0:T(8,128)(2,1)S(1)}, bf16[40,256]{1,0:T(8,128)(2,1)S(1)}, u32[]{:S(2)}, u32[]{:S(2)}) collective-permute-start(bf16[40,256]{1,0:T(8,128)(2,1)S(1)} %get-tuple-element.27), channel_id=1, source_target_pairs={{0,1},{1,0},{2,3},{3,2},{4,5},{5,4},{6,7},{7,6},{8,9},{9,8},{10,11... | collective-permute-start | bytes 61448 | tf_op jit(solution)/shard_map/ppermute | solution.py:482
  55.8 0.8 collective-permute-done.2.far_ref
  56.6 0.0 all-to-all-done.1.arrived_ref
  56.6 1.1 %filter_column.1 = bf16[16,80,256]{2,1,0:T(8,128)(2,1)} custom-call(bf16[4,80,256]{2,1,0:T(8,128)(2,1)S(1)} %all-to-all-done.1.arrived_ref, bf16[40,256]{1,0:T(8,128)(2,1)S(1)} %get-tuple-element.28.near_ref, bf16[40,256]{1,0:T(8,128)(2,1)S(1)} %collective-permute-done.2.far_ref), custom_call_target="tpu_custom_call" | custom-call | tf_op jit(solution)/shard_map/filter_column/pallas_call | solution.py:352
  57.7 3.6 %all-to-all-start.2 = ((bf16[16,80,256]{2,1,0:T(8,128)(2,1)}), bf16[16,80,256]{2,1,0:T(8,128)(2,1)S(1)}, u32[]{:S(2)}, u32[]{:S(2)}) async-start(bf16[16,80,256]{2,1,0:T(8,128)(2,1)} %filter_column.1), calls=%async_computation.2 | async-start | bytes 1310720 | tf_op jit(solution)/shard_map/all_to_all | solution.py:459
  61.3 0.7 constant_dynamic-slice_fusion.coords_ref
  62.0 4.1 %collective-permute-start.4 = (s32[3,512]{1,0:T(4,128)S(1)}, s32[3,512]{1,0:T(4,128)S(1)}, u32[]{:S(2)}, u32[]{:S(2)}) collective-permute-start(s32[3,512]{1,0:T(4,128)S(1)} %constant_dynamic-slice_fusion.coords_ref), channel_id=1, source_target_pairs={{0,32},{1,33},{2,34},{3,35},{4,36},{5,37},{6,38},{7,39},{8,40},{9,... | collective-permute-start | bytes 18440 | tf_op jit(solution)/shard_map/ppermute | solution.py:486
  66.2 0.0 copy-done.1
  66.2 2.2 %shard_map.91.tables_ref = bf16[512,1280]{1,0:T(8,128)(2,1)S(1)} custom-call(s32[1]{0:T(128)} %bitcast.place_ref, f32[4,8,1280]{2,1,0:T(8,128)S(1)} %copy-done.1, s32[3,512]{1,0:T(4,128)S(1)} %constant_dynamic-slice_fusion.coords_ref), custom_call_target="tpu_custom_call" | custom-call | flops 393216000 | bytes 1310720 | tf_op jit(solution)/shard_map/pallas_call | solution.py:376
  68.4 0.0 collective-permute-done.4.coords_ref
  68.4 2.2 %shard_map.92.tables_ref = bf16[512,1280]{1,0:T(8,128)(2,1)S(1)} custom-call(s32[1]{0:T(128)} %bitcast.place_ref, f32[4,8,1280]{2,1,0:T(8,128)S(1)} %copy-done.1, s32[3,512]{1,0:T(4,128)S(1)} %collective-permute-done.4.coords_ref), custom_call_target="tpu_custom_call" | custom-call | flops 393216000 | bytes 1310720 | tf_op jit(solution)/shard_map/pallas_call | solution.py:376
  70.6 3.1 %all-to-all-done.2 = bf16[16,80,256]{2,1,0:T(8,128)(2,1)S(1)} async-done(((bf16[16,80,256]{2,1,0:T(8,128)(2,1)}), bf16[16,80,256]{2,1,0:T(8,128)(2,1)S(1)}, u32[]{:S(2)}, u32[]{:S(2)}) %all-to-all-start.2) | async-done | bytes 655392 | tf_op jit(solution)/shard_map/all_to_all | solution.py:459
  73.6 0.5 message_far.1
  74.1 0.0 copy-start
  74.1 0.0 copy-start.3
  74.1 0.0 copy-start.4
  74.2 0.0 copy-start.6
  74.2 4.1 %collective-permute-start.5 = (bf16[256,256]{1,0:T(8,128)(2,1)S(1)}, bf16[256,256]{1,0:T(8,128)(2,1)S(1)}, u32[]{:S(2)}, u32[]{:S(2)}) collective-permute-start(bf16[256,256]{1,0:T(8,128)(2,1)S(1)} %get-tuple-element.25), channel_id=1, source_target_pairs={{0,32},{1,33},{2,34},{3,35},{4,36},{5,37},{6,38},{7,39},{8,40},{9,... | collective-permute-start | bytes 393224 | tf_op jit(solution)/shard_map/ppermute | solution.py:492
  78.3 3.5 %collective-permute-start.6 = (bf16[256,256]{1,0:T(8,128)(2,1)S(1)}, bf16[256,256]{1,0:T(8,128)(2,1)S(1)}, u32[]{:S(2)}, u32[]{:S(2)}) collective-permute-start(bf16[256,256]{1,0:T(8,128)(2,1)S(1)} %get-tuple-element.26), channel_id=1, source_target_pairs={{0,33},{1,32},{2,35},{3,34},{4,37},{5,36},{6,39},{7,38},{8,41},{9,... | collective-permute-start | bytes 393224 | tf_op jit(solution)/shard_map/ppermute | solution.py:493
  81.8 0.5 message_near.1
  82.3 2.3 %collective-permute-start.3 = (bf16[256,256]{1,0:T(8,128)(2,1)S(1)}, bf16[256,256]{1,0:T(8,128)(2,1)S(1)}, u32[]{:S(2)}, u32[]{:S(2)}) collective-permute-start(bf16[256,256]{1,0:T(8,128)(2,1)S(1)} %get-tuple-element.24), channel_id=1, source_target_pairs={{0,1},{1,0},{2,3},{3,2},{4,5},{5,4},{6,7},{7,6},{8,9},{9,8},{10,11... | collective-permute-start | bytes 393224 | tf_op jit(solution)/shard_map/ppermute | solution.py:495
  84.6 0.0 collective-permute-done.5.b_ref
  84.6 0.3 collective-permute-done.6.c_ref
  84.9 0.7 collective-permute-done.3.a_ref
  85.6 0.0 copy-done
  85.6 0.0 copy-done.3
  85.6 0.0 copy-done.4
  85.6 0.0 copy-done.6
  85.6 1.1 %update.1 = bf16[256,256]{1,0:T(8,128)(2,1)} custom-call(bf16[2048,256]{1,0:T(8,128)(2,1)S(1)} %copy-done, f32[256,256]{1,0:T(8,128)S(1)} %get-tuple-element.23.own_ref, bf16[256,256]{1,0:T(8,128)(2,1)S(1)} %collective-permute-done.3.a_ref, bf16[256,256]{1,0:T(8,128)(2,1)S(1)} %collective-permute-done.5.b_ref, ...), custom_call_target="tpu_custom_call" | custom-call | tf_op jit(solution)/shard_map/update/pallas_call | solution.py:448
  (3 shorter events, 0.0 us)
Async XLA Ops:
  6.2 7.8 %copy-start.2 = (f32[512,256]{1,0:T(8,128)S(1)}, f32[512,256]{1,0:T(8,128)}, u32[]{:S(2)}) copy-start(f32[512,256]{1,0:T(8,128)} %weights_ref.1) | copy-start | bytes 1572868
  6.2 7.7 %copy-start.5 = (s32[3,512]{1,0:T(4,128)S(1)}, s32[3,512]{1,0:T(4,128)}, u32[]{:S(2)}) copy-start(s32[3,512]{1,0:T(4,128)} %miller_ref) | copy-start | bytes 18436
  6.2 25.0 %all-to-all-start = ((bf16[16,160,256]{2,1,0:T(8,128)(2,1)}), bf16[16,160,256]{2,1,0:T(8,128)(2,1)S(1)}, u32[]{:S(2)}, u32[]{:S(2)}) async-start(bf16[16,160,256]{2,1,0:T(8,128)(2,1)} %factors.1), calls=%async_computation | async-start | bytes 2621440 | tf_op jit(solution)/shard_map/all_to_all | solution.py:459
  14.3 14.1 %collective-permute-start = (bf16[80,256]{1,0:T(8,128)(2,1)S(1)}, bf16[80,256]{1,0:T(8,128)(2,1)S(1)}, u32[]{:S(2)}, u32[]{:S(2)}) collective-permute-start(bf16[80,256]{1,0:T(8,128)(2,1)S(1)} %grid_weights.1), channel_id=1, source_target_pairs={{0,6},{1,7},{2,4},{3,5},{4,2},{5,3},{6,0},{7,1},{8,14},{9,15},{10,... | collective-permute-start | bytes 122888 | tf_op jit(solution)/shard_map/ppermute | solution.py:476
  32.0 24.6 %all-to-all-start.1 = ((bf16[4,80,256]{2,1,0:T(8,128)(2,1)}), bf16[4,80,256]{2,1,0:T(8,128)(2,1)S(1)}, u32[]{:S(2)}, u32[]{:S(2)}) async-start(bf16[4,80,256]{2,1,0:T(8,128)(2,1)} %plane_sum.1), calls=%async_computation.1 | async-start | bytes 327680 | tf_op jit(solution)/shard_map/all_to_all | solution.py:459
  39.3 26.8 %copy-start.1 = (f32[4,8,1280]{2,1,0:T(8,128)S(1)}, f32[4,8,1280]{2,1,0:T(8,128)}, u32[]{:S(2)}) copy-start(f32[4,8,1280]{2,1,0:T(8,128)} %constant.57.clone.steps_ref) | copy-start | bytes 491524
  39.3 10.4 %collective-permute-start.1 = (bf16[80,256]{1,0:T(8,128)(2,1)S(1)}, bf16[80,256]{1,0:T(8,128)(2,1)S(1)}, u32[]{:S(2)}, u32[]{:S(2)}) collective-permute-start(bf16[80,256]{1,0:T(8,128)(2,1)S(1)} %add.24), channel_id=1, source_target_pairs={{0,2},{1,3},{2,0},{3,1},{4,6},{5,7},{6,4},{7,5},{8,10},{9,11},{10,... | collective-permute-start | bytes 122888 | tf_op jit(solution)/shard_map/ppermute | solution.py:477
  49.7 6.9 %collective-permute-start.2 = (bf16[40,256]{1,0:T(8,128)(2,1)S(1)}, bf16[40,256]{1,0:T(8,128)(2,1)S(1)}, u32[]{:S(2)}, u32[]{:S(2)}) collective-permute-start(bf16[40,256]{1,0:T(8,128)(2,1)S(1)} %get-tuple-element.27), channel_id=1, source_target_pairs={{0,1},{1,0},{2,3},{3,2},{4,5},{5,4},{6,7},{7,6},{8,9},{9,8},{10,11... | collective-permute-start | bytes 61448 | tf_op jit(solution)/shard_map/ppermute | solution.py:482
  57.7 16.0 %all-to-all-start.2 = ((bf16[16,80,256]{2,1,0:T(8,128)(2,1)}), bf16[16,80,256]{2,1,0:T(8,128)(2,1)S(1)}, u32[]{:S(2)}, u32[]{:S(2)}) async-start(bf16[16,80,256]{2,1,0:T(8,128)(2,1)} %filter_column.1), calls=%async_computation.2 | async-start | bytes 1310720 | tf_op jit(solution)/shard_map/all_to_all | solution.py:459
  62.0 6.4 %collective-permute-start.4 = (s32[3,512]{1,0:T(4,128)S(1)}, s32[3,512]{1,0:T(4,128)S(1)}, u32[]{:S(2)}, u32[]{:S(2)}) collective-permute-start(s32[3,512]{1,0:T(4,128)S(1)} %constant_dynamic-slice_fusion.coords_ref), channel_id=1, source_target_pairs={{0,32},{1,33},{2,34},{3,35},{4,36},{5,37},{6,38},{7,39},{8,40},{9,... | collective-permute-start | bytes 18440 | tf_op jit(solution)/shard_map/ppermute | solution.py:486
  74.1 11.5 %copy-start = (bf16[2048,256]{1,0:T(8,128)(2,1)S(1)}, bf16[2048,256]{1,0:T(8,128)(2,1)}, u32[]{:S(2)}) copy-start(bf16[2048,256]{1,0:T(8,128)(2,1)} %features_ref.3) | copy-start | bytes 3145732
  74.1 11.5 %copy-start.3 = (bf16[256,256]{1,0:T(8,128)(2,1)S(1)}, bf16[256,256]{1,0:T(8,128)(2,1)}, u32[]{:S(2)}) copy-start(bf16[256,256]{1,0:T(8,128)(2,1)} %w_in_ref.1) | copy-start | bytes 393220
  74.1 11.4 %copy-start.4 = (bf16[256,256]{1,0:T(8,128)(2,1)S(1)}, bf16[256,256]{1,0:T(8,128)(2,1)}, u32[]{:S(2)}) copy-start(bf16[256,256]{1,0:T(8,128)(2,1)} %w_out_ref.1) | copy-start | bytes 393220
  74.2 11.4 %copy-start.6 = (f32[256]{0:T(256)S(1)}, f32[256]{0:T(256)}, u32[]{:S(2)}) copy-start(f32[256]{0:T(256)} %param.13) | copy-start | bytes 3076
  74.2 10.5 %collective-permute-start.5 = (bf16[256,256]{1,0:T(8,128)(2,1)S(1)}, bf16[256,256]{1,0:T(8,128)(2,1)S(1)}, u32[]{:S(2)}, u32[]{:S(2)}) collective-permute-start(bf16[256,256]{1,0:T(8,128)(2,1)S(1)} %get-tuple-element.25), channel_id=1, source_target_pairs={{0,32},{1,33},{2,34},{3,35},{4,36},{5,37},{6,38},{7,39},{8,40},{9,... | collective-permute-start | bytes 393224 | tf_op jit(solution)/shard_map/ppermute | solution.py:492
  78.3 6.7 %collective-permute-start.6 = (bf16[256,256]{1,0:T(8,128)(2,1)S(1)}, bf16[256,256]{1,0:T(8,128)(2,1)S(1)}, u32[]{:S(2)}, u32[]{:S(2)}) collective-permute-start(bf16[256,256]{1,0:T(8,128)(2,1)S(1)} %get-tuple-element.26), channel_id=1, source_target_pairs={{0,33},{1,32},{2,35},{3,34},{4,37},{5,36},{6,39},{7,38},{8,41},{9,... | collective-permute-start | bytes 393224 | tf_op jit(solution)/shard_map/ppermute | solution.py:493
  82.3 3.3 %collective-permute-start.3 = (bf16[256,256]{1,0:T(8,128)(2,1)S(1)}, bf16[256,256]{1,0:T(8,128)(2,1)S(1)}, u32[]{:S(2)}, u32[]{:S(2)}) collective-permute-start(bf16[256,256]{1,0:T(8,128)(2,1)S(1)} %get-tuple-element.24), channel_id=1, source_target_pairs={{0,1},{1,0},{2,3},{3,2},{4,5},{5,4},{6,7},{7,6},{8,9},{9,8},{10,11... | collective-permute-start | bytes 393224 | tf_op jit(solution)/shard_map/ppermute | solution.py:495
